TPU v7x, 128 devices: a whole 4x4x4 slice. The times are simulated.
128 devices in a mesh: tile: 16 (over z, y), band: 8 (over x, core).
Axes of the slice: x: 4, y: 4, z: 4, core: 2. Of those that a mesh axis runs over, the one named last changes fastest.
Arguments:
- points: float32 [32768, 3, 128], P(('tile', 'band')), may hold values from -6 to 6
- normals: float32 [32768, 3, 128], P(('tile', 'band')), may hold values from -4 to 4
- poses: float32 [6, 1024], P(None, ('tile', 'band')), may hold values from -4 to 4
- directions: float32 [2, 6, 1024], P(None, None, ('tile', 'band')), may hold values from -6 to 6
- local_pairs: int32 [2, 32768], P(None, ('tile', 'band')), may hold values from 0 to 255
- local_maps: int32 [32768, 128], P(('tile', 'band')), may hold values from 0 to 127
- remote_src: int32 [128, 1024], P(('tile', 'band')), may hold values from 0 to 255
- remote_maps: int32 [128, 1024, 128], P(('tile', 'band')), may hold values from 0 to 127
- remote_dst: int32 [128, 1024], P(('tile', 'band')), may hold values from 0 to 255
- counts: int32 [128, 128], P(('tile', 'band')), may hold values from 4 to 8, as said below
Outputs:
- gradient: float32 [6, 1024], P(None, ('tile', 'band'))
- hess_products: float32 [2, 6, 1024], P(None, None, ('tile', 'band'))
Inputs may be any that keep to these rules, and one draw needn't show every extreme that they name: `counts`: in every row some device pair uses all 8 slots.
All inputs are finite; a program needn't handle non-finite values.
Results may differ from a plain program's by a relative error of at most 0.0003.
Values sent between devices are 32-bit elements; how exact they have to be, the bound alone decides.
A program may use at most 64 MiB of HBM per device.

v0:
```python
import math

import jax
import jax.numpy as jnp
from jax import lax
from jax.sharding import PartitionSpec as P

BF = 32


def rotations(poses):
    half_angle = poses[0:3] * 0.5
    inverse = 1.0 / jnp.sqrt(
        1.0
        + half_angle[0] * half_angle[0]
        + half_angle[1] * half_angle[1]
        + half_angle[2] * half_angle[2]
    )
    quat_x = half_angle[0] * inverse
    quat_y = half_angle[1] * inverse
    quat_z = half_angle[2] * inverse
    rotation = [
        [
            1.0 - 2.0 * (quat_y * quat_y + quat_z * quat_z),
            2.0 * (quat_x * quat_y - inverse * quat_z),
            2.0 * (quat_x * quat_z + inverse * quat_y),
        ],
        [
            2.0 * (quat_x * quat_y + inverse * quat_z),
            1.0 - 2.0 * (quat_x * quat_x + quat_z * quat_z),
            2.0 * (quat_y * quat_z - inverse * quat_x),
        ],
        [
            2.0 * (quat_x * quat_z - inverse * quat_y),
            2.0 * (quat_y * quat_z + inverse * quat_x),
            1.0 - 2.0 * (quat_x * quat_x + quat_y * quat_y),
        ],
    ]
    return (rotation, poses[3:6])


def to_world(points, normals, poses, per_pose):
    rotation, translation = rotations(poses)

    def spread(values):
        return jnp.repeat(values, per_pose)[:, None]

    world_rows = []
    normal_rows = []
    for i in range(3):
        coeffs = [spread(rotation[i][j]) for j in range(3)]
        world_rows.append(
            coeffs[0] * points[:, 0]
            + coeffs[1] * points[:, 1]
            + coeffs[2] * points[:, 2]
            + spread(translation[i])
        )
        normal_rows.append(
            coeffs[0] * normals[:, 0] + coeffs[1] * normals[:, 1] + coeffs[2] * normals[:, 2]
        )
    return (jnp.stack(world_rows, axis=1), jnp.stack(normal_rows, axis=1))


def cross_rows(left, right):
    return [
        left[:, 1] * right[:, 2] - left[:, 2] * right[:, 1],
        left[:, 2] * right[:, 0] - left[:, 0] * right[:, 2],
        left[:, 0] * right[:, 1] - left[:, 1] * right[:, 0],
    ]


def pick_points(world_pts, normal_pts, point_maps):
    stacked = jnp.concatenate([world_pts, normal_pts], axis=1)
    pair_count = stacked.shape[0]
    point_count = stacked.shape[2]
    per_step = math.gcd(pair_count, 64)
    positions = jnp.arange(point_count, dtype=jnp.int32)

    def select_block(operands):
        values, indices = operands
        selector = (indices[:, :, None] == positions[None, None, :]).astype(jnp.float32)
        return jnp.einsum("gcm,gkm->gck", values, selector, precision=lax.Precision.HIGHEST)

    picked = lax.map(
        select_block,
        (
            stacked.reshape(pair_count // per_step, per_step, 6, point_count),
            point_maps.reshape(pair_count // per_step, per_step, point_count),
        ),
    )
    picked = picked.reshape(pair_count, 6, point_count)
    return (picked[:, 0:3], picked[:, 3:6])


def pair_terms(world_a, world_b, normal_b, dirs_a, dirs_b, valid_mask, blocks_frag):
    count = world_a.shape[2]
    offset = world_a - world_b
    residual = (
        normal_b[:, 0] * offset[:, 0]
        + normal_b[:, 1] * offset[:, 1]
        + normal_b[:, 2] * offset[:, 2]
    ) * valid_mask[:, None]
    normal_list = [normal_b[:, 0], normal_b[:, 1], normal_b[:, 2]]
    jac_a = jnp.stack(cross_rows(world_a, normal_b) + normal_list, axis=1)
    jac_b = -jnp.stack(cross_rows(world_b, normal_b) + normal_list, axis=1)
    grad_scale = 1.0 / count
    hess_scale = 1.0 / (count * blocks_frag)
    parts_a = [jnp.sum(residual[:, None] * jac_a, axis=2) * grad_scale]
    parts_b = [jnp.sum(residual[:, None] * jac_b, axis=2) * grad_scale]
    for v in range(2):
        along_dir = (
            jnp.sum(jac_a * dirs_a[:, 6 * v : 6 * v + 6, None], axis=1)
            + jnp.sum(jac_b * dirs_b[:, 6 * v : 6 * v + 6, None], axis=1)
        ) * valid_mask[:, None]
        parts_a.append(jnp.sum(along_dir[:, None] * jac_a, axis=2) * hess_scale)
        parts_b.append(jnp.sum(along_dir[:, None] * jac_b, axis=2) * hess_scale)
    return (jnp.concatenate(parts_a, axis=1), jnp.concatenate(parts_b, axis=1))


def frag_sums(blocks, terms, frag_count):
    onehot = (blocks[:, None] // BF == jnp.arange(frag_count, dtype=jnp.int32)[None, :]).astype(
        jnp.float32
    )
    return jnp.dot(onehot.T, terms, precision=lax.Precision.HIGHEST)


def local(
    points,
    normals,
    poses,
    directions,
    local_pairs,
    local_maps,
    remote_src,
    remote_maps,
    remote_dst,
    counts,
):
    n_tile = lax.axis_size("tile")
    n_band = lax.axis_size("band")
    devices = n_tile * n_band
    frag_count = poses.shape[1]
    world_pts, normal_pts = to_world(points, normals, poses, BF)
    frag_dirs = directions.reshape(12, frag_count).T
    send_blocks = remote_dst[0]
    send_frags = send_blocks // BF
    cargo_rows = jnp.concatenate([world_pts[send_blocks], normal_pts[send_blocks]], axis=1)
    extras = frag_dirs[send_frags]
    slot_count = cargo_rows.shape[0]
    per_peer = slot_count // devices
    arrived_rows, arrived_extra = (
        lax.all_to_all(cargo_rows, ("tile", "band"), split_axis=0, concat_axis=0, tiled=True),
        lax.all_to_all(extras, ("tile", "band"), split_axis=0, concat_axis=0, tiled=True),
    )
    peer_world = arrived_rows[:, 0:3]
    peer_normal = arrived_rows[:, 3:6]
    world_b, normal_b = pick_points(
        world_pts[local_pairs[1]], normal_pts[local_pairs[1]], local_maps
    )
    local_ones = jnp.ones((local_pairs.shape[1],), jnp.float32)
    local_a, local_b = pair_terms(
        world_pts[local_pairs[0]],
        world_b,
        normal_b,
        frag_dirs[local_pairs[0] // BF],
        frag_dirs[local_pairs[1] // BF],
        local_ones,
        BF,
    )
    source_blocks = remote_src[0]
    used_slots = counts[0]
    valid_mask = (
        (jnp.arange(per_peer, dtype=jnp.int32)[None, :] < used_slots[:, None])
        .astype(jnp.float32)
        .reshape(-1)
    )
    world_b, normal_b = pick_points(peer_world, peer_normal, remote_maps[0])
    remote_a, remote_b = pair_terms(
        world_pts[source_blocks],
        world_b,
        normal_b,
        frag_dirs[source_blocks // BF],
        arrived_extra,
        valid_mask,
        BF,
    )
    returned = lax.all_to_all(remote_b, ("tile", "band"), split_axis=0, concat_axis=0, tiled=True)
    totals = frag_sums(local_pairs[0], local_a, frag_count) + frag_sums(
        local_pairs[1], local_b, frag_count
    )
    totals = (
        totals
        + frag_sums(source_blocks, remote_a, frag_count)
        + frag_sums(send_blocks, returned, frag_count)
    )
    gradient = totals[:, 0:6].T
    hess_products = totals[:, 6:18].T.reshape(2, 6, frag_count)
    return (gradient, hess_products)


def solution(mesh):
    placed = (
        P(("tile", "band"), None, None),
        P(("tile", "band"), None, None),
        P(None, ("tile", "band")),
        P(None, None, ("tile", "band")),
        P(None, ("tile", "band")),
        P(("tile", "band"), None),
        P(("tile", "band"), None),
        P(("tile", "band"), None, None),
        P(("tile", "band"), None),
        P(("tile", "band"), None),
    )
    return jax.shard_map(
        local,
        mesh=mesh,
        in_specs=placed,
        out_specs=(P(None, ("tile", "band")), P(None, None, ("tile", "band"))),
        check_vma=False,
    )
```

profile of v0, /device:TPU:1, one launch (start us, length us, event | category | flops | bytes accessed | tf_op | source)
XLA Modules:
  0.0 329.3 jit_solution(14190310749413842944)
XLA Ops:
  0.7 0.8 copy.154
  2.3 4.0 %gather_fusion.9 = f32[1024,12]{1,0:T(8,128)} fusion(f32[8,12]{1,0:T(8,128)S(1)} %bitcast.193, s32[1024]{0:T(1024)S(1)} %broadcast_clamp_fusion), kind=kCustom, calls=%fused_computation.9 | custom fusion | bytes 102400 | tf_op jit(solution)/shard_map/gather | solution.py:148
  6.3 12.0 %all-to-all-start.1 = ((f32[128,8,12]{2,1,0:T(8,128)}), f32[128,8,12]{2,1,0:T(8,128)}, u32[]{:S(2)}, u32[]{:S(2)}) async-start(f32[128,8,12]{2,1,0:T(8,128)} %bitcast.31), calls=%async_computation.1 | async-start | bytes 1048576 | tf_op jit(solution)/shard_map/all_to_all | solution.py:153
  22.4 1.0 gather_fusion.1
  23.4 1.0 gather_fusion
  24.4 1.2 pad_maximum_fusion.6
  25.6 22.4 %while.22 = (s32[]{:T(128)}, f32[4,64,6,128]{3,2,1,0:T(8,128)S(1)}, f32[4,64,6,128]{3,2,1,0:T(8,128)}, s32[4,64,128]{2,1,0:T(8,128)}, s32[]{:T(128)}) while((s32[]{:T(128)}, f32[4,64,6,128]{3,2,1,0:T(8,128)S(1)}, f32[4,64,6,128]{3,2,1,0:T(8,128)}, s32[4,64,128]{2,1,0:T(8,128)}, s32[]{:T(128)}) %tuple.107), condition=%wide.region_1.2_spmd.clone, body=%wide.region_0.1_spmd.clone.sunk | while | flops 76546048 | bytes 623689 | solution.py:84
  25.6 0.8 dynamic-slice_bitcast_fusion.4
  26.3 4.8 %fusion.77 = f32[4,64,6,128]{3,2,1,0:T(8,128)S(1)} fusion(f32[4,64,6,128]{3,2,1,0:T(8,128)S(1)} %get-tuple-element.244, s32[]{:T(128)S(6)} %copy.176, s32[64,128]{1,0:T(8,128)S(1)} %dynamic-slice_bitcast_fusion.4, f32[4,64,6,128]{3,2,1,0:T(8,128)} %get-tuple-element.250), kind=kOutput, calls=%fused_computation.16.clone.1 | convolution fusion | flops 76546048 | bytes 558080 | tf_op jit(solution)/shard_map/while/body/eval_jaxpr/gcm,gkm->gck/dot_general | solution.py:82
  31.1 0.8 dynamic-slice_bitcast_fusion.4
  31.9 4.8 %fusion.77 = f32[4,64,6,128]{3,2,1,0:T(8,128)S(1)} fusion(f32[4,64,6,128]{3,2,1,0:T(8,128)S(1)} %get-tuple-element.244, s32[]{:T(128)S(6)} %copy.176, s32[64,128]{1,0:T(8,128)S(1)} %dynamic-slice_bitcast_fusion.4, f32[4,64,6,128]{3,2,1,0:T(8,128)} %get-tuple-element.250), kind=kOutput, calls=%fused_computation.16.clone.1 | convolution fusion | flops 76546048 | bytes 558080 | tf_op jit(solution)/shard_map/while/body/eval_jaxpr/gcm,gkm->gck/dot_general | solution.py:82
  36.7 0.8 dynamic-slice_bitcast_fusion.4
  37.5 4.8 %fusion.77 = f32[4,64,6,128]{3,2,1,0:T(8,128)S(1)} fusion(f32[4,64,6,128]{3,2,1,0:T(8,128)S(1)} %get-tuple-element.244, s32[]{:T(128)S(6)} %copy.176, s32[64,128]{1,0:T(8,128)S(1)} %dynamic-slice_bitcast_fusion.4, f32[4,64,6,128]{3,2,1,0:T(8,128)} %get-tuple-element.250), kind=kOutput, calls=%fused_computation.16.clone.1 | convolution fusion | flops 76546048 | bytes 558080 | tf_op jit(solution)/shard_map/while/body/eval_jaxpr/gcm,gkm->gck/dot_general | solution.py:82
  42.3 0.8 dynamic-slice_bitcast_fusion.4
  43.1 4.8 %fusion.77 = f32[4,64,6,128]{3,2,1,0:T(8,128)S(1)} fusion(f32[4,64,6,128]{3,2,1,0:T(8,128)S(1)} %get-tuple-element.244, s32[]{:T(128)S(6)} %copy.176, s32[64,128]{1,0:T(8,128)S(1)} %dynamic-slice_bitcast_fusion.4, f32[4,64,6,128]{3,2,1,0:T(8,128)} %get-tuple-element.250), kind=kOutput, calls=%fused_computation.16.clone.1 | convolution fusion | flops 76546048 | bytes 558080 | tf_op jit(solution)/shard_map/while/body/eval_jaxpr/gcm,gkm->gck/dot_general | solution.py:82
  48.0 1.0 gather_fusion.2
  49.0 1.2 fusion.66
  50.2 1.8 multiply_subtract_fusion.11
  51.9 3.6 %gather_fusion.6 = f32[1024,3,128]{2,1,0:T(4,128)S(1)} fusion(f32[256,3,128]{2,1,0:T(4,128)S(1)} %copy.151, s32[1024]{0:T(1024)S(1)} %broadcast_clamp_fusion.3), kind=kCustom, calls=%fused_computation.6 | custom fusion | bytes 3149824 | tf_op jit(solution)/shard_map/gather | solution.py:147
  55.5 8.0 %gather_fusion.5 = f32[1024,3,128]{2,1,0:T(4,128)} fusion(f32[256,3,128]{2,1,0:T(4,128)S(1)} %copy.150, s32[1024]{0:T(1024)S(1)} %broadcast_clamp_fusion.3), kind=kCustom, calls=%fused_computation.5 | custom fusion | bytes 3149824 | tf_op jit(solution)/shard_map/gather | solution.py:147
  63.5 5.8 %multiply_subtract_fusion.8 = (f32[256,1,128]{2,1,0:T(1,128)S(1)}, f32[256,1,128]{2,1,0:T(1,128)S(1)}, f32[256,1,128]{2,1,0:T(1,128)S(1)}, f32[256,1,128]{2,1,0:T(1,128)}) fusion(f32[256,6,128]{2,1,0:T(8,128)} %bitcast.202, f32[256,3,128]{2,1,0:T(4,128)} %get-tuple-element.148), kind=kLoop, calls=%fused_computation.94 | loop fusion | flops 458752 | bytes 1703936 | tf_op jit(solution)/shard_map/sub | solution.py:66
  69.3 1.3 gather_fusion.4
  70.6 1.3 gather_fusion.3
  72.0 1.4 fusion.69
  73.4 6.2 %multiply_reduce_fusion.19 = (f32[256,6]{1,0:T(8,128)}, f32[256,128]{1,0:T(8,128)S(1)}, f32[256,128]{1,0:T(8,128)S(1)}, f32[256,128]{1,0:T(8,128)S(1)}) fusion(f32[256,128]{1,0:T(8,128)} %bitcast.205, f32[256,3,128]{2,1,0:T(4,128)S(1)} %copy-done.2, f32[256,1,128]{2,1,0:T(1,128)} %get-tuple-element.141, f32[256,1,128]{2,1,0:T(1,128)} %get-tuple-element.142, ...), kind=kLoop, calls=%fused_computation.62 | loop fusion | flops 2849280 | bytes 1728512 | tf_op jit(solution)/shard_map/reduce_sum | solution.py:108
  79.6 3.0 multiply_reduce_fusion.12
  82.7 2.2 multiply_reduce_fusion.16
  85.1 2.8 pad_maximum_fusion.2
  88.5 3.6 %gather_fusion.7 = f32[1024,3,128]{2,1,0:T(4,128)S(1)} fusion(f32[256,3,128]{2,1,0:T(4,128)S(1)} %copy.150, s32[1024]{0:T(1024)S(1)} %broadcast_clamp_fusion.2), kind=kCustom, calls=%fused_computation.7 | custom fusion | bytes 3149824 | tf_op jit(solution)/shard_map/gather | solution.py:179
  92.1 2.8 gather_fusion.8
  94.9 10.2 %all-to-all-start = ((f32[1024,6,128]{2,1,0:T(8,128)}), f32[1024,6,128]{2,1,0:T(8,128)}, u32[]{:S(2)}, u32[]{:S(2)}) async-start(f32[1024,6,128]{2,1,0:T(8,128)} %pad_maximum_fusion.2), calls=%async_computation | async-start | bytes 8388608 | tf_op jit(solution)/shard_map/all_to_all | solution.py:152
  105.9 1.0 fusion.68
  106.9 2.3 fusion.67
  109.2 48.6 %all-to-all-done = f32[1024,6,128]{2,1,0:T(8,128)} async-done(((f32[1024,6,128]{2,1,0:T(8,128)}), f32[1024,6,128]{2,1,0:T(8,128)}, u32[]{:S(2)}, u32[]{:S(2)}) %all-to-all-start) | async-done | bytes 3145760 | tf_op jit(solution)/shard_map/all_to_all | solution.py:152
  157.8 94.9 %while.23 = (s32[]{:T(128)}, f32[16,64,6,128]{3,2,1,0:T(8,128)}, f32[16,64,6,128]{3,2,1,0:T(8,128)}, s32[16,64,128]{2,1,0:T(8,128)}, s32[]{:T(128)}) while((s32[]{:T(128)}, f32[16,64,6,128]{3,2,1,0:T(8,128)}, f32[16,64,6,128]{3,2,1,0:T(8,128)}, s32[16,64,128]{2,1,0:T(8,128)}, s32[]{:T(128)}) %tuple.108), condition=%wide.region_13.14_spmd.clone, body=%wide.region_12.13_spmd.clone.sunk | while | flops 76546048 | bytes 623689 | solution.py:84
  157.8 0.8 dynamic-slice_bitcast_fusion.5
  158.6 5.2 %fusion.79 = f32[16,64,6,128]{3,2,1,0:T(8,128)} fusion(f32[16,64,6,128]{3,2,1,0:T(8,128)} %get-tuple-element.259, s32[]{:T(128)S(6)} %copy.182, s32[64,128]{1,0:T(8,128)S(1)} %dynamic-slice_bitcast_fusion.5, f32[16,64,6,128]{3,2,1,0:T(8,128)} %get-tuple-element.265), kind=kOutput, calls=%fused_computation.25.clone.1 | convolution fusion | flops 76546048 | bytes 558080 | tf_op jit(solution)/shard_map/while/body/eval_jaxpr/gcm,gkm->gck/dot_general | solution.py:82
  163.7 0.8 dynamic-slice_bitcast_fusion.5
  164.5 5.2 %fusion.79 = f32[16,64,6,128]{3,2,1,0:T(8,128)} fusion(f32[16,64,6,128]{3,2,1,0:T(8,128)} %get-tuple-element.259, s32[]{:T(128)S(6)} %copy.182, s32[64,128]{1,0:T(8,128)S(1)} %dynamic-slice_bitcast_fusion.5, f32[16,64,6,128]{3,2,1,0:T(8,128)} %get-tuple-element.265), kind=kOutput, calls=%fused_computation.25.clone.1 | convolution fusion | flops 76546048 | bytes 558080 | tf_op jit(solution)/shard_map/while/body/eval_jaxpr/gcm,gkm->gck/dot_general | solution.py:82
  170.4 5.2 %fusion.79 = f32[16,64,6,128]{3,2,1,0:T(8,128)} fusion(f32[16,64,6,128]{3,2,1,0:T(8,128)} %get-tuple-element.259, s32[]{:T(128)S(6)} %copy.182, s32[64,128]{1,0:T(8,128)S(1)} %dynamic-slice_bitcast_fusion.5, f32[16,64,6,128]{3,2,1,0:T(8,128)} %get-tuple-element.265), kind=kOutput, calls=%fused_computation.25.clone.1 | convolution fusion | flops 76546048 | bytes 558080 | tf_op jit(solution)/shard_map/while/body/eval_jaxpr/gcm,gkm->gck/dot_general | solution.py:82
  176.4 5.2 %fusion.79 = f32[16,64,6,128]{3,2,1,0:T(8,128)} fusion(f32[16,64,6,128]{3,2,1,0:T(8,128)} %get-tuple-element.259, s32[]{:T(128)S(6)} %copy.182, s32[64,128]{1,0:T(8,128)S(1)} %dynamic-slice_bitcast_fusion.5, f32[16,64,6,128]{3,2,1,0:T(8,128)} %get-tuple-element.265), kind=kOutput, calls=%fused_computation.25.clone.1 | convolution fusion | flops 76546048 | bytes 558080 | tf_op jit(solution)/shard_map/while/body/eval_jaxpr/gcm,gkm->gck/dot_general | solution.py:82
  182.3 5.2 %fusion.79 = f32[16,64,6,128]{3,2,1,0:T(8,128)} fusion(f32[16,64,6,128]{3,2,1,0:T(8,128)} %get-tuple-element.259, s32[]{:T(128)S(6)} %copy.182, s32[64,128]{1,0:T(8,128)S(1)} %dynamic-slice_bitcast_fusion.5, f32[16,64,6,128]{3,2,1,0:T(8,128)} %get-tuple-element.265), kind=kOutput, calls=%fused_computation.25.clone.1 | convolution fusion | flops 76546048 | bytes 558080 | tf_op jit(solution)/shard_map/while/body/eval_jaxpr/gcm,gkm->gck/dot_general | solution.py:82
  188.2 5.2 %fusion.79 = f32[16,64,6,128]{3,2,1,0:T(8,128)} fusion(f32[16,64,6,128]{3,2,1,0:T(8,128)} %get-tuple-element.259, s32[]{:T(128)S(6)} %copy.182, s32[64,128]{1,0:T(8,128)S(1)} %dynamic-slice_bitcast_fusion.5, f32[16,64,6,128]{3,2,1,0:T(8,128)} %get-tuple-element.265), kind=kOutput, calls=%fused_computation.25.clone.1 | convolution fusion | flops 76546048 | bytes 558080 | tf_op jit(solution)/shard_map/while/body/eval_jaxpr/gcm,gkm->gck/dot_general | solution.py:82
  194.2 5.2 %fusion.79 = f32[16,64,6,128]{3,2,1,0:T(8,128)} fusion(f32[16,64,6,128]{3,2,1,0:T(8,128)} %get-tuple-element.259, s32[]{:T(128)S(6)} %copy.182, s32[64,128]{1,0:T(8,128)S(1)} %dynamic-slice_bitcast_fusion.5, f32[16,64,6,128]{3,2,1,0:T(8,128)} %get-tuple-element.265), kind=kOutput, calls=%fused_computation.25.clone.1 | convolution fusion | flops 76546048 | bytes 558080 | tf_op jit(solution)/shard_map/while/body/eval_jaxpr/gcm,gkm->gck/dot_general | solution.py:82
  200.1 5.2 %fusion.79 = f32[16,64,6,128]{3,2,1,0:T(8,128)} fusion(f32[16,64,6,128]{3,2,1,0:T(8,128)} %get-tuple-element.259, s32[]{:T(128)S(6)} %copy.182, s32[64,128]{1,0:T(8,128)S(1)} %dynamic-slice_bitcast_fusion.5, f32[16,64,6,128]{3,2,1,0:T(8,128)} %get-tuple-element.265), kind=kOutput, calls=%fused_computation.25.clone.1 | convolution fusion | flops 76546048 | bytes 558080 | tf_op jit(solution)/shard_map/while/body/eval_jaxpr/gcm,gkm->gck/dot_general | solution.py:82
  206.1 5.2 %fusion.79 = f32[16,64,6,128]{3,2,1,0:T(8,128)} fusion(f32[16,64,6,128]{3,2,1,0:T(8,128)} %get-tuple-element.259, s32[]{:T(128)S(6)} %copy.182, s32[64,128]{1,0:T(8,128)S(1)} %dynamic-slice_bitcast_fusion.5, f32[16,64,6,128]{3,2,1,0:T(8,128)} %get-tuple-element.265), kind=kOutput, calls=%fused_computation.25.clone.1 | convolution fusion | flops 76546048 | bytes 558080 | tf_op jit(solution)/shard_map/while/body/eval_jaxpr/gcm,gkm->gck/dot_general | solution.py:82
  212.0 5.2 %fusion.79 = f32[16,64,6,128]{3,2,1,0:T(8,128)} fusion(f32[16,64,6,128]{3,2,1,0:T(8,128)} %get-tuple-element.259, s32[]{:T(128)S(6)} %copy.182, s32[64,128]{1,0:T(8,128)S(1)} %dynamic-slice_bitcast_fusion.5, f32[16,64,6,128]{3,2,1,0:T(8,128)} %get-tuple-element.265), kind=kOutput, calls=%fused_computation.25.clone.1 | convolution fusion | flops 76546048 | bytes 558080 | tf_op jit(solution)/shard_map/while/body/eval_jaxpr/gcm,gkm->gck/dot_general | solution.py:82
  217.9 5.2 %fusion.79 = f32[16,64,6,128]{3,2,1,0:T(8,128)} fusion(f32[16,64,6,128]{3,2,1,0:T(8,128)} %get-tuple-element.259, s32[]{:T(128)S(6)} %copy.182, s32[64,128]{1,0:T(8,128)S(1)} %dynamic-slice_bitcast_fusion.5, f32[16,64,6,128]{3,2,1,0:T(8,128)} %get-tuple-element.265), kind=kOutput, calls=%fused_computation.25.clone.1 | convolution fusion | flops 76546048 | bytes 558080 | tf_op jit(solution)/shard_map/while/body/eval_jaxpr/gcm,gkm->gck/dot_general | solution.py:82
  223.9 5.2 %fusion.79 = f32[16,64,6,128]{3,2,1,0:T(8,128)} fusion(f32[16,64,6,128]{3,2,1,0:T(8,128)} %get-tuple-element.259, s32[]{:T(128)S(6)} %copy.182, s32[64,128]{1,0:T(8,128)S(1)} %dynamic-slice_bitcast_fusion.5, f32[16,64,6,128]{3,2,1,0:T(8,128)} %get-tuple-element.265), kind=kOutput, calls=%fused_computation.25.clone.1 | convolution fusion | flops 76546048 | bytes 558080 | tf_op jit(solution)/shard_map/while/body/eval_jaxpr/gcm,gkm->gck/dot_general | solution.py:82
  229.8 5.2 %fusion.79 = f32[16,64,6,128]{3,2,1,0:T(8,128)} fusion(f32[16,64,6,128]{3,2,1,0:T(8,128)} %get-tuple-element.259, s32[]{:T(128)S(6)} %copy.182, s32[64,128]{1,0:T(8,128)S(1)} %dynamic-slice_bitcast_fusion.5, f32[16,64,6,128]{3,2,1,0:T(8,128)} %get-tuple-element.265), kind=kOutput, calls=%fused_computation.25.clone.1 | convolution fusion | flops 76546048 | bytes 558080 | tf_op jit(solution)/shard_map/while/body/eval_jaxpr/gcm,gkm->gck/dot_general | solution.py:82
  235.7 5.2 %fusion.79 = f32[16,64,6,128]{3,2,1,0:T(8,128)} fusion(f32[16,64,6,128]{3,2,1,0:T(8,128)} %get-tuple-element.259, s32[]{:T(128)S(6)} %copy.182, s32[64,128]{1,0:T(8,128)S(1)} %dynamic-slice_bitcast_fusion.5, f32[16,64,6,128]{3,2,1,0:T(8,128)} %get-tuple-element.265), kind=kOutput, calls=%fused_computation.25.clone.1 | convolution fusion | flops 76546048 | bytes 558080 | tf_op jit(solution)/shard_map/while/body/eval_jaxpr/gcm,gkm->gck/dot_general | solution.py:82
  241.6 5.2 %fusion.79 = f32[16,64,6,128]{3,2,1,0:T(8,128)} fusion(f32[16,64,6,128]{3,2,1,0:T(8,128)} %get-tuple-element.259, s32[]{:T(128)S(6)} %copy.182, s32[64,128]{1,0:T(8,128)S(1)} %dynamic-slice_bitcast_fusion.5, f32[16,64,6,128]{3,2,1,0:T(8,128)} %get-tuple-element.265), kind=kOutput, calls=%fused_computation.25.clone.1 | convolution fusion | flops 76546048 | bytes 558080 | tf_op jit(solution)/shard_map/while/body/eval_jaxpr/gcm,gkm->gck/dot_general | solution.py:82
  247.6 5.2 %fusion.79 = f32[16,64,6,128]{3,2,1,0:T(8,128)} fusion(f32[16,64,6,128]{3,2,1,0:T(8,128)} %get-tuple-element.259, s32[]{:T(128)S(6)} %copy.182, s32[64,128]{1,0:T(8,128)S(1)} %dynamic-slice_bitcast_fusion.5, f32[16,64,6,128]{3,2,1,0:T(8,128)} %get-tuple-element.265), kind=kOutput, calls=%fused_computation.25.clone.1 | convolution fusion | flops 76546048 | bytes 558080 | tf_op jit(solution)/shard_map/while/body/eval_jaxpr/gcm,gkm->gck/dot_general | solution.py:82
  252.8 4.9 %fusion.65 = (f32[1024,3,128]{2,1,0:T(4,128)S(1)}, f32[1024,3,128]{2,1,0:T(4,128)S(1)}) fusion(f32[1024,6,128]{2,1,0:T(8,128)} %bitcast.197, f32[1024,3,128]{2,1,0:T(4,128)S(1)} %gather_fusion.7), kind=kLoop, calls=%fused_computation.225 | loop fusion | flops 393216 | bytes 7864320 | tf_op jit(solution)/shard_map/slice | solution.py:99
  257.7 2.6 multiply_subtract_fusion.5
  260.4 5.3 %multiply_subtract_fusion.2 = (f32[1024,1,128]{2,1,0:T(1,128)S(1)}, f32[1024,1,128]{2,1,0:T(1,128)S(1)}, f32[1024,1,128]{2,1,0:T(1,128)S(1)}, f32[1024,1,128]{2,1,0:T(1,128)S(1)}) fusion(f32[1024,6,128]{2,1,0:T(8,128)S(1)} %bitcast.199, f32[1024]{0:T(1024)S(1)} %reshape.853, f32[1024,3,128]{2,1,0:T(4,128)S(1)} %get-tuple-element.138), kind=kLoop, calls=%fused_computation.75 | loop fusion | flops 1966080 | bytes 6819840 | tf_op jit(solution)/shard_map/sub | solution.py:66
  265.7 17.8 %multiply_reduce_fusion.9 = (f32[1024,6]{1,0:T(8,128)S(1)}, f32[1024,128]{1,0:T(8,128)S(1)}, f32[1024,128]{1,0:T(8,128)S(1)}, f32[1024,128]{1,0:T(8,128)S(1)}) fusion(f32[1024,128]{1,0:T(8,128)S(1)} %bitcast.203, f32[1024,3,128]{2,1,0:T(4,128)S(1)} %get-tuple-element.137, f32[1024,1,128]{2,1,0:T(1,128)S(1)} %get-tuple-element.131, ...), kind=kLoop, calls=%fused_computation.43 | loop fusion | flops 11397120 | bytes 6914048 | tf_op jit(solution)/shard_map/reduce_sum | solution.py:108
  283.7 16.0 %multiply_reduce_fusion.2 = (f32[1024,6]{1,0:T(8,128)S(1)}, f32[1024,128]{1,0:T(8,128)S(1)}, f32[1024,6]{1,0:T(8,128)S(1)}) fusion(f32[1024,128]{1,0:T(8,128)S(1)} %bitcast.204, f32[1024,3,128]{2,1,0:T(4,128)S(1)} %get-tuple-element.137, f32[1024,1,128]{2,1,0:T(1,128)S(1)} %get-tuple-element.135, f32[1024,1,128]{2,1,0:T(1,128)S(1)} %get-tuple-element.134, ...), kind=kLoop, calls=%fused_computation.36 | loop fusion | flops 7720960 | bytes 4792320 | tf_op jit(solution)/shard_map/reduce_sum | solution.py:109
  300.0 7.0 %multiply_reduce_fusion.6 = (f32[1024,6]{1,0:T(8,128)S(1)}, f32[1024,6]{1,0:T(8,128)S(1)}, f32[1024,6]{1,0:T(8,128)S(1)}) fusion(f32[1024,128]{1,0:T(8,128)S(1)} %add_multiply_fusion.1, f32[1024,3,128]{2,1,0:T(4,128)S(1)} %get-tuple-element.137, f32[1024,1,128]{2,1,0:T(1,128)S(1)} %get-tuple-element.131, f32[1024,1,128]{2,1,0:T(1,128)S(1)} %get-tuple-element.132, ...), kind=kLoop, calls=%fused_computation.40 | loop fusion | flops 10205184 | bytes 5840896 | tf_op jit(solution)/shard_map/reduce_sum | solution.py:115
  309.0 0.8 copy.169
  309.9 1.1 reshape.934
  310.9 4.3 %all-to-all-start.2 = ((f32[128,1,144]{2,1,0:T(1,128)}), f32[128,1,144]{2,1,0:T(1,128)S(1)}, u32[]{:S(2)}, u32[]{:S(2)}) async-start(f32[128,1,144]{2,1,0:T(1,128)} %reshape.934), calls=%async_computation.2 | async-start | bytes 262144 | tf_op jit(solution)/shard_map/all_to_all | solution.py:187
  315.8 9.6 %all-to-all-done.2 = f32[128,1,144]{2,1,0:T(1,128)S(1)} async-done(((f32[128,1,144]{2,1,0:T(1,128)}), f32[128,1,144]{2,1,0:T(1,128)S(1)}, u32[]{:S(2)}, u32[]{:S(2)}) %all-to-all-start.2) | async-done | bytes 73760 | tf_op jit(solution)/shard_map/all_to_all | solution.py:187
  325.9 1.0 reduce
  (164 shorter events, 22.8 us)
Async XLA Ops:
  0.6 17.6 %copy-start.23 = (f32[6,8]{1,0:T(8,128)S(1)}, f32[6,8]{1,0:T(8,128)}, u32[]{:S(2)}) copy-start(f32[6,8]{1,0:T(8,128)} %param.16) | copy-start | bytes 580
  0.6 17.7 %copy-start.20 = (s32[2,256]{1,0:T(2,128)S(1)}, s32[2,256]{1,0:T(2,128)}, u32[]{:S(2)}) copy-start(s32[2,256]{1,0:T(2,128)} %param.18) | copy-start | bytes 6148
  0.7 19.7 %copy-start.17 = (f32[256,3,128]{2,0,1:T(8,128)S(1)}, f32[256,3,128]{2,0,1:T(8,128)}, u32[]{:S(2)}) copy-start(f32[256,3,128]{2,0,1:T(8,128)} %param.15) | copy-start | bytes 1179652
  2.3 19.2 %copy-start.7 = (f32[256,3,128]{2,0,1:T(8,128)S(1)}, f32[256,3,128]{2,0,1:T(8,128)}, u32[]{:S(2)}) copy-start(f32[256,3,128]{2,0,1:T(8,128)} %param.14) | copy-start | bytes 1179652
  6.3 88.6 %all-to-all-start.1 = ((f32[128,8,12]{2,1,0:T(8,128)}), f32[128,8,12]{2,1,0:T(8,128)}, u32[]{:S(2)}, u32[]{:S(2)}) async-start(f32[128,8,12]{2,1,0:T(8,128)} %bitcast.31), calls=%async_computation.1 | async-start | bytes 1048576 | tf_op jit(solution)/shard_map/all_to_all | solution.py:153
  47.9 4.0 %copy-start.3 = (f32[4,64,6,128]{3,2,1,0:T(8,128)}, f32[4,64,6,128]{3,2,1,0:T(8,128)S(1)}, u32[]{:S(2)}) copy-start(f32[4,64,6,128]{3,2,1,0:T(8,128)S(1)} %get-tuple-element.56) | copy-start | bytes 2359300
  55.5 17.9 %copy-start.2 = (f32[256,3,128]{2,1,0:T(4,128)S(1)}, f32[256,3,128]{2,1,0:T(4,128)}, u32[]{:S(2)}) copy-start(f32[256,3,128]{2,1,0:T(4,128)} %get-tuple-element.147) | copy-start | bytes 1179652
  72.0 10.7 %copy-start.8 = (f32[256,1,128]{2,1,0:T(1,128)S(1)}, f32[256,1,128]{2,1,0:T(1,128)}, u32[]{:S(2)}) copy-start(f32[256,1,128]{2,1,0:T(1,128)} %get-tuple-element.140) | copy-start | bytes 393220
  72.0 10.7 %copy-start.9 = (f32[256,1,128]{2,1,0:T(1,128)S(1)}, f32[256,1,128]{2,1,0:T(1,128)}, u32[]{:S(2)}) copy-start(f32[256,1,128]{2,1,0:T(1,128)} %get-tuple-element.141) | copy-start | bytes 393220
  72.0 10.7 %copy-start.10 = (f32[256,1,128]{2,1,0:T(1,128)S(1)}, f32[256,1,128]{2,1,0:T(1,128)}, u32[]{:S(2)}) copy-start(f32[256,1,128]{2,1,0:T(1,128)} %get-tuple-element.142) | copy-start | bytes 393220
  72.0 12.8 %copy-start.24 = (s32[1,128]{1,0:T(1,128)S(1)}, s32[1,128]{1,0:T(1,128)}, u32[]{:S(2)}) copy-start(s32[1,128]{1,0:T(1,128)} %param.23) | copy-start | bytes 1540
  72.0 12.9 %copy-start.18 = (s32[1,1024]{1,0:T(1,128)S(1)}, s32[1,1024]{1,0:T(1,128)}, u32[]{:S(2)}) copy-start(s32[1,1024]{1,0:T(1,128)} %param.20) | copy-start | bytes 12292
  72.0 13.0 %copy-start.1 = (f32[1024,3,128]{2,1,0:T(4,128)S(1)}, f32[1024,3,128]{2,1,0:T(4,128)}, u32[]{:S(2)}) copy-start(f32[1024,3,128]{2,1,0:T(4,128)} %gather_fusion.5) | copy-start | bytes 4718596
  85.0 2.9 copy-start.16
  85.0 3.0 copy-start.15
  85.0 3.0 copy-start.11
  85.0 3.1 copy-start.14
  85.0 3.2 copy-start.13
  85.0 3.3 copy-start.12
  94.9 10.3 %copy-start.22 = (s32[1,256]{1,0:T(1,128)S(1)}, s32[1,256]{1,0:T(1,128)}, u32[]{:S(2)}) copy-start(s32[1,256]{1,0:T(1,128)} %get-tuple-element.179) | copy-start | bytes 3076
  94.9 10.3 %copy-start.21 = (s32[1,256]{1,0:T(1,128)S(1)}, s32[1,256]{1,0:T(1,128)}, u32[]{:S(2)}) copy-start(s32[1,256]{1,0:T(1,128)} %get-tuple-element.178) | copy-start | bytes 3076
  94.9 10.7 %copy-start.19 = (s32[1,1024]{1,0:T(1,128)S(1)}, s32[1,1024]{1,0:T(1,128)}, u32[]{:S(2)}) copy-start(s32[1,1024]{1,0:T(1,128)} %param.22) | copy-start | bytes 12292
  94.9 62.9 %all-to-all-start = ((f32[1024,6,128]{2,1,0:T(8,128)}), f32[1024,6,128]{2,1,0:T(8,128)}, u32[]{:S(2)}, u32[]{:S(2)}) async-start(f32[1024,6,128]{2,1,0:T(8,128)} %pad_maximum_fusion.2), calls=%async_computation | async-start | bytes 8388608 | tf_op jit(solution)/shard_map/all_to_all | solution.py:152
  252.8 5.0 %copy-start = (f32[16,64,6,128]{3,2,1,0:T(8,128)S(1)}, f32[16,64,6,128]{3,2,1,0:T(8,128)}, u32[]{:S(2)}) copy-start(f32[16,64,6,128]{3,2,1,0:T(8,128)} %get-tuple-element.57) | copy-start | bytes 9437188
  260.4 5.3 %copy-start.4 = (f32[1024,6]{1,0:T(8,128)S(1)}, f32[1024,6]{1,0:T(8,128)}, u32[]{:S(2)}) copy-start(f32[1024,6]{1,0:T(8,128)} %get-tuple-element.152) | copy-start | bytes 73732
  260.4 5.3 %copy-start.5 = (f32[1024,6]{1,0:T(8,128)S(1)}, f32[1024,6]{1,0:T(8,128)}, u32[]{:S(2)}) copy-start(f32[1024,6]{1,0:T(8,128)} %get-tuple-element.150) | copy-start | bytes 73732
  265.7 18.0 %copy-start.6 = (f32[1024,6]{1,0:T(8,128)S(1)}, f32[1024,6]{1,0:T(8,128)}, u32[]{:S(2)}) copy-start(f32[1024,6]{1,0:T(8,128)} %get-tuple-element.149) | copy-start | bytes 73732
  310.9 14.5 %all-to-all-start.2 = ((f32[128,1,144]{2,1,0:T(1,128)}), f32[128,1,144]{2,1,0:T(1,128)S(1)}, u32[]{:S(2)}, u32[]{:S(2)}) async-start(f32[128,1,144]{2,1,0:T(1,128)} %reshape.934), calls=%async_computation.2 | async-start | bytes 262144 | tf_op jit(solution)/shard_map/all_to_all | solution.py:187
where the time goes:
time: 332 us; the launch traced here: 329 us
  matrix products  104 us (31%)
  other arithmetic  81.4 us (25%)
  waiting for transfers between devices  58.2 us (18%)
  local copies, waits for them, and re-layouts  58 us (17%)
  starting transfers between devices  26.5 us (8%)
    dot_general x20, matrix products, select_block(): jnp.einsum('gcm,gkm->gck', values, selector, precision=lax.Precision.HIGH...  102 us
    all_to_all x1, waiting for transfers between devices, local(): lax.all_to_all(cargo_rows, ('tile', 'band'), split_axis=0, concat_axis=0,...  48.6 us
    reduce_sum x2, other arithmetic, pair_terms(): parts_a = [jnp.sum(residual[:, None] * jac_a, axis=2) * grad_scale]  23.9 us
    reduce_sum x2, other arithmetic, pair_terms(): parts_b = [jnp.sum(residual[:, None] * jac_b, axis=2) * grad_scale]  19.1 us
    sub x4, other arithmetic, cross_rows(): left[:, 1] * right[:, 2] - left[:, 2] * right[:, 1]  15.5 us
    eq x20, local copies, waits for them, and re-layouts, select_block(): indices[:, :, None] == positions[None, None, :]  15.3 us
    all_to_all x1, starting transfers between devices, local(): lax.all_to_all(extras, ('tile', 'band'), split_axis=0, concat_axis=0, til...  12 us
    all_to_all x1, starting transfers between devices, local(): lax.all_to_all(cargo_rows, ('tile', 'band'), split_axis=0, concat_axis=0,...  10.2 us
  transfers between devices with their start and end apart: 3, of which 2 were waited for; matrix products, arithmetic and copies ran while one was open for 24% of the time, Pallas kernels for 0%

commit v1 on v0

v1 whole, which is shorter than its diff:
```python
import jax
import jax.numpy as jnp
import numpy as np
from jax import lax
from jax.experimental import pallas as pl
from jax.experimental.pallas import tpu as pltpu
from jax.sharding import PartitionSpec as P

BF = 32
CAP = 8
N_QTY = 27


def rotations(poses):
    half_angle = poses[0:3] * 0.5
    inverse = 1.0 / jnp.sqrt(
        1.0
        + half_angle[0] * half_angle[0]
        + half_angle[1] * half_angle[1]
        + half_angle[2] * half_angle[2]
    )
    quat_x = half_angle[0] * inverse
    quat_y = half_angle[1] * inverse
    quat_z = half_angle[2] * inverse
    rotation = [
        [
            1.0 - 2.0 * (quat_y * quat_y + quat_z * quat_z),
            2.0 * (quat_x * quat_y - inverse * quat_z),
            2.0 * (quat_x * quat_z + inverse * quat_y),
        ],
        [
            2.0 * (quat_x * quat_y + inverse * quat_z),
            1.0 - 2.0 * (quat_x * quat_x + quat_z * quat_z),
            2.0 * (quat_y * quat_z - inverse * quat_x),
        ],
        [
            2.0 * (quat_x * quat_z - inverse * quat_y),
            2.0 * (quat_y * quat_z + inverse * quat_x),
            1.0 - 2.0 * (quat_x * quat_x + quat_y * quat_y),
        ],
    ]
    return (rotation, poses[3:6])


def to_world_rows(points, normals, poses, per_pose):
    rotation, translation = rotations(poses)

    def spread(values):
        return jnp.repeat(values, per_pose)[:, None]

    world_rows = []
    normal_rows = []
    for i in range(3):
        coeffs = [spread(rotation[i][j]) for j in range(3)]
        world_rows.append(
            coeffs[0] * points[:, 0]
            + coeffs[1] * points[:, 1]
            + coeffs[2] * points[:, 2]
            + spread(translation[i])
        )
        normal_rows.append(
            coeffs[0] * normals[:, 0] + coeffs[1] * normals[:, 1] + coeffs[2] * normals[:, 2]
        )
    return jnp.stack(world_rows + normal_rows, axis=0)


def _lane_of(q):
    lane = 3
    for j in range(5):
        if ((q >> j) & 1) == 0:
            lane += 64 >> j
    return lane


_LANES = np.array([_lane_of(q) for q in range(N_QTY)], np.int32)


def _lane_reduce(vals, lane):
    h = 64
    while len(vals) > 1:
        merged = []
        for i in range(0, len(vals), 2):
            left = vals[i] + pltpu.roll(vals[i], h, 1)
            right = vals[i + 1] + pltpu.roll(vals[i + 1], 128 - h, 1)
            merged.append(jnp.where((lane & h) != 0, left, right))
        vals = merged
        h //= 2
    x = vals[0]
    while h >= 1:
        x = x + pltpu.roll(x, h, 1)
        h //= 2
    return x


def _terms_kernel(xa_ref, tb_ref, map_ref, aux_ref, out_ref):
    groups = out_ref.shape[0] // 8
    lane = lax.broadcasted_iota(jnp.int32, (8, 128), 1)

    def body(g, carry):
        rows = pl.ds(pl.multiple_of(g * 8, 8), 8)
        idx = map_ref[rows, :]
        xa = [xa_ref[c, rows, :] for c in range(3)]
        picked = [
            jnp.take_along_axis(tb_ref[c, rows, :], idx, axis=1, mode="promise_in_bounds")
            for c in range(6)
        ]
        xb = picked[0:3]
        nb = picked[3:6]
        aux = aux_ref[rows, :]

        def col(q):
            return jnp.broadcast_to(aux[:, q : q + 1], (8, 128))

        valid = col(24)
        off = [xa[c] - xb[c] for c in range(3)]
        res = (nb[0] * off[0] + nb[1] * off[1] + nb[2] * off[2]) * valid
        ja = [
            xa[1] * nb[2] - xa[2] * nb[1],
            xa[2] * nb[0] - xa[0] * nb[2],
            xa[0] * nb[1] - xa[1] * nb[0],
            nb[0],
            nb[1],
            nb[2],
        ]
        jb = [
            -(xb[1] * nb[2] - xb[2] * nb[1]),
            -(xb[2] * nb[0] - xb[0] * nb[2]),
            -(xb[0] * nb[1] - xb[1] * nb[0]),
            -nb[0],
            -nb[1],
            -nb[2],
        ]
        weights = [res]
        for v in range(2):
            sa = ja[0] * col(6 * v)
            sb = jb[0] * col(12 + 6 * v)
            for c in range(1, 6):
                sa = sa + ja[c] * col(6 * v + c)
                sb = sb + jb[c] * col(12 + 6 * v + c)
            weights.append((sa + sb) * valid)
        vals = []
        for w in weights:
            vals.extend([w * ja[c] for c in range(6)])
        for w in weights:
            vals.extend([w * jb[c] for c in range(3)])
        zero = jnp.zeros((8, 128), jnp.float32)
        vals.extend([zero] * (32 - len(vals)))
        out_ref[rows, :] = _lane_reduce(vals, lane)
        return carry

    lax.fori_loop(0, groups, body, 0)


def pair_sums(xa, tb, maps, aux, block=256):
    pairs = maps.shape[0]
    block = min(block, pairs)
    return pl.pallas_call(
        _terms_kernel,
        out_shape=jax.ShapeDtypeStruct((pairs, 128), jnp.float32),
        grid=(pairs // block,),
        in_specs=[
            pl.BlockSpec((3, block, 128), lambda i: (0, i, 0)),
            pl.BlockSpec((6, block, 128), lambda i: (0, i, 0)),
            pl.BlockSpec((block, 128), lambda i: (i, 0)),
            pl.BlockSpec((block, 128), lambda i: (i, 0)),
        ],
        out_specs=pl.BlockSpec((block, 128), lambda i: (i, 0)),
    )(xa, tb, maps, aux)


def split_terms(out):
    sel = out[:, _LANES]
    ga = sel[:, 0:6] * (1.0 / 128)
    ha = sel[:, 6:18] * (1.0 / 4096)
    gb = jnp.concatenate([sel[:, 18:21], -sel[:, 3:6]], axis=1) * (1.0 / 128)
    hb0 = jnp.concatenate([sel[:, 21:24], -sel[:, 9:12]], axis=1) * (1.0 / 4096)
    hb1 = jnp.concatenate([sel[:, 24:27], -sel[:, 15:18]], axis=1) * (1.0 / 4096)
    return jnp.concatenate([ga, ha], axis=1), jnp.concatenate([gb, hb0, hb1], axis=1)


def frag_sums(blocks, terms, frag_count):
    onehot = (blocks[:, None] // BF == jnp.arange(frag_count, dtype=jnp.int32)[None, :]).astype(
        jnp.float32
    )
    return jnp.dot(onehot.T, terms, precision=lax.Precision.HIGHEST)


def make_aux(dirs_a, dirs_b, valid):
    pairs = dirs_a.shape[0]
    return jnp.concatenate(
        [dirs_a, dirs_b, valid[:, None], jnp.zeros((pairs, 128 - 25), jnp.float32)], axis=1
    )


def local(
    points,
    normals,
    poses,
    directions,
    local_pairs,
    local_maps,
    remote_src,
    remote_maps,
    remote_dst,
    counts,
):
    axes = ("tile", "band")
    frag_count = poses.shape[1]
    rows6 = to_world_rows(points, normals, poses, BF)
    frag_dirs = directions.reshape(12, frag_count).T
    peers = counts.shape[1]

    source_blocks = remote_src[0]
    valid = (
        (jnp.arange(CAP, dtype=jnp.int32)[None, :] < counts[0][:, None])
        .astype(jnp.float32)
        .reshape(-1)
    )
    xa_send = jnp.transpose(rows6[0:3][:, source_blocks], (1, 0, 2))
    map_send = remote_maps[0].astype(jnp.float32)[:, None, :]
    main = jnp.concatenate([xa_send, map_send], axis=1).reshape(peers, CAP * 4, 128)
    side = jnp.concatenate([frag_dirs[source_blocks // BF], valid[:, None]], axis=1)
    side = side.reshape(peers, CAP * 13)
    side = jnp.concatenate([side, jnp.zeros((peers, 128 - CAP * 13), jnp.float32)], axis=1)
    cargo = jnp.concatenate([main, side[:, None, :]], axis=1)
    arrived = lax.all_to_all(cargo, axes, split_axis=0, concat_axis=0, tiled=True)

    src_l = local_pairs[0]
    tgt_l = local_pairs[1]
    ones = jnp.ones((src_l.shape[0],), jnp.float32)
    out_l = pair_sums(
        rows6[0:3][:, src_l],
        rows6[:, tgt_l],
        local_maps,
        make_aux(frag_dirs[src_l // BF], frag_dirs[tgt_l // BF], ones),
    )
    local_a, local_b = split_terms(out_l)

    target_blocks = remote_dst[0]
    main_in = arrived[:, 0 : CAP * 4].reshape(peers * CAP, 4, 128)
    side_in = arrived[:, CAP * 4, 0 : CAP * 13].reshape(peers * CAP, 13)
    out_r = pair_sums(
        jnp.transpose(main_in[:, 0:3], (1, 0, 2)),
        rows6[:, target_blocks],
        main_in[:, 3].astype(jnp.int32),
        make_aux(side_in[:, 0:12], frag_dirs[target_blocks // BF], side_in[:, 12]),
    )
    remote_a, remote_b = split_terms(out_r)
    returned = lax.all_to_all(
        remote_a.reshape(peers, CAP * 18), axes, split_axis=0, concat_axis=0, tiled=True
    ).reshape(peers * CAP, 18)

    totals = frag_sums(src_l, local_a, frag_count) + frag_sums(tgt_l, local_b, frag_count)
    totals = (
        totals
        + frag_sums(target_blocks, remote_b, frag_count)
        + frag_sums(source_blocks, returned, frag_count)
    )
    gradient = totals[:, 0:6].T
    hess_products = totals[:, 6:18].T.reshape(2, 6, frag_count)
    return (gradient, hess_products)


def solution(mesh):
    placed = (
        P(("tile", "band"), None, None),
        P(("tile", "band"), None, None),
        P(None, ("tile", "band")),
        P(None, None, ("tile", "band")),
        P(None, ("tile", "band")),
        P(("tile", "band"), None),
        P(("tile", "band"), None),
        P(("tile", "band"), None, None),
        P(("tile", "band"), None),
        P(("tile", "band"), None),
    )
    return jax.shard_map(
        local,
        mesh=mesh,
        in_specs=placed,
        out_specs=(P(None, ("tile", "band")), P(None, None, ("tile", "band"))),
        check_vma=False,
    )
```

time: 332 us -> 200 us (0.60)
  Pallas kernels: 0 us -> 104 us
  matrix products: 104 us -> 1.81 us
  other arithmetic: 81.4 us -> 13.6 us
  waiting for transfers between devices: 58.2 us -> 9.42 us
  local copies, waits for them, and re-layouts: 58 us -> 48.3 us
  starting transfers between devices: 26.5 us -> 21.7 us
    pallas_call x0 -> x2, Pallas kernels: none -> 104 us  [pair_sums(): pl.pallas_call(_terms_kernel, out_shape=jax.ShapeDtypeStruct((pairs, 128)...]
    dot_general x20 -> x0, matrix products: 102 us -> none  [select_block(): jnp.einsum('gcm,gkm->gck', values, selector, precision=lax.Precision.HIGH...]
    reduce_sum x6 -> x0, other arithmetic: 52.2 us -> none  [the longest x2 23.9 us: pair_terms(): parts_a = [jnp.sum(residual[:, None] * jac_a, axis=2) * grad_scale]]
    all_to_all x3 -> x2, waiting for transfers between devices: 58.2 us -> 9.42 us  [the longest x1 9.41 us: local(): lax.all_to_all(remote_a.reshape(peers, CAP * 18), axes, split_axis=0, con...]
    sub x4 -> x0, other arithmetic: 15.5 us -> none  [cross_rows(): left[:, 1] * right[:, 2] - left[:, 2] * right[:, 1]]
    eq x20 -> x0, local copies, waits for them, and re-layouts: 15.3 us -> none  [select_block(): indices[:, :, None] == positions[None, None, :]]
    slice x2, other arithmetic: 6.15 us -> 0.03 us  [split_terms(): gb = jnp.concatenate([sel[:, 18:21], -sel[:, 3:6]], axis=1) * (1.0 / 128)]
    all_to_all x3 -> x2, starting transfers between devices: 26.5 us -> 21.7 us  [the longest x1 11.9 us: local(): lax.all_to_all(cargo, axes, split_axis=0, concat_axis=0, tiled=True)]
  transfers between devices with their start and end apart: 3 -> 2, of which waited for: 2 -> 1; matrix products, arithmetic and copies ran while one was open for 24% -> 13% of each run, Pallas kernels for 0% -> 11%
where the time goes in v1:
time: 200 us
  Pallas kernels  104 us (52%)
  local copies, waits for them, and re-layouts  48.3 us (24%)
  starting transfers between devices  21.7 us (11%)
  other arithmetic  13.6 us (7%)
  waiting for transfers between devices  9.42 us (5%)
    pallas_call x2, Pallas kernels, pair_sums(): pl.pallas_call(_terms_kernel, out_shape=jax.ShapeDtypeStruct((pairs, 128)...  104 us
    gather x2, local copies, waits for them, and re-layouts, local(): rows6[:, target_blocks]  13.5 us
    all_to_all x1, starting transfers between devices, local(): lax.all_to_all(cargo, axes, split_axis=0, concat_axis=0, tiled=True)  11.9 us
    all_to_all x1, starting transfers between devices, local(): lax.all_to_all(remote_a.reshape(peers, CAP * 18), axes, split_axis=0, con...  9.76 us
    all_to_all x1, waiting for transfers between devices, local(): lax.all_to_all(remote_a.reshape(peers, CAP * 18), axes, split_axis=0, con...  9.41 us
    add x1, other arithmetic, to_world_rows(): coeffs[0] * points[:, 0] + coeffs[1] * points[:, 1]  4.91 us
    unnamed x22, local copies, waits for them, and re-layouts  4.09 us
  transfers between devices with their start and end apart: 2, of which 1 were waited for; matrix products, arithmetic and copies ran while one was open for 13% of the time, Pallas kernels for 11%

profile of v1, /device:TPU:1, one launch (start us, length us, event | category | flops | bytes accessed | tf_op | source)
XLA Modules:
  0.0 199.6 jit_solution(10044652289196503204)
XLA Ops:
  0.6 0.8 slice_bitcast_fusion.4
  1.4 0.7 slice_multiply_fusion.4
  2.2 0.1 mul.406
  2.4 0.1 mul.416
  2.5 0.1 mul.399
  2.7 0.1 add.352
  3.0 0.1 mul.435
  3.4 0.1 mul.421
  3.9 0.1 add.359
  4.0 0.8 copy.48
  4.8 0.1 reshape.1456
  4.8 0.7 compare_select_fusion.9
  5.6 0.7 fusion.16
  6.3 1.1 fusion.38
  7.4 1.1 fusion.37
  8.5 0.2 reshape.1543
  8.6 2.8 %gather_fusion.6 = f32[1024,12]{1,0:T(8,128)S(1)} fusion(f32[8,12]{1,0:T(8,128)S(1)} %bitcast.175, s32[1024]{0:T(1024)S(1)} %broadcast_clamp_fusion.1), kind=kCustom, calls=%fused_computation.6 | custom fusion | bytes 102400 | tf_op jit(solution)/shard_map/gather | solution.py:222
  11.5 0.2 pad_maximum_fusion.3
  11.7 0.2 reshape.1458
  11.9 0.6 copy-done.3
  12.5 0.6 concatenate.57
  13.2 4.9 %add_add_fusion.2 = (f32[1,256,128]{2,0,1:T(1,128)S(1)}, f32[1,256,128]{2,0,1:T(1,128)S(1)}, f32[1,256,128]{2,0,1:T(1,128)S(1)}, f32[1,256,128]{2,0,1:T(1,128)},...) fusion(f32[1,256,128]{2,0,1:T(1,128)S(1)} %bitcast.196, f32[1,256,128]{2,0,1:T(1,128)S(1)} %bitcast.197, ...), kind=kLoop, calls=%fused_computation.35 | loop fusion | flops 1081344 | bytes 1585152 | tf_op jit(solution)/shard_map/add | solution.py:56
  18.1 0.3 pad_maximum_fusion.2
  18.4 3.6 %gather_fusion.5 = f32[1024,3,128]{2,1,0:T(4,128)S(1)} fusion(f32[3,256,128]{2,0,1:T(4,128)S(1)} %pad_maximum_fusion.2, s32[1024]{0:T(1024)S(1)} %broadcast_clamp_fusion.3), kind=kCustom, calls=%fused_computation.5 | custom fusion | bytes 3149824 | tf_op jit(solution)/shard_map/gather | solution.py:219
  22.0 0.9 pad_maximum_fusion.1
  23.0 1.7 pad_maximum_fusion
  24.7 11.9 %all-to-all-start = ((f32[128,33,128]{2,1,0:T(8,128)}), f32[128,33,128]{2,1,0:T(8,128)}, u32[]{:S(2)}, u32[]{:S(2)}) async-start(f32[128,33,128]{2,1,0:T(8,128)} %pad_maximum_fusion), calls=%async_computation | async-start | bytes 5242880 | tf_op jit(solution)/shard_map/all_to_all | solution.py:226
  37.0 0.7 gather_fusion.3
  37.7 0.7 gather_fusion.2
  38.4 1.0 gather_fusion
  39.4 0.8 copy.68
  40.2 1.2 stack.5
  41.5 1.0 gather_fusion.1
  42.5 1.0 copy.67
  43.5 0.8 maximum_maximum_fusion.1.aux_ref
  44.3 21.9 %shard_map.140 = f32[256,128]{1,0:T(8,128)} custom-call(f32[3,256,128]{2,1,0:T(8,128)} %bitcast.191, f32[6,256,128]{2,1,0:T(8,128)} %bitcast.188, s32[256,128]{1,0:T(8,128)} %map_ref.1, f32[256,128]{1,0:T(8,128)} %maximum_maximum_fusion.1.aux_ref), custom_call_target="tpu_custom_call" | custom-call | tf_op jit(solution)/shard_map/pallas_call | solution.py:157
  66.2 1.0 copy.49
  67.2 0.6 gather_fusion.4
  67.8 2.8 %gather_fusion.8 = f32[1024,12]{1,0:T(8,128)S(1)} fusion(f32[8,12]{1,0:T(8,128)S(1)} %bitcast.178, s32[1024]{0:T(1024)S(1)} %broadcast_clamp_fusion), kind=kCustom, calls=%fused_computation.8 | custom fusion | bytes 102400 | tf_op jit(solution)/shard_map/gather | solution.py:246
  70.6 9.0 %gather_fusion.7 = f32[1024,6,128]{2,1,0:T(8,128)} fusion(f32[6,256,128]{2,0,1:T(8,128)S(1)} %stack.5, s32[1024]{0:T(1024)S(1)} %broadcast_clamp_fusion.2), kind=kCustom, calls=%fused_computation.7 | custom fusion | bytes 6295552 | tf_op jit(solution)/shard_map/gather | solution.py:244
  79.7 4.5 %copy.65 = f32[1024,6,128]{2,0,1:T(8,128)} copy(f32[1024,6,128]{2,1,0:T(8,128)} %gather_fusion.7) | data formatting | bytes 6291456 | tf_op jit(solution)/shard_map/gather | solution.py:244
  84.3 0.3 fusion.12
  84.6 0.3 convolution_add_fusion.1
  84.8 1.2 slice_reduce_fusion
  86.1 0.2 reshape_squeeze.3
  86.3 0.2 slice.214
  86.5 1.8 slice.209
  88.3 0.5 slice.211
  88.8 0.9 convert_bitcast_fusion.map_ref
  89.7 1.3 copy.66
  90.9 1.1 maximum_maximum_fusion.aux_ref
  92.1 81.8 %shard_map.141 = f32[1024,128]{1,0:T(8,128)} custom-call(f32[3,1024,128]{2,1,0:T(8,128)} %bitcast.183, f32[6,1024,128]{2,1,0:T(8,128)} %bitcast.179, s32[1024,128]{1,0:T(8,128)} %convert_bitcast_fusion.map_ref, f32[1024,128]{1,0:T(8,128)} %maximum_maximum_fusion.aux_ref), custom_call_target="tpu_custom_call" | custom-call | tf_op jit(solution)/shard_map/pallas_call | solution.py:157
  173.8 1.2 copy.54
  175.1 0.6 gather_fusion.9
  175.8 0.2 copy.55
  176.0 1.1 all_to_all.12
  177.0 9.8 %all-to-all-start.1 = ((f32[128,1,144]{2,1,0:T(1,128)}), f32[128,1,144]{2,1,0:T(1,128)S(1)}, u32[]{:S(2)}, u32[]{:S(2)}) async-start(f32[128,1,144]{2,1,0:T(1,128)} %all_to_all.12), calls=%async_computation.1 | async-start | bytes 262144 | tf_op jit(solution)/shard_map/all_to_all | solution.py:249
  186.9 0.6 convolution_add_fusion
  187.4 9.4 %all-to-all-done.1 = f32[128,1,144]{2,1,0:T(1,128)S(1)} async-done(((f32[128,1,144]{2,1,0:T(1,128)}), f32[128,1,144]{2,1,0:T(1,128)S(1)}, u32[]{:S(2)}, u32[]{:S(2)}) %all-to-all-start.1) | async-done | bytes 73760 | tf_op jit(solution)/shard_map/all_to_all | solution.py:249
  196.8 0.3 reduce.1
  197.2 0.2 reshape.1460
  197.4 0.7 convolution_add_fusion.2
  198.1 0.7 copy.57
  198.9 0.7 copy.58
  (72 shorter events, 1.9 us)
Async XLA Ops:
  11.5 1.0 copy-start.3
  22.0 1.0 copy-start.4
  24.7 12.1 %copy-start.8 = (s32[27]{0:T(128)S(1)}, s32[27]{0:T(128)}, u32[]{:S(2)}) copy-start(s32[27]{0:T(128)} %constant.115) | copy-start | bytes 328
  24.7 12.1 %copy-start.7 = (s32[2,256]{1,0:T(2,128)S(1)}, s32[2,256]{1,0:T(2,128)}, u32[]{:S(2)}) copy-start(s32[2,256]{1,0:T(2,128)} %param.17) | copy-start | bytes 6148
  24.7 12.2 %copy-start.5 = (s32[1,1024]{1,0:T(1,128)S(1)}, s32[1,1024]{1,0:T(1,128)}, u32[]{:S(2)}) copy-start(s32[1,1024]{1,0:T(1,128)} %param.21) | copy-start | bytes 12292
  24.7 60.1 %all-to-all-start = ((f32[128,33,128]{2,1,0:T(8,128)}), f32[128,33,128]{2,1,0:T(8,128)}, u32[]{:S(2)}, u32[]{:S(2)}) async-start(f32[128,33,128]{2,1,0:T(8,128)} %pad_maximum_fusion), calls=%async_computation | async-start | bytes 5242880 | tf_op jit(solution)/shard_map/all_to_all | solution.py:226
  36.6 3.6 %copy-start = (f32[1,256,128]{2,0,1:T(1,128)S(1)}, f32[1,256,128]{2,0,1:T(1,128)}, u32[]{:S(2)}) copy-start(f32[1,256,128]{2,0,1:T(1,128)} %get-tuple-element.36) | copy-start | bytes 393220
  36.6 3.6 %copy-start.1 = (f32[1,256,128]{2,0,1:T(1,128)S(1)}, f32[1,256,128]{2,0,1:T(1,128)}, u32[]{:S(2)}) copy-start(f32[1,256,128]{2,0,1:T(1,128)} %get-tuple-element.37) | copy-start | bytes 393220
  36.6 3.6 %copy-start.2 = (f32[1,256,128]{2,0,1:T(1,128)S(1)}, f32[1,256,128]{2,0,1:T(1,128)}, u32[]{:S(2)}) copy-start(f32[1,256,128]{2,0,1:T(1,128)} %get-tuple-element.38) | copy-start | bytes 393220
  79.7 4.9 %copy-start.6 = (s32[1,1024]{1,0:T(1,128)S(1)}, s32[1,1024]{1,0:T(1,128)}, u32[]{:S(2)}) copy-start(s32[1,1024]{1,0:T(1,128)} %param.19) | copy-start | bytes 12292
  177.0 19.8 %all-to-all-start.1 = ((f32[128,1,144]{2,1,0:T(1,128)}), f32[128,1,144]{2,1,0:T(1,128)S(1)}, u32[]{:S(2)}, u32[]{:S(2)}) async-start(f32[128,1,144]{2,1,0:T(1,128)} %all_to_all.12), calls=%async_computation.1 | async-start | bytes 262144 | tf_op jit(solution)/shard_map/all_to_all | solution.py:249

commit v2 on v1

--- a/solution.py
+++ b/solution.py
@@ -1,6 +1,5 @@
 import jax
 import jax.numpy as jnp
-import numpy as np
 from jax import lax
 from jax.experimental import pallas as pl
 from jax.experimental.pallas import tpu as pltpu
@@ -64,53 +63,23 @@
     return jnp.stack(world_rows + normal_rows, axis=0)
 
 
-def _lane_of(q):
-    lane = 3
-    for j in range(5):
-        if ((q >> j) & 1) == 0:
-            lane += 64 >> j
-    return lane
-
-
-_LANES = np.array([_lane_of(q) for q in range(N_QTY)], np.int32)
-
-
-def _lane_reduce(vals, lane):
-    h = 64
-    while len(vals) > 1:
-        merged = []
-        for i in range(0, len(vals), 2):
-            left = vals[i] + pltpu.roll(vals[i], h, 1)
-            right = vals[i + 1] + pltpu.roll(vals[i + 1], 128 - h, 1)
-            merged.append(jnp.where((lane & h) != 0, left, right))
-        vals = merged
-        h //= 2
-    x = vals[0]
-    while h >= 1:
-        x = x + pltpu.roll(x, h, 1)
-        h //= 2
-    return x
-
-
-def _terms_kernel(xa_ref, tb_ref, map_ref, aux_ref, out_ref):
-    groups = out_ref.shape[0] // 8
-    lane = lax.broadcasted_iota(jnp.int32, (8, 128), 1)
-
-    def body(g, carry):
-        rows = pl.ds(pl.multiple_of(g * 8, 8), 8)
-        idx = map_ref[rows, :]
-        xa = [xa_ref[c, rows, :] for c in range(3)]
-        picked = [
-            jnp.take_along_axis(tb_ref[c, rows, :], idx, axis=1, mode="promise_in_bounds")
-            for c in range(6)
-        ]
-        xb = picked[0:3]
-        nb = picked[3:6]
-        aux = aux_ref[rows, :]
-
-        def col(q):
-            return jnp.broadcast_to(aux[:, q : q + 1], (8, 128))
-
+def _terms_kernel(xa_ref, tb_ref, map_ref, aux_ref, out_ref, xt_ref, gt_ref):
+    chunk = out_ref.shape[1]
+    idx = map_ref[...]
+    for c in range(3):
+        xt_ref[c] = xa_ref[c].T
+    for c in range(6):
+        picked = jnp.take_along_axis(tb_ref[c], idx, axis=1, mode="promise_in_bounds")
+        gt_ref[c] = picked.T
+
+    def col(q):
+        return jnp.broadcast_to(aux_ref[q : q + 1, :], (8, chunk))
+
+    def body(s, accs):
+        rows = pl.ds(pl.multiple_of(s * 8, 8), 8)
+        xa = [xt_ref[c, rows, :] for c in range(3)]
+        xb = [gt_ref[c, rows, :] for c in range(3)]
+        nb = [gt_ref[3 + c, rows, :] for c in range(3)]
         valid = col(24)
         off = [xa[c] - xb[c] for c in range(3)]
         res = (nb[0] * off[0] + nb[1] * off[1] + nb[2] * off[2]) * valid
@@ -143,33 +112,37 @@
             vals.extend([w * ja[c] for c in range(6)])
         for w in weights:
             vals.extend([w * jb[c] for c in range(3)])
-        zero = jnp.zeros((8, 128), jnp.float32)
-        vals.extend([zero] * (32 - len(vals)))
-        out_ref[rows, :] = _lane_reduce(vals, lane)
-        return carry
-
-    lax.fori_loop(0, groups, body, 0)
-
-
-def pair_sums(xa, tb, maps, aux, block=256):
+        return tuple(a + v for a, v in zip(accs, vals))
+
+    zero = jnp.zeros((8, chunk), jnp.float32)
+    accs = lax.fori_loop(0, 128 // 8, body, (zero,) * N_QTY)
+    for q in range(N_QTY):
+        out_ref[q : q + 1, :] = jnp.sum(accs[q], axis=0, keepdims=True)
+    out_ref[N_QTY:, :] = jnp.zeros((32 - N_QTY, chunk), jnp.float32)
+
+
+def pair_sums(xa, tb, maps, aux, chunk=128):
     pairs = maps.shape[0]
-    block = min(block, pairs)
     return pl.pallas_call(
         _terms_kernel,
-        out_shape=jax.ShapeDtypeStruct((pairs, 128), jnp.float32),
-        grid=(pairs // block,),
+        out_shape=jax.ShapeDtypeStruct((32, pairs), jnp.float32),
+        grid=(pairs // chunk,),
         in_specs=[
-            pl.BlockSpec((3, block, 128), lambda i: (0, i, 0)),
-            pl.BlockSpec((6, block, 128), lambda i: (0, i, 0)),
-            pl.BlockSpec((block, 128), lambda i: (i, 0)),
-            pl.BlockSpec((block, 128), lambda i: (i, 0)),
-        ],
-        out_specs=pl.BlockSpec((block, 128), lambda i: (i, 0)),
+            pl.BlockSpec((3, chunk, 128), lambda i: (0, i, 0)),
+            pl.BlockSpec((6, chunk, 128), lambda i: (0, i, 0)),
+            pl.BlockSpec((chunk, 128), lambda i: (i, 0)),
+            pl.BlockSpec((32, chunk), lambda i: (0, i)),
+        ],
+        out_specs=pl.BlockSpec((32, chunk), lambda i: (0, i)),
+        scratch_shapes=[
+            pltpu.VMEM((3, 128, chunk), jnp.float32),
+            pltpu.VMEM((6, 128, chunk), jnp.float32),
+        ],
     )(xa, tb, maps, aux)
 
 
 def split_terms(out):
-    sel = out[:, _LANES]
+    sel = out[0:N_QTY].T
     ga = sel[:, 0:6] * (1.0 / 128)
     ha = sel[:, 6:18] * (1.0 / 4096)
     gb = jnp.concatenate([sel[:, 18:21], -sel[:, 3:6]], axis=1) * (1.0 / 128)
@@ -188,7 +161,7 @@
 def make_aux(dirs_a, dirs_b, valid):
     pairs = dirs_a.shape[0]
     return jnp.concatenate(
-        [dirs_a, dirs_b, valid[:, None], jnp.zeros((pairs, 128 - 25), jnp.float32)], axis=1
+        [dirs_a.T, dirs_b.T, valid[None, :], jnp.zeros((32 - 25, pairs), jnp.float32)], axis=0
     )
 
 

time: 200 us -> 110 us (0.55)
  Pallas kernels: 104 us -> 13.9 us
  waiting for transfers between devices: 9.42 us -> 15.7 us
  starting transfers between devices: 21.7 us -> 16.4 us
    pallas_call x2, Pallas kernels: 104 us -> 13.9 us  [pair_sums(): pl.pallas_call(_terms_kernel, out_shape=jax.ShapeDtypeStruct((32, pairs),...]
    all_to_all x1, waiting for transfers between devices: 0.01 us -> 6.13 us  [local(): lax.all_to_all(cargo, axes, split_axis=0, concat_axis=0, tiled=True)]
    all_to_all x1, starting transfers between devices: 9.76 us -> 4.48 us  [local(): lax.all_to_all(remote_a.reshape(peers, CAP * 18), axes, split_axis=0, con...]
    pallas_call x2 -> x0, local copies, waits for them, and re-layouts: 2.23 us -> none  [pair_sums(): pl.pallas_call(_terms_kernel, out_shape=jax.ShapeDtypeStruct((pairs, 128)...]
    unnamed x22 -> x21, local copies, waits for them, and re-layouts: 4.09 us -> 4.28 us
  transfers between devices with their start and end apart: 2 -> 2, of which waited for: 1 -> 2; matrix products, arithmetic and copies ran while one was open for 13% -> 24% of each run, Pallas kernels for 11% -> 3%
where the time goes in v2:
time: 110 us; the launch traced here: 109 us
  local copies, waits for them, and re-layouts  47.3 us (43%)
  starting transfers between devices  16.4 us (15%)
  waiting for transfers between devices  15.7 us (14%)
  Pallas kernels  13.9 us (13%)
  other arithmetic  13.2 us (12%)
  matrix products  1.81 us (2%)
    pallas_call x2, Pallas kernels, pair_sums(): pl.pallas_call(_terms_kernel, out_shape=jax.ShapeDtypeStruct((32, pairs),...  13.9 us
    gather x2, local copies, waits for them, and re-layouts, local(): rows6[:, target_blocks]  13.6 us
    all_to_all x1, starting transfers between devices, local(): lax.all_to_all(cargo, axes, split_axis=0, concat_axis=0, tiled=True)  11.9 us
    all_to_all x1, waiting for transfers between devices, local(): lax.all_to_all(remote_a.reshape(peers, CAP * 18), axes, split_axis=0, con...  9.55 us
    all_to_all x1, waiting for transfers between devices, local(): lax.all_to_all(cargo, axes, split_axis=0, concat_axis=0, tiled=True)  6.13 us
    add x1, other arithmetic, to_world_rows(): coeffs[0] * points[:, 0] + coeffs[1] * points[:, 1]  4.94 us
    all_to_all x1, starting transfers between devices, local(): lax.all_to_all(remote_a.reshape(peers, CAP * 18), axes, split_axis=0, con...  4.48 us
    unnamed x21, local copies, waits for them, and re-layouts  4.28 us
  transfers between devices with their start and end apart: 2, of which 2 were waited for; matrix products, arithmetic and copies ran while one was open for 24% of the time, Pallas kernels for 3%

profile of v2, /device:TPU:1, one launch (start us, length us, event | category | flops | bytes accessed | tf_op | source)
XLA Modules:
  0.0 109.4 jit_solution(9370684414543209893)
XLA Ops:
  0.6 0.8 slice_bitcast_fusion.6
  1.4 0.7 slice_multiply_fusion.4
  2.2 0.1 mul.406
  2.4 0.1 mul.416
  2.5 0.1 mul.399
  3.0 0.1 mul.435
  3.4 0.1 mul.421
  3.9 0.1 add.355
  4.0 0.8 copy.65
  4.8 0.1 reshape.1456
  4.8 0.7 compare_select_fusion.9
  5.6 0.7 fusion.16
  6.3 1.1 fusion.38
  7.4 1.1 fusion.37
  8.5 0.2 reshape.1527
  8.6 2.8 %gather_fusion.5 = f32[1024,12]{1,0:T(8,128)S(1)} fusion(f32[8,12]{1,0:T(8,128)S(1)} %bitcast.182, s32[1024]{0:T(1024)S(1)} %broadcast_clamp_fusion.1), kind=kCustom, calls=%fused_computation.5 | custom fusion | bytes 102400 | tf_op jit(solution)/shard_map/gather | solution.py:195
  11.5 0.2 pad_maximum_fusion.3
  11.7 0.2 reshape.1458
  11.9 0.6 copy-done.3
  12.5 0.6 concatenate.57
  13.2 4.9 %add_add_fusion.2 = (f32[1,256,128]{2,0,1:T(1,128)S(1)}, f32[1,256,128]{2,0,1:T(1,128)S(1)}, f32[1,256,128]{2,0,1:T(1,128)S(1)}, f32[1,256,128]{2,0,1:T(1,128)},...) fusion(f32[1,256,128]{2,0,1:T(1,128)S(1)} %bitcast.197, f32[1,256,128]{2,0,1:T(1,128)S(1)} %bitcast.198, ...), kind=kLoop, calls=%fused_computation.34 | loop fusion | flops 1081344 | bytes 1585152 | tf_op jit(solution)/shard_map/add | solution.py:55
  18.1 0.3 pad_maximum_fusion.2
  18.5 3.6 %gather_fusion.4 = f32[1024,3,128]{2,1,0:T(4,128)S(1)} fusion(f32[3,256,128]{2,0,1:T(4,128)S(1)} %pad_maximum_fusion.2, s32[1024]{0:T(1024)S(1)} %broadcast_clamp_fusion.3), kind=kCustom, calls=%fused_computation.4 | custom fusion | bytes 3149824 | tf_op jit(solution)/shard_map/gather | solution.py:192
  22.0 0.9 pad_maximum_fusion.1
  23.0 1.7 %pad_maximum_fusion = f32[128,33,128]{2,1,0:T(8,128)} fusion(f32[128,1,128]{2,1,0:T(1,128)S(1)} %bitcast.202, f32[128,32,128]{2,1,0:T(8,128)S(1)} %bitcast.189), kind=kLoop, calls=%fused_computation.9 | loop fusion | flops 540672 | bytes 4325376 | tf_op jit(solution)/shard_map/concatenate | solution.py:198
  24.7 11.9 %all-to-all-start = ((f32[128,33,128]{2,1,0:T(8,128)}), f32[128,33,128]{2,1,0:T(8,128)}, u32[]{:S(2)}, u32[]{:S(2)}) async-start(f32[128,33,128]{2,1,0:T(8,128)} %pad_maximum_fusion), calls=%async_computation | async-start | bytes 5242880 | tf_op jit(solution)/shard_map/all_to_all | solution.py:199
  37.0 0.7 gather_fusion.3
  37.8 0.7 gather_fusion.2
  38.6 1.0 gather_fusion
  39.6 0.8 copy.88
  40.4 1.2 %stack.5 = f32[6,256,128]{2,0,1:T(8,128)S(1)} concatenate(f32[1,256,128]{2,0,1:T(1,128)S(1)} %get-tuple-element.20, f32[1,256,128]{2,0,1:T(1,128)S(1)} %get-tuple-element.22, f32[1,256,128]{2,0,1:T(1,128)S(1)} %get-tuple-element.21, f32[1,256,128]{2,0,1:T(1,128)S(1)} %copy-done, f32[1,256,128]{2,0,1:T(1,128)S(1)} %copy-done.1, f32[1,256,128]{2,0,1:T(1,128)S(1)} %copy-done.2), dimensions={0} | concatenate | bytes 1572864 | tf_op jit(solution)/shard_map/stack | solution.py:63
  41.6 1.0 gather_fusion.1
  42.7 1.0 copy.87
  43.7 0.7 maximum_maximum_fusion.1.aux_ref
  44.4 3.7 %shard_map.113 = f32[32,256]{1,0:T(8,128)} custom-call(f32[3,256,128]{2,1,0:T(8,128)} %bitcast.195, f32[6,256,128]{2,1,0:T(8,128)} %bitcast.192, s32[256,128]{1,0:T(8,128)} %map_ref.1, f32[32,256]{1,0:T(8,128)} %maximum_maximum_fusion.1.aux_ref), custom_call_target="tpu_custom_call" | custom-call | tf_op jit(solution)/shard_map/pallas_call | solution.py:126
  48.1 0.8 slice_bitcast_fusion.1
  48.9 2.8 %gather_fusion.7 = f32[1024,12]{1,0:T(8,128)S(1)} fusion(f32[8,12]{1,0:T(8,128)S(1)} %bitcast.185, s32[1024]{0:T(1024)S(1)} %broadcast_clamp_fusion), kind=kCustom, calls=%fused_computation.7 | custom fusion | bytes 102400 | tf_op jit(solution)/shard_map/gather | solution.py:219
  51.7 0.2 copy.73
  51.9 9.1 %gather_fusion.6 = f32[1024,6,128]{2,1,0:T(8,128)} fusion(f32[6,256,128]{2,0,1:T(8,128)S(1)} %stack.5, s32[1024]{0:T(1024)S(1)} %broadcast_clamp_fusion.2), kind=kCustom, calls=%fused_computation.6 | custom fusion | bytes 6295552 | tf_op jit(solution)/shard_map/gather | solution.py:217
  61.0 4.5 %copy.85 = f32[1024,6,128]{2,0,1:T(8,128)} copy(f32[1024,6,128]{2,1,0:T(8,128)} %gather_fusion.6) | data formatting | bytes 6291456 | tf_op jit(solution)/shard_map/gather | solution.py:217
  65.6 0.3 fusion.12
  65.9 0.3 convolution_add_fusion.1
  66.2 6.1 %all-to-all-done = f32[128,33,128]{2,1,0:T(8,128)} async-done(((f32[128,33,128]{2,1,0:T(8,128)}), f32[128,33,128]{2,1,0:T(8,128)}, u32[]{:S(2)}, u32[]{:S(2)}) %all-to-all-start) | async-done | bytes 2162720 | tf_op jit(solution)/shard_map/all_to_all | solution.py:199
  72.3 1.2 %slice_reduce_fusion.1 = f32[128,104]{1,0:T(8,128)S(1)} fusion(f32[128,33,128]{2,1,0:T(8,128)} %all-to-all-done), kind=kLoop, calls=%fused_computation.46 | loop fusion | bytes 106496 | tf_op jit(solution)/shard_map/slice | solution.py:214
  73.5 0.2 reshape_squeeze.3
  73.7 0.4 slice_reduce_fusion
  74.1 0.2 copy.80
  74.3 1.8 %slice.214 = f32[128,32,128]{2,1,0:T(8,128)S(1)} slice(f32[128,33,128]{2,1,0:T(8,128)} %all-to-all-done), slice={[0:128], [0:32], [0:128]} | slice | bytes 4194304 | tf_op jit(solution)/shard_map/slice | solution.py:213
  76.1 0.5 slice.216
  76.6 0.9 convert_bitcast_fusion.map_ref
  77.5 1.3 %copy.86 = f32[1024,3,128]{2,0,1:T(8,128)} copy(f32[1024,3,128]{2,1,0:T(4,128)S(1)} %bitcast.188) | data formatting | bytes 3145728
  78.7 0.7 maximum_maximum_fusion.aux_ref
  79.5 10.2 %shard_map.114 = f32[32,1024]{1,0:T(8,128)} custom-call(f32[3,1024,128]{2,1,0:T(8,128)} %bitcast.190, f32[6,1024,128]{2,1,0:T(8,128)} %bitcast.186, s32[1024,128]{1,0:T(8,128)} %convert_bitcast_fusion.map_ref, f32[32,1024]{1,0:T(8,128)} %maximum_maximum_fusion.aux_ref), custom_call_target="tpu_custom_call" | custom-call | tf_op jit(solution)/shard_map/pallas_call | solution.py:126
  89.6 0.9 slice_bitcast_fusion
  90.6 0.2 copy.74
  90.9 1.1 all_to_all.12
  91.9 4.5 %all-to-all-start.1 = ((f32[128,1,144]{2,1,0:T(1,128)}), f32[128,1,144]{2,1,0:T(1,128)S(1)}, u32[]{:S(2)}, u32[]{:S(2)}) async-start(f32[128,1,144]{2,1,0:T(1,128)} %all_to_all.12), calls=%async_computation.1 | async-start | bytes 262144 | tf_op jit(solution)/shard_map/all_to_all | solution.py:222
  96.5 0.6 convolution_add_fusion
  97.0 9.6 %all-to-all-done.1 = f32[128,1,144]{2,1,0:T(1,128)S(1)} async-done(((f32[128,1,144]{2,1,0:T(1,128)}), f32[128,1,144]{2,1,0:T(1,128)S(1)}, u32[]{:S(2)}, u32[]{:S(2)}) %all-to-all-start.1) | async-done | bytes 73760 | tf_op jit(solution)/shard_map/all_to_all | solution.py:222
  106.6 0.3 reduce.2
  106.9 0.2 reshape.1460
  107.1 0.7 convolution_add_fusion.2
  107.9 0.7 copy.76
  108.7 0.7 copy.77
  (71 shorter events, 2.1 us)
Async XLA Ops:
  11.5 1.0 copy-start.3
  22.0 1.0 copy-start.4
  24.7 12.1 %copy-start.7 = (s32[2,256]{1,0:T(2,128)S(1)}, s32[2,256]{1,0:T(2,128)}, u32[]{:S(2)}) copy-start(s32[2,256]{1,0:T(2,128)} %param.14) | copy-start | bytes 6148
  24.7 12.1 %copy-start.5 = (s32[1,1024]{1,0:T(1,128)S(1)}, s32[1,1024]{1,0:T(1,128)}, u32[]{:S(2)}) copy-start(s32[1,1024]{1,0:T(1,128)} %param.18) | copy-start | bytes 12292
  24.7 47.6 %all-to-all-start = ((f32[128,33,128]{2,1,0:T(8,128)}), f32[128,33,128]{2,1,0:T(8,128)}, u32[]{:S(2)}, u32[]{:S(2)}) async-start(f32[128,33,128]{2,1,0:T(8,128)} %pad_maximum_fusion), calls=%async_computation | async-start | bytes 5242880 | tf_op jit(solution)/shard_map/all_to_all | solution.py:199
  36.9 3.5 %copy-start = (f32[1,256,128]{2,0,1:T(1,128)S(1)}, f32[1,256,128]{2,0,1:T(1,128)}, u32[]{:S(2)}) copy-start(f32[1,256,128]{2,0,1:T(1,128)} %get-tuple-element.38) | copy-start | bytes 393220
  36.9 3.5 %copy-start.1 = (f32[1,256,128]{2,0,1:T(1,128)S(1)}, f32[1,256,128]{2,0,1:T(1,128)}, u32[]{:S(2)}) copy-start(f32[1,256,128]{2,0,1:T(1,128)} %get-tuple-element.39) | copy-start | bytes 393220
  36.9 3.4 %copy-start.2 = (f32[1,256,128]{2,0,1:T(1,128)S(1)}, f32[1,256,128]{2,0,1:T(1,128)}, u32[]{:S(2)}) copy-start(f32[1,256,128]{2,0,1:T(1,128)} %get-tuple-element.40) | copy-start | bytes 393220
  61.0 4.9 %copy-start.6 = (s32[1,1024]{1,0:T(1,128)S(1)}, s32[1,1024]{1,0:T(1,128)}, u32[]{:S(2)}) copy-start(s32[1,1024]{1,0:T(1,128)} %param.16) | copy-start | bytes 12292
  91.9 14.7 %all-to-all-start.1 = ((f32[128,1,144]{2,1,0:T(1,128)}), f32[128,1,144]{2,1,0:T(1,128)S(1)}, u32[]{:S(2)}, u32[]{:S(2)}) async-start(f32[128,1,144]{2,1,0:T(1,128)} %all_to_all.12), calls=%async_computation.1 | async-start | bytes 262144 | tf_op jit(solution)/shard_map/all_to_all | solution.py:222

commit v3 on v2

--- a/solution.py
+++ b/solution.py
@@ -1,3 +1,5 @@
+import functools
+
 import jax
 import jax.numpy as jnp
 from jax import lax
@@ -8,6 +10,7 @@
 BF = 32
 CAP = 8
 N_QTY = 27
+MESH = pl.DeviceIdType.MESH
 
 
 def rotations(poses):
@@ -151,6 +154,80 @@
     return jnp.concatenate([ga, ha], axis=1), jnp.concatenate([gb, hb0, hb1], axis=1)
 
 
+def _exchange_kernel(n_band, x_ref, out_ref, send_sems, recv_sems, own_sem):
+    peers = x_ref.shape[0]
+    me = lax.axis_index("tile") * n_band + lax.axis_index("band")
+
+    def peer_of(k):
+        p = lax.rem(me + k, peers)
+        return p, (p // n_band, p % n_band)
+
+    barrier = pltpu.get_barrier_semaphore()
+
+    def greet(k, carry):
+        _, dev = peer_of(k)
+        pl.semaphore_signal(barrier, inc=1, device_id=dev, device_id_type=MESH)
+        return carry
+
+    lax.fori_loop(1, peers, greet, 0)
+    pl.semaphore_wait(barrier, peers - 1)
+
+    own = pltpu.make_async_copy(x_ref.at[me], out_ref.at[me], own_sem)
+    own.start()
+
+    def outgoing(k):
+        p, dev = peer_of(k)
+        return pltpu.make_async_remote_copy(
+            src_ref=x_ref.at[p],
+            dst_ref=out_ref.at[me],
+            send_sem=send_sems.at[p],
+            recv_sem=recv_sems.at[me],
+            device_id=dev,
+            device_id_type=MESH,
+        )
+
+    def incoming(k):
+        p, dev = peer_of(k)
+        return pltpu.make_async_remote_copy(
+            src_ref=x_ref.at[p],
+            dst_ref=out_ref.at[p],
+            send_sem=send_sems.at[p],
+            recv_sem=recv_sems.at[p],
+            device_id=dev,
+            device_id_type=MESH,
+        )
+
+    def start(k, carry):
+        outgoing(k).start()
+        return carry
+
+    lax.fori_loop(1, peers, start, 0)
+
+    def finish(k, carry):
+        outgoing(k).wait_send()
+        incoming(k).wait_recv()
+        return carry
+
+    lax.fori_loop(1, peers, finish, 0)
+    own.wait()
+
+
+def exchange(x, n_band, collective_id):
+    peers = x.shape[0]
+    return pl.pallas_call(
+        functools.partial(_exchange_kernel, n_band),
+        out_shape=jax.ShapeDtypeStruct(x.shape, x.dtype),
+        in_specs=[pl.BlockSpec(memory_space=pl.ANY)],
+        out_specs=pl.BlockSpec(memory_space=pl.ANY),
+        scratch_shapes=[
+            pltpu.SemaphoreType.DMA((peers,)),
+            pltpu.SemaphoreType.DMA((peers,)),
+            pltpu.SemaphoreType.DMA(()),
+        ],
+        compiler_params=pltpu.CompilerParams(collective_id=collective_id, has_side_effects=True),
+    )(x)
+
+
 def frag_sums(blocks, terms, frag_count):
     onehot = (blocks[:, None] // BF == jnp.arange(frag_count, dtype=jnp.int32)[None, :]).astype(
         jnp.float32
@@ -177,7 +254,7 @@
     remote_dst,
     counts,
 ):
-    axes = ("tile", "band")
+    n_band = lax.axis_size("band")
     frag_count = poses.shape[1]
     rows6 = to_world_rows(points, normals, poses, BF)
     frag_dirs = directions.reshape(12, frag_count).T
@@ -196,7 +273,7 @@
     side = side.reshape(peers, CAP * 13)
     side = jnp.concatenate([side, jnp.zeros((peers, 128 - CAP * 13), jnp.float32)], axis=1)
     cargo = jnp.concatenate([main, side[:, None, :]], axis=1)
-    arrived = lax.all_to_all(cargo, axes, split_axis=0, concat_axis=0, tiled=True)
+    arrived = exchange(cargo, n_band, 0)
 
     src_l = local_pairs[0]
     tgt_l = local_pairs[1]
@@ -219,9 +296,7 @@
         make_aux(side_in[:, 0:12], frag_dirs[target_blocks // BF], side_in[:, 12]),
     )
     remote_a, remote_b = split_terms(out_r)
-    returned = lax.all_to_all(
-        remote_a.reshape(peers, CAP * 18), axes, split_axis=0, concat_axis=0, tiled=True
-    ).reshape(peers * CAP, 18)
+    returned = exchange(remote_a.reshape(peers, 1, CAP * 18), n_band, 1).reshape(peers * CAP, 18)
 
     totals = frag_sums(src_l, local_a, frag_count) + frag_sums(tgt_l, local_b, frag_count)
     totals = (

time: 110 us -> 152 us (1.38)
  Pallas kernels: 13.9 us -> 77 us
  starting transfers between devices: 16.4 us -> 0 us
  waiting for transfers between devices: 15.7 us -> 0 us
  other arithmetic: 13.2 us -> 18.7 us
  local copies, waits for them, and re-layouts: 47.3 us -> 52 us
    pallas_call x0 -> x2, Pallas kernels: none -> 63.2 us  [exchange(): pl.pallas_call(functools.partial(_exchange_kernel, n_band), out_shape=jax...]
    all_to_all x2 -> x0, starting transfers between devices: 16.4 us -> none  [the longest x1 11.9 us: local(): lax.all_to_all(cargo, axes, split_axis=0, concat_axis=0, tiled=True)]
    all_to_all x2 -> x0, waiting for transfers between devices: 15.7 us -> none  [the longest x1 9.55 us: local(): lax.all_to_all(remote_a.reshape(peers, CAP * 18), axes, split_axis=0, con...]
    gather x1, local copies, waits for them, and re-layouts: 3.56 us -> 7.97 us  [local(): xa_send = jnp.transpose(rows6[0:3][:, source_blocks], (1, 0, 2))]
    concatenate x1, other arithmetic: 0.95 us -> 2.54 us  [local(): jnp.concatenate([xa_send, map_send], axis=1).reshape(peers, CAP * 4, 128)]
    unnamed x21 -> x9, local copies, waits for them, and re-layouts: 4.28 us -> 4.73 us
  transfers between devices with their start and end apart: 2 -> 0, of which waited for: 2 -> 0; matrix products, arithmetic and copies ran while one was open for 24% -> 0% of each run, Pallas kernels for 3% -> 0%
where the time goes in v3:
time: 152 us; the launch traced here: 151 us
  Pallas kernels  77 us (51%)
  local copies, waits for them, and re-layouts  52 us (34%)
  other arithmetic  18.7 us (12%)
  matrix products  1.81 us (1%)
    pallas_call x2, Pallas kernels, exchange(): pl.pallas_call(functools.partial(_exchange_kernel, n_band), out_shape=jax...  63.2 us
    pallas_call x2, Pallas kernels, pair_sums(): pl.pallas_call(_terms_kernel, out_shape=jax.ShapeDtypeStruct((32, pairs),...  13.9 us
    gather x2, local copies, waits for them, and re-layouts, local(): rows6[:, target_blocks]  13.5 us
    gather x1, local copies, waits for them, and re-layouts, local(): xa_send = jnp.transpose(rows6[0:3][:, source_blocks], (1, 0, 2))  7.97 us
    unnamed x9, local copies, waits for them, and re-layouts  4.73 us
    add x1, other arithmetic, to_world_rows(): coeffs[0] * points[:, 0] + coeffs[1] * points[:, 1]  3.99 us

profile of v3, /device:TPU:1, one launch (start us, length us, event | category | flops | bytes accessed | tf_op | source)
XLA Modules:
  0.0 150.6 jit_solution(2506085985387438571)
XLA Ops:
  0.8 0.8 slice_bitcast_fusion.6
  1.6 0.7 slice_multiply_fusion.4
  2.3 0.8 fusion.41
  3.2 0.1 mul.406
  3.4 0.1 mul.416
  3.5 0.1 mul.399
  3.7 0.1 add.348
  3.8 0.1 mul.431
  4.3 0.1 mul.412
  4.9 0.1 add.355
  4.9 0.7 add_select_fusion.1
  5.6 0.7 add_select_fusion
  6.3 0.8 compare_select_fusion.11
  7.2 0.8 copy.68
  8.0 0.7 compare_select_fusion.9
  8.8 0.7 compare_select_fusion
  9.5 0.7 fusion.16
  10.3 0.7 gather_fusion.3
  11.1 0.7 gather_fusion.2
  11.9 0.7 maximum_maximum_fusion.1.aux_ref
  12.7 4.0 %add_add_fusion.2 = (f32[1,256,128]{2,0,1:T(1,128)S(1)}, f32[1,256,128]{2,0,1:T(1,128)S(1)}, f32[1,256,128]{2,0,1:T(1,128)S(1)}, f32[1,256,128]{2,0,1:T(1,128)S(...) fusion(f32[1,256,128]{2,0,1:T(1,128)S(1)} %bitcast.197, f32[1,256,128]{2,0,1:T(1,128)S(1)} %bitcast.198, ...), kind=kLoop, calls=%fused_computation.34 | loop fusion | flops 1081344 | bytes 1585152 | tf_op jit(solution)/shard_map/add | solution.py:58
  16.7 0.2 reshape.1526
  16.8 2.8 %gather_fusion.7 = f32[1024,12]{1,0:T(8,128)S(1)} fusion(f32[8,12]{1,0:T(8,128)S(1)} %bitcast.184, s32[1024]{0:T(1024)S(1)} %broadcast_clamp_fusion), kind=kCustom, calls=%fused_computation.7 | custom fusion | bytes 102400 | tf_op jit(solution)/shard_map/gather | solution.py:296
  19.7 0.2 copy.76
  19.9 2.8 %gather_fusion.5 = f32[1024,12]{1,0:T(8,128)S(1)} fusion(f32[8,12]{1,0:T(8,128)S(1)} %bitcast.185, s32[1024]{0:T(1024)S(1)} %broadcast_clamp_fusion.1), kind=kCustom, calls=%fused_computation.5 | custom fusion | bytes 102400 | tf_op jit(solution)/shard_map/gather | solution.py:272
  22.7 0.2 pad_maximum_fusion.3
  22.9 0.2 reshape.1456
  23.1 0.3 pad_maximum_fusion.2
  23.4 1.2 stack.5
  24.7 1.0 gather_fusion
  25.7 0.8 copy.91
  26.5 1.1 convert_element_type.35
  27.6 1.0 gather_fusion.1
  28.6 1.0 copy.90
  29.6 3.7 %shard_map.113 = f32[32,256]{1,0:T(8,128)} custom-call(f32[3,256,128]{2,1,0:T(8,128)} %bitcast.195, f32[6,256,128]{2,1,0:T(8,128)} %bitcast.192, s32[256,128]{1,0:T(8,128)} %map_ref.1, f32[32,256]{1,0:T(8,128)} %maximum_maximum_fusion.1.aux_ref), custom_call_target="tpu_custom_call" | custom-call | tf_op jit(solution)/shard_map/pallas_call | solution.py:129
  33.4 0.8 slice_bitcast_fusion.1
  34.1 0.3 fusion.12
  34.5 0.3 convolution_add_fusion.1
  34.7 8.0 %gather_fusion.4 = f32[1024,3,128]{2,1,0:T(4,128)} fusion(f32[3,256,128]{2,0,1:T(4,128)S(1)} %pad_maximum_fusion.2, s32[1024]{0:T(1024)S(1)} %broadcast_clamp_fusion.3), kind=kCustom, calls=%fused_computation.4 | custom fusion | bytes 3149824 | tf_op jit(solution)/shard_map/gather | solution.py:269
  42.7 2.5 %pad_maximum_fusion.1 = f32[1024,4,128]{2,1,0:T(4,128)S(1)} fusion(f32[1024,1,128]{2,1,0:T(1,128)S(1)} %bitcast.193, f32[1024,3,128]{2,1,0:T(4,128)} %gather_fusion.4), kind=kLoop, calls=%fused_computation.10 | loop fusion | flops 524288 | bytes 4194304 | tf_op jit(solution)/shard_map/concatenate | solution.py:271
  45.2 1.8 %pad_maximum_fusion.x_ref = f32[128,33,128]{2,1,0:T(8,128)} fusion(f32[128,1,128]{2,1,0:T(1,128)S(1)} %bitcast.202, f32[128,32,128]{2,1,0:T(8,128)S(1)} %bitcast.189), kind=kLoop, calls=%fused_computation.9 | loop fusion | flops 540672 | bytes 4325376 | tf_op jit(solution)/shard_map/concatenate | solution.py:275
  47.0 47.3 %shard_map.114 = f32[128,33,128]{2,1,0:T(8,128)} custom-call(f32[128,33,128]{2,1,0:T(8,128)} %pad_maximum_fusion.x_ref), custom_call_target="tpu_custom_call" | custom-call | tf_op jit(solution)/shard_map/pallas_call | solution.py:217
  94.3 1.2 slice_reduce_fusion.1
  95.5 1.8 %slice.172 = f32[128,32,128]{2,1,0:T(8,128)S(1)} slice(f32[128,33,128]{2,1,0:T(8,128)} %shard_map.114), slice={[0:128], [0:32], [0:128]} | slice | bytes 4194304 | tf_op jit(solution)/shard_map/slice | solution.py:290
  97.3 1.0 reshape_squeeze.3
  98.3 1.4 slice_reduce_fusion
  99.7 1.2 copy.83
  101.0 0.7 maximum_maximum_fusion.aux_ref
  101.7 0.5 slice.215
  102.3 0.9 convert_bitcast_fusion.map_ref
  103.1 1.3 copy.89
  104.5 9.0 %gather_fusion.6 = f32[1024,6,128]{2,1,0:T(8,128)} fusion(f32[6,256,128]{2,0,1:T(8,128)S(1)} %stack.5, s32[1024]{0:T(1024)S(1)} %broadcast_clamp_fusion.2), kind=kCustom, calls=%fused_computation.6 | custom fusion | bytes 6295552 | tf_op jit(solution)/shard_map/gather | solution.py:294
  113.5 4.5 %copy.88 = f32[1024,6,128]{2,0,1:T(8,128)} copy(f32[1024,6,128]{2,1,0:T(8,128)} %gather_fusion.6) | data formatting | bytes 6291456 | tf_op jit(solution)/shard_map/gather | solution.py:294
  118.0 10.2 %shard_map.115 = f32[32,1024]{1,0:T(8,128)} custom-call(f32[3,1024,128]{2,1,0:T(8,128)} %bitcast.190, f32[6,1024,128]{2,1,0:T(8,128)} %bitcast.186, s32[1024,128]{1,0:T(8,128)} %convert_bitcast_fusion.map_ref, f32[32,1024]{1,0:T(8,128)} %maximum_maximum_fusion.aux_ref), custom_call_target="tpu_custom_call" | custom-call | tf_op jit(solution)/shard_map/pallas_call | solution.py:129
  128.2 0.9 slice_bitcast_fusion
  129.2 0.6 convolution_add_fusion
  129.8 0.2 copy.77
  130.0 1.1 reshape.1527.x_ref
  131.1 15.8 %shard_map.116 = f32[128,1,144]{2,1,0:T(1,128)} custom-call(f32[128,1,144]{2,1,0:T(1,128)} %reshape.1527.x_ref), custom_call_target="tpu_custom_call" | custom-call | tf_op jit(solution)/shard_map/pallas_call | solution.py:217
  146.9 1.2 reduce.2
  148.1 0.2 reshape.1459
  148.3 0.7 convolution_add_fusion.2
  149.1 0.7 copy.79
  149.9 0.7 copy.80
  (57 shorter events, 2.1 us)
Async XLA Ops:
  0.6 12.0 %copy-start.1 = (f32[256,3,128]{2,0,1:T(8,128)S(1)}, f32[256,3,128]{2,0,1:T(8,128)}, u32[]{:S(2)}) copy-start(f32[256,3,128]{2,0,1:T(8,128)} %param.11) | copy-start | bytes 1179652
  0.6 11.9 %copy-start = (f32[256,3,128]{2,0,1:T(8,128)S(1)}, f32[256,3,128]{2,0,1:T(8,128)}, u32[]{:S(2)}) copy-start(f32[256,3,128]{2,0,1:T(8,128)} %param.10) | copy-start | bytes 1179652

commit v4 on v2

--- a/solution.py
+++ b/solution.py
@@ -1,3 +1,5 @@
+import functools
+
 import jax
 import jax.numpy as jnp
 from jax import lax
@@ -60,16 +62,31 @@
         normal_rows.append(
             coeffs[0] * normals[:, 0] + coeffs[1] * normals[:, 1] + coeffs[2] * normals[:, 2]
         )
-    return jnp.stack(world_rows + normal_rows, axis=0)
-
-
-def _terms_kernel(xa_ref, tb_ref, map_ref, aux_ref, out_ref, xt_ref, gt_ref):
+    return jnp.stack(world_rows + normal_rows, axis=1)
+
+
+def _terms_kernel(map_in_a, a_blk, a_row, t_idx, a_ref, w_ref, map_ref, aux_ref, out_ref, xs_ref, ts_ref, ms_ref, xt_ref, gt_ref):
     chunk = out_ref.shape[1]
-    idx = map_ref[...]
+    base = pl.program_id(0) * chunk
+
+    def fill(j, carry):
+        blk = a_blk[base + j]
+        row = a_row[base + j]
+        tgt = t_idx[base + j]
+        for c in range(3):
+            xs_ref[c, pl.ds(j, 1), :] = a_ref[blk, pl.ds(row + c, 1), :]
+        for c in range(6):
+            ts_ref[c, pl.ds(j, 1), :] = w_ref[tgt, pl.ds(c, 1), :]
+        if map_in_a:
+            ms_ref[pl.ds(j, 1), :] = a_ref[blk, pl.ds(row + 3, 1), :].astype(jnp.int32)
+        return carry
+
+    lax.fori_loop(0, chunk, fill, 0)
+    idx = ms_ref[...] if map_in_a else map_ref[...]
     for c in range(3):
-        xt_ref[c] = xa_ref[c].T
+        xt_ref[c] = xs_ref[c].T
     for c in range(6):
-        picked = jnp.take_along_axis(tb_ref[c], idx, axis=1, mode="promise_in_bounds")
+        picked = jnp.take_along_axis(ts_ref[c], idx, axis=1, mode="promise_in_bounds")
         gt_ref[c] = picked.T
 
     def col(q):
@@ -121,24 +138,36 @@
     out_ref[N_QTY:, :] = jnp.zeros((32 - N_QTY, chunk), jnp.float32)
 
 
-def pair_sums(xa, tb, maps, aux, chunk=128):
-    pairs = maps.shape[0]
+def pair_sums(a_blk, a_row, t_idx, a_src, world, maps, aux, chunk=128):
+    pairs = a_blk.shape[0]
+    map_in_a = maps is None
+    if map_in_a:
+        maps = jnp.zeros((8, 128), jnp.int32)
+        map_spec = pl.BlockSpec((8, 128), lambda i, *_: (0, 0))
+    else:
+        map_spec = pl.BlockSpec((chunk, 128), lambda i, *_: (i, 0))
     return pl.pallas_call(
-        _terms_kernel,
+        functools.partial(_terms_kernel, map_in_a),
         out_shape=jax.ShapeDtypeStruct((32, pairs), jnp.float32),
-        grid=(pairs // chunk,),
-        in_specs=[
-            pl.BlockSpec((3, chunk, 128), lambda i: (0, i, 0)),
-            pl.BlockSpec((6, chunk, 128), lambda i: (0, i, 0)),
-            pl.BlockSpec((chunk, 128), lambda i: (i, 0)),
-            pl.BlockSpec((32, chunk), lambda i: (0, i)),
-        ],
-        out_specs=pl.BlockSpec((32, chunk), lambda i: (0, i)),
-        scratch_shapes=[
-            pltpu.VMEM((3, 128, chunk), jnp.float32),
-            pltpu.VMEM((6, 128, chunk), jnp.float32),
-        ],
-    )(xa, tb, maps, aux)
+        grid_spec=pltpu.PrefetchScalarGridSpec(
+            num_scalar_prefetch=3,
+            grid=(pairs // chunk,),
+            in_specs=[
+                pl.BlockSpec(a_src.shape, lambda i, *_: (0, 0, 0)),
+                pl.BlockSpec(world.shape, lambda i, *_: (0, 0, 0)),
+                map_spec,
+                pl.BlockSpec((32, chunk), lambda i, *_: (0, i)),
+            ],
+            out_specs=pl.BlockSpec((32, chunk), lambda i, *_: (0, i)),
+            scratch_shapes=[
+                pltpu.VMEM((3, chunk, 128), jnp.float32),
+                pltpu.VMEM((6, chunk, 128), jnp.float32),
+                pltpu.VMEM((chunk, 128), jnp.int32),
+                pltpu.VMEM((3, 128, chunk), jnp.float32),
+                pltpu.VMEM((6, 128, chunk), jnp.float32),
+            ],
+        ),
+    )(a_blk, a_row, t_idx, a_src, world, maps, aux)
 
 
 def split_terms(out):
@@ -179,7 +208,7 @@
 ):
     axes = ("tile", "band")
     frag_count = poses.shape[1]
-    rows6 = to_world_rows(points, normals, poses, BF)
+    world = to_world_rows(points, normals, poses, BF)
     frag_dirs = directions.reshape(12, frag_count).T
     peers = counts.shape[1]
 
@@ -189,7 +218,7 @@
         .astype(jnp.float32)
         .reshape(-1)
     )
-    xa_send = jnp.transpose(rows6[0:3][:, source_blocks], (1, 0, 2))
+    xa_send = world[source_blocks, 0:3]
     map_send = remote_maps[0].astype(jnp.float32)[:, None, :]
     main = jnp.concatenate([xa_send, map_send], axis=1).reshape(peers, CAP * 4, 128)
     side = jnp.concatenate([frag_dirs[source_blocks // BF], valid[:, None]], axis=1)
@@ -202,20 +231,26 @@
     tgt_l = local_pairs[1]
     ones = jnp.ones((src_l.shape[0],), jnp.float32)
     out_l = pair_sums(
-        rows6[0:3][:, src_l],
-        rows6[:, tgt_l],
+        src_l,
+        jnp.zeros_like(src_l),
+        tgt_l,
+        world,
+        world,
         local_maps,
         make_aux(frag_dirs[src_l // BF], frag_dirs[tgt_l // BF], ones),
     )
     local_a, local_b = split_terms(out_l)
 
     target_blocks = remote_dst[0]
-    main_in = arrived[:, 0 : CAP * 4].reshape(peers * CAP, 4, 128)
+    slots = jnp.arange(peers * CAP, dtype=jnp.int32)
     side_in = arrived[:, CAP * 4, 0 : CAP * 13].reshape(peers * CAP, 13)
     out_r = pair_sums(
-        jnp.transpose(main_in[:, 0:3], (1, 0, 2)),
-        rows6[:, target_blocks],
-        main_in[:, 3].astype(jnp.int32),
+        slots // CAP,
+        (slots % CAP) * 4,
+        target_blocks,
+        arrived,
+        world,
+        None,
         make_aux(side_in[:, 0:12], frag_dirs[target_blocks // BF], side_in[:, 12]),
     )
     remote_a, remote_b = split_terms(out_r)

time: 110 us -> 121 us (1.10)
  local copies, waits for them, and re-layouts: 47.3 us -> 28.7 us
  Pallas kernels: 13.9 us -> 32.2 us
  waiting for transfers between devices: 15.7 us -> 29.2 us
  other arithmetic: 13.2 us -> 11.7 us
    pallas_call x2, Pallas kernels: 13.9 us -> 32.2 us  [pair_sums(): pl.pallas_call(functools.partial(_terms_kernel, map_in_a), out_shape=jax....]
    gather x7 -> x1, local copies, waits for them, and re-layouts: 21 us -> 4.27 us  [local(): xa_send = world[source_blocks, 0:3]]
    all_to_all x1, waiting for transfers between devices: 6.13 us -> 19.7 us  [local(): lax.all_to_all(cargo, axes, split_axis=0, concat_axis=0, tiled=True)]
    unnamed x21 -> x24, local copies, waits for them, and re-layouts: 4.28 us -> 1.7 us
    slice x2 -> x0, local copies, waits for them, and re-layouts: 2.33 us -> none  [the longest x1 1.79 us: local(): main_in = arrived[:, 0:CAP * 4].reshape(peers * CAP, 4, 128)]
    add x1, other arithmetic: 4.94 us -> 3.17 us  [to_world_rows(): coeffs[0] * points[:, 0] + coeffs[1] * points[:, 1]]
    concatenate x0 -> x1, local copies, waits for them, and re-layouts: none -> 1.35 us  [local(): jnp.concatenate([xa_send, map_send], axis=1).reshape(peers, CAP * 4, 128)]
  transfers between devices with their start and end apart: 2 -> 2, of which waited for: 2 -> 2; matrix products, arithmetic and copies ran while one was open for 24% -> 8% of each run, Pallas kernels for 3% -> 6%
where the time goes in v4:
time: 121 us
  Pallas kernels  32.2 us (27%)
  waiting for transfers between devices  29.2 us (24%)
  local copies, waits for them, and re-layouts  28.7 us (24%)
  starting transfers between devices  16 us (13%)
  other arithmetic  11.7 us (10%)
  matrix products  1.8 us (1%)
    pallas_call x2, Pallas kernels, pair_sums(): pl.pallas_call(functools.partial(_terms_kernel, map_in_a), out_shape=jax....  32.2 us
    all_to_all x1, waiting for transfers between devices, local(): lax.all_to_all(cargo, axes, split_axis=0, concat_axis=0, tiled=True)  19.7 us
    all_to_all x1, starting transfers between devices, local(): lax.all_to_all(cargo, axes, split_axis=0, concat_axis=0, tiled=True)  11.5 us
    all_to_all x1, waiting for transfers between devices, local(): lax.all_to_all(remote_a.reshape(peers, CAP * 18), axes, split_axis=0, con...  9.54 us
    all_to_all x1, starting transfers between devices, local(): lax.all_to_all(remote_a.reshape(peers, CAP * 18), axes, split_axis=0, con...  4.48 us
    gather x1, local copies, waits for them, and re-layouts, local(): xa_send = world[source_blocks, 0:3]  4.27 us
    gather x1, local copies, waits for them, and re-layouts, local(): frag_dirs[source_blocks // BF]  4 us
    add x1, other arithmetic, to_world_rows(): coeffs[0] * points[:, 0] + coeffs[1] * points[:, 1]  3.17 us
  transfers between devices with their start and end apart: 2, of which 2 were waited for; matrix products, arithmetic and copies ran while one was open for 8% of the time, Pallas kernels for 6%

profile of v4, /device:TPU:1, one launch (start us, length us, event | category | flops | bytes accessed | tf_op | source)
XLA Modules:
  0.0 120.7 jit_solution(12174960739777610646)
XLA Ops:
  0.6 0.7 slice_multiply_fusion.4
  1.4 0.8 slice_bitcast_fusion.4
  2.2 0.1 mul.314
  2.4 0.1 mul.329
  2.5 0.1 mul.304
  2.7 0.1 mul.310
  2.8 0.1 mul.325
  3.0 0.1 mul.337
  3.1 0.1 mul.297
  3.3 0.1 mul.319
  3.4 0.1 mul.333
  3.5 1.1 fusion.48
  4.6 1.1 fusion.47
  6.0 0.1 add.254
  6.1 0.1 mul.315
  6.2 0.1 mul.330
  6.3 0.1 mul.298
  6.4 3.2 %add_add_fusion = (f32[256,1,128]{2,1,0:T(1,128)S(1)}, f32[256,1,128]{2,1,0:T(1,128)S(1)}, f32[256,1,128]{2,1,0:T(1,128)S(1)}, f32[256,1,128]{2,1,0:T(1,128)S(1)...) fusion(f32[256,1,128]{2,1,0:T(1,128)S(1)} %bitcast.178, f32[256,1,128]{2,1,0:T(1,128)S(1)} %bitcast.177, ...), kind=kLoop, calls=%fused_computation.24 | loop fusion | flops 1081344 | bytes 1975296 | tf_op jit(solution)/shard_map/add | solution.py:57
  9.6 1.2 %stack.2.a_ref.w_ref = f32[256,6,128]{2,1,0:T(8,128)S(1)} concatenate(f32[256,1,128]{2,1,0:T(1,128)S(1)} %get-tuple-element.24, f32[256,1,128]{2,1,0:T(1,128)S(1)} %get-tuple-element.23, f32[256,1,128]{2,1,0:T(1,128)S(1)} %get-tuple-element.22, f32[256,1,128]{2,1,0:T(1,128)S(1)} %get-tuple-element.25, f32[256,1,128]{2,1,0:T(1,128)S(1)} %get-tuple-element.26, ...), dimensions={1} | concatenate | bytes 1572864 | tf_op jit(solution)/shard_map/stack | solution.py:65
  10.9 0.2 copy.112
  11.1 0.9 convert_bitcast_fusion
  12.0 4.3 %gather_fusion.2 = f32[1024,3,128]{2,0,1:T(8,128)S(1)} fusion(f32[256,6,128]{2,0,1:T(8,128)S(1)} %copy.112, s32[1024]{0:T(1024)S(1)} %bitcast.170), kind=kCustom, calls=%fused_computation.2 | custom fusion | bytes 3153920 | tf_op jit(solution)/shard_map/gather | solution.py:221
  16.3 1.2 %pad_maximum_fusion.1 = f32[1024,4,128]{2,0,1:T(8,128)S(1)} fusion(f32[1024,1,128]{2,0,1:T(8,128)} %convert_bitcast_fusion, f32[1024,3,128]{2,0,1:T(8,128)S(1)} %gather_fusion.2), kind=kLoop, calls=%fused_computation.6 | loop fusion | flops 524288 | bytes 4194304 | tf_op jit(solution)/shard_map/concatenate | solution.py:223
  17.5 1.4 %copy.113 = f32[1024,4,128]{2,1,0:T(4,128)S(1)} copy(f32[1024,4,128]{2,0,1:T(8,128)S(1)} %pad_maximum_fusion.1) | data formatting | bytes 4194304 | tf_op jit(solution)/shard_map/concatenate | solution.py:223
  18.9 0.1 copy.109
  19.0 0.1 reshape.720
  19.1 0.1 fusion.16
  19.2 0.2 reshape.764
  19.4 4.0 %gather_fusion.3 = f32[1024,12]{1,0:T(8,128)} fusion(f32[8,12]{1,0:T(8,128)S(1)} %bitcast.166, s32[1024]{0:T(1024)S(1)} %broadcast_clamp_fusion.1), kind=kCustom, calls=%fused_computation.3 | custom fusion | bytes 102400 | tf_op jit(solution)/shard_map/gather | solution.py:224
  23.4 1.2 %pad_maximum_fusion.2 = f32[1024,13]{1,0:T(8,128)S(1)} fusion(f32[1024,1]{1,0:T(8,128)S(1)} %reshape.764, f32[1024,12]{1,0:T(8,128)} %gather_fusion.3), kind=kLoop, calls=%fused_computation.11 | loop fusion | flops 13312 | bytes 106496 | tf_op jit(solution)/shard_map/concatenate | solution.py:224
  24.6 0.2 reshape.722
  24.8 1.7 %pad_maximum_fusion = f32[128,33,128]{2,1,0:T(8,128)} fusion(f32[128,1,128]{2,1,0:T(1,128)S(1)} %bitcast.182, f32[128,32,128]{2,1,0:T(8,128)S(1)} %bitcast.171), kind=kLoop, calls=%fused_computation.5 | loop fusion | flops 540672 | bytes 4325376 | tf_op jit(solution)/shard_map/concatenate | solution.py:227
  26.5 11.5 %all-to-all-start = ((f32[128,33,128]{2,1,0:T(8,128)}), f32[128,33,128]{2,1,0:T(8,128)S(1)}, u32[]{:S(2)}, u32[]{:S(2)}) async-start(f32[128,33,128]{2,1,0:T(8,128)} %pad_maximum_fusion), calls=%async_computation | async-start | bytes 5242880 | tf_op jit(solution)/shard_map/all_to_all | solution.py:228
  38.1 0.6 fusion.51
  38.7 0.7 gather_fusion
  39.5 0.7 gather_fusion.1
  40.5 0.7 maximum_maximum_fusion.1.aux_ref
  41.2 0.6 broadcast.501.a_row
  41.8 7.5 %shard_map.113 = f32[32,256]{1,0:T(8,128)} custom-call(s32[256]{0:T(256)} %bitcast.195, s32[256]{0:T(256)} %broadcast.501.a_row, s32[256]{0:T(256)} %bitcast.193, f32[256,6,128]{2,1,0:T(8,128)} %copy-done, f32[256,6,128]{2,1,0:T(8,128)} %copy-done, s32[256,128]{1,0:T(8,128)} %map_ref.1, f32[32,256]{1,0:T(8,128)} %maximum_maximum_fusion.1.aux_ref), custom_call_target="tpu_custom_call" | custom-call | tf_op jit(solution)/shard_map/pallas_call | solution.py:149
  49.3 0.8 slice_bitcast_fusion.1
  50.1 2.8 %gather_fusion.4 = f32[1024,12]{1,0:T(8,128)S(1)} fusion(f32[8,12]{1,0:T(8,128)S(1)} %bitcast.169, s32[1024]{0:T(1024)S(1)} %broadcast_clamp_fusion), kind=kCustom, calls=%fused_computation.4 | custom fusion | bytes 102400 | tf_op jit(solution)/shard_map/gather | solution.py:254
  52.9 0.2 copy.116
  53.1 0.6 add_select_fusion.1
  53.8 0.3 fusion.12
  54.1 0.3 convolution_add_fusion.1
  54.4 19.7 %all-to-all-done.a_ref = f32[128,33,128]{2,1,0:T(8,128)S(1)} async-done(((f32[128,33,128]{2,1,0:T(8,128)}), f32[128,33,128]{2,1,0:T(8,128)S(1)}, u32[]{:S(2)}, u32[]{:S(2)}) %all-to-all-start) | async-done | bytes 2162720 | tf_op jit(solution)/shard_map/all_to_all | solution.py:228
  74.0 0.2 slice_reduce_fusion.1
  74.2 0.2 reshape_squeeze.3
  74.4 0.4 slice_reduce_fusion
  74.8 0.2 copy.127
  75.0 0.7 maximum_maximum_fusion.aux_ref
  75.7 0.6 broadcast_in_dim.75.map_ref
  76.3 24.7 %shard_map.114 = f32[32,1024]{1,0:T(8,128)} custom-call(s32[1024]{0:T(1024)} %get-tuple-element.62.a_blk, s32[1024]{0:T(1024)} %get-tuple-element.63.a_row, s32[1024]{0:T(1024)} %bitcast.187, f32[128,33,128]{2,1,0:T(8,128)} %copy-done.1, f32[256,6,128]{2,1,0:T(8,128)} %copy-done, s32[8,128]{1,0:T(8,128)} %broadcast_in_dim.75.map_ref, ...), custom_call_target="tpu_custom_call" | custom-call | tf_op jit(solution)/shard_map/pallas_call | solution.py:149
  101.0 0.9 slice_bitcast_fusion
  102.0 0.2 copy.117
  102.2 1.1 all_to_all.12
  103.3 4.5 %all-to-all-start.1 = ((f32[128,1,144]{2,1,0:T(1,128)}), f32[128,1,144]{2,1,0:T(1,128)S(1)}, u32[]{:S(2)}, u32[]{:S(2)}) async-start(f32[128,1,144]{2,1,0:T(1,128)} %all_to_all.12), calls=%async_computation.1 | async-start | bytes 262144 | tf_op jit(solution)/shard_map/all_to_all | solution.py:257
  107.8 0.6 convolution_add_fusion
  108.4 9.5 %all-to-all-done.1 = f32[128,1,144]{2,1,0:T(1,128)S(1)} async-done(((f32[128,1,144]{2,1,0:T(1,128)}), f32[128,1,144]{2,1,0:T(1,128)S(1)}, u32[]{:S(2)}, u32[]{:S(2)}) %all-to-all-start.1) | async-done | bytes 73760 | tf_op jit(solution)/shard_map/all_to_all | solution.py:257
  117.9 0.3 reduce.2
  118.2 0.2 reshape.723
  118.4 0.7 convolution_add_fusion.2
  119.3 0.7 copy.120
  120.0 0.7 copy.119
  (69 shorter events, 1.8 us)
Async XLA Ops:
  9.6 1.4 %copy-start.4 = (s32[1,1024]{1,0:T(1,128)S(1)}, s32[1,1024]{1,0:T(1,128)}, u32[]{:S(2)}) copy-start(s32[1,1024]{1,0:T(1,128)} %param.16) | copy-start | bytes 12292
  9.6 1.5 %copy-start.2 = (s32[1,1024,128]{2,1,0:T(8,128)S(1)}, s32[1,1024,128]{2,1,0:T(8,128)}, u32[]{:S(2)}) copy-start(s32[1,1024,128]{2,1,0:T(8,128)} %param.17) | copy-start | bytes 1572868
  10.9 5.4 %copy-start = (f32[256,6,128]{2,1,0:T(8,128)}, f32[256,6,128]{2,1,0:T(8,128)S(1)}, u32[]{:S(2)}) copy-start(f32[256,6,128]{2,1,0:T(8,128)S(1)} %stack.2.a_ref.w_ref) | copy-start | bytes 2359300
  17.5 1.4 %copy-start.8 = (f32[2,6,8]{2,0,1:T(2,128)S(1)}, f32[2,6,8]{2,0,1:T(2,128)}, u32[]{:S(2)}) copy-start(f32[2,6,8]{2,0,1:T(2,128)} %param.13) | copy-start | bytes 1156
  17.5 1.6 %copy-start.9 = (s32[1,128]{1,0:T(1,128)S(1)}, s32[1,128]{1,0:T(1,128)}, u32[]{:S(2)}) copy-start(s32[1,128]{1,0:T(1,128)} %param.19) | copy-start | bytes 1540
  26.5 11.5 %copy-start.7 = (s32[2,256]{1,0:T(2,128)S(1)}, s32[2,256]{1,0:T(2,128)}, u32[]{:S(2)}) copy-start(s32[2,256]{1,0:T(2,128)} %param.14) | copy-start | bytes 6148
  26.5 12.1 %copy-start.3 = (s32[1,1024]{1,0:T(1,128)S(1)}, s32[1,1024]{1,0:T(1,128)}, u32[]{:S(2)}) copy-start(s32[1,1024]{1,0:T(1,128)} %param.18) | copy-start | bytes 12292
  26.5 47.5 %all-to-all-start = ((f32[128,33,128]{2,1,0:T(8,128)}), f32[128,33,128]{2,1,0:T(8,128)S(1)}, u32[]{:S(2)}, u32[]{:S(2)}) async-start(f32[128,33,128]{2,1,0:T(8,128)} %pad_maximum_fusion), calls=%async_computation | async-start | bytes 5242880 | tf_op jit(solution)/shard_map/all_to_all | solution.py:228
  50.0 3.7 %copy-start.6 = (s32[1,256]{1,0:T(1,128)S(1)}, s32[1,256]{1,0:T(1,128)}, u32[]{:S(2)}) copy-start(s32[1,256]{1,0:T(1,128)} %get-tuple-element.59) | copy-start | bytes 3076
  50.1 3.7 %copy-start.5 = (s32[1,256]{1,0:T(1,128)S(1)}, s32[1,256]{1,0:T(1,128)}, u32[]{:S(2)}) copy-start(s32[1,256]{1,0:T(1,128)} %get-tuple-element.58) | copy-start | bytes 3076
  74.0 2.2 %copy-start.1 = (f32[128,33,128]{2,1,0:T(8,128)}, f32[128,33,128]{2,1,0:T(8,128)S(1)}, u32[]{:S(2)}) copy-start(f32[128,33,128]{2,1,0:T(8,128)S(1)} %all-to-all-done.a_ref) | copy-start | bytes 6488068
  103.3 14.7 %all-to-all-start.1 = ((f32[128,1,144]{2,1,0:T(1,128)}), f32[128,1,144]{2,1,0:T(1,128)S(1)}, u32[]{:S(2)}, u32[]{:S(2)}) async-start(f32[128,1,144]{2,1,0:T(1,128)} %all_to_all.12), calls=%async_computation.1 | async-start | bytes 262144 | tf_op jit(solution)/shard_map/all_to_all | solution.py:257

commit v5 on v2

--- a/solution.py
+++ b/solution.py
@@ -1,3 +1,5 @@
+import functools
+
 import jax
 import jax.numpy as jnp
 from jax import lax
@@ -63,11 +65,19 @@
     return jnp.stack(world_rows + normal_rows, axis=0)
 
 
-def _terms_kernel(xa_ref, tb_ref, map_ref, aux_ref, out_ref, xt_ref, gt_ref):
+def _terms_kernel(from_cargo, xa_ref, tb_ref, map_ref, aux_ref, out_ref, xt_ref, gt_ref):
     chunk = out_ref.shape[1]
-    idx = map_ref[...]
-    for c in range(3):
-        xt_ref[c] = xa_ref[c].T
+    if from_cargo:
+        def cargo_rows(r):
+            return xa_ref[:, pl.ds(r, CAP, stride=4), :].reshape(chunk, 128)
+
+        idx = cargo_rows(3).astype(jnp.int32)
+        for c in range(3):
+            xt_ref[c] = cargo_rows(c).T
+    else:
+        idx = map_ref[...]
+        for c in range(3):
+            xt_ref[c] = xa_ref[c].T
     for c in range(6):
         picked = jnp.take_along_axis(tb_ref[c], idx, axis=1, mode="promise_in_bounds")
         gt_ref[c] = picked.T
@@ -122,15 +132,23 @@
 
 
 def pair_sums(xa, tb, maps, aux, chunk=128):
-    pairs = maps.shape[0]
+    pairs = tb.shape[1]
+    from_cargo = maps is None
+    if from_cargo:
+        xa_spec = pl.BlockSpec((chunk // CAP, xa.shape[1], 128), lambda i: (i, 0, 0))
+        maps = jnp.zeros((8, 128), jnp.int32)
+        map_spec = pl.BlockSpec((8, 128), lambda i: (0, 0))
+    else:
+        xa_spec = pl.BlockSpec((3, chunk, 128), lambda i: (0, i, 0))
+        map_spec = pl.BlockSpec((chunk, 128), lambda i: (i, 0))
     return pl.pallas_call(
-        _terms_kernel,
+        functools.partial(_terms_kernel, from_cargo),
         out_shape=jax.ShapeDtypeStruct((32, pairs), jnp.float32),
         grid=(pairs // chunk,),
         in_specs=[
-            pl.BlockSpec((3, chunk, 128), lambda i: (0, i, 0)),
+            xa_spec,
             pl.BlockSpec((6, chunk, 128), lambda i: (0, i, 0)),
-            pl.BlockSpec((chunk, 128), lambda i: (i, 0)),
+            map_spec,
             pl.BlockSpec((32, chunk), lambda i: (0, i)),
         ],
         out_specs=pl.BlockSpec((32, chunk), lambda i: (0, i)),
@@ -189,10 +207,17 @@
         .astype(jnp.float32)
         .reshape(-1)
     )
-    xa_send = jnp.transpose(rows6[0:3][:, source_blocks], (1, 0, 2))
+    pick = (source_blocks[:, None] == jnp.arange(points.shape[0], dtype=jnp.int32)[None, :]).astype(
+        jnp.float32
+    )
+    xa_send = jnp.einsum("sb,cbk->sck", pick, rows6[0:3], precision=lax.Precision.HIGHEST)
     map_send = remote_maps[0].astype(jnp.float32)[:, None, :]
     main = jnp.concatenate([xa_send, map_send], axis=1).reshape(peers, CAP * 4, 128)
-    side = jnp.concatenate([frag_dirs[source_blocks // BF], valid[:, None]], axis=1)
+    frag_pick = (
+        source_blocks[:, None] // BF == jnp.arange(frag_count, dtype=jnp.int32)[None, :]
+    ).astype(jnp.float32)
+    dirs_send = jnp.dot(frag_pick, frag_dirs, precision=lax.Precision.HIGHEST)
+    side = jnp.concatenate([dirs_send, valid[:, None]], axis=1)
     side = side.reshape(peers, CAP * 13)
     side = jnp.concatenate([side, jnp.zeros((peers, 128 - CAP * 13), jnp.float32)], axis=1)
     cargo = jnp.concatenate([main, side[:, None, :]], axis=1)
@@ -210,12 +235,11 @@
     local_a, local_b = split_terms(out_l)
 
     target_blocks = remote_dst[0]
-    main_in = arrived[:, 0 : CAP * 4].reshape(peers * CAP, 4, 128)
     side_in = arrived[:, CAP * 4, 0 : CAP * 13].reshape(peers * CAP, 13)
     out_r = pair_sums(
-        jnp.transpose(main_in[:, 0:3], (1, 0, 2)),
+        arrived,
         rows6[:, target_blocks],
-        main_in[:, 3].astype(jnp.int32),
+        None,
         make_aux(side_in[:, 0:12], frag_dirs[target_blocks // BF], side_in[:, 12]),
     )
     remote_a, remote_b = split_terms(out_r)

time: 110 us -> 94.9 us (0.86)
  local copies, waits for them, and re-layouts: 47.3 us -> 35.5 us
  other arithmetic: 13.2 us -> 8.25 us
  matrix products: 1.81 us -> 3.33 us
    gather x2 -> x0, local copies, waits for them, and re-layouts: 6.37 us -> none  [the longest x1 3.56 us: local(): xa_send = jnp.transpose(rows6[0:3][:, source_blocks], (1, 0, 2))]
    add x1 -> x0, other arithmetic: 4.94 us -> none  [to_world_rows(): coeffs[0] * points[:, 0] + coeffs[1] * points[:, 1]]
    slice x4 -> x0, local copies, waits for them, and re-layouts: 4.45 us -> none  [the longest x1 1.79 us: local(): main_in = arrived[:, 0:CAP * 4].reshape(peers * CAP, 4, 128)]
    unnamed x21 -> x14, local copies, waits for them, and re-layouts: 4.28 us -> 2.37 us
    concatenate x0 -> x2, local copies, waits for them, and re-layouts: none -> 1.57 us  [the longest x1 1.35 us: local(): jnp.concatenate([xa_send, map_send], axis=1).reshape(peers, CAP * 4, 128)]
    dot_general x0 -> x2, matrix products: none -> 1.52 us  [the longest x1 1.05 us: local(): jnp.einsum('sb,cbk->sck', pick, rows6[0:3], precision=lax.Precision.HIGHEST)]
  transfers between devices with their start and end apart: 2 -> 2, of which waited for: 2 -> 2; matrix products, arithmetic and copies ran while one was open for 24% -> 28% of each run, Pallas kernels for 3% -> 4%
where the time goes in v5:
time: 94.9 us; the launch traced here: 94.1 us
  local copies, waits for them, and re-layouts  35.5 us (37%)
  starting transfers between devices  16.4 us (17%)
  waiting for transfers between devices  15.7 us (17%)
  Pallas kernels  13.9 us (15%)
  other arithmetic  8.25 us (9%)
  matrix products  3.33 us (4%)
  between operations  1.1 us (1%)
    pallas_call x2, Pallas kernels, pair_sums(): pl.pallas_call(functools.partial(_terms_kernel, from_cargo), out_shape=ja...  13.9 us
    gather x2, local copies, waits for them, and re-layouts, local(): rows6[:, target_blocks]  13.6 us
    all_to_all x1, starting transfers between devices, local(): lax.all_to_all(cargo, axes, split_axis=0, concat_axis=0, tiled=True)  11.9 us
    all_to_all x1, waiting for transfers between devices, local(): lax.all_to_all(remote_a.reshape(peers, CAP * 18), axes, split_axis=0, con...  9.54 us
    all_to_all x1, waiting for transfers between devices, local(): lax.all_to_all(cargo, axes, split_axis=0, concat_axis=0, tiled=True)  6.13 us
    all_to_all x1, starting transfers between devices, local(): lax.all_to_all(remote_a.reshape(peers, CAP * 18), axes, split_axis=0, con...  4.47 us
    gather x2, local copies, waits for them, and re-layouts, local(): frag_dirs[target_blocks // BF]  2.99 us
    unnamed x14, local copies, waits for them, and re-layouts  2.37 us
  transfers between devices with their start and end apart: 2, of which 2 were waited for; matrix products, arithmetic and copies ran while one was open for 28% of the time, Pallas kernels for 4%

profile of v5, /device:TPU:1, one launch (start us, length us, event | category | flops | bytes accessed | tf_op | source)
XLA Modules:
  0.0 94.1 jit_solution(15361778516218299203)
XLA Ops:
  0.7 0.8 slice_bitcast_fusion.4
  1.5 0.7 slice_multiply_fusion.4
  2.3 0.1 add.327
  2.4 0.1 mul.412
  2.6 0.1 mul.406
  2.7 0.1 mul.399
  2.9 0.1 add.334
  3.5 0.1 add.341
  3.9 0.1 mul.431
  4.0 0.8 copy.56
  4.9 0.7 fusion.40
  5.6 0.1 reshape.1376
  5.7 0.7 add_select_fusion
  6.4 0.5 fusion.3
  6.9 0.2 copy.60
  7.1 0.2 reshape.1373
  7.3 1.1 %convert_bitcast_fusion = f32[1024,1,128]{2,0,1:T(8,128)S(1)} fusion(s32[1,1024,128]{2,1,0:T(8,128)} %param.17), kind=kLoop, calls=%fused_computation.19 | loop fusion | flops 131072 | bytes 1048576 | tf_op jit(solution)/shard_map/convert_element_type | solution.py:214
  8.4 0.2 constant_dynamic-update-slice_fusion.2
  8.6 0.2 constant_dynamic-update-slice_fusion.1
  8.8 0.2 constant_dynamic-update-slice_fusion
  9.1 1.1 %fusion.1 = f32[1024,3,128]{2,0,1:T(8,128)S(1)} fusion(s32[1024]{0:T(1024)S(1)} %bitcast.268, f32[1,256,128]{2,1,0:T(8,128)S(1)} %get-tuple-element.11, f32[1,256,128]{2,1,0:T(8,128)S(1)} %get-tuple-element.13, f32[1,256,128]{2,1,0:T(8,128)S(1)} %get-tuple-element.15), kind=kOutput, calls=%fused_computation.14 | convolution fusion | flops 1208418304 | bytes 1970176 | tf_op jit(solution)/shard_map/sb,cbk->sck/dot_general | solution.py:213
  10.1 0.1 pad_maximum_fusion.1
  10.3 1.4 %copy.59 = f32[1024,4,128]{2,1,0:T(4,128)S(1)} copy(f32[1024,4,128]{2,0,1:T(8,128)S(1)} %pad_maximum_fusion.1) | data formatting | bytes 4194304 | tf_op jit(solution)/shard_map/concatenate | solution.py:215
  11.6 1.7 %pad_maximum_fusion = f32[128,33,128]{2,1,0:T(8,128)} fusion(f32[128,1,128]{2,1,0:T(1,128)S(1)} %bitcast.261, f32[128,32,128]{2,1,0:T(8,128)S(1)} %bitcast.257), kind=kLoop, calls=%fused_computation.7 | loop fusion | flops 540672 | bytes 4325376 | tf_op jit(solution)/shard_map/concatenate | solution.py:223
  13.4 11.9 %all-to-all-start = ((f32[128,33,128]{2,1,0:T(8,128)}), f32[128,33,128]{2,1,0:T(8,128)}, u32[]{:S(2)}, u32[]{:S(2)}) async-start(f32[128,33,128]{2,1,0:T(8,128)} %pad_maximum_fusion), calls=%async_computation | async-start | bytes 5242880 | tf_op jit(solution)/shard_map/all_to_all | solution.py:224
  25.3 0.3 copy.52
  25.6 1.0 %gather_fusion = f32[256,3,128]{2,1,0:T(4,128)S(1)} fusion(f32[3,256,128]{2,0,1:T(4,128)S(1)} %copy.52, s32[1024]{0:T(1024)S(1)} %get-tuple-element.52), kind=kCustom, calls=%fused_computation | custom fusion | bytes 787456 | tf_op jit(solution)/shard_map/gather | solution.py:230
  26.6 0.8 copy.75
  27.4 0.2 fusion.11
  27.6 0.2 fusion.13
  27.8 0.2 fusion.15
  27.9 0.5 copy.54
  28.4 1.0 %gather_fusion.1 = f32[256,6,128]{2,1,0:T(8,128)S(1)} fusion(f32[6,256,128]{2,0,1:T(8,128)S(1)} %copy.54, s32[1024]{0:T(1024)S(1)} %get-tuple-element.51), kind=kCustom, calls=%fused_computation.1 | custom fusion | bytes 1573888 | tf_op jit(solution)/shard_map/gather | solution.py:231
  29.5 1.1 %copy.74 = f32[256,6,128]{2,0,1:T(8,128)} copy(f32[256,6,128]{2,1,0:T(8,128)S(1)} %gather_fusion.1) | data formatting | bytes 1572864 | tf_op jit(solution)/shard_map/gather | solution.py:231
  30.5 0.7 gather_fusion.3
  31.3 0.7 gather_fusion.2
  32.3 0.7 maximum_maximum_fusion.1.aux_ref
  33.0 3.7 %shard_map.113 = f32[32,256]{1,0:T(8,128)} custom-call(f32[3,256,128]{2,1,0:T(8,128)} %bitcast.260, f32[6,256,128]{2,1,0:T(8,128)} %bitcast.259, s32[256,128]{1,0:T(8,128)} %map_ref.1, f32[32,256]{1,0:T(8,128)} %maximum_maximum_fusion.1.aux_ref), custom_call_target="tpu_custom_call" | custom-call | tf_op jit(solution)/shard_map/pallas_call | solution.py:144
  36.7 0.8 slice_bitcast_fusion.1
  37.6 9.1 %gather_fusion.4 = f32[1024,6,128]{2,1,0:T(8,128)} fusion(f32[6,256,128]{2,0,1:T(8,128)S(1)} %copy.54, s32[1024]{0:T(1024)S(1)} %get-tuple-element.54), kind=kCustom, calls=%fused_computation.4 | custom fusion | bytes 6295552 | tf_op jit(solution)/shard_map/gather | solution.py:241
  46.7 4.5 %copy.73 = f32[1024,6,128]{2,0,1:T(8,128)} copy(f32[1024,6,128]{2,1,0:T(8,128)} %gather_fusion.4) | data formatting | bytes 6291456 | tf_op jit(solution)/shard_map/gather | solution.py:241
  51.1 2.8 %gather_fusion.5 = f32[1024,12]{1,0:T(8,128)S(1)} fusion(f32[8,12]{1,0:T(8,128)S(1)} %bitcast.255, s32[1024]{0:T(1024)S(1)} %get-tuple-element.53), kind=kCustom, calls=%fused_computation.5 | custom fusion | bytes 102400 | tf_op jit(solution)/shard_map/gather | solution.py:243
  54.0 0.2 copy.64
  54.3 0.3 fusion.36
  54.6 0.3 convolution_add_fusion.1
  54.8 6.1 %all-to-all-done.xa_ref = f32[128,33,128]{2,1,0:T(8,128)} async-done(((f32[128,33,128]{2,1,0:T(8,128)}), f32[128,33,128]{2,1,0:T(8,128)}, u32[]{:S(2)}, u32[]{:S(2)}) %all-to-all-start) | async-done | bytes 2162720 | tf_op jit(solution)/shard_map/all_to_all | solution.py:224
  61.0 1.2 %slice_reduce_fusion.1 = f32[128,104]{1,0:T(8,128)S(1)} fusion(f32[128,33,128]{2,1,0:T(8,128)} %all-to-all-done.xa_ref), kind=kLoop, calls=%fused_computation.78 | loop fusion | bytes 106496 | tf_op jit(solution)/shard_map/slice | solution.py:238
  62.2 0.2 reshape_squeeze.3
  62.4 0.4 slice_reduce_fusion
  62.7 0.2 copy.69
  62.9 0.7 maximum_maximum_fusion.aux_ref
  63.7 0.6 broadcast_in_dim.77.map_ref
  64.3 10.1 %shard_map.114 = f32[32,1024]{1,0:T(8,128)} custom-call(f32[128,33,128]{2,1,0:T(8,128)} %all-to-all-done.xa_ref, f32[6,1024,128]{2,1,0:T(8,128)} %bitcast.256, s32[8,128]{1,0:T(8,128)} %broadcast_in_dim.77.map_ref, f32[32,1024]{1,0:T(8,128)} %maximum_maximum_fusion.aux_ref), custom_call_target="tpu_custom_call" | custom-call | tf_op jit(solution)/shard_map/pallas_call | solution.py:144
  74.4 0.9 slice_bitcast_fusion
  75.4 0.2 copy.65
  75.6 1.1 %all_to_all.12 = f32[128,1,144]{2,1,0:T(1,128)} reshape(f32[1024,18]{1,0:T(8,128)S(1)} %copy.65) | data formatting | bytes 147456 | tf_op jit(solution)/shard_map/all_to_all | solution.py:246
  76.7 4.5 %all-to-all-start.1 = ((f32[128,1,144]{2,1,0:T(1,128)}), f32[128,1,144]{2,1,0:T(1,128)S(1)}, u32[]{:S(2)}, u32[]{:S(2)}) async-start(f32[128,1,144]{2,1,0:T(1,128)} %all_to_all.12), calls=%async_computation.1 | async-start | bytes 262144 | tf_op jit(solution)/shard_map/all_to_all | solution.py:246
  81.2 0.6 convolution_add_fusion
  81.8 9.5 %all-to-all-done.1 = f32[128,1,144]{2,1,0:T(1,128)S(1)} async-done(((f32[128,1,144]{2,1,0:T(1,128)}), f32[128,1,144]{2,1,0:T(1,128)S(1)}, u32[]{:S(2)}, u32[]{:S(2)}) %all-to-all-start.1) | async-done | bytes 73760 | tf_op jit(solution)/shard_map/all_to_all | solution.py:246
  91.3 0.3 reduce.2
  91.7 0.2 reshape.1374
  91.9 0.7 convolution_add_fusion.2
  92.7 0.7 copy.67
  93.4 0.7 copy.68
  (64 shorter events, 2.1 us)
Async XLA Ops:
  0.6 8.4 %copy-start.2 = (s32[1,1024]{1,0:T(1,128)S(1)}, s32[1,1024]{1,0:T(1,128)}, u32[]{:S(2)}) copy-start(s32[1,1024]{1,0:T(1,128)} %param.16) | copy-start | bytes 12292
  0.6 7.8 %copy-start = (f32[256,3,128]{2,0,1:T(8,128)S(1)}, f32[256,3,128]{2,0,1:T(8,128)}, u32[]{:S(2)}) copy-start(f32[256,3,128]{2,0,1:T(8,128)} %param.10) | copy-start | bytes 1179652
  13.4 12.2 %copy-start.4 = (s32[2,256]{1,0:T(2,128)S(1)}, s32[2,256]{1,0:T(2,128)}, u32[]{:S(2)}) copy-start(s32[2,256]{1,0:T(2,128)} %param.14) | copy-start | bytes 6148
  13.4 47.6 %all-to-all-start = ((f32[128,33,128]{2,1,0:T(8,128)}), f32[128,33,128]{2,1,0:T(8,128)}, u32[]{:S(2)}, u32[]{:S(2)}) async-start(f32[128,33,128]{2,1,0:T(8,128)} %pad_maximum_fusion), calls=%async_computation | async-start | bytes 5242880 | tf_op jit(solution)/shard_map/all_to_all | solution.py:224
  25.3 2.2 %copy-start.1 = (f32[256,3,128]{2,0,1:T(8,128)S(1)}, f32[256,3,128]{2,0,1:T(8,128)}, u32[]{:S(2)}) copy-start(f32[256,3,128]{2,0,1:T(8,128)} %param.11) | copy-start | bytes 1179652
  29.5 8.0 %copy-start.3 = (s32[1,1024]{1,0:T(1,128)S(1)}, s32[1,1024]{1,0:T(1,128)}, u32[]{:S(2)}) copy-start(s32[1,1024]{1,0:T(1,128)} %param.18) | copy-start | bytes 12292
  76.7 14.6 %all-to-all-start.1 = ((f32[128,1,144]{2,1,0:T(1,128)}), f32[128,1,144]{2,1,0:T(1,128)S(1)}, u32[]{:S(2)}, u32[]{:S(2)}) async-start(f32[128,1,144]{2,1,0:T(1,128)} %all_to_all.12), calls=%async_computation.1 | async-start | bytes 262144 | tf_op jit(solution)/shard_map/all_to_all | solution.py:246

commit v6 on v5

--- a/solution.py
+++ b/solution.py
@@ -90,9 +90,8 @@
         xa = [xt_ref[c, rows, :] for c in range(3)]
         xb = [gt_ref[c, rows, :] for c in range(3)]
         nb = [gt_ref[3 + c, rows, :] for c in range(3)]
-        valid = col(24)
         off = [xa[c] - xb[c] for c in range(3)]
-        res = (nb[0] * off[0] + nb[1] * off[1] + nb[2] * off[2]) * valid
+        res = nb[0] * off[0] + nb[1] * off[1] + nb[2] * off[2]
         ja = [
             xa[1] * nb[2] - xa[2] * nb[1],
             xa[2] * nb[0] - xa[0] * nb[2],
@@ -101,33 +100,34 @@
             nb[1],
             nb[2],
         ]
-        jb = [
-            -(xb[1] * nb[2] - xb[2] * nb[1]),
-            -(xb[2] * nb[0] - xb[0] * nb[2]),
-            -(xb[0] * nb[1] - xb[1] * nb[0]),
-            -nb[0],
-            -nb[1],
-            -nb[2],
+        kb = [
+            xb[1] * nb[2] - xb[2] * nb[1],
+            xb[2] * nb[0] - xb[0] * nb[2],
+            xb[0] * nb[1] - xb[1] * nb[0],
+            nb[0],
+            nb[1],
+            nb[2],
         ]
         weights = [res]
         for v in range(2):
             sa = ja[0] * col(6 * v)
-            sb = jb[0] * col(12 + 6 * v)
+            sb = kb[0] * col(12 + 6 * v)
             for c in range(1, 6):
                 sa = sa + ja[c] * col(6 * v + c)
-                sb = sb + jb[c] * col(12 + 6 * v + c)
-            weights.append((sa + sb) * valid)
+                sb = sb + kb[c] * col(12 + 6 * v + c)
+            weights.append(sa - sb)
         vals = []
         for w in weights:
             vals.extend([w * ja[c] for c in range(6)])
         for w in weights:
-            vals.extend([w * jb[c] for c in range(3)])
+            vals.extend([w * kb[c] for c in range(3)])
         return tuple(a + v for a, v in zip(accs, vals))
 
     zero = jnp.zeros((8, chunk), jnp.float32)
-    accs = lax.fori_loop(0, 128 // 8, body, (zero,) * N_QTY)
+    accs = lax.fori_loop(0, 128 // 8, body, (zero,) * N_QTY, unroll=2)
+    valid = aux_ref[24:25, :]
     for q in range(N_QTY):
-        out_ref[q : q + 1, :] = jnp.sum(accs[q], axis=0, keepdims=True)
+        out_ref[q : q + 1, :] = jnp.sum(accs[q], axis=0, keepdims=True) * valid
     out_ref[N_QTY:, :] = jnp.zeros((32 - N_QTY, chunk), jnp.float32)
 
 
@@ -163,9 +163,9 @@
     sel = out[0:N_QTY].T
     ga = sel[:, 0:6] * (1.0 / 128)
     ha = sel[:, 6:18] * (1.0 / 4096)
-    gb = jnp.concatenate([sel[:, 18:21], -sel[:, 3:6]], axis=1) * (1.0 / 128)
-    hb0 = jnp.concatenate([sel[:, 21:24], -sel[:, 9:12]], axis=1) * (1.0 / 4096)
-    hb1 = jnp.concatenate([sel[:, 24:27], -sel[:, 15:18]], axis=1) * (1.0 / 4096)
+    gb = -jnp.concatenate([sel[:, 18:21], sel[:, 3:6]], axis=1) * (1.0 / 128)
+    hb0 = -jnp.concatenate([sel[:, 21:24], sel[:, 9:12]], axis=1) * (1.0 / 4096)
+    hb1 = -jnp.concatenate([sel[:, 24:27], sel[:, 15:18]], axis=1) * (1.0 / 4096)
     return jnp.concatenate([ga, ha], axis=1), jnp.concatenate([gb, hb0, hb1], axis=1)
 
 

time: 94.9 us -> 94.3 us (level)
  no operation moved by 1% of the time
where the time goes in v6:
time: 94.3 us; the launch traced here: 93.5 us
  local copies, waits for them, and re-layouts  35.5 us (38%)
  starting transfers between devices  16.4 us (17%)
  waiting for transfers between devices  15.9 us (17%)
  Pallas kernels  13.1 us (14%)
  other arithmetic  8.21 us (9%)
  matrix products  3.33 us (4%)
  between operations  1.1 us (1%)
    gather x2, local copies, waits for them, and re-layouts, local(): rows6[:, target_blocks]  13.6 us
    pallas_call x2, Pallas kernels, pair_sums(): pl.pallas_call(functools.partial(_terms_kernel, from_cargo), out_shape=ja...  13.1 us
    all_to_all x1, starting transfers between devices, local(): lax.all_to_all(cargo, axes, split_axis=0, concat_axis=0, tiled=True)  11.9 us
    all_to_all x1, waiting for transfers between devices, local(): lax.all_to_all(remote_a.reshape(peers, CAP * 18), axes, split_axis=0, con...  9.54 us
    all_to_all x1, waiting for transfers between devices, local(): lax.all_to_all(cargo, axes, split_axis=0, concat_axis=0, tiled=True)  6.37 us
    all_to_all x1, starting transfers between devices, local(): lax.all_to_all(remote_a.reshape(peers, CAP * 18), axes, split_axis=0, con...  4.47 us
    gather x2, local copies, waits for them, and re-layouts, local(): frag_dirs[target_blocks // BF]  2.99 us
    unnamed x14, local copies, waits for them, and re-layouts  2.37 us
  transfers between devices with their start and end apart: 2, of which 2 were waited for; matrix products, arithmetic and copies ran while one was open for 28% of the time, Pallas kernels for 4%

profile of v6, /device:TPU:1, one launch (start us, length us, event | category | flops | bytes accessed | tf_op | source)
XLA Modules:
  0.0 93.5 jit_solution(4611980470130627169)
XLA Ops:
  0.7 0.8 slice_bitcast_fusion.4
  1.5 0.7 slice_multiply_fusion.4
  2.3 0.1 add.327
  2.4 0.1 mul.412
  2.6 0.1 mul.406
  2.7 0.1 mul.399
  2.9 0.1 add.334
  3.5 0.1 add.341
  3.9 0.1 mul.431
  4.0 0.8 copy.56
  4.9 0.7 fusion.40
  5.6 0.1 reshape.1376
  5.7 0.7 add_select_fusion
  6.4 0.5 fusion.3
  6.9 0.2 copy.60
  7.1 0.2 reshape.1373
  7.3 1.1 %convert_bitcast_fusion = f32[1024,1,128]{2,0,1:T(8,128)S(1)} fusion(s32[1,1024,128]{2,1,0:T(8,128)} %param.17), kind=kLoop, calls=%fused_computation.19 | loop fusion | flops 131072 | bytes 1048576 | tf_op jit(solution)/shard_map/convert_element_type | solution.py:214
  8.4 0.2 constant_dynamic-update-slice_fusion.2
  8.6 0.2 constant_dynamic-update-slice_fusion.1
  8.8 0.2 constant_dynamic-update-slice_fusion
  9.1 1.1 %fusion.1 = f32[1024,3,128]{2,0,1:T(8,128)S(1)} fusion(s32[1024]{0:T(1024)S(1)} %bitcast.268, f32[1,256,128]{2,1,0:T(8,128)S(1)} %get-tuple-element.11, f32[1,256,128]{2,1,0:T(8,128)S(1)} %get-tuple-element.13, f32[1,256,128]{2,1,0:T(8,128)S(1)} %get-tuple-element.15), kind=kOutput, calls=%fused_computation.14 | convolution fusion | flops 1208418304 | bytes 1970176 | tf_op jit(solution)/shard_map/sb,cbk->sck/dot_general | solution.py:213
  10.1 0.1 pad_maximum_fusion.1
  10.3 1.4 %copy.59 = f32[1024,4,128]{2,1,0:T(4,128)S(1)} copy(f32[1024,4,128]{2,0,1:T(8,128)S(1)} %pad_maximum_fusion.1) | data formatting | bytes 4194304 | tf_op jit(solution)/shard_map/concatenate | solution.py:215
  11.6 1.7 %pad_maximum_fusion = f32[128,33,128]{2,1,0:T(8,128)} fusion(f32[128,1,128]{2,1,0:T(1,128)S(1)} %bitcast.261, f32[128,32,128]{2,1,0:T(8,128)S(1)} %bitcast.257), kind=kLoop, calls=%fused_computation.7 | loop fusion | flops 540672 | bytes 4325376 | tf_op jit(solution)/shard_map/concatenate | solution.py:223
  13.4 11.9 %all-to-all-start = ((f32[128,33,128]{2,1,0:T(8,128)}), f32[128,33,128]{2,1,0:T(8,128)}, u32[]{:S(2)}, u32[]{:S(2)}) async-start(f32[128,33,128]{2,1,0:T(8,128)} %pad_maximum_fusion), calls=%async_computation | async-start | bytes 5242880 | tf_op jit(solution)/shard_map/all_to_all | solution.py:224
  25.3 0.3 copy.52
  25.6 1.0 %gather_fusion = f32[256,3,128]{2,1,0:T(4,128)S(1)} fusion(f32[3,256,128]{2,0,1:T(4,128)S(1)} %copy.52, s32[1024]{0:T(1024)S(1)} %get-tuple-element.52), kind=kCustom, calls=%fused_computation | custom fusion | bytes 787456 | tf_op jit(solution)/shard_map/gather | solution.py:230
  26.6 0.8 copy.75
  27.4 0.2 fusion.11
  27.6 0.2 fusion.13
  27.8 0.2 fusion.15
  27.9 0.5 copy.54
  28.4 1.0 %gather_fusion.1 = f32[256,6,128]{2,1,0:T(8,128)S(1)} fusion(f32[6,256,128]{2,0,1:T(8,128)S(1)} %copy.54, s32[1024]{0:T(1024)S(1)} %get-tuple-element.51), kind=kCustom, calls=%fused_computation.1 | custom fusion | bytes 1573888 | tf_op jit(solution)/shard_map/gather | solution.py:231
  29.5 1.1 %copy.74 = f32[256,6,128]{2,0,1:T(8,128)} copy(f32[256,6,128]{2,1,0:T(8,128)S(1)} %gather_fusion.1) | data formatting | bytes 1572864 | tf_op jit(solution)/shard_map/gather | solution.py:231
  30.5 0.7 gather_fusion.3
  31.3 0.7 gather_fusion.2
  32.3 0.7 maximum_maximum_fusion.1.aux_ref
  33.0 3.5 %shard_map.113 = f32[32,256]{1,0:T(8,128)} custom-call(f32[3,256,128]{2,1,0:T(8,128)} %bitcast.260, f32[6,256,128]{2,1,0:T(8,128)} %bitcast.259, s32[256,128]{1,0:T(8,128)} %map_ref.1, f32[32,256]{1,0:T(8,128)} %maximum_maximum_fusion.1.aux_ref), custom_call_target="tpu_custom_call" | custom-call | tf_op jit(solution)/shard_map/pallas_call | solution.py:144
  36.5 0.8 slice_bitcast_fusion.1
  37.3 9.1 %gather_fusion.4 = f32[1024,6,128]{2,1,0:T(8,128)} fusion(f32[6,256,128]{2,0,1:T(8,128)S(1)} %copy.54, s32[1024]{0:T(1024)S(1)} %get-tuple-element.54), kind=kCustom, calls=%fused_computation.4 | custom fusion | bytes 6295552 | tf_op jit(solution)/shard_map/gather | solution.py:241
  46.4 4.5 %copy.73 = f32[1024,6,128]{2,0,1:T(8,128)} copy(f32[1024,6,128]{2,1,0:T(8,128)} %gather_fusion.4) | data formatting | bytes 6291456 | tf_op jit(solution)/shard_map/gather | solution.py:241
  50.9 2.8 %gather_fusion.5 = f32[1024,12]{1,0:T(8,128)S(1)} fusion(f32[8,12]{1,0:T(8,128)S(1)} %bitcast.255, s32[1024]{0:T(1024)S(1)} %get-tuple-element.53), kind=kCustom, calls=%fused_computation.5 | custom fusion | bytes 102400 | tf_op jit(solution)/shard_map/gather | solution.py:243
  53.7 0.2 copy.64
  54.0 0.3 fusion.36
  54.3 0.3 convolution_add_fusion.1
  54.6 6.4 %all-to-all-done.xa_ref = f32[128,33,128]{2,1,0:T(8,128)} async-done(((f32[128,33,128]{2,1,0:T(8,128)}), f32[128,33,128]{2,1,0:T(8,128)}, u32[]{:S(2)}, u32[]{:S(2)}) %all-to-all-start) | async-done | bytes 2162720 | tf_op jit(solution)/shard_map/all_to_all | solution.py:224
  61.0 1.2 %slice_reduce_fusion.1 = f32[128,104]{1,0:T(8,128)S(1)} fusion(f32[128,33,128]{2,1,0:T(8,128)} %all-to-all-done.xa_ref), kind=kLoop, calls=%fused_computation.78 | loop fusion | bytes 106496 | tf_op jit(solution)/shard_map/slice | solution.py:238
  62.2 0.2 reshape_squeeze.3
  62.4 0.4 slice_reduce_fusion
  62.7 0.2 copy.69
  62.9 0.7 maximum_maximum_fusion.aux_ref
  63.7 0.6 broadcast_in_dim.77.map_ref
  64.3 9.6 %shard_map.114 = f32[32,1024]{1,0:T(8,128)} custom-call(f32[128,33,128]{2,1,0:T(8,128)} %all-to-all-done.xa_ref, f32[6,1024,128]{2,1,0:T(8,128)} %bitcast.256, s32[8,128]{1,0:T(8,128)} %broadcast_in_dim.77.map_ref, f32[32,1024]{1,0:T(8,128)} %maximum_maximum_fusion.aux_ref), custom_call_target="tpu_custom_call" | custom-call | tf_op jit(solution)/shard_map/pallas_call | solution.py:144
  73.8 0.9 slice_bitcast_fusion
  74.8 0.2 copy.65
  75.1 1.1 %all_to_all.12 = f32[128,1,144]{2,1,0:T(1,128)} reshape(f32[1024,18]{1,0:T(8,128)S(1)} %copy.65) | data formatting | bytes 147456 | tf_op jit(solution)/shard_map/all_to_all | solution.py:246
  76.1 4.5 %all-to-all-start.1 = ((f32[128,1,144]{2,1,0:T(1,128)}), f32[128,1,144]{2,1,0:T(1,128)S(1)}, u32[]{:S(2)}, u32[]{:S(2)}) async-start(f32[128,1,144]{2,1,0:T(1,128)} %all_to_all.12), calls=%async_computation.1 | async-start | bytes 262144 | tf_op jit(solution)/shard_map/all_to_all | solution.py:246
  80.7 0.6 convolution_add_fusion
  81.2 9.5 %all-to-all-done.1 = f32[128,1,144]{2,1,0:T(1,128)S(1)} async-done(((f32[128,1,144]{2,1,0:T(1,128)}), f32[128,1,144]{2,1,0:T(1,128)S(1)}, u32[]{:S(2)}, u32[]{:S(2)}) %all-to-all-start.1) | async-done | bytes 73760 | tf_op jit(solution)/shard_map/all_to_all | solution.py:246
  90.8 0.3 reduce.2
  91.1 0.2 reshape.1374
  91.3 0.7 convolution_add_fusion.2
  92.1 0.7 copy.67
  92.8 0.7 copy.68
  (64 shorter events, 2.1 us)
Async XLA Ops:
  0.6 8.4 %copy-start.2 = (s32[1,1024]{1,0:T(1,128)S(1)}, s32[1,1024]{1,0:T(1,128)}, u32[]{:S(2)}) copy-start(s32[1,1024]{1,0:T(1,128)} %param.16) | copy-start | bytes 12292
  0.6 7.8 %copy-start = (f32[256,3,128]{2,0,1:T(8,128)S(1)}, f32[256,3,128]{2,0,1:T(8,128)}, u32[]{:S(2)}) copy-start(f32[256,3,128]{2,0,1:T(8,128)} %param.10) | copy-start | bytes 1179652
  13.4 12.2 %copy-start.4 = (s32[2,256]{1,0:T(2,128)S(1)}, s32[2,256]{1,0:T(2,128)}, u32[]{:S(2)}) copy-start(s32[2,256]{1,0:T(2,128)} %param.14) | copy-start | bytes 6148
  13.4 47.6 %all-to-all-start = ((f32[128,33,128]{2,1,0:T(8,128)}), f32[128,33,128]{2,1,0:T(8,128)}, u32[]{:S(2)}, u32[]{:S(2)}) async-start(f32[128,33,128]{2,1,0:T(8,128)} %pad_maximum_fusion), calls=%async_computation | async-start | bytes 5242880 | tf_op jit(solution)/shard_map/all_to_all | solution.py:224
  25.3 2.2 %copy-start.1 = (f32[256,3,128]{2,0,1:T(8,128)S(1)}, f32[256,3,128]{2,0,1:T(8,128)}, u32[]{:S(2)}) copy-start(f32[256,3,128]{2,0,1:T(8,128)} %param.11) | copy-start | bytes 1179652
  29.5 7.8 %copy-start.3 = (s32[1,1024]{1,0:T(1,128)S(1)}, s32[1,1024]{1,0:T(1,128)}, u32[]{:S(2)}) copy-start(s32[1,1024]{1,0:T(1,128)} %param.18) | copy-start | bytes 12292
  76.1 14.6 %all-to-all-start.1 = ((f32[128,1,144]{2,1,0:T(1,128)}), f32[128,1,144]{2,1,0:T(1,128)S(1)}, u32[]{:S(2)}, u32[]{:S(2)}) async-start(f32[128,1,144]{2,1,0:T(1,128)} %all_to_all.12), calls=%async_computation.1 | async-start | bytes 262144 | tf_op jit(solution)/shard_map/all_to_all | solution.py:246

commit v7 on v6

--- a/solution.py
+++ b/solution.py
@@ -69,7 +69,7 @@
     chunk = out_ref.shape[1]
     if from_cargo:
         def cargo_rows(r):
-            return xa_ref[:, pl.ds(r, CAP, stride=4), :].reshape(chunk, 128)
+            return xa_ref[pl.ds(r, CAP, stride=4)].reshape(chunk, 128)
 
         idx = cargo_rows(3).astype(jnp.int32)
         for c in range(3):
@@ -135,8 +135,8 @@
     pairs = tb.shape[1]
     from_cargo = maps is None
     if from_cargo:
-        xa_spec = pl.BlockSpec((chunk // CAP, xa.shape[1], 128), lambda i: (i, 0, 0))
-        maps = jnp.zeros((8, 128), jnp.int32)
+        xa_spec = pl.BlockSpec((xa.shape[0], chunk // CAP, 128), lambda i: (0, i, 0))
+        maps = aux
         map_spec = pl.BlockSpec((8, 128), lambda i: (0, 0))
     else:
         xa_spec = pl.BlockSpec((3, chunk, 128), lambda i: (0, i, 0))
@@ -173,7 +173,7 @@
     onehot = (blocks[:, None] // BF == jnp.arange(frag_count, dtype=jnp.int32)[None, :]).astype(
         jnp.float32
     )
-    return jnp.dot(onehot.T, terms, precision=lax.Precision.HIGHEST)
+    return jnp.dot(terms.T, onehot, precision=lax.Precision.HIGHEST)
 
 
 def make_aux(dirs_a, dirs_b, valid):
@@ -207,12 +207,13 @@
         .astype(jnp.float32)
         .reshape(-1)
     )
-    pick = (source_blocks[:, None] == jnp.arange(points.shape[0], dtype=jnp.int32)[None, :]).astype(
-        jnp.float32
-    )
-    xa_send = jnp.einsum("sb,cbk->sck", pick, rows6[0:3], precision=lax.Precision.HIGHEST)
-    map_send = remote_maps[0].astype(jnp.float32)[:, None, :]
-    main = jnp.concatenate([xa_send, map_send], axis=1).reshape(peers, CAP * 4, 128)
+    pick = (
+        source_blocks.reshape(peers, CAP)[:, :, None]
+        == jnp.arange(points.shape[0], dtype=jnp.int32)[None, None, :]
+    ).astype(jnp.float32)
+    xa_send = jnp.einsum("psb,cbk->scpk", pick, rows6[0:3], precision=lax.Precision.HIGHEST)
+    map_send = jnp.transpose(remote_maps[0].reshape(peers, CAP, 128), (1, 0, 2))
+    main = jnp.concatenate([xa_send, map_send.astype(jnp.float32)[:, None]], axis=1)
     frag_pick = (
         source_blocks[:, None] // BF == jnp.arange(frag_count, dtype=jnp.int32)[None, :]
     ).astype(jnp.float32)
@@ -220,8 +221,8 @@
     side = jnp.concatenate([dirs_send, valid[:, None]], axis=1)
     side = side.reshape(peers, CAP * 13)
     side = jnp.concatenate([side, jnp.zeros((peers, 128 - CAP * 13), jnp.float32)], axis=1)
-    cargo = jnp.concatenate([main, side[:, None, :]], axis=1)
-    arrived = lax.all_to_all(cargo, axes, split_axis=0, concat_axis=0, tiled=True)
+    cargo = jnp.concatenate([main.reshape(CAP * 4, peers, 128), side[None]], axis=0)
+    arrived = lax.all_to_all(cargo, axes, split_axis=1, concat_axis=1, tiled=True)
 
     src_l = local_pairs[0]
     tgt_l = local_pairs[1]
@@ -234,8 +235,18 @@
     )
     local_a, local_b = split_terms(out_l)
 
-    target_blocks = remote_dst[0]
-    side_in = arrived[:, CAP * 4, 0 : CAP * 13].reshape(peers * CAP, 13)
+    chunks = peers * CAP // 128
+
+    def to_chunks(x):
+        x = x.reshape((chunks, 128 // CAP, CAP) + x.shape[1:])
+        return jnp.swapaxes(x, 1, 2).reshape((peers * CAP,) + x.shape[3:])
+
+    def from_chunks(x):
+        x = x.reshape((chunks, CAP, 128 // CAP) + x.shape[1:])
+        return jnp.swapaxes(x, 1, 2).reshape((peers * CAP,) + x.shape[3:])
+
+    target_blocks = to_chunks(remote_dst[0])
+    side_in = to_chunks(arrived[CAP * 4, :, 0 : CAP * 13].reshape(peers * CAP, 13))
     out_r = pair_sums(
         arrived,
         rows6[:, target_blocks],
@@ -244,7 +255,7 @@
     )
     remote_a, remote_b = split_terms(out_r)
     returned = lax.all_to_all(
-        remote_a.reshape(peers, CAP * 18), axes, split_axis=0, concat_axis=0, tiled=True
+        from_chunks(remote_a).reshape(peers, CAP * 18), axes, split_axis=0, concat_axis=0, tiled=True
     ).reshape(peers * CAP, 18)
 
     totals = frag_sums(src_l, local_a, frag_count) + frag_sums(tgt_l, local_b, frag_count)
@@ -253,8 +264,8 @@
         + frag_sums(target_blocks, remote_b, frag_count)
         + frag_sums(source_blocks, returned, frag_count)
     )
-    gradient = totals[:, 0:6].T
-    hess_products = totals[:, 6:18].T.reshape(2, 6, frag_count)
+    gradient = totals[0:6]
+    hess_products = totals[6:18].reshape(2, 6, frag_count)
     return (gradient, hess_products)
 
 

time: 94.3 us -> 103 us (1.092)
  local copies, waits for them, and re-layouts: 35.5 us -> 44.7 us
    all_to_all x1 -> x2, local copies, waits for them, and re-layouts: 1.07 us -> 4.58 us  [the longest x1 3.5 us: local(): lax.all_to_all(cargo, axes, split_axis=1, concat_axis=1, tiled=True)]
    concatenate x3 -> x2, local copies, waits for them, and re-layouts: 1.57 us -> 4.61 us  [the longest x1 2.77 us: local(): jnp.concatenate([main.reshape(CAP * 4, peers, 128), side[None]], axis=0)]
    unnamed x5 -> x7, other arithmetic: 0.94 us -> 2.19 us
    convert_element_type x1, other arithmetic: 1.08 us -> 0.04 us  [local(): map_send.astype(jnp.float32)[:, None]]
    unnamed x14 -> x22, local copies, waits for them, and re-layouts: 2.37 us -> 3.26 us
    slice x2 -> x5, local copies, waits for them, and re-layouts: 1.57 us -> 2.33 us  [the longest x2 1.16 us: local(): arrived[CAP * 4, :, 0:CAP * 13].reshape(peers * CAP, 13)]
  transfers between devices with their start and end apart: 2 -> 2, of which waited for: 2 -> 2; matrix products, arithmetic and copies ran while one was open for 28% -> 27% of each run, Pallas kernels for 4% -> 3%
where the time goes in v7:
time: 103 us; the launch traced here: 102 us
  local copies, waits for them, and re-layouts  44.7 us (43%)
  starting transfers between devices  16.4 us (16%)
  waiting for transfers between devices  14.9 us (14%)
  Pallas kernels  13 us (13%)
  other arithmetic  8.32 us (8%)
  matrix products  3.43 us (3%)
  between operations  1.19 us (1%)
    gather x2, local copies, waits for them, and re-layouts, local(): rows6[:, target_blocks]  13.6 us
    pallas_call x2, Pallas kernels, pair_sums(): pl.pallas_call(functools.partial(_terms_kernel, from_cargo), out_shape=ja...  13 us
    all_to_all x1, starting transfers between devices, local(): lax.all_to_all(cargo, axes, split_axis=1, concat_axis=1, tiled=True)  11.9 us
    all_to_all x1, waiting for transfers between devices, local(): lax.all_to_all(from_chunks(remote_a).reshape(peers, CAP * 18), axes, spli...  9.41 us
    all_to_all x1, waiting for transfers between devices, local(): lax.all_to_all(cargo, axes, split_axis=1, concat_axis=1, tiled=True)  5.49 us
    all_to_all x1, starting transfers between devices, local(): lax.all_to_all(from_chunks(remote_a).reshape(peers, CAP * 18), axes, spli...  4.48 us
    all_to_all x1, local copies, waits for them, and re-layouts, local(): lax.all_to_all(cargo, axes, split_axis=1, concat_axis=1, tiled=True)  3.5 us
    unnamed x22, local copies, waits for them, and re-layouts  3.26 us
  transfers between devices with their start and end apart: 2, of which 2 were waited for; matrix products, arithmetic and copies ran while one was open for 27% of the time, Pallas kernels for 3%

profile of v7, /device:TPU:1, one launch (start us, length us, event | category | flops | bytes accessed | tf_op | source)
XLA Modules:
  0.0 101.9 jit_solution(16304411335855396806)
XLA Ops:
  0.6 0.8 slice_bitcast_fusion.4
  1.4 0.7 slice_multiply_fusion.4
  2.8 0.7 add_select_fusion.1
  4.7 0.5 broadcast.793
  5.2 1.3 %reduce.8 = s32[1024]{0:T(1024)S(1)} reduce(s32[1,1024]{1,0:T(1,128)} %param.16, s32[]{:T(128)} %broadcast.793), dimensions={0}, to_apply=%param.16.reduce_sub_computation.3 | reduce | bytes 8196 | tf_op args[6]
  6.5 0.8 copy.94
  7.5 0.8 fusion.34
  8.3 0.1 reshape.1380
  8.4 1.1 %fusion.65 = (f32[256,1,128]{2,0,1:T(8,128)S(1)}, f32[256,1,128]{2,0,1:T(8,128)S(1)}, f32[256,1,128]{2,0,1:T(8,128)S(1)}) fusion(f32[256,3,128]{2,0,1:T(8,128)} %param.10), kind=kLoop, calls=%fused_computation.186 | loop fusion | bytes 786432 | tf_op jit(solution)/shard_map/slice | solution.py:57
  9.5 0.1 copy.115
  9.6 0.1 copy.116
  9.7 0.1 copy.117
  9.8 0.5 fusion.2
  10.3 0.2 copy.100
  10.5 0.2 reshape.1373
  10.8 0.2 copy.98
  11.1 0.9 convolution_bitcast_fusion
  12.1 0.2 pad_maximum_fusion.1
  12.3 1.8 %copy.99 = f32[8,4,128,128]{3,2,1,0:T(8,128)} copy(f32[8,4,128,128]{2,3,0,1:T(8,128)S(1)} %pad_maximum_fusion.1) | data formatting | bytes 4194304 | tf_op jit(solution)/shard_map/concatenate | solution.py:216
  14.1 1.7 %pad_maximum_fusion = f32[33,128,128]{2,1,0:T(8,128)S(1)} fusion(f32[1,128,128]{2,1,0:T(8,128)S(1)} %pad_bitcast_fusion, f32[32,128,128]{2,1,0:T(8,128)} %bitcast.267), kind=kLoop, calls=%fused_computation.7 | loop fusion | flops 540672 | bytes 4325376 | tf_op jit(solution)/shard_map/concatenate | solution.py:224
  15.8 2.8 %copy.101 = f32[33,128,128]{2,0,1:T(8,128)} copy(f32[33,128,128]{2,1,0:T(8,128)S(1)} %pad_maximum_fusion) | data formatting | bytes 4325376 | tf_op jit(solution)/shard_map/concatenate | solution.py:224
  18.6 11.9 %all-to-all-start = ((f32[33,128,128]{2,0,1:T(8,128)}), f32[33,128,128]{2,0,1:T(8,128)}, u32[]{:S(2)}, u32[]{:S(2)}) async-start(f32[33,128,128]{2,0,1:T(8,128)} %copy.101), calls=%async_computation | async-start | bytes 5242880 | tf_op jit(solution)/shard_map/all_to_all | solution.py:225
  30.7 0.7 reduce.7
  31.6 0.1 reshape.1374
  31.8 0.7 gather_fusion.3
  32.6 0.7 gather_fusion.2
  33.4 0.1 copy.118
  33.5 0.1 copy.119
  33.6 0.1 copy.120
  33.9 0.4 copy.92
  34.3 0.2 copy.87
  34.5 1.0 gather_fusion
  35.5 0.8 copy.126
  36.3 1.0 %gather_fusion.1 = f32[256,6,128]{2,1,0:T(8,128)S(1)} fusion(f32[6,256,128]{2,0,1:T(8,128)S(1)} %copy.92, s32[1024]{0:T(1024)S(1)} %get-tuple-element.57), kind=kCustom, calls=%fused_computation.1 | custom fusion | bytes 1573888 | tf_op jit(solution)/shard_map/gather | solution.py:232
  37.3 1.0 %copy.125 = f32[256,6,128]{2,0,1:T(8,128)} copy(f32[256,6,128]{2,1,0:T(8,128)S(1)} %gather_fusion.1) | data formatting | bytes 1572864 | tf_op jit(solution)/shard_map/gather | solution.py:232
  38.4 0.7 maximum_maximum_fusion.1.aux_ref
  39.1 3.5 %shard_map.113 = f32[32,256]{1,0:T(8,128)} custom-call(f32[3,256,128]{2,1,0:T(8,128)} %bitcast.272, f32[6,256,128]{2,1,0:T(8,128)} %bitcast.268, s32[256,128]{1,0:T(8,128)} %map_ref.1, f32[32,256]{1,0:T(8,128)} %maximum_maximum_fusion.1.aux_ref), custom_call_target="tpu_custom_call" | custom-call | tf_op jit(solution)/shard_map/pallas_call | solution.py:144
  42.6 0.8 slice_bitcast_fusion.2
  43.4 2.8 %gather_fusion.5 = f32[1024,12]{1,0:T(8,128)S(1)} fusion(f32[8,12]{1,0:T(8,128)S(1)} %bitcast.265, s32[1024]{0:T(1024)S(1)} %get-tuple-element.59), kind=kCustom, calls=%fused_computation.5 | custom fusion | bytes 102400 | tf_op jit(solution)/shard_map/gather | solution.py:254
  46.2 0.2 copy.107
  46.4 9.1 %gather_fusion.4 = f32[1024,6,128]{2,1,0:T(8,128)} fusion(f32[6,256,128]{2,0,1:T(8,128)S(1)} %copy.92, s32[1024]{0:T(1024)S(1)} %get-tuple-element.60), kind=kCustom, calls=%fused_computation.4 | custom fusion | bytes 6295552 | tf_op jit(solution)/shard_map/gather | solution.py:252
  55.5 4.5 %copy.124 = f32[1024,6,128]{2,0,1:T(8,128)} copy(f32[1024,6,128]{2,1,0:T(8,128)} %gather_fusion.4) | data formatting | bytes 6291456 | tf_op jit(solution)/shard_map/gather | solution.py:252
  60.1 0.3 fusion.26
  60.4 0.3 convolution_add_fusion.2
  60.7 5.5 %all-to-all-done = f32[33,128,128]{2,0,1:T(8,128)} async-done(((f32[33,128,128]{2,0,1:T(8,128)}), f32[33,128,128]{2,0,1:T(8,128)}, u32[]{:S(2)}, u32[]{:S(2)}) %all-to-all-start) | async-done | bytes 2162720 | tf_op jit(solution)/shard_map/all_to_all | solution.py:225
  66.2 1.1 %slice.198 = f32[1,128,104]{2,0,1:T(1,128)S(1)} slice(f32[33,128,128]{2,0,1:T(8,128)} %all-to-all-done), slice={[32:33], [0:128], [0:104]} | slice | bytes 106496 | tf_op jit(solution)/shard_map/slice | solution.py:249
  67.3 0.1 copy.105
  67.4 0.2 reshape_reshape_squeeze.3
  67.7 0.2 reshape.1375
  67.9 0.7 maximum_maximum_fusion.map_ref.aux_ref
  68.6 3.5 %copy.108.xa_ref = f32[33,128,128]{2,1,0:T(8,128)} copy(f32[33,128,128]{2,0,1:T(8,128)} %all-to-all-done) | data formatting | bytes 4325376 | tf_op jit(solution)/shard_map/all_to_all | solution.py:225
  72.1 9.5 %shard_map.114 = f32[32,1024]{1,0:T(8,128)} custom-call(f32[33,128,128]{2,1,0:T(8,128)} %copy.108.xa_ref, f32[6,1024,128]{2,1,0:T(8,128)} %bitcast.266, f32[32,1024]{1,0:T(8,128)} %maximum_maximum_fusion.map_ref.aux_ref, f32[32,1024]{1,0:T(8,128)} %maximum_maximum_fusion.map_ref.aux_ref), custom_call_target="tpu_custom_call" | custom-call | tf_op jit(solution)/shard_map/pallas_call | solution.py:144
  81.7 0.9 slice_bitcast_fusion
  82.7 0.2 reshape.1377
  82.9 0.5 copy.110
  83.4 1.1 %all_to_all.12 = f32[128,1,144]{2,1,0:T(1,128)} reshape(f32[8,16,8,18]{3,2,1,0:T(8,128)S(1)} %copy.110) | data formatting | bytes 147456 | tf_op jit(solution)/shard_map/all_to_all | solution.py:257
  84.5 4.5 %all-to-all-start.1 = ((f32[128,1,144]{2,1,0:T(1,128)}), f32[128,1,144]{2,1,0:T(1,128)S(1)}, u32[]{:S(2)}, u32[]{:S(2)}) async-start(f32[128,1,144]{2,1,0:T(1,128)} %all_to_all.12), calls=%async_computation.1 | async-start | bytes 262144 | tf_op jit(solution)/shard_map/all_to_all | solution.py:257
  89.0 0.7 convolution_add_fusion.1
  89.7 9.4 %all-to-all-done.1 = f32[128,1,144]{2,1,0:T(1,128)S(1)} async-done(((f32[128,1,144]{2,1,0:T(1,128)}), f32[128,1,144]{2,1,0:T(1,128)S(1)}, u32[]{:S(2)}, u32[]{:S(2)}) %all-to-all-start.1) | async-done | bytes 73760 | tf_op jit(solution)/shard_map/all_to_all | solution.py:257
  99.1 0.3 reduce.2
  99.4 0.2 reshape.1378
  99.7 0.7 convolution_add_fusion
  100.4 0.7 copy.112
  101.2 0.7 copy.113
  (88 shorter events, 3.4 us)
Async XLA Ops:
  0.6 10.1 %copy-start.2 = (s32[1,1024,128]{2,1,0:T(8,128)S(1)}, s32[1,1024,128]{2,1,0:T(8,128)}, u32[]{:S(2)}) copy-start(s32[1,1024,128]{2,1,0:T(8,128)} %param.17) | copy-start | bytes 1572868
  11.1 1.0 copy-start
  18.6 12.1 %copy-start.5 = (s32[1,1024]{1,0:T(1,128)S(1)}, s32[1,1024]{1,0:T(1,128)}, u32[]{:S(2)}) copy-start(s32[1,1024]{1,0:T(1,128)} %param.18) | copy-start | bytes 12292
  18.6 12.8 %copy-start.4 = (s32[2,256]{1,0:T(2,128)S(1)}, s32[2,256]{1,0:T(2,128)}, u32[]{:S(2)}) copy-start(s32[2,256]{1,0:T(2,128)} %param.14) | copy-start | bytes 6148
  18.6 47.6 %all-to-all-start = ((f32[33,128,128]{2,0,1:T(8,128)}), f32[33,128,128]{2,0,1:T(8,128)}, u32[]{:S(2)}, u32[]{:S(2)}) async-start(f32[33,128,128]{2,0,1:T(8,128)} %copy.101), calls=%async_computation | async-start | bytes 5242880 | tf_op jit(solution)/shard_map/all_to_all | solution.py:225
  30.5 2.8 %copy-start.3 = (f32[256,3,128]{2,0,1:T(8,128)S(1)}, f32[256,3,128]{2,0,1:T(8,128)}, u32[]{:S(2)}) copy-start(f32[256,3,128]{2,0,1:T(8,128)} %param.11) | copy-start | bytes 1179652
  31.6 2.1 %copy-start.1 = (f32[6,256,128]{1,2,0:T(8,128)S(1)}, f32[6,256,128]{1,2,0:T(8,128)}, u32[]{:S(2)}) copy-start(f32[6,256,128]{1,2,0:T(8,128)} %copy-done) | copy-start | bytes 2359300
  84.5 14.7 %all-to-all-start.1 = ((f32[128,1,144]{2,1,0:T(1,128)}), f32[128,1,144]{2,1,0:T(1,128)S(1)}, u32[]{:S(2)}, u32[]{:S(2)}) async-start(f32[128,1,144]{2,1,0:T(1,128)} %all_to_all.12), calls=%async_computation.1 | async-start | bytes 262144 | tf_op jit(solution)/shard_map/all_to_all | solution.py:257

commit v8 on v6

--- a/solution.py
+++ b/solution.py
@@ -65,15 +65,17 @@
     return jnp.stack(world_rows + normal_rows, axis=0)
 
 
-def _terms_kernel(from_cargo, xa_ref, tb_ref, map_ref, aux_ref, out_ref, xt_ref, gt_ref):
+def _terms_kernel(from_cargo, xa_ref, tb_ref, map_ref, aux_ref, out_ref, xt_ref, gt_ref, cs_ref):
     chunk = out_ref.shape[1]
     if from_cargo:
-        def cargo_rows(r):
-            return xa_ref[:, pl.ds(r, CAP, stride=4), :].reshape(chunk, 128)
-
-        idx = cargo_rows(3).astype(jnp.int32)
+        peers = chunk // CAP
+        for r in range(4):
+            for s in range(CAP):
+                lanes = pl.ds((r * CAP + s) * 128, 128)
+                cs_ref[r, pl.ds(s, peers, stride=CAP), :] = xa_ref[:, lanes]
+        idx = cs_ref[3].astype(jnp.int32)
         for c in range(3):
-            xt_ref[c] = cargo_rows(c).T
+            xt_ref[c] = cs_ref[c].T
     else:
         idx = map_ref[...]
         for c in range(3):
@@ -135,8 +137,8 @@
     pairs = tb.shape[1]
     from_cargo = maps is None
     if from_cargo:
-        xa_spec = pl.BlockSpec((chunk // CAP, xa.shape[1], 128), lambda i: (i, 0, 0))
-        maps = jnp.zeros((8, 128), jnp.int32)
+        xa_spec = pl.BlockSpec((chunk // CAP, xa.shape[1]), lambda i: (i, 0))
+        maps = aux
         map_spec = pl.BlockSpec((8, 128), lambda i: (0, 0))
     else:
         xa_spec = pl.BlockSpec((3, chunk, 128), lambda i: (0, i, 0))
@@ -155,8 +157,47 @@
         scratch_shapes=[
             pltpu.VMEM((3, 128, chunk), jnp.float32),
             pltpu.VMEM((6, 128, chunk), jnp.float32),
+            pltpu.VMEM((4, chunk, 128), jnp.float32),
         ],
     )(xa, tb, maps, aux)
+
+
+def _cargo_kernel(src_ref, w_ref, map_ref, side_ref, out_ref, rows_ref):
+    chunk = map_ref.shape[0]
+    peers = chunk // CAP
+    pick = (
+        src_ref[...] == lax.broadcasted_iota(jnp.int32, (chunk, w_ref.shape[1]), 1)
+    ).astype(jnp.float32)
+    for c in range(3):
+        rows_ref[...] = jnp.dot(
+            pick, w_ref[c], precision=lax.Precision.HIGHEST, preferred_element_type=jnp.float32
+        )
+        for s in range(CAP):
+            lanes = pl.ds((c * CAP + s) * 128, 128)
+            out_ref[:, lanes] = rows_ref[pl.ds(s, peers, stride=CAP), :]
+    for s in range(CAP):
+        lanes = pl.ds((3 * CAP + s) * 128, 128)
+        out_ref[:, lanes] = map_ref[pl.ds(s, peers, stride=CAP), :].astype(jnp.float32)
+    out_ref[:, pl.ds(4 * CAP * 128, 128)] = side_ref[...]
+
+
+def build_cargo(source_blocks, world3, maps, side, chunk=128):
+    slots = maps.shape[0]
+    peers = chunk // CAP
+    width = (4 * CAP + 1) * 128
+    return pl.pallas_call(
+        _cargo_kernel,
+        out_shape=jax.ShapeDtypeStruct((slots // CAP, width), jnp.float32),
+        grid=(slots // chunk,),
+        in_specs=[
+            pl.BlockSpec((chunk, 1), lambda i: (i, 0)),
+            pl.BlockSpec(world3.shape, lambda i: (0, 0, 0)),
+            pl.BlockSpec((chunk, 128), lambda i: (i, 0)),
+            pl.BlockSpec((peers, 128), lambda i: (i, 0)),
+        ],
+        out_specs=pl.BlockSpec((peers, width), lambda i: (i, 0)),
+        scratch_shapes=[pltpu.VMEM((chunk, 128), jnp.float32)],
+    )(source_blocks[:, None], world3, maps, side)
 
 
 def split_terms(out):
@@ -207,12 +248,6 @@
         .astype(jnp.float32)
         .reshape(-1)
     )
-    pick = (source_blocks[:, None] == jnp.arange(points.shape[0], dtype=jnp.int32)[None, :]).astype(
-        jnp.float32
-    )
-    xa_send = jnp.einsum("sb,cbk->sck", pick, rows6[0:3], precision=lax.Precision.HIGHEST)
-    map_send = remote_maps[0].astype(jnp.float32)[:, None, :]
-    main = jnp.concatenate([xa_send, map_send], axis=1).reshape(peers, CAP * 4, 128)
     frag_pick = (
         source_blocks[:, None] // BF == jnp.arange(frag_count, dtype=jnp.int32)[None, :]
     ).astype(jnp.float32)
@@ -220,7 +255,7 @@
     side = jnp.concatenate([dirs_send, valid[:, None]], axis=1)
     side = side.reshape(peers, CAP * 13)
     side = jnp.concatenate([side, jnp.zeros((peers, 128 - CAP * 13), jnp.float32)], axis=1)
-    cargo = jnp.concatenate([main, side[:, None, :]], axis=1)
+    cargo = build_cargo(source_blocks, rows6[0:3], remote_maps[0], side)
     arrived = lax.all_to_all(cargo, axes, split_axis=0, concat_axis=0, tiled=True)
 
     src_l = local_pairs[0]
@@ -235,7 +270,7 @@
     local_a, local_b = split_terms(out_l)
 
     target_blocks = remote_dst[0]
-    side_in = arrived[:, CAP * 4, 0 : CAP * 13].reshape(peers * CAP, 13)
+    side_in = arrived[:, CAP * 4 * 128 : CAP * 4 * 128 + CAP * 13].reshape(peers * CAP, 13)
     out_r = pair_sums(
         arrived,
         rows6[:, target_blocks],

time: 94.3 us -> 105 us (1.11)
  Pallas kernels: 13.1 us -> 20.7 us
  local copies, waits for them, and re-layouts: 35.5 us -> 41.7 us
  waiting for transfers between devices: 15.9 us -> 11.1 us
  starting transfers between devices: 16.4 us -> 20 us
  other arithmetic: 8.21 us -> 7.07 us
  matrix products: 3.33 us -> 2.28 us
    pallas_call x0 -> x1, Pallas kernels: none -> 7.63 us  [build_cargo(): pl.pallas_call(_cargo_kernel, out_shape=jax.ShapeDtypeStruct((slots // CA...]
    all_to_all x0 -> x1, local copies, waits for them, and re-layouts: none -> 5.25 us  [local(): lax.all_to_all(cargo, axes, split_axis=0, concat_axis=0, tiled=True)]
    all_to_all x1, waiting for transfers between devices: 6.37 us -> 1.66 us  [local(): lax.all_to_all(cargo, axes, split_axis=0, concat_axis=0, tiled=True)]
    all_to_all x1, starting transfers between devices: 4.47 us -> 8.13 us  [local(): lax.all_to_all(remote_a.reshape(peers, CAP * 18), axes, split_axis=0, con...]
    concatenate x2 -> x0, other arithmetic: 1.86 us -> none  [the longest x1 1.72 us: local(): cargo = jnp.concatenate([main, side[:, None, :]], axis=1)]
    unnamed x14 -> x17, local copies, waits for them, and re-layouts: 2.37 us -> 4.12 us
    another operation x1, local copies, waits for them, and re-layouts: 0.18 us -> 1.7 us  [build_cargo(): source_blocks[:, None]]
    concatenate x1 -> x0, local copies, waits for them, and re-layouts: 1.35 us -> none  [local(): jnp.concatenate([xa_send, map_send], axis=1).reshape(peers, CAP * 4, 128)]
  transfers between devices with their start and end apart: 2 -> 2, of which waited for: 2 -> 2; matrix products, arithmetic and copies ran while one was open for 28% -> 25% of each run, Pallas kernels for 4% -> 3%
where the time goes in v8:
time: 105 us; the launch traced here: 104 us
  local copies, waits for them, and re-layouts  41.7 us (40%)
  Pallas kernels  20.7 us (20%)
  starting transfers between devices  20 us (19%)
  waiting for transfers between devices  11.1 us (11%)
  other arithmetic  7.07 us (7%)
  matrix products  2.28 us (2%)
  between operations  1.06 us (1%)
    gather x2, local copies, waits for them, and re-layouts, local(): rows6[:, target_blocks]  13.6 us
    pallas_call x2, Pallas kernels, pair_sums(): pl.pallas_call(functools.partial(_terms_kernel, from_cargo), out_shape=ja...  13 us
    all_to_all x1, starting transfers between devices, local(): lax.all_to_all(cargo, axes, split_axis=0, concat_axis=0, tiled=True)  11.9 us
    all_to_all x1, waiting for transfers between devices, local(): lax.all_to_all(remote_a.reshape(peers, CAP * 18), axes, split_axis=0, con...  9.4 us
    all_to_all x1, starting transfers between devices, local(): lax.all_to_all(remote_a.reshape(peers, CAP * 18), axes, split_axis=0, con...  8.13 us
    pallas_call x1, Pallas kernels, build_cargo(): pl.pallas_call(_cargo_kernel, out_shape=jax.ShapeDtypeStruct((slots // CA...  7.63 us
    all_to_all x1, local copies, waits for them, and re-layouts, local(): lax.all_to_all(cargo, axes, split_axis=0, concat_axis=0, tiled=True)  5.25 us
    unnamed x17, local copies, waits for them, and re-layouts  4.12 us
  transfers between devices with their start and end apart: 2, of which 2 were waited for; matrix products, arithmetic and copies ran while one was open for 25% of the time, Pallas kernels for 3%

profile of v8, /device:TPU:1, one launch (start us, length us, event | category | flops | bytes accessed | tf_op | source)
XLA Modules:
  0.0 103.8 jit_solution(2465947442342399505)
XLA Ops:
  0.6 0.8 slice_bitcast_fusion.4
  1.4 0.7 slice_multiply_fusion.4
  2.3 0.1 add.327
  2.4 0.1 mul.412
  2.6 0.1 mul.406
  2.7 0.1 mul.399
  2.9 0.1 add.334
  3.0 0.1 mul.427
  3.6 0.1 mul.439
  4.0 0.8 copy.55
  4.8 0.1 reshape.1361
  4.9 1.7 %copy.59.src_ref = s32[1024,1]{1,0:T(8,128)} copy(s32[1024,1]{0,1:T(1,128)} %bitcast.268) | data formatting | bytes 8192 | tf_op jit(solution)/shard_map/broadcast_in_dim;squeeze | solution.py:200
  6.6 0.7 fusion.36
  7.3 0.1 reshape.1366
  7.4 0.7 add_select_fusion
  8.1 0.5 fusion
  8.6 0.2 copy.58
  8.8 0.2 reshape.1362
  9.0 0.6 concatenate.50.side_ref
  9.6 1.2 %constant_dynamic-update-slice_fusion.2 = (f32[6,256,128]{2,1,0:T(8,128)S(1)}, f32[1,256,128]{2,1,0:T(8,128)S(1)}) fusion(f32[256]{0:T(256)S(1)} %add.327, f32[256,3,128]{2,0,1:T(8,128)} %param.10, f32[256]{0:T(256)S(1)} %mul.412, f32[256]{0:T(256)S(1)} %mul.406, f32[256]{0:T(256)S(1)} %mul.399), kind=kLoop, calls=%fused_computation.99 | loop fusion | flops 196607 | bytes 659456
  10.9 0.2 constant_dynamic-update-slice_fusion.1
  11.1 0.2 constant_dynamic-update-slice_fusion
  11.3 0.8 pad_maximum_fusion.w_ref
  12.1 7.6 %shard_map.114 = f32[128,4224]{1,0:T(8,128)} custom-call(s32[1024,1]{1,0:T(8,128)} %copy.59.src_ref, f32[3,256,128]{2,1,0:T(8,128)} %pad_maximum_fusion.w_ref, s32[1024,128]{1,0:T(8,128)} %bitcast.262, f32[128,128]{1,0:T(8,128)} %concatenate.50.side_ref), custom_call_target="tpu_custom_call" | custom-call | tf_op jit(solution)/shard_map/pallas_call | solution.py:188
  19.7 5.2 %copy.60 = f32[128,1,4224]{2,1,0:T(1,128)} copy(f32[128,1,4224]{2,0,1:T(8,128)} %bitcast.258) | data formatting | bytes 4325376 | tf_op jit(solution)/shard_map/all_to_all | solution.py:259
  25.0 11.9 %all-to-all-start = ((f32[128,1,4224]{2,1,0:T(1,128)}), f32[128,1,4224]{2,1,0:T(1,128)}, u32[]{:S(2)}, u32[]{:S(2)}) async-start(f32[128,1,4224]{2,1,0:T(1,128)} %copy.60), calls=%async_computation | async-start | bytes 4325376 | tf_op jit(solution)/shard_map/all_to_all | solution.py:259
  36.9 0.3 copy.51
  37.2 1.0 gather_fusion
  38.2 0.8 copy.78
  39.0 0.2 fusion.7
  39.2 0.2 fusion.9
  39.4 0.2 fusion.11
  39.6 0.5 copy.53
  40.0 1.0 gather_fusion.1
  41.1 1.0 copy.77
  42.1 0.7 gather_fusion.3
  42.9 0.7 gather_fusion.2
  43.9 0.7 maximum_maximum_fusion.1.aux_ref
  44.6 3.5 %shard_map.113 = f32[32,256]{1,0:T(8,128)} custom-call(f32[3,256,128]{2,1,0:T(8,128)} %bitcast.261, f32[6,256,128]{2,1,0:T(8,128)} %bitcast.260, s32[256,128]{1,0:T(8,128)} %map_ref.1, f32[32,256]{1,0:T(8,128)} %maximum_maximum_fusion.1.aux_ref), custom_call_target="tpu_custom_call" | custom-call | tf_op jit(solution)/shard_map/pallas_call | solution.py:146
  48.1 0.8 slice_bitcast_fusion.1
  48.9 9.1 %gather_fusion.4 = f32[1024,6,128]{2,1,0:T(8,128)} fusion(f32[6,256,128]{2,0,1:T(8,128)S(1)} %copy.53, s32[1024]{0:T(1024)S(1)} %get-tuple-element.54), kind=kCustom, calls=%fused_computation.4 | custom fusion | bytes 6295552 | tf_op jit(solution)/shard_map/gather | solution.py:276
  58.0 4.5 %copy.75 = f32[1024,6,128]{2,0,1:T(8,128)} copy(f32[1024,6,128]{2,1,0:T(8,128)} %gather_fusion.4) | data formatting | bytes 6291456 | tf_op jit(solution)/shard_map/gather | solution.py:276
  62.5 2.8 %gather_fusion.5 = f32[1024,12]{1,0:T(8,128)S(1)} fusion(f32[8,12]{1,0:T(8,128)S(1)} %bitcast.254, s32[1024]{0:T(1024)S(1)} %get-tuple-element.53), kind=kCustom, calls=%fused_computation.5 | custom fusion | bytes 102400 | tf_op jit(solution)/shard_map/gather | solution.py:278
  65.3 0.2 copy.64
  65.6 0.3 fusion.32
  65.9 0.3 convolution_add_fusion.1
  66.1 1.7 %all-to-all-done = f32[128,1,4224]{2,1,0:T(1,128)} async-done(((f32[128,1,4224]{2,1,0:T(1,128)}), f32[128,1,4224]{2,1,0:T(1,128)}, u32[]{:S(2)}, u32[]{:S(2)}) %all-to-all-start) | async-done | bytes 2162720 | tf_op jit(solution)/shard_map/all_to_all | solution.py:259
  67.8 1.7 %copy.76 = f32[128,1,4224]{2,0,1:T(8,128)S(1)} copy(f32[128,1,4224]{2,1,0:T(1,128)} %all-to-all-done) | data formatting | bytes 4325376
  69.6 0.2 reshape.1363
  69.8 0.4 slice_reduce_fusion
  70.1 0.2 copy.70
  70.3 0.7 maximum_maximum_fusion.map_ref.aux_ref
  71.1 9.5 %shard_map.115 = f32[32,1024]{1,0:T(8,128)} custom-call(f32[128,4224]{1,0:T(8,128)} %bitcast.257, f32[6,1024,128]{2,1,0:T(8,128)} %bitcast.255, f32[32,1024]{1,0:T(8,128)} %maximum_maximum_fusion.map_ref.aux_ref, f32[32,1024]{1,0:T(8,128)} %maximum_maximum_fusion.map_ref.aux_ref), custom_call_target="tpu_custom_call" | custom-call | tf_op jit(solution)/shard_map/pallas_call | solution.py:146
  80.6 0.9 slice_bitcast_fusion
  81.6 0.2 copy.65
  81.8 1.1 %all_to_all.18 = f32[128,1,144]{2,1,0:T(1,128)} reshape(f32[1024,18]{1,0:T(8,128)S(1)} %copy.65) | data formatting | bytes 147456 | tf_op jit(solution)/shard_map/all_to_all | solution.py:281
  82.9 8.1 %all-to-all-start.1 = ((f32[128,1,144]{2,1,0:T(1,128)}), f32[128,1,144]{2,1,0:T(1,128)S(1)}, u32[]{:S(2)}, u32[]{:S(2)}) async-start(f32[128,1,144]{2,1,0:T(1,128)} %all_to_all.18), calls=%async_computation.1 | async-start | bytes 262144 | tf_op jit(solution)/shard_map/all_to_all | solution.py:281
  91.1 0.6 convolution_add_fusion
  91.7 9.4 %all-to-all-done.1 = f32[128,1,144]{2,1,0:T(1,128)S(1)} async-done(((f32[128,1,144]{2,1,0:T(1,128)}), f32[128,1,144]{2,1,0:T(1,128)S(1)}, u32[]{:S(2)}, u32[]{:S(2)}) %all-to-all-start.1) | async-done | bytes 73760 | tf_op jit(solution)/shard_map/all_to_all | solution.py:281
  101.1 0.3 reduce.1
  101.4 0.2 reshape.1364
  101.6 0.7 convolution_add_fusion.2
  102.4 0.7 copy.67
  103.1 0.7 copy.68
  (64 shorter events, 2.0 us)
Async XLA Ops:
  0.6 10.2 %copy-start.2 = (f32[256,3,128]{2,0,1:T(8,128)S(1)}, f32[256,3,128]{2,0,1:T(8,128)}, u32[]{:S(2)}) copy-start(f32[256,3,128]{2,0,1:T(8,128)} %param.10) | copy-start | bytes 1179652
  25.0 11.9 %copy-start.1 = (f32[3,256,128]{2,1,0:T(8,128)S(1)}, f32[3,256,128]{2,1,0:T(8,128)}, u32[]{:S(2)}) copy-start(f32[3,256,128]{2,1,0:T(8,128)} %pad_maximum_fusion.w_ref) | copy-start | bytes 1179652
  25.0 12.2 %copy-start.5 = (s32[2,256]{1,0:T(2,128)S(1)}, s32[2,256]{1,0:T(2,128)}, u32[]{:S(2)}) copy-start(s32[2,256]{1,0:T(2,128)} %param.14) | copy-start | bytes 6148
  25.0 14.0 %copy-start.3 = (f32[256,3,128]{2,0,1:T(8,128)S(1)}, f32[256,3,128]{2,0,1:T(8,128)}, u32[]{:S(2)}) copy-start(f32[256,3,128]{2,0,1:T(8,128)} %param.11) | copy-start | bytes 1179652
  25.0 42.8 %all-to-all-start = ((f32[128,1,4224]{2,1,0:T(1,128)}), f32[128,1,4224]{2,1,0:T(1,128)}, u32[]{:S(2)}, u32[]{:S(2)}) async-start(f32[128,1,4224]{2,1,0:T(1,128)} %copy.60), calls=%async_computation | async-start | bytes 4325376 | tf_op jit(solution)/shard_map/all_to_all | solution.py:259
  41.1 7.8 %copy-start.4 = (s32[1,1024]{1,0:T(1,128)S(1)}, s32[1,1024]{1,0:T(1,128)}, u32[]{:S(2)}) copy-start(s32[1,1024]{1,0:T(1,128)} %param.18) | copy-start | bytes 12292
  69.6 1.5 %copy-start = (f32[128,1,4224]{2,0,1:T(8,128)}, f32[128,1,4224]{2,0,1:T(8,128)S(1)}, u32[]{:S(2)}) copy-start(f32[128,1,4224]{2,0,1:T(8,128)S(1)} %copy.76) | copy-start | bytes 6488068
  82.9 18.2 %all-to-all-start.1 = ((f32[128,1,144]{2,1,0:T(1,128)}), f32[128,1,144]{2,1,0:T(1,128)S(1)}, u32[]{:S(2)}, u32[]{:S(2)}) async-start(f32[128,1,144]{2,1,0:T(1,128)} %all_to_all.18), calls=%async_computation.1 | async-start | bytes 262144 | tf_op jit(solution)/shard_map/all_to_all | solution.py:281

commit v9 on v8

--- a/solution.py
+++ b/solution.py
@@ -72,7 +72,7 @@
         for r in range(4):
             for s in range(CAP):
                 lanes = pl.ds((r * CAP + s) * 128, 128)
-                cs_ref[r, pl.ds(s, peers, stride=CAP), :] = xa_ref[:, lanes]
+                cs_ref[r, pl.ds(s, peers, stride=CAP), :] = xa_ref[:, 0, lanes]
         idx = cs_ref[3].astype(jnp.int32)
         for c in range(3):
             xt_ref[c] = cs_ref[c].T
@@ -137,7 +137,7 @@
     pairs = tb.shape[1]
     from_cargo = maps is None
     if from_cargo:
-        xa_spec = pl.BlockSpec((chunk // CAP, xa.shape[1]), lambda i: (i, 0))
+        xa_spec = pl.BlockSpec((chunk // CAP, 1, xa.shape[2]), lambda i: (i, 0, 0))
         maps = aux
         map_spec = pl.BlockSpec((8, 128), lambda i: (0, 0))
     else:
@@ -162,42 +162,33 @@
     )(xa, tb, maps, aux)
 
 
-def _cargo_kernel(src_ref, w_ref, map_ref, side_ref, out_ref, rows_ref):
-    chunk = map_ref.shape[0]
-    peers = chunk // CAP
-    pick = (
-        src_ref[...] == lax.broadcasted_iota(jnp.int32, (chunk, w_ref.shape[1]), 1)
-    ).astype(jnp.float32)
+def _cargo_kernel(xa_ref, map_ref, side_ref, out_ref):
+    peers = side_ref.shape[0]
     for c in range(3):
-        rows_ref[...] = jnp.dot(
-            pick, w_ref[c], precision=lax.Precision.HIGHEST, preferred_element_type=jnp.float32
-        )
         for s in range(CAP):
             lanes = pl.ds((c * CAP + s) * 128, 128)
-            out_ref[:, lanes] = rows_ref[pl.ds(s, peers, stride=CAP), :]
+            out_ref[:, 0, lanes] = xa_ref[c, pl.ds(s, peers, stride=CAP), :]
     for s in range(CAP):
         lanes = pl.ds((3 * CAP + s) * 128, 128)
-        out_ref[:, lanes] = map_ref[pl.ds(s, peers, stride=CAP), :].astype(jnp.float32)
-    out_ref[:, pl.ds(4 * CAP * 128, 128)] = side_ref[...]
-
-
-def build_cargo(source_blocks, world3, maps, side, chunk=128):
+        out_ref[:, 0, lanes] = map_ref[pl.ds(s, peers, stride=CAP), :].astype(jnp.float32)
+    out_ref[:, 0, pl.ds(4 * CAP * 128, 128)] = side_ref[...]
+
+
+def build_cargo(xa3, maps, side, chunk=128):
     slots = maps.shape[0]
     peers = chunk // CAP
     width = (4 * CAP + 1) * 128
     return pl.pallas_call(
         _cargo_kernel,
-        out_shape=jax.ShapeDtypeStruct((slots // CAP, width), jnp.float32),
+        out_shape=jax.ShapeDtypeStruct((slots // CAP, 1, width), jnp.float32),
         grid=(slots // chunk,),
         in_specs=[
-            pl.BlockSpec((chunk, 1), lambda i: (i, 0)),
-            pl.BlockSpec(world3.shape, lambda i: (0, 0, 0)),
+            pl.BlockSpec((3, chunk, 128), lambda i: (0, i, 0)),
             pl.BlockSpec((chunk, 128), lambda i: (i, 0)),
             pl.BlockSpec((peers, 128), lambda i: (i, 0)),
         ],
-        out_specs=pl.BlockSpec((peers, width), lambda i: (i, 0)),
-        scratch_shapes=[pltpu.VMEM((chunk, 128), jnp.float32)],
-    )(source_blocks[:, None], world3, maps, side)
+        out_specs=pl.BlockSpec((peers, 1, width), lambda i: (i, 0, 0)),
+    )(xa3, maps, side)
 
 
 def split_terms(out):
@@ -255,7 +246,11 @@
     side = jnp.concatenate([dirs_send, valid[:, None]], axis=1)
     side = side.reshape(peers, CAP * 13)
     side = jnp.concatenate([side, jnp.zeros((peers, 128 - CAP * 13), jnp.float32)], axis=1)
-    cargo = build_cargo(source_blocks, rows6[0:3], remote_maps[0], side)
+    pick = (source_blocks[:, None] == jnp.arange(points.shape[0], dtype=jnp.int32)[None, :]).astype(
+        jnp.float32
+    )
+    xa3 = jnp.einsum("sb,cbk->csk", pick, rows6[0:3], precision=lax.Precision.HIGHEST)
+    cargo = build_cargo(xa3, remote_maps[0], side)
     arrived = lax.all_to_all(cargo, axes, split_axis=0, concat_axis=0, tiled=True)
 
     src_l = local_pairs[0]
@@ -270,7 +265,7 @@
     local_a, local_b = split_terms(out_l)
 
     target_blocks = remote_dst[0]
-    side_in = arrived[:, CAP * 4 * 128 : CAP * 4 * 128 + CAP * 13].reshape(peers * CAP, 13)
+    side_in = arrived[:, 0, CAP * 4 * 128 : CAP * 4 * 128 + CAP * 13].reshape(peers * CAP, 13)
     out_r = pair_sums(
         arrived,
         rows6[:, target_blocks],

time: 105 us -> 102 us (0.971)
  local copies, waits for them, and re-layouts: 41.7 us -> 39.2 us
  matrix products: 2.28 us -> 4.5 us
  waiting for transfers between devices: 11.1 us -> 9.41 us
  Pallas kernels: 20.7 us -> 19.3 us
  starting transfers between devices: 20 us -> 21.3 us
    all_to_all x1 -> x0, local copies, waits for them, and re-layouts: 5.25 us -> none  [local(): lax.all_to_all(cargo, axes, split_axis=0, concat_axis=0, tiled=True)]
    slice x1 -> x3, local copies, waits for them, and re-layouts: 0.01 us -> 2.31 us  [the longest x1 1.06 us: to_world_rows(): points[:, 0]]
    gather x2, local copies, waits for them, and re-layouts: 2.06 us -> 4.33 us  [local(): rows6[:, tgt_l]]
    dot_general x0 -> x1, matrix products: none -> 2.22 us  [local(): jnp.einsum('sb,cbk->csk', pick, rows6[0:3], precision=lax.Precision.HIGHEST)]
    all_to_all x1, waiting for transfers between devices: 1.66 us -> 0.01 us  [local(): lax.all_to_all(cargo, axes, split_axis=0, concat_axis=0, tiled=True)]
    all_to_all x1, starting transfers between devices: 8.13 us -> 9.76 us  [local(): lax.all_to_all(remote_a.reshape(peers, CAP * 18), axes, split_axis=0, con...]
    another operation x1, local copies, waits for them, and re-layouts: 1.7 us -> 0.18 us  [local(): arrived[:, 0, CAP * 4 * 128:CAP * 4 * 128 + CAP * 13]]
    pallas_call x1, Pallas kernels: 7.63 us -> 6.2 us  [build_cargo(): pl.pallas_call(_cargo_kernel, out_shape=jax.ShapeDtypeStruct((slots // CA...]
  transfers between devices with their start and end apart: 2 -> 2, of which waited for: 2 -> 1; matrix products, arithmetic and copies ran while one was open for 25% -> 32% of each run, Pallas kernels for 3% -> 3%
where the time goes in v9:
time: 102 us; the launch traced here: 101 us
  local copies, waits for them, and re-layouts  39.2 us (38%)
  starting transfers between devices  21.3 us (21%)
  Pallas kernels  19.3 us (19%)
  waiting for transfers between devices  9.41 us (9%)
  other arithmetic  6.32 us (6%)
  matrix products  4.5 us (4%)
  between operations  1.07 us (1%)
    gather x2, local copies, waits for them, and re-layouts, local(): rows6[:, target_blocks]  13.6 us
    pallas_call x2, Pallas kernels, pair_sums(): pl.pallas_call(functools.partial(_terms_kernel, from_cargo), out_shape=ja...  13.1 us
    all_to_all x1, starting transfers between devices, local(): lax.all_to_all(cargo, axes, split_axis=0, concat_axis=0, tiled=True)  11.5 us
    all_to_all x1, starting transfers between devices, local(): lax.all_to_all(remote_a.reshape(peers, CAP * 18), axes, split_axis=0, con...  9.76 us
    all_to_all x1, waiting for transfers between devices, local(): lax.all_to_all(remote_a.reshape(peers, CAP * 18), axes, split_axis=0, con...  9.4 us
    pallas_call x1, Pallas kernels, build_cargo(): pl.pallas_call(_cargo_kernel, out_shape=jax.ShapeDtypeStruct((slots // CA...  6.2 us
    gather x2, local copies, waits for them, and re-layouts, local(): rows6[:, tgt_l]  4.33 us
    gather x2, local copies, waits for them, and re-layouts, local(): frag_dirs[target_blocks // BF]  2.99 us
  transfers between devices with their start and end apart: 2, of which 1 were waited for; matrix products, arithmetic and copies ran while one was open for 32% of the time, Pallas kernels for 3%

profile of v9, /device:TPU:1, one launch (start us, length us, event | category | flops | bytes accessed | tf_op | source)
XLA Modules:
  0.0 101.0 jit_solution(2524706825943316556)
XLA Ops:
  0.6 0.8 slice_bitcast_fusion.4
  1.4 0.7 slice_multiply_fusion.4
  2.3 0.1 add.327
  2.3 1.1 %fusion.70 = (f32[256,1,128]{2,0,1:T(8,128)S(1)}, f32[256,1,128]{2,0,1:T(8,128)S(1)}, f32[256,1,128]{2,0,1:T(8,128)S(1)}) fusion(f32[256,3,128]{2,0,1:T(8,128)} %param.10), kind=kLoop, calls=%fused_computation.187 | loop fusion | bytes 786432 | tf_op jit(solution)/shard_map/slice | solution.py:57
  3.4 0.1 copy.96
  3.6 0.1 mul.412
  3.6 0.1 copy.95
  3.8 0.1 mul.406
  3.9 0.1 copy.94
  4.4 0.1 mul.427
  5.0 0.1 mul.439
  5.4 0.8 copy.80
  6.1 0.1 reshape.1357
  6.2 0.7 fusion.39
  7.0 0.1 reshape.1361
  7.1 0.7 add_select_fusion
  7.8 0.5 fusion.2
  8.3 0.2 copy.84
  8.5 0.2 reshape.1358
  8.7 0.6 concatenate.50.side_ref
  9.4 2.2 %convolution_bitcast_fusion.xa_ref = f32[3,1024,128]{2,1,0:T(8,128)} fusion(s32[1024]{0:T(1024)S(1)} %bitcast.266, f32[1,256,128]{1,2,0:T(8,128)S(1)} %get-tuple-element.11, f32[1,256,128]{1,2,0:T(8,128)S(1)} %get-tuple-element.13, f32[1,256,128]{1,2,0:T(8,128)S(1)} %get-tuple-element.15), kind=kOutput, calls=%fused_computation.7 | convolution fusion | flops 1208418304 | bytes 1970176 | tf_op jit(solution)/shard_map/sb,cbk->csk/dot_general | solution.py:252
  11.7 6.2 %shard_map.114 = f32[128,1,4224]{2,1,0:T(1,128)} custom-call(f32[3,1024,128]{2,1,0:T(8,128)} %convolution_bitcast_fusion.xa_ref, s32[1024,128]{1,0:T(8,128)} %bitcast.259, f32[128,128]{1,0:T(8,128)} %concatenate.50.side_ref), custom_call_target="tpu_custom_call" | custom-call | tf_op jit(solution)/shard_map/pallas_call | solution.py:181
  17.9 11.5 %all-to-all-start = ((f32[128,1,4224]{2,1,0:T(1,128)}), f32[128,1,4224]{2,1,0:T(1,128)S(1)}, u32[]{:S(2)}, u32[]{:S(2)}) async-start(f32[128,1,4224]{2,1,0:T(1,128)} %shard_map.114), calls=%async_computation | async-start | bytes 4325376 | tf_op jit(solution)/shard_map/all_to_all | solution.py:254
  29.4 0.2 copy.73
  29.7 1.0 gather_fusion
  30.7 0.8 copy.106
  31.5 1.1 %fusion.69 = (f32[256,1,128]{2,0,1:T(8,128)S(1)}, f32[256,1,128]{2,0,1:T(8,128)S(1)}, f32[256,1,128]{2,0,1:T(8,128)S(1)}) fusion(f32[256,3,128]{2,0,1:T(8,128)} %param.11), kind=kLoop, calls=%fused_computation.186 | loop fusion | bytes 786432 | tf_op jit(solution)/shard_map/slice | solution.py:63
  32.5 0.1 copy.99
  32.6 0.1 copy.98
  32.7 0.1 copy.97
  32.8 0.7 fusion.10
  33.5 0.7 fusion.12
  34.2 0.7 fusion.14
  34.9 1.6 %copy.78 = f32[6,256,128]{2,0,1:T(8,128)S(1)} copy(f32[6,256,128]{1,2,0:T(8,128)} %fusion.14) | data formatting | bytes 1572864 | tf_op jit(solution)/shard_map/stack | solution.py:65
  36.5 2.0 %gather_fusion.1 = f32[256,6,128]{2,1,0:T(8,128)} fusion(f32[6,256,128]{2,0,1:T(8,128)S(1)} %copy.78, s32[1024]{0:T(1024)S(1)} %get-tuple-element.57), kind=kCustom, calls=%fused_computation.1 | custom fusion | bytes 1573888 | tf_op jit(solution)/shard_map/gather | solution.py:261
  38.5 2.3 %copy.105 = f32[256,6,128]{2,0,1:T(8,128)} copy(f32[256,6,128]{2,1,0:T(8,128)} %gather_fusion.1) | data formatting | bytes 1572864 | tf_op jit(solution)/shard_map/gather | solution.py:261
  40.8 0.7 gather_fusion.3
  41.6 0.7 gather_fusion.2
  42.6 0.7 maximum_maximum_fusion.1.aux_ref
  43.3 3.5 %shard_map.113 = f32[32,256]{1,0:T(8,128)} custom-call(f32[3,256,128]{2,1,0:T(8,128)} %bitcast.258, f32[6,256,128]{2,1,0:T(8,128)} %bitcast.257, s32[256,128]{1,0:T(8,128)} %map_ref.1, f32[32,256]{1,0:T(8,128)} %maximum_maximum_fusion.1.aux_ref), custom_call_target="tpu_custom_call" | custom-call | tf_op jit(solution)/shard_map/pallas_call | solution.py:146
  46.8 0.8 slice_bitcast_fusion.1
  47.6 9.1 %gather_fusion.4 = f32[1024,6,128]{2,1,0:T(8,128)} fusion(f32[6,256,128]{2,0,1:T(8,128)S(1)} %copy.78, s32[1024]{0:T(1024)S(1)} %get-tuple-element.60), kind=kCustom, calls=%fused_computation.4 | custom fusion | bytes 6295552 | tf_op jit(solution)/shard_map/gather | solution.py:271
  56.7 4.5 %copy.104 = f32[1024,6,128]{2,0,1:T(8,128)} copy(f32[1024,6,128]{2,1,0:T(8,128)} %gather_fusion.4) | data formatting | bytes 6291456 | tf_op jit(solution)/shard_map/gather | solution.py:271
  61.2 2.8 %gather_fusion.5 = f32[1024,12]{1,0:T(8,128)S(1)} fusion(f32[8,12]{1,0:T(8,128)S(1)} %bitcast.254, s32[1024]{0:T(1024)S(1)} %get-tuple-element.59), kind=kCustom, calls=%fused_computation.5 | custom fusion | bytes 102400 | tf_op jit(solution)/shard_map/gather | solution.py:273
  64.0 0.2 copy.88
  64.3 0.3 fusion.35
  64.6 0.3 convolution_add_fusion.1
  64.9 0.2 slice_reduce_fusion.1
  65.1 0.2 reshape_squeeze.3
  65.3 0.4 slice_reduce_fusion
  65.6 0.2 copy.100
  65.8 0.7 maximum_maximum_fusion.map_ref.aux_ref
  66.6 9.6 %shard_map.115 = f32[32,1024]{1,0:T(8,128)} custom-call(f32[128,1,4224]{2,1,0:T(1,128)} %copy-done, f32[6,1024,128]{2,1,0:T(8,128)} %bitcast.255, f32[32,1024]{1,0:T(8,128)} %maximum_maximum_fusion.map_ref.aux_ref, f32[32,1024]{1,0:T(8,128)} %maximum_maximum_fusion.map_ref.aux_ref), custom_call_target="tpu_custom_call" | custom-call | tf_op jit(solution)/shard_map/pallas_call | solution.py:146
  76.2 0.9 slice_bitcast_fusion
  77.2 0.2 copy.89
  77.4 1.1 %all_to_all.12 = f32[128,1,144]{2,1,0:T(1,128)} reshape(f32[1024,18]{1,0:T(8,128)S(1)} %copy.89) | data formatting | bytes 147456 | tf_op jit(solution)/shard_map/all_to_all | solution.py:276
  78.5 9.8 %all-to-all-start.1 = ((f32[128,1,144]{2,1,0:T(1,128)}), f32[128,1,144]{2,1,0:T(1,128)S(1)}, u32[]{:S(2)}, u32[]{:S(2)}) async-start(f32[128,1,144]{2,1,0:T(1,128)} %all_to_all.12), calls=%async_computation.1 | async-start | bytes 262144 | tf_op jit(solution)/shard_map/all_to_all | solution.py:276
  88.3 0.6 convolution_add_fusion
  88.9 9.4 %all-to-all-done.1 = f32[128,1,144]{2,1,0:T(1,128)S(1)} async-done(((f32[128,1,144]{2,1,0:T(1,128)}), f32[128,1,144]{2,1,0:T(1,128)S(1)}, u32[]{:S(2)}, u32[]{:S(2)}) %all-to-all-start.1) | async-done | bytes 73760 | tf_op jit(solution)/shard_map/all_to_all | solution.py:276
  98.3 0.3 reduce.2
  98.6 0.2 reshape.1359
  98.8 0.7 convolution_add_fusion.2
  99.6 0.7 copy.91
  100.3 0.7 copy.92
  (68 shorter events, 2.3 us)
Async XLA Ops:
  0.6 8.8 %copy-start.2 = (s32[1,1024]{1,0:T(1,128)S(1)}, s32[1,1024]{1,0:T(1,128)}, u32[]{:S(2)}) copy-start(s32[1,1024]{1,0:T(1,128)} %param.16) | copy-start | bytes 12292
  9.4 8.4 %copy-start.1 = (f32[6,256,128]{1,2,0:T(8,128)}, f32[6,256,128]{1,2,0:T(8,128)S(1)}, u32[]{:S(2)}) copy-start(f32[6,256,128]{1,2,0:T(8,128)S(1)} %get-tuple-element.10) | copy-start | bytes 2359300
  17.9 11.8 %copy-start.4 = (s32[2,256]{1,0:T(2,128)S(1)}, s32[2,256]{1,0:T(2,128)}, u32[]{:S(2)}) copy-start(s32[2,256]{1,0:T(2,128)} %param.14) | copy-start | bytes 6148
  17.9 47.0 %all-to-all-start = ((f32[128,1,4224]{2,1,0:T(1,128)}), f32[128,1,4224]{2,1,0:T(1,128)S(1)}, u32[]{:S(2)}, u32[]{:S(2)}) async-start(f32[128,1,4224]{2,1,0:T(1,128)} %shard_map.114), calls=%async_computation | async-start | bytes 4325376 | tf_op jit(solution)/shard_map/all_to_all | solution.py:254
  38.5 9.1 %copy-start.3 = (s32[1,1024]{1,0:T(1,128)S(1)}, s32[1,1024]{1,0:T(1,128)}, u32[]{:S(2)}) copy-start(s32[1,1024]{1,0:T(1,128)} %param.18) | copy-start | bytes 12292
  64.9 1.7 %copy-start = (f32[128,1,4224]{2,1,0:T(1,128)}, f32[128,1,4224]{2,1,0:T(1,128)S(1)}, u32[]{:S(2)}) copy-start(f32[128,1,4224]{2,1,0:T(1,128)S(1)} %all-to-all-done.xa_ref) | copy-start | bytes 6488068
  78.5 19.8 %all-to-all-start.1 = ((f32[128,1,144]{2,1,0:T(1,128)}), f32[128,1,144]{2,1,0:T(1,128)S(1)}, u32[]{:S(2)}, u32[]{:S(2)}) async-start(f32[128,1,144]{2,1,0:T(1,128)} %all_to_all.12), calls=%async_computation.1 | async-start | bytes 262144 | tf_op jit(solution)/shard_map/all_to_all | solution.py:276

commit v10 on v9

--- a/solution.py
+++ b/solution.py
@@ -69,10 +69,10 @@
     chunk = out_ref.shape[1]
     if from_cargo:
         peers = chunk // CAP
-        for r in range(4):
-            for s in range(CAP):
-                lanes = pl.ds((r * CAP + s) * 128, 128)
-                cs_ref[r, pl.ds(s, peers, stride=CAP), :] = xa_ref[:, 0, lanes]
+        height = 4 * CAP + 1
+        for p in range(peers):
+            for r in range(4):
+                cs_ref[r, pl.ds(p * CAP, CAP), :] = xa_ref[pl.ds(p * height + r * CAP, CAP), :]
         idx = cs_ref[3].astype(jnp.int32)
         for c in range(3):
             xt_ref[c] = cs_ref[c].T
@@ -137,7 +137,8 @@
     pairs = tb.shape[1]
     from_cargo = maps is None
     if from_cargo:
-        xa_spec = pl.BlockSpec((chunk // CAP, 1, xa.shape[2]), lambda i: (i, 0, 0))
+        xa = xa.reshape(-1, 128)
+        xa_spec = pl.BlockSpec((chunk // CAP * (4 * CAP + 1), 128), lambda i: (i, 0))
         maps = aux
         map_spec = pl.BlockSpec((8, 128), lambda i: (0, 0))
     else:
@@ -164,31 +165,31 @@
 
 def _cargo_kernel(xa_ref, map_ref, side_ref, out_ref):
     peers = side_ref.shape[0]
-    for c in range(3):
-        for s in range(CAP):
-            lanes = pl.ds((c * CAP + s) * 128, 128)
-            out_ref[:, 0, lanes] = xa_ref[c, pl.ds(s, peers, stride=CAP), :]
-    for s in range(CAP):
-        lanes = pl.ds((3 * CAP + s) * 128, 128)
-        out_ref[:, 0, lanes] = map_ref[pl.ds(s, peers, stride=CAP), :].astype(jnp.float32)
-    out_ref[:, 0, pl.ds(4 * CAP * 128, 128)] = side_ref[...]
+    height = 4 * CAP + 1
+    for p in range(peers):
+        slots = pl.ds(p * CAP, CAP)
+        for c in range(3):
+            out_ref[pl.ds(p * height + c * CAP, CAP), :] = xa_ref[c, slots, :]
+        out_ref[pl.ds(p * height + 3 * CAP, CAP), :] = map_ref[slots, :].astype(jnp.float32)
+        out_ref[pl.ds(p * height + 4 * CAP, 1), :] = side_ref[pl.ds(p, 1), :]
 
 
 def build_cargo(xa3, maps, side, chunk=128):
     slots = maps.shape[0]
     peers = chunk // CAP
-    width = (4 * CAP + 1) * 128
-    return pl.pallas_call(
+    height = 4 * CAP + 1
+    cargo = pl.pallas_call(
         _cargo_kernel,
-        out_shape=jax.ShapeDtypeStruct((slots // CAP, 1, width), jnp.float32),
+        out_shape=jax.ShapeDtypeStruct((slots // CAP * height, 128), jnp.float32),
         grid=(slots // chunk,),
         in_specs=[
             pl.BlockSpec((3, chunk, 128), lambda i: (0, i, 0)),
             pl.BlockSpec((chunk, 128), lambda i: (i, 0)),
             pl.BlockSpec((peers, 128), lambda i: (i, 0)),
         ],
-        out_specs=pl.BlockSpec((peers, 1, width), lambda i: (i, 0, 0)),
+        out_specs=pl.BlockSpec((peers * height, 128), lambda i: (i, 0)),
     )(xa3, maps, side)
+    return cargo.reshape(slots // CAP, 1, height * 128)
 
 
 def split_terms(out):
@@ -199,6 +200,13 @@
     hb0 = -jnp.concatenate([sel[:, 21:24], sel[:, 9:12]], axis=1) * (1.0 / 4096)
     hb1 = -jnp.concatenate([sel[:, 24:27], sel[:, 15:18]], axis=1) * (1.0 / 4096)
     return jnp.concatenate([ga, ha], axis=1), jnp.concatenate([gb, hb0, hb1], axis=1)
+
+
+def pick_rows(blocks, rows):
+    onehot = (blocks[:, None] == jnp.arange(rows.shape[1], dtype=jnp.int32)[None, :]).astype(
+        jnp.float32
+    )
+    return jnp.einsum("sb,cbk->csk", onehot, rows, precision=lax.Precision.HIGHEST)
 
 
 def frag_sums(blocks, terms, frag_count):
@@ -246,19 +254,15 @@
     side = jnp.concatenate([dirs_send, valid[:, None]], axis=1)
     side = side.reshape(peers, CAP * 13)
     side = jnp.concatenate([side, jnp.zeros((peers, 128 - CAP * 13), jnp.float32)], axis=1)
-    pick = (source_blocks[:, None] == jnp.arange(points.shape[0], dtype=jnp.int32)[None, :]).astype(
-        jnp.float32
-    )
-    xa3 = jnp.einsum("sb,cbk->csk", pick, rows6[0:3], precision=lax.Precision.HIGHEST)
-    cargo = build_cargo(xa3, remote_maps[0], side)
+    cargo = build_cargo(pick_rows(source_blocks, rows6[0:3]), remote_maps[0], side)
     arrived = lax.all_to_all(cargo, axes, split_axis=0, concat_axis=0, tiled=True)
 
     src_l = local_pairs[0]
     tgt_l = local_pairs[1]
     ones = jnp.ones((src_l.shape[0],), jnp.float32)
     out_l = pair_sums(
-        rows6[0:3][:, src_l],
-        rows6[:, tgt_l],
+        pick_rows(src_l, rows6[0:3]),
+        pick_rows(tgt_l, rows6),
         local_maps,
         make_aux(frag_dirs[src_l // BF], frag_dirs[tgt_l // BF], ones),
     )
@@ -268,7 +272,7 @@
     side_in = arrived[:, 0, CAP * 4 * 128 : CAP * 4 * 128 + CAP * 13].reshape(peers * CAP, 13)
     out_r = pair_sums(
         arrived,
-        rows6[:, target_blocks],
+        pick_rows(target_blocks, rows6),
         None,
         make_aux(side_in[:, 0:12], frag_dirs[target_blocks // BF], side_in[:, 12]),
     )

time: 102 us -> 96.1 us (0.942)
  local copies, waits for them, and re-layouts: 39.2 us -> 21.5 us
  matrix products: 4.5 us -> 12.7 us
  other arithmetic: 6.32 us -> 10.4 us
  starting transfers between devices: 21.3 us -> 20.1 us
  waiting for transfers between devices: 9.41 us -> 10.6 us
    gather x6 -> x0, local copies, waits for them, and re-layouts: 19.7 us -> none  [the longest x2 13.6 us: local(): rows6[:, target_blocks]]
    dot_general x1 -> x4, matrix products: 2.22 us -> 9.71 us  [pick_rows(): jnp.einsum('sb,cbk->csk', onehot, rows, precision=lax.Precision.HIGHEST)]
    another operation x2 -> x0, local copies, waits for them, and re-layouts: 1.78 us -> none  [to_world_rows(): return jnp.stack(world_rows + normal_rows, axis=0)]
    all_to_all x1, waiting for transfers between devices: 0.01 us -> 1.17 us  [local(): lax.all_to_all(cargo, axes, split_axis=0, concat_axis=0, tiled=True)]
    all_to_all x1, starting transfers between devices: 9.76 us -> 8.6 us  [local(): lax.all_to_all(remote_a.reshape(peers, CAP * 18), axes, split_axis=0, con...]
    concatenate x2, local copies, waits for them, and re-layouts: 0.15 us -> 1.25 us  [make_aux(): jnp.concatenate([dirs_a.T, dirs_b.T, valid[None, :], jnp.zeros((32 - 25,...]
    unnamed x20 -> x28, local copies, waits for them, and re-layouts: 2.93 us -> 3.85 us
  transfers between devices with their start and end apart: 2 -> 2, of which waited for: 1 -> 2; matrix products, arithmetic and copies ran while one was open for 32% -> 28% of each run, Pallas kernels for 3% -> 4%
where the time goes in v10:
time: 96.1 us; the launch traced here: 95 us
  local copies, waits for them, and re-layouts  21.5 us (22%)
  starting transfers between devices  20.1 us (21%)
  Pallas kernels  18.7 us (19%)
  matrix products  12.7 us (13%)
  waiting for transfers between devices  10.6 us (11%)
  other arithmetic  10.4 us (11%)
  between operations  1 us (1%)
    pallas_call x2, Pallas kernels, pair_sums(): pl.pallas_call(functools.partial(_terms_kernel, from_cargo), out_shape=ja...  13 us
    all_to_all x1, starting transfers between devices, local(): lax.all_to_all(cargo, axes, split_axis=0, concat_axis=0, tiled=True)  11.5 us
    dot_general x4, matrix products, pick_rows(): jnp.einsum('sb,cbk->csk', onehot, rows, precision=lax.Precision.HIGHEST)  9.71 us
    all_to_all x1, waiting for transfers between devices, local(): lax.all_to_all(remote_a.reshape(peers, CAP * 18), axes, split_axis=0, con...  9.41 us
    all_to_all x1, starting transfers between devices, local(): lax.all_to_all(remote_a.reshape(peers, CAP * 18), axes, split_axis=0, con...  8.6 us
    pallas_call x1, Pallas kernels, build_cargo(): pl.pallas_call(_cargo_kernel, out_shape=jax.ShapeDtypeStruct((slots // CA...  5.67 us
    unnamed x28, local copies, waits for them, and re-layouts  3.85 us
    gather x2, local copies, waits for them, and re-layouts, local(): frag_dirs[target_blocks // BF]  2.99 us
  transfers between devices with their start and end apart: 2, of which 2 were waited for; matrix products, arithmetic and copies ran while one was open for 28% of the time, Pallas kernels for 4%

profile of v10, /device:TPU:1, one launch (start us, length us, event | category | flops | bytes accessed | tf_op | source)
XLA Modules:
  0.0 95.0 jit_solution(6422533509362916167)
XLA Ops:
  0.6 0.8 slice_bitcast_fusion.4
  1.4 0.7 slice_multiply_fusion.4
  2.5 0.1 mul.399
  2.8 0.7 add_select_fusion
  4.7 0.8 copy.75
  5.5 0.7 fusion.48
  6.3 0.1 reshape.1306
  6.4 1.1 %fusion.81 = (f32[256,1,128]{2,0,1:T(8,128)S(1)}, f32[256,1,128]{2,0,1:T(8,128)S(1)}, f32[256,1,128]{2,0,1:T(8,128)S(1)}) fusion(f32[256,3,128]{2,0,1:T(8,128)} %param.10), kind=kLoop, calls=%fused_computation.189 | loop fusion | bytes 786432 | tf_op jit(solution)/shard_map/slice | solution.py:57
  7.5 0.1 copy.92
  7.6 0.1 copy.93
  7.7 0.1 copy.94
  7.8 0.5 fusion.5
  8.3 0.2 copy.79
  8.5 0.2 reshape.1301
  8.7 0.6 concatenate.50.side_ref
  9.5 2.2 %convolution_bitcast_fusion.1.xa_ref = f32[3,1024,128]{2,1,0:T(8,128)} fusion(s32[1024]{0:T(1024)S(1)} %bitcast.271, f32[1,256,128]{1,2,0:T(8,128)S(1)} %get-tuple-element.11, f32[1,256,128]{1,2,0:T(8,128)S(1)} %get-tuple-element.13, f32[1,256,128]{1,2,0:T(8,128)S(1)} %get-tuple-element.15), kind=kOutput, calls=%fused_computation.4 | convolution fusion | flops 1208418304 | bytes 1970176 | tf_op jit(solution)/shard_map/sb,cbk->csk/dot_general | solution.py:209
  11.7 5.7 %shard_map.114 = f32[4224,128]{1,0:T(8,128)} custom-call(f32[3,1024,128]{2,1,0:T(8,128)} %convolution_bitcast_fusion.1.xa_ref, s32[1024,128]{1,0:T(8,128)} %bitcast.262, f32[128,128]{1,0:T(8,128)} %concatenate.50.side_ref), custom_call_target="tpu_custom_call" | custom-call | tf_op jit(solution)/shard_map/pallas_call | solution.py:181
  17.4 11.5 %all-to-all-start = ((f32[128,1,4224]{2,1,0:T(1,128)}), f32[128,1,4224]{2,1,0:T(1,128)S(1)}, u32[]{:S(2)}, u32[]{:S(2)}) async-start(f32[128,1,4224]{2,1,0:T(1,128)} %bitcast.260), calls=%async_computation | async-start | bytes 4325376 | tf_op jit(solution)/shard_map/all_to_all | solution.py:258
  28.9 0.6 fusion.84
  29.5 0.6 pad.31.clone
  30.1 0.7 pad.32.clone
  30.8 0.7 gather_fusion.1
  31.6 0.7 gather_fusion
  32.5 1.7 %fusion.80 = (f32[256,1,128]{2,0,1:T(8,128)S(1)}, f32[256,1,128]{2,0,1:T(8,128)S(1)}, f32[256,1,128]{2,0,1:T(8,128)}) fusion(f32[256,3,128]{2,0,1:T(8,128)} %param.11), kind=kLoop, calls=%fused_computation.188 | loop fusion | bytes 786432 | tf_op jit(solution)/shard_map/slice | solution.py:63
  34.2 0.1 copy.95
  34.3 0.1 copy.96
  34.4 1.0 %copy.97 = f32[256,1,128]{0,2,1:T(8,128)S(1)} copy(f32[256,1,128]{2,0,1:T(8,128)} %get-tuple-element.20) | data formatting | bytes 262144
  35.4 0.7 fusion.19
  36.2 2.2 %convolution_bitcast_fusion.3.xa_ref = f32[3,256,128]{2,1,0:T(8,128)} fusion(f32[1,256,128]{1,2,0:T(8,128)} %copy-done.2, f32[1,256,128]{1,2,0:T(8,128)} %copy-done.1, f32[1,256,128]{1,2,0:T(8,128)S(1)} %get-tuple-element.15, s32[256]{0:T(256)} %bitcast.273), kind=kOutput, calls=%fused_computation.6 | convolution fusion | flops 302252032 | bytes 787456 | tf_op jit(solution)/shard_map/sb,cbk->csk/dot_general | solution.py:209
  38.3 2.1 %convolution_bitcast_fusion.2.tb_ref = f32[6,256,128]{2,1,0:T(8,128)} fusion(f32[6,256,128]{1,2,0:T(8,128)S(1)} %fusion.21, s32[256]{0:T(256)} %bitcast.275), kind=kOutput, calls=%fused_computation.5 | convolution fusion | flops 604045312 | bytes 1573888 | tf_op jit(solution)/shard_map/sb,cbk->csk/dot_general | solution.py:209
  40.5 1.4 %maximum_maximum_fusion.1.aux_ref = f32[32,256]{1,0:T(8,128)} fusion(f32[12,256]{1,0:T(8,128)S(1)} %bitcast.265, f32[12,256]{1,0:T(8,128)S(1)} %bitcast.266, f32[32]{0:T(128)} %pad.32.clone, f32[32]{0:T(128)} %pad.31.clone), kind=kLoop, calls=%fused_computation.89 | loop fusion | flops 24576 | bytes 57600 | tf_op jit(solution)/shard_map/concatenate | solution.py:221
  41.8 3.5 %shard_map.113 = f32[32,256]{1,0:T(8,128)} custom-call(f32[3,256,128]{2,1,0:T(8,128)} %convolution_bitcast_fusion.3.xa_ref, f32[6,256,128]{2,1,0:T(8,128)} %convolution_bitcast_fusion.2.tb_ref, s32[256,128]{1,0:T(8,128)} %map_ref.1, f32[32,256]{1,0:T(8,128)} %maximum_maximum_fusion.1.aux_ref), custom_call_target="tpu_custom_call" | custom-call | tf_op jit(solution)/shard_map/pallas_call | solution.py:147
  45.3 0.8 slice_bitcast_fusion.1
  46.1 0.6 fusion.83
  46.7 0.6 fusion.60
  47.3 2.8 %gather_fusion.2 = f32[1024,12]{1,0:T(8,128)S(1)} fusion(f32[8,12]{1,0:T(8,128)S(1)} %bitcast.258, s32[1024]{0:T(1024)S(1)} %broadcast_clamp_fusion), kind=kCustom, calls=%fused_computation.2 | custom fusion | bytes 102400 | tf_op jit(solution)/shard_map/gather | solution.py:277
  50.1 0.2 copy.83
  50.3 0.7 fusion.62
  51.0 0.7 fusion.61
  51.7 0.7 and_select_fusion.4
  52.4 0.7 and_select_fusion.3
  53.0 0.7 slice_multiply_fusion.3
  53.7 0.7 slice_multiply_fusion.2
  54.5 0.3 fusion.44
  54.8 1.0 %convolution_add_fusion.1 = f32[8,18]{1,0:T(8,128)S(1)} fusion(f32[8,18]{1,0:T(8,128)S(1)} %fusion.44, s32[256]{0:T(256)S(1)} %and_select_fusion.3, f32[256,6]{0,1:T(8,128)S(1)} %fusion.62, f32[256,6]{0,1:T(8,128)S(1)} %fusion.61, f32[256,6]{0,1:T(8,128)} %fusion.60), kind=kOutput, calls=%fused_computation.8 | convolution fusion | flops 455824 | bytes 20608 | tf_op jit(solution)/shard_map/dot_general | solution.py:216
  55.7 3.2 %convolution_bitcast_fusion.tb_ref = f32[6,1024,128]{2,1,0:T(8,128)} fusion(f32[6,256,128]{1,2,0:T(8,128)S(1)} %fusion.21, s32[1024]{0:T(1024)S(1)} %bitcast.268), kind=kOutput, calls=%fused_computation.3 | convolution fusion | flops 2416181248 | bytes 3936256 | tf_op jit(solution)/shard_map/sb,cbk->csk/dot_general | solution.py:209
  58.9 1.2 %all-to-all-done = f32[128,1,4224]{2,1,0:T(1,128)S(1)} async-done(((f32[128,1,4224]{2,1,0:T(1,128)}), f32[128,1,4224]{2,1,0:T(1,128)S(1)}, u32[]{:S(2)}, u32[]{:S(2)}) %all-to-all-start) | async-done | bytes 2162720 | tf_op jit(solution)/shard_map/all_to_all | solution.py:258
  60.1 0.2 slice_reduce_fusion.1
  60.3 0.2 reshape_squeeze.3
  60.5 0.4 slice_reduce_fusion
  60.8 0.2 copy.98
  61.0 0.7 maximum_maximum_fusion.map_ref.aux_ref
  61.8 9.5 %shard_map.115 = f32[32,1024]{1,0:T(8,128)} custom-call(f32[4224,128]{1,0:T(8,128)} %bitcast.259, f32[6,1024,128]{2,1,0:T(8,128)} %convolution_bitcast_fusion.tb_ref, f32[32,1024]{1,0:T(8,128)} %maximum_maximum_fusion.map_ref.aux_ref, f32[32,1024]{1,0:T(8,128)} %maximum_maximum_fusion.map_ref.aux_ref), custom_call_target="tpu_custom_call" | custom-call | tf_op jit(solution)/shard_map/pallas_call | solution.py:147
  71.3 0.9 slice_bitcast_fusion
  72.3 0.2 copy.84
  72.5 1.1 %all_to_all.12 = f32[128,1,144]{2,1,0:T(1,128)} reshape(f32[1024,18]{1,0:T(8,128)S(1)} %copy.84) | data formatting | bytes 147456 | tf_op jit(solution)/shard_map/all_to_all | solution.py:280
  73.6 8.6 %all-to-all-start.1 = ((f32[128,1,144]{2,1,0:T(1,128)}), f32[128,1,144]{2,1,0:T(1,128)S(1)}, u32[]{:S(2)}, u32[]{:S(2)}) async-start(f32[128,1,144]{2,1,0:T(1,128)} %all_to_all.12), calls=%async_computation.1 | async-start | bytes 262144 | tf_op jit(solution)/shard_map/all_to_all | solution.py:280
  82.2 0.6 convolution_add_fusion
  82.8 9.4 %all-to-all-done.1 = f32[128,1,144]{2,1,0:T(1,128)S(1)} async-done(((f32[128,1,144]{2,1,0:T(1,128)}), f32[128,1,144]{2,1,0:T(1,128)S(1)}, u32[]{:S(2)}, u32[]{:S(2)}) %all-to-all-start.1) | async-done | bytes 73760 | tf_op jit(solution)/shard_map/all_to_all | solution.py:280
  92.2 0.3 reduce.2
  92.5 0.2 reshape.1304
  92.7 0.7 convolution_add_fusion.2
  93.5 0.7 copy.86
  94.3 0.7 copy.87
  (68 shorter events, 2.5 us)
Async XLA Ops:
  4.4 5.0 %copy-start.6 = (f32[256]{0:T(256)}, f32[256]{0:T(256)S(1)}, u32[]{:S(2)}) copy-start(f32[256]{0:T(256)S(1)} %mul.416) | copy-start | bytes 3076
  7.4 2.0 %copy-start.5 = (s32[1,1024]{1,0:T(1,128)S(1)}, s32[1,1024]{1,0:T(1,128)}, u32[]{:S(2)}) copy-start(s32[1,1024]{1,0:T(1,128)} %param.16) | copy-start | bytes 12292
  9.4 8.0 %copy-start.1 = (f32[1,256,128]{1,2,0:T(8,128)}, f32[1,256,128]{1,2,0:T(8,128)S(1)}, u32[]{:S(2)}) copy-start(f32[1,256,128]{1,2,0:T(8,128)S(1)} %get-tuple-element.13) | copy-start | bytes 393220
  9.4 7.9 %copy-start.2 = (f32[1,256,128]{1,2,0:T(8,128)}, f32[1,256,128]{1,2,0:T(8,128)S(1)}, u32[]{:S(2)}) copy-start(f32[1,256,128]{1,2,0:T(8,128)S(1)} %get-tuple-element.11) | copy-start | bytes 393220
  17.4 11.5 %copy-start.7 = (s32[2,256]{1,0:T(2,128)S(1)}, s32[2,256]{1,0:T(2,128)}, u32[]{:S(2)}) copy-start(s32[2,256]{1,0:T(2,128)} %param.14) | copy-start | bytes 6148
  17.4 13.4 %copy-start.4 = (s32[1,1024]{1,0:T(1,128)S(1)}, s32[1,1024]{1,0:T(1,128)}, u32[]{:S(2)}) copy-start(s32[1,1024]{1,0:T(1,128)} %param.18) | copy-start | bytes 12292
  17.4 42.7 %all-to-all-start = ((f32[128,1,4224]{2,1,0:T(1,128)}), f32[128,1,4224]{2,1,0:T(1,128)S(1)}, u32[]{:S(2)}, u32[]{:S(2)}) async-start(f32[128,1,4224]{2,1,0:T(1,128)} %bitcast.260), calls=%async_computation | async-start | bytes 4325376 | tf_op jit(solution)/shard_map/all_to_all | solution.py:258
  46.1 0.6 copy-start.3
  55.7 5.3 %copy-start.8 = (f32[32]{0:T(128)S(1)}, f32[32]{0:T(128)}, u32[]{:S(2)}) copy-start(f32[32]{0:T(128)} %pad.32.clone) | copy-start | bytes 388
  60.1 1.7 %copy-start = (f32[128,1,4224]{2,1,0:T(1,128)}, f32[128,1,4224]{2,1,0:T(1,128)S(1)}, u32[]{:S(2)}) copy-start(f32[128,1,4224]{2,1,0:T(1,128)S(1)} %all-to-all-done) | copy-start | bytes 6488068
  73.6 18.6 %all-to-all-start.1 = ((f32[128,1,144]{2,1,0:T(1,128)}), f32[128,1,144]{2,1,0:T(1,128)S(1)}, u32[]{:S(2)}, u32[]{:S(2)}) async-start(f32[128,1,144]{2,1,0:T(1,128)} %all_to_all.12), calls=%async_computation.1 | async-start | bytes 262144 | tf_op jit(solution)/shard_map/all_to_all | solution.py:280

commit v11 on v10

--- a/solution.py
+++ b/solution.py
@@ -164,30 +164,29 @@
 
 
 def _cargo_kernel(xa_ref, map_ref, side_ref, out_ref):
-    peers = side_ref.shape[0]
     height = 4 * CAP + 1
-    for p in range(peers):
-        slots = pl.ds(p * CAP, CAP)
-        for c in range(3):
-            out_ref[pl.ds(p * height + c * CAP, CAP), :] = xa_ref[c, slots, :]
-        out_ref[pl.ds(p * height + 3 * CAP, CAP), :] = map_ref[slots, :].astype(jnp.float32)
-        out_ref[pl.ds(p * height + 4 * CAP, 1), :] = side_ref[pl.ds(p, 1), :]
-
-
-def build_cargo(xa3, maps, side, chunk=128):
+    group = 8
+
+    def body(g, carry):
+        for q in range(group):
+            p = g * group + q
+            base = pl.multiple_of(g * (group * height), 8) + q * height
+            slots = pl.ds(pl.multiple_of(p * CAP, CAP), CAP)
+            for c in range(3):
+                out_ref[pl.ds(base + c * CAP, CAP), :] = xa_ref[c, slots, :]
+            out_ref[pl.ds(base + 3 * CAP, CAP), :] = map_ref[slots, :].astype(jnp.float32)
+            out_ref[pl.ds(base + 4 * CAP, 1), :] = side_ref[pl.ds(p, 1), :]
+        return carry
+
+    lax.fori_loop(0, side_ref.shape[0] // group, body, 0)
+
+
+def build_cargo(xa3, maps, side):
     slots = maps.shape[0]
-    peers = chunk // CAP
     height = 4 * CAP + 1
     cargo = pl.pallas_call(
         _cargo_kernel,
         out_shape=jax.ShapeDtypeStruct((slots // CAP * height, 128), jnp.float32),
-        grid=(slots // chunk,),
-        in_specs=[
-            pl.BlockSpec((3, chunk, 128), lambda i: (0, i, 0)),
-            pl.BlockSpec((chunk, 128), lambda i: (i, 0)),
-            pl.BlockSpec((peers, 128), lambda i: (i, 0)),
-        ],
-        out_specs=pl.BlockSpec((peers * height, 128), lambda i: (i, 0)),
     )(xa3, maps, side)
     return cargo.reshape(slots // CAP, 1, height * 128)
 

time: 96.1 us -> 93.5 us (0.973)
  Pallas kernels: 18.7 us -> 16.2 us
    pallas_call x1, Pallas kernels: 5.67 us -> 3.18 us  [build_cargo(): pl.pallas_call(_cargo_kernel, out_shape=jax.ShapeDtypeStruct((slots // CA...]
  transfers between devices with their start and end apart: 2 -> 2, of which waited for: 2 -> 2; matrix products, arithmetic and copies ran while one was open for 28% -> 29% of each run, Pallas kernels for 4% -> 4%
where the time goes in v11:
time: 93.5 us; the launch traced here: 92.5 us
  local copies, waits for them, and re-layouts  21.5 us (23%)
  starting transfers between devices  20.1 us (21%)
  Pallas kernels  16.2 us (17%)
  matrix products  12.7 us (14%)
  waiting for transfers between devices  10.6 us (11%)
  other arithmetic  10.4 us (11%)
  between operations  1 us (1%)
    pallas_call x2, Pallas kernels, pair_sums(): pl.pallas_call(functools.partial(_terms_kernel, from_cargo), out_shape=ja...  13 us
    all_to_all x1, starting transfers between devices, local(): lax.all_to_all(cargo, axes, split_axis=0, concat_axis=0, tiled=True)  11.5 us
    dot_general x4, matrix products, pick_rows(): jnp.einsum('sb,cbk->csk', onehot, rows, precision=lax.Precision.HIGHEST)  9.72 us
    all_to_all x1, waiting for transfers between devices, local(): lax.all_to_all(remote_a.reshape(peers, CAP * 18), axes, split_axis=0, con...  9.41 us
    all_to_all x1, starting transfers between devices, local(): lax.all_to_all(remote_a.reshape(peers, CAP * 18), axes, split_axis=0, con...  8.59 us
    unnamed x28, local copies, waits for them, and re-layouts  3.85 us
    pallas_call x1, Pallas kernels, build_cargo(): pl.pallas_call(_cargo_kernel, out_shape=jax.ShapeDtypeStruct((slots // CA...  3.18 us
    gather x2, local copies, waits for them, and re-layouts, local(): frag_dirs[target_blocks // BF]  2.99 us
  transfers between devices with their start and end apart: 2, of which 2 were waited for; matrix products, arithmetic and copies ran while one was open for 29% of the time, Pallas kernels for 4%

profile of v11, /device:TPU:1, one launch (start us, length us, event | category | flops | bytes accessed | tf_op | source)
XLA Modules:
  0.0 92.5 jit_solution(9906344827040928127)
XLA Ops:
  0.6 0.8 slice_bitcast_fusion.4
  1.4 0.7 slice_multiply_fusion.4
  2.5 0.1 mul.399
  2.8 0.7 add_select_fusion
  4.7 0.8 copy.75
  5.5 0.7 fusion.48
  6.3 0.1 reshape.1306
  6.4 1.1 %fusion.81 = (f32[256,1,128]{2,0,1:T(8,128)S(1)}, f32[256,1,128]{2,0,1:T(8,128)S(1)}, f32[256,1,128]{2,0,1:T(8,128)S(1)}) fusion(f32[256,3,128]{2,0,1:T(8,128)} %param.10), kind=kLoop, calls=%fused_computation.189 | loop fusion | bytes 786432 | tf_op jit(solution)/shard_map/slice | solution.py:57
  7.5 0.1 copy.92
  7.6 0.1 copy.93
  7.7 0.1 copy.94
  7.8 0.5 fusion.5
  8.3 0.2 copy.79
  8.5 0.2 reshape.1301
  8.7 0.6 concatenate.50.side_ref
  9.5 2.2 %convolution_bitcast_fusion.1.xa_ref = f32[3,1024,128]{2,1,0:T(8,128)} fusion(s32[1024]{0:T(1024)S(1)} %bitcast.271, f32[1,256,128]{1,2,0:T(8,128)S(1)} %get-tuple-element.11, f32[1,256,128]{1,2,0:T(8,128)S(1)} %get-tuple-element.13, f32[1,256,128]{1,2,0:T(8,128)S(1)} %get-tuple-element.15), kind=kOutput, calls=%fused_computation.4 | convolution fusion | flops 1208418304 | bytes 1970176 | tf_op jit(solution)/shard_map/sb,cbk->csk/dot_general | solution.py:208
  11.7 3.2 %shard_map.114 = f32[4224,128]{1,0:T(8,128)} custom-call(f32[3,1024,128]{2,1,0:T(8,128)} %convolution_bitcast_fusion.1.xa_ref, s32[1024,128]{1,0:T(8,128)} %bitcast.262, f32[128,128]{1,0:T(8,128)} %concatenate.50.side_ref), custom_call_target="tpu_custom_call" | custom-call | tf_op jit(solution)/shard_map/pallas_call | solution.py:187
  14.9 11.5 %all-to-all-start = ((f32[128,1,4224]{2,1,0:T(1,128)}), f32[128,1,4224]{2,1,0:T(1,128)S(1)}, u32[]{:S(2)}, u32[]{:S(2)}) async-start(f32[128,1,4224]{2,1,0:T(1,128)} %bitcast.260), calls=%async_computation | async-start | bytes 4325376 | tf_op jit(solution)/shard_map/all_to_all | solution.py:257
  26.4 0.6 fusion.84
  27.0 0.6 pad.31.clone
  27.6 0.7 pad.32.clone
  28.3 0.7 gather_fusion.1
  29.1 0.7 gather_fusion
  30.0 1.7 %fusion.80 = (f32[256,1,128]{2,0,1:T(8,128)S(1)}, f32[256,1,128]{2,0,1:T(8,128)S(1)}, f32[256,1,128]{2,0,1:T(8,128)}) fusion(f32[256,3,128]{2,0,1:T(8,128)} %param.11), kind=kLoop, calls=%fused_computation.188 | loop fusion | bytes 786432 | tf_op jit(solution)/shard_map/slice | solution.py:63
  31.7 0.1 copy.95
  31.8 0.1 copy.96
  31.9 1.0 %copy.97 = f32[256,1,128]{0,2,1:T(8,128)S(1)} copy(f32[256,1,128]{2,0,1:T(8,128)} %get-tuple-element.20) | data formatting | bytes 262144
  32.9 0.7 fusion.19
  33.7 2.2 %convolution_bitcast_fusion.3.xa_ref = f32[3,256,128]{2,1,0:T(8,128)} fusion(f32[1,256,128]{1,2,0:T(8,128)} %copy-done.2, f32[1,256,128]{1,2,0:T(8,128)} %copy-done.1, f32[1,256,128]{1,2,0:T(8,128)S(1)} %get-tuple-element.15, s32[256]{0:T(256)} %bitcast.273), kind=kOutput, calls=%fused_computation.6 | convolution fusion | flops 302252032 | bytes 787456 | tf_op jit(solution)/shard_map/sb,cbk->csk/dot_general | solution.py:208
  35.8 2.1 %convolution_bitcast_fusion.2.tb_ref = f32[6,256,128]{2,1,0:T(8,128)} fusion(f32[6,256,128]{1,2,0:T(8,128)S(1)} %fusion.21, s32[256]{0:T(256)} %bitcast.275), kind=kOutput, calls=%fused_computation.5 | convolution fusion | flops 604045312 | bytes 1573888 | tf_op jit(solution)/shard_map/sb,cbk->csk/dot_general | solution.py:208
  38.0 1.4 %maximum_maximum_fusion.1.aux_ref = f32[32,256]{1,0:T(8,128)} fusion(f32[12,256]{1,0:T(8,128)S(1)} %bitcast.265, f32[12,256]{1,0:T(8,128)S(1)} %bitcast.266, f32[32]{0:T(128)} %pad.32.clone, f32[32]{0:T(128)} %pad.31.clone), kind=kLoop, calls=%fused_computation.89 | loop fusion | flops 24576 | bytes 57600 | tf_op jit(solution)/shard_map/concatenate | solution.py:220
  39.3 3.5 %shard_map.113 = f32[32,256]{1,0:T(8,128)} custom-call(f32[3,256,128]{2,1,0:T(8,128)} %convolution_bitcast_fusion.3.xa_ref, f32[6,256,128]{2,1,0:T(8,128)} %convolution_bitcast_fusion.2.tb_ref, s32[256,128]{1,0:T(8,128)} %map_ref.1, f32[32,256]{1,0:T(8,128)} %maximum_maximum_fusion.1.aux_ref), custom_call_target="tpu_custom_call" | custom-call | tf_op jit(solution)/shard_map/pallas_call | solution.py:147
  42.8 0.8 slice_bitcast_fusion.1
  43.6 0.6 fusion.83
  44.2 0.6 fusion.60
  44.8 2.8 %gather_fusion.2 = f32[1024,12]{1,0:T(8,128)S(1)} fusion(f32[8,12]{1,0:T(8,128)S(1)} %bitcast.258, s32[1024]{0:T(1024)S(1)} %broadcast_clamp_fusion), kind=kCustom, calls=%fused_computation.2 | custom fusion | bytes 102400 | tf_op jit(solution)/shard_map/gather | solution.py:276
  47.6 0.2 copy.83
  47.8 0.7 fusion.62
  48.5 0.7 fusion.61
  49.2 0.7 and_select_fusion.4
  49.9 0.7 and_select_fusion.3
  50.5 0.7 slice_multiply_fusion.3
  51.2 0.7 slice_multiply_fusion.2
  52.0 0.3 fusion.44
  52.3 1.0 %convolution_add_fusion.1 = f32[8,18]{1,0:T(8,128)S(1)} fusion(f32[8,18]{1,0:T(8,128)S(1)} %fusion.44, s32[256]{0:T(256)S(1)} %and_select_fusion.3, f32[256,6]{0,1:T(8,128)S(1)} %fusion.62, f32[256,6]{0,1:T(8,128)S(1)} %fusion.61, f32[256,6]{0,1:T(8,128)} %fusion.60), kind=kOutput, calls=%fused_computation.8 | convolution fusion | flops 455824 | bytes 20608 | tf_op jit(solution)/shard_map/dot_general | solution.py:215
  53.2 3.2 %convolution_bitcast_fusion.tb_ref = f32[6,1024,128]{2,1,0:T(8,128)} fusion(f32[6,256,128]{1,2,0:T(8,128)S(1)} %fusion.21, s32[1024]{0:T(1024)S(1)} %bitcast.268), kind=kOutput, calls=%fused_computation.3 | convolution fusion | flops 2416181248 | bytes 3936256 | tf_op jit(solution)/shard_map/sb,cbk->csk/dot_general | solution.py:208
  56.4 1.2 %all-to-all-done = f32[128,1,4224]{2,1,0:T(1,128)S(1)} async-done(((f32[128,1,4224]{2,1,0:T(1,128)}), f32[128,1,4224]{2,1,0:T(1,128)S(1)}, u32[]{:S(2)}, u32[]{:S(2)}) %all-to-all-start) | async-done | bytes 2162720 | tf_op jit(solution)/shard_map/all_to_all | solution.py:257
  57.6 0.2 slice_reduce_fusion.1
  57.8 0.2 reshape_squeeze.3
  58.0 0.4 slice_reduce_fusion
  58.3 0.2 copy.98
  58.5 0.7 maximum_maximum_fusion.map_ref.aux_ref
  59.3 9.5 %shard_map.115 = f32[32,1024]{1,0:T(8,128)} custom-call(f32[4224,128]{1,0:T(8,128)} %bitcast.259, f32[6,1024,128]{2,1,0:T(8,128)} %convolution_bitcast_fusion.tb_ref, f32[32,1024]{1,0:T(8,128)} %maximum_maximum_fusion.map_ref.aux_ref, f32[32,1024]{1,0:T(8,128)} %maximum_maximum_fusion.map_ref.aux_ref), custom_call_target="tpu_custom_call" | custom-call | tf_op jit(solution)/shard_map/pallas_call | solution.py:147
  68.8 0.9 slice_bitcast_fusion
  69.8 0.2 copy.84
  70.0 1.1 %all_to_all.12 = f32[128,1,144]{2,1,0:T(1,128)} reshape(f32[1024,18]{1,0:T(8,128)S(1)} %copy.84) | data formatting | bytes 147456 | tf_op jit(solution)/shard_map/all_to_all | solution.py:279
  71.1 8.6 %all-to-all-start.1 = ((f32[128,1,144]{2,1,0:T(1,128)}), f32[128,1,144]{2,1,0:T(1,128)S(1)}, u32[]{:S(2)}, u32[]{:S(2)}) async-start(f32[128,1,144]{2,1,0:T(1,128)} %all_to_all.12), calls=%async_computation.1 | async-start | bytes 262144 | tf_op jit(solution)/shard_map/all_to_all | solution.py:279
  79.7 0.6 convolution_add_fusion
  80.3 9.4 %all-to-all-done.1 = f32[128,1,144]{2,1,0:T(1,128)S(1)} async-done(((f32[128,1,144]{2,1,0:T(1,128)}), f32[128,1,144]{2,1,0:T(1,128)S(1)}, u32[]{:S(2)}, u32[]{:S(2)}) %all-to-all-start.1) | async-done | bytes 73760 | tf_op jit(solution)/shard_map/all_to_all | solution.py:279
  89.7 0.3 reduce.2
  90.0 0.2 reshape.1304
  90.2 0.7 convolution_add_fusion.2
  91.0 0.7 copy.86
  91.8 0.7 copy.87
  (68 shorter events, 2.5 us)
Async XLA Ops:
  4.4 5.0 %copy-start.6 = (f32[256]{0:T(256)}, f32[256]{0:T(256)S(1)}, u32[]{:S(2)}) copy-start(f32[256]{0:T(256)S(1)} %mul.416) | copy-start | bytes 3076
  7.4 2.0 %copy-start.5 = (s32[1,1024]{1,0:T(1,128)S(1)}, s32[1,1024]{1,0:T(1,128)}, u32[]{:S(2)}) copy-start(s32[1,1024]{1,0:T(1,128)} %param.16) | copy-start | bytes 12292
  9.4 5.5 %copy-start.1 = (f32[1,256,128]{1,2,0:T(8,128)}, f32[1,256,128]{1,2,0:T(8,128)S(1)}, u32[]{:S(2)}) copy-start(f32[1,256,128]{1,2,0:T(8,128)S(1)} %get-tuple-element.13) | copy-start | bytes 393220
  9.4 5.4 %copy-start.2 = (f32[1,256,128]{1,2,0:T(8,128)}, f32[1,256,128]{1,2,0:T(8,128)S(1)}, u32[]{:S(2)}) copy-start(f32[1,256,128]{1,2,0:T(8,128)S(1)} %get-tuple-element.11) | copy-start | bytes 393220
  14.9 11.5 %copy-start.7 = (s32[2,256]{1,0:T(2,128)S(1)}, s32[2,256]{1,0:T(2,128)}, u32[]{:S(2)}) copy-start(s32[2,256]{1,0:T(2,128)} %param.14) | copy-start | bytes 6148
  14.9 13.4 %copy-start.4 = (s32[1,1024]{1,0:T(1,128)S(1)}, s32[1,1024]{1,0:T(1,128)}, u32[]{:S(2)}) copy-start(s32[1,1024]{1,0:T(1,128)} %param.18) | copy-start | bytes 12292
  14.9 42.7 %all-to-all-start = ((f32[128,1,4224]{2,1,0:T(1,128)}), f32[128,1,4224]{2,1,0:T(1,128)S(1)}, u32[]{:S(2)}, u32[]{:S(2)}) async-start(f32[128,1,4224]{2,1,0:T(1,128)} %bitcast.260), calls=%async_computation | async-start | bytes 4325376 | tf_op jit(solution)/shard_map/all_to_all | solution.py:257
  43.6 0.6 copy-start.3
  53.2 5.3 %copy-start.8 = (f32[32]{0:T(128)S(1)}, f32[32]{0:T(128)}, u32[]{:S(2)}) copy-start(f32[32]{0:T(128)} %pad.32.clone) | copy-start | bytes 388
  57.6 1.7 %copy-start = (f32[128,1,4224]{2,1,0:T(1,128)}, f32[128,1,4224]{2,1,0:T(1,128)S(1)}, u32[]{:S(2)}) copy-start(f32[128,1,4224]{2,1,0:T(1,128)S(1)} %all-to-all-done) | copy-start | bytes 6488068
  71.1 18.6 %all-to-all-start.1 = ((f32[128,1,144]{2,1,0:T(1,128)}), f32[128,1,144]{2,1,0:T(1,128)S(1)}, u32[]{:S(2)}, u32[]{:S(2)}) async-start(f32[128,1,144]{2,1,0:T(1,128)} %all_to_all.12), calls=%async_computation.1 | async-start | bytes 262144 | tf_op jit(solution)/shard_map/all_to_all | solution.py:279

commit v12 on v11

--- a/solution.py
+++ b/solution.py
@@ -126,7 +126,7 @@
         return tuple(a + v for a, v in zip(accs, vals))
 
     zero = jnp.zeros((8, chunk), jnp.float32)
-    accs = lax.fori_loop(0, 128 // 8, body, (zero,) * N_QTY, unroll=2)
+    accs = lax.fori_loop(0, 128 // 8, body, (zero,) * N_QTY, unroll=8)
     valid = aux_ref[24:25, :]
     for q in range(N_QTY):
         out_ref[q : q + 1, :] = jnp.sum(accs[q], axis=0, keepdims=True) * valid

time: 93.5 us -> 93.1 us (level)
  no operation moved by 1% of the time
where the time goes in v12:
time: 93.1 us; the launch traced here: 92 us
  local copies, waits for them, and re-layouts  21.5 us (23%)
  starting transfers between devices  20 us (21%)
  Pallas kernels  15.7 us (17%)
  matrix products  12.7 us (14%)
  waiting for transfers between devices  10.7 us (11%)
  other arithmetic  10.4 us (11%)
  between operations  1 us (1%)
    pallas_call x2, Pallas kernels, pair_sums(): pl.pallas_call(functools.partial(_terms_kernel, from_cargo), out_shape=ja...  12.6 us
    all_to_all x1, starting transfers between devices, local(): lax.all_to_all(cargo, axes, split_axis=0, concat_axis=0, tiled=True)  11.5 us
    dot_general x4, matrix products, pick_rows(): jnp.einsum('sb,cbk->csk', onehot, rows, precision=lax.Precision.HIGHEST)  9.72 us
    all_to_all x1, waiting for transfers between devices, local(): lax.all_to_all(remote_a.reshape(peers, CAP * 18), axes, split_axis=0, con...  9.41 us
    all_to_all x1, starting transfers between devices, local(): lax.all_to_all(remote_a.reshape(peers, CAP * 18), axes, split_axis=0, con...  8.46 us
    unnamed x28, local copies, waits for them, and re-layouts  3.85 us
    pallas_call x1, Pallas kernels, build_cargo(): pl.pallas_call(_cargo_kernel, out_shape=jax.ShapeDtypeStruct((slots // CA...  3.18 us
    gather x2, local copies, waits for them, and re-layouts, local(): frag_dirs[target_blocks // BF]  2.99 us
  transfers between devices with their start and end apart: 2, of which 2 were waited for; matrix products, arithmetic and copies ran while one was open for 29% of the time, Pallas kernels for 4%

profile of v12, /device:TPU:1, one launch (start us, length us, event | category | flops | bytes accessed | tf_op | source)
XLA Modules:
  0.0 92.0 jit_solution(669581493695040455)
XLA Ops:
  0.6 0.8 slice_bitcast_fusion.4
  1.4 0.7 slice_multiply_fusion.4
  2.5 0.1 mul.399
  2.8 0.7 add_select_fusion
  4.7 0.8 copy.75
  5.5 0.7 fusion.48
  6.3 0.1 reshape.1306
  6.4 1.1 %fusion.81 = (f32[256,1,128]{2,0,1:T(8,128)S(1)}, f32[256,1,128]{2,0,1:T(8,128)S(1)}, f32[256,1,128]{2,0,1:T(8,128)S(1)}) fusion(f32[256,3,128]{2,0,1:T(8,128)} %param.10), kind=kLoop, calls=%fused_computation.189 | loop fusion | bytes 786432 | tf_op jit(solution)/shard_map/slice | solution.py:57
  7.5 0.1 copy.92
  7.6 0.1 copy.93
  7.7 0.1 copy.94
  7.8 0.5 fusion.5
  8.3 0.2 copy.79
  8.5 0.2 reshape.1301
  8.7 0.6 concatenate.50.side_ref
  9.5 2.2 %convolution_bitcast_fusion.1.xa_ref = f32[3,1024,128]{2,1,0:T(8,128)} fusion(s32[1024]{0:T(1024)S(1)} %bitcast.271, f32[1,256,128]{1,2,0:T(8,128)S(1)} %get-tuple-element.11, f32[1,256,128]{1,2,0:T(8,128)S(1)} %get-tuple-element.13, f32[1,256,128]{1,2,0:T(8,128)S(1)} %get-tuple-element.15), kind=kOutput, calls=%fused_computation.4 | convolution fusion | flops 1208418304 | bytes 1970176 | tf_op jit(solution)/shard_map/sb,cbk->csk/dot_general | solution.py:208
  11.7 3.2 %shard_map.114 = f32[4224,128]{1,0:T(8,128)} custom-call(f32[3,1024,128]{2,1,0:T(8,128)} %convolution_bitcast_fusion.1.xa_ref, s32[1024,128]{1,0:T(8,128)} %bitcast.262, f32[128,128]{1,0:T(8,128)} %concatenate.50.side_ref), custom_call_target="tpu_custom_call" | custom-call | tf_op jit(solution)/shard_map/pallas_call | solution.py:187
  14.9 11.5 %all-to-all-start = ((f32[128,1,4224]{2,1,0:T(1,128)}), f32[128,1,4224]{2,1,0:T(1,128)S(1)}, u32[]{:S(2)}, u32[]{:S(2)}) async-start(f32[128,1,4224]{2,1,0:T(1,128)} %bitcast.260), calls=%async_computation | async-start | bytes 4325376 | tf_op jit(solution)/shard_map/all_to_all | solution.py:257
  26.4 0.6 fusion.84
  27.0 0.6 pad.31.clone
  27.6 0.7 pad.32.clone
  28.3 0.7 gather_fusion.1
  29.1 0.7 gather_fusion
  30.0 1.7 %fusion.80 = (f32[256,1,128]{2,0,1:T(8,128)S(1)}, f32[256,1,128]{2,0,1:T(8,128)S(1)}, f32[256,1,128]{2,0,1:T(8,128)}) fusion(f32[256,3,128]{2,0,1:T(8,128)} %param.11), kind=kLoop, calls=%fused_computation.188 | loop fusion | bytes 786432 | tf_op jit(solution)/shard_map/slice | solution.py:63
  31.7 0.1 copy.95
  31.8 0.1 copy.96
  31.9 1.0 %copy.97 = f32[256,1,128]{0,2,1:T(8,128)S(1)} copy(f32[256,1,128]{2,0,1:T(8,128)} %get-tuple-element.20) | data formatting | bytes 262144
  32.9 0.7 fusion.19
  33.7 2.2 %convolution_bitcast_fusion.3.xa_ref = f32[3,256,128]{2,1,0:T(8,128)} fusion(f32[1,256,128]{1,2,0:T(8,128)} %copy-done.2, f32[1,256,128]{1,2,0:T(8,128)} %copy-done.1, f32[1,256,128]{1,2,0:T(8,128)S(1)} %get-tuple-element.15, s32[256]{0:T(256)} %bitcast.273), kind=kOutput, calls=%fused_computation.6 | convolution fusion | flops 302252032 | bytes 787456 | tf_op jit(solution)/shard_map/sb,cbk->csk/dot_general | solution.py:208
  35.8 2.1 %convolution_bitcast_fusion.2.tb_ref = f32[6,256,128]{2,1,0:T(8,128)} fusion(f32[6,256,128]{1,2,0:T(8,128)S(1)} %fusion.21, s32[256]{0:T(256)} %bitcast.275), kind=kOutput, calls=%fused_computation.5 | convolution fusion | flops 604045312 | bytes 1573888 | tf_op jit(solution)/shard_map/sb,cbk->csk/dot_general | solution.py:208
  38.0 1.4 %maximum_maximum_fusion.1.aux_ref = f32[32,256]{1,0:T(8,128)} fusion(f32[12,256]{1,0:T(8,128)S(1)} %bitcast.265, f32[12,256]{1,0:T(8,128)S(1)} %bitcast.266, f32[32]{0:T(128)} %pad.32.clone, f32[32]{0:T(128)} %pad.31.clone), kind=kLoop, calls=%fused_computation.89 | loop fusion | flops 24576 | bytes 57600 | tf_op jit(solution)/shard_map/concatenate | solution.py:220
  39.3 3.3 %shard_map.113 = f32[32,256]{1,0:T(8,128)} custom-call(f32[3,256,128]{2,1,0:T(8,128)} %convolution_bitcast_fusion.3.xa_ref, f32[6,256,128]{2,1,0:T(8,128)} %convolution_bitcast_fusion.2.tb_ref, s32[256,128]{1,0:T(8,128)} %map_ref.1, f32[32,256]{1,0:T(8,128)} %maximum_maximum_fusion.1.aux_ref), custom_call_target="tpu_custom_call" | custom-call | tf_op jit(solution)/shard_map/pallas_call | solution.py:147
  42.7 0.8 slice_bitcast_fusion.1
  43.4 0.6 fusion.83
  44.1 0.6 fusion.60
  44.7 2.8 %gather_fusion.2 = f32[1024,12]{1,0:T(8,128)S(1)} fusion(f32[8,12]{1,0:T(8,128)S(1)} %bitcast.258, s32[1024]{0:T(1024)S(1)} %broadcast_clamp_fusion), kind=kCustom, calls=%fused_computation.2 | custom fusion | bytes 102400 | tf_op jit(solution)/shard_map/gather | solution.py:276
  47.5 0.2 copy.83
  47.6 0.7 fusion.62
  48.4 0.7 fusion.61
  49.1 0.7 and_select_fusion.4
  49.7 0.7 and_select_fusion.3
  50.4 0.7 slice_multiply_fusion.3
  51.1 0.7 slice_multiply_fusion.2
  51.9 0.3 fusion.44
  52.1 1.0 %convolution_add_fusion.1 = f32[8,18]{1,0:T(8,128)S(1)} fusion(f32[8,18]{1,0:T(8,128)S(1)} %fusion.44, s32[256]{0:T(256)S(1)} %and_select_fusion.3, f32[256,6]{0,1:T(8,128)S(1)} %fusion.62, f32[256,6]{0,1:T(8,128)S(1)} %fusion.61, f32[256,6]{0,1:T(8,128)} %fusion.60), kind=kOutput, calls=%fused_computation.8 | convolution fusion | flops 455824 | bytes 20608 | tf_op jit(solution)/shard_map/dot_general | solution.py:215
  53.1 3.2 %convolution_bitcast_fusion.tb_ref = f32[6,1024,128]{2,1,0:T(8,128)} fusion(f32[6,256,128]{1,2,0:T(8,128)S(1)} %fusion.21, s32[1024]{0:T(1024)S(1)} %bitcast.268), kind=kOutput, calls=%fused_computation.3 | convolution fusion | flops 2416181248 | bytes 3936256 | tf_op jit(solution)/shard_map/sb,cbk->csk/dot_general | solution.py:208
  56.3 1.3 %all-to-all-done = f32[128,1,4224]{2,1,0:T(1,128)S(1)} async-done(((f32[128,1,4224]{2,1,0:T(1,128)}), f32[128,1,4224]{2,1,0:T(1,128)S(1)}, u32[]{:S(2)}, u32[]{:S(2)}) %all-to-all-start) | async-done | bytes 2162720 | tf_op jit(solution)/shard_map/all_to_all | solution.py:257
  57.6 0.2 slice_reduce_fusion.1
  57.8 0.2 reshape_squeeze.3
  58.0 0.4 slice_reduce_fusion
  58.3 0.2 copy.98
  58.5 0.7 maximum_maximum_fusion.map_ref.aux_ref
  59.3 9.2 %shard_map.115 = f32[32,1024]{1,0:T(8,128)} custom-call(f32[4224,128]{1,0:T(8,128)} %bitcast.259, f32[6,1024,128]{2,1,0:T(8,128)} %convolution_bitcast_fusion.tb_ref, f32[32,1024]{1,0:T(8,128)} %maximum_maximum_fusion.map_ref.aux_ref, f32[32,1024]{1,0:T(8,128)} %maximum_maximum_fusion.map_ref.aux_ref), custom_call_target="tpu_custom_call" | custom-call | tf_op jit(solution)/shard_map/pallas_call | solution.py:147
  68.5 0.9 slice_bitcast_fusion
  69.5 0.2 copy.84
  69.7 1.1 %all_to_all.12 = f32[128,1,144]{2,1,0:T(1,128)} reshape(f32[1024,18]{1,0:T(8,128)S(1)} %copy.84) | data formatting | bytes 147456 | tf_op jit(solution)/shard_map/all_to_all | solution.py:279
  70.8 8.5 %all-to-all-start.1 = ((f32[128,1,144]{2,1,0:T(1,128)}), f32[128,1,144]{2,1,0:T(1,128)S(1)}, u32[]{:S(2)}, u32[]{:S(2)}) async-start(f32[128,1,144]{2,1,0:T(1,128)} %all_to_all.12), calls=%async_computation.1 | async-start | bytes 262144 | tf_op jit(solution)/shard_map/all_to_all | solution.py:279
  79.3 0.6 convolution_add_fusion
  79.9 9.4 %all-to-all-done.1 = f32[128,1,144]{2,1,0:T(1,128)S(1)} async-done(((f32[128,1,144]{2,1,0:T(1,128)}), f32[128,1,144]{2,1,0:T(1,128)S(1)}, u32[]{:S(2)}, u32[]{:S(2)}) %all-to-all-start.1) | async-done | bytes 73760 | tf_op jit(solution)/shard_map/all_to_all | solution.py:279
  89.3 0.3 reduce.2
  89.6 0.2 reshape.1304
  89.8 0.7 convolution_add_fusion.2
  90.6 0.7 copy.86
  91.4 0.7 copy.87
  (68 shorter events, 2.5 us)
Async XLA Ops:
  4.4 5.0 %copy-start.6 = (f32[256]{0:T(256)}, f32[256]{0:T(256)S(1)}, u32[]{:S(2)}) copy-start(f32[256]{0:T(256)S(1)} %mul.416) | copy-start | bytes 3076
  7.4 2.0 %copy-start.5 = (s32[1,1024]{1,0:T(1,128)S(1)}, s32[1,1024]{1,0:T(1,128)}, u32[]{:S(2)}) copy-start(s32[1,1024]{1,0:T(1,128)} %param.16) | copy-start | bytes 12292
  9.4 5.5 %copy-start.1 = (f32[1,256,128]{1,2,0:T(8,128)}, f32[1,256,128]{1,2,0:T(8,128)S(1)}, u32[]{:S(2)}) copy-start(f32[1,256,128]{1,2,0:T(8,128)S(1)} %get-tuple-element.13) | copy-start | bytes 393220
  9.4 5.4 %copy-start.2 = (f32[1,256,128]{1,2,0:T(8,128)}, f32[1,256,128]{1,2,0:T(8,128)S(1)}, u32[]{:S(2)}) copy-start(f32[1,256,128]{1,2,0:T(8,128)S(1)} %get-tuple-element.11) | copy-start | bytes 393220
  14.9 11.5 %copy-start.7 = (s32[2,256]{1,0:T(2,128)S(1)}, s32[2,256]{1,0:T(2,128)}, u32[]{:S(2)}) copy-start(s32[2,256]{1,0:T(2,128)} %param.14) | copy-start | bytes 6148
  14.9 13.4 %copy-start.4 = (s32[1,1024]{1,0:T(1,128)S(1)}, s32[1,1024]{1,0:T(1,128)}, u32[]{:S(2)}) copy-start(s32[1,1024]{1,0:T(1,128)} %param.18) | copy-start | bytes 12292
  14.9 42.7 %all-to-all-start = ((f32[128,1,4224]{2,1,0:T(1,128)}), f32[128,1,4224]{2,1,0:T(1,128)S(1)}, u32[]{:S(2)}, u32[]{:S(2)}) async-start(f32[128,1,4224]{2,1,0:T(1,128)} %bitcast.260), calls=%async_computation | async-start | bytes 4325376 | tf_op jit(solution)/shard_map/all_to_all | solution.py:257
  43.4 0.6 copy-start.3
  53.1 5.4 %copy-start.8 = (f32[32]{0:T(128)S(1)}, f32[32]{0:T(128)}, u32[]{:S(2)}) copy-start(f32[32]{0:T(128)} %pad.32.clone) | copy-start | bytes 388
  57.6 1.7 %copy-start = (f32[128,1,4224]{2,1,0:T(1,128)}, f32[128,1,4224]{2,1,0:T(1,128)S(1)}, u32[]{:S(2)}) copy-start(f32[128,1,4224]{2,1,0:T(1,128)S(1)} %all-to-all-done) | copy-start | bytes 6488068
  70.8 18.5 %all-to-all-start.1 = ((f32[128,1,144]{2,1,0:T(1,128)}), f32[128,1,144]{2,1,0:T(1,128)S(1)}, u32[]{:S(2)}, u32[]{:S(2)}) async-start(f32[128,1,144]{2,1,0:T(1,128)} %all_to_all.12), calls=%async_computation.1 | async-start | bytes 262144 | tf_op jit(solution)/shard_map/all_to_all | solution.py:279

commit v13 on v12

--- a/solution.py
+++ b/solution.py
@@ -10,6 +10,7 @@
 BF = 32
 CAP = 8
 N_QTY = 27
+MESH = pl.DeviceIdType.MESH
 
 
 def rotations(poses):
@@ -201,6 +202,80 @@
     return jnp.concatenate([ga, ha], axis=1), jnp.concatenate([gb, hb0, hb1], axis=1)
 
 
+def _exchange_kernel(n_band, x_ref, out_ref, send_sems, recv_sems, own_sem):
+    peers = x_ref.shape[0]
+    me = lax.axis_index("tile") * n_band + lax.axis_index("band")
+
+    def peer_of(k):
+        p = lax.rem(me + k, peers)
+        return p, (p // n_band, p % n_band)
+
+    barrier = pltpu.get_barrier_semaphore()
+
+    def greet(k, carry):
+        _, dev = peer_of(k)
+        pl.semaphore_signal(barrier, inc=1, device_id=dev, device_id_type=MESH)
+        return carry
+
+    lax.fori_loop(1, peers, greet, 0)
+    pl.semaphore_wait(barrier, peers - 1)
+
+    own = pltpu.make_async_copy(x_ref.at[me], out_ref.at[me], own_sem)
+    own.start()
+
+    def outgoing(k):
+        p, dev = peer_of(k)
+        return pltpu.make_async_remote_copy(
+            src_ref=x_ref.at[p],
+            dst_ref=out_ref.at[me],
+            send_sem=send_sems.at[p],
+            recv_sem=recv_sems.at[me],
+            device_id=dev,
+            device_id_type=MESH,
+        )
+
+    def incoming(k):
+        p, dev = peer_of(k)
+        return pltpu.make_async_remote_copy(
+            src_ref=x_ref.at[p],
+            dst_ref=out_ref.at[p],
+            send_sem=send_sems.at[p],
+            recv_sem=recv_sems.at[p],
+            device_id=dev,
+            device_id_type=MESH,
+        )
+
+    def start(k, carry):
+        outgoing(k).start()
+        return carry
+
+    lax.fori_loop(1, peers, start, 0)
+
+    def finish(k, carry):
+        outgoing(k).wait_send()
+        incoming(k).wait_recv()
+        return carry
+
+    lax.fori_loop(1, peers, finish, 0)
+    own.wait()
+
+
+def exchange(x, n_band, collective_id):
+    peers = x.shape[0]
+    return pl.pallas_call(
+        functools.partial(_exchange_kernel, n_band),
+        out_shape=jax.ShapeDtypeStruct(x.shape, x.dtype),
+        in_specs=[pl.BlockSpec(memory_space=pl.ANY)],
+        out_specs=pl.BlockSpec(memory_space=pl.ANY),
+        scratch_shapes=[
+            pltpu.SemaphoreType.DMA((peers,)),
+            pltpu.SemaphoreType.DMA((peers,)),
+            pltpu.SemaphoreType.DMA(()),
+        ],
+        compiler_params=pltpu.CompilerParams(collective_id=collective_id, has_side_effects=True),
+    )(x)
+
+
 def pick_rows(blocks, rows):
     onehot = (blocks[:, None] == jnp.arange(rows.shape[1], dtype=jnp.int32)[None, :]).astype(
         jnp.float32
@@ -235,6 +310,7 @@
     counts,
 ):
     axes = ("tile", "band")
+    n_band = lax.axis_size("band")
     frag_count = poses.shape[1]
     rows6 = to_world_rows(points, normals, poses, BF)
     frag_dirs = directions.reshape(12, frag_count).T
@@ -276,9 +352,7 @@
         make_aux(side_in[:, 0:12], frag_dirs[target_blocks // BF], side_in[:, 12]),
     )
     remote_a, remote_b = split_terms(out_r)
-    returned = lax.all_to_all(
-        remote_a.reshape(peers, CAP * 18), axes, split_axis=0, concat_axis=0, tiled=True
-    ).reshape(peers * CAP, 18)
+    returned = exchange(remote_a.reshape(peers, 1, CAP * 18), n_band, 0).reshape(peers * CAP, 18)
 
     totals = frag_sums(src_l, local_a, frag_count) + frag_sums(tgt_l, local_b, frag_count)
     totals = (

time: 93.1 us -> 92.8 us (level)
  Pallas kernels: 15.7 us -> 32.4 us
  waiting for transfers between devices: 10.7 us -> 1.42 us
  starting transfers between devices: 20 us -> 11.5 us
    pallas_call x0 -> x1, Pallas kernels: none -> 16.6 us  [exchange(): pl.pallas_call(functools.partial(_exchange_kernel, n_band), out_shape=jax...]
    all_to_all x1 -> x0, waiting for transfers between devices: 9.41 us -> none  [local(): lax.all_to_all(remote_a.reshape(peers, CAP * 18), axes, split_axis=0, con...]
    all_to_all x1 -> x0, starting transfers between devices: 8.46 us -> none  [local(): lax.all_to_all(remote_a.reshape(peers, CAP * 18), axes, split_axis=0, con...]
    pallas_call x0 -> x1, other arithmetic: none -> 1.22 us  [exchange(): pl.pallas_call(functools.partial(_exchange_kernel, n_band), out_shape=jax...]
    all_to_all x1 -> x0, local copies, waits for them, and re-layouts: 1.07 us -> none  [local(): lax.all_to_all(remote_a.reshape(peers, CAP * 18), axes, split_axis=0, con...]
    reshape x1 -> x2, local copies, waits for them, and re-layouts: 0.2 us -> 1.26 us  [the longest x1 1.07 us: local(): remote_a.reshape(peers, 1, CAP * 18)]
  transfers between devices with their start and end apart: 2 -> 1, of which waited for: 2 -> 1; matrix products, arithmetic and copies ran while one was open for 29% -> 29% of each run, Pallas kernels for 4% -> 4%
where the time goes in v13:
time: 92.8 us; the launch traced here: 91.7 us
  Pallas kernels  32.4 us (35%)
  local copies, waits for them, and re-layouts  21.5 us (23%)
  matrix products  12.7 us (14%)
  starting transfers between devices  11.5 us (12%)
  other arithmetic  11.2 us (12%)
  waiting for transfers between devices  1.42 us (2%)
  between operations  1 us (1%)
    pallas_call x1, Pallas kernels, exchange(): pl.pallas_call(functools.partial(_exchange_kernel, n_band), out_shape=jax...  16.6 us
    pallas_call x2, Pallas kernels, pair_sums(): pl.pallas_call(functools.partial(_terms_kernel, from_cargo), out_shape=ja...  12.6 us
    all_to_all x1, starting transfers between devices, local(): lax.all_to_all(cargo, axes, split_axis=0, concat_axis=0, tiled=True)  11.5 us
    dot_general x4, matrix products, pick_rows(): jnp.einsum('sb,cbk->csk', onehot, rows, precision=lax.Precision.HIGHEST)  9.67 us
    unnamed x28, local copies, waits for them, and re-layouts  3.85 us
    pallas_call x1, Pallas kernels, build_cargo(): pl.pallas_call(_cargo_kernel, out_shape=jax.ShapeDtypeStruct((slots // CA...  3.18 us
    gather x2, local copies, waits for them, and re-layouts, local(): frag_dirs[target_blocks // BF]  2.99 us
    dot_general x4, matrix products, frag_sums(): return jnp.dot(onehot.T, terms, precision=lax.Precision.HIGHEST)  2.53 us
  transfers between devices with their start and end apart: 1, of which 1 were waited for; matrix products, arithmetic and copies ran while one was open for 29% of the time, Pallas kernels for 4%

profile of v13, /device:TPU:1, one launch (start us, length us, event | category | flops | bytes accessed | tf_op | source)
XLA Modules:
  0.0 91.7 jit_solution(10237802786890639747)
XLA Ops:
  0.6 0.8 slice_bitcast_fusion.4
  1.4 0.7 slice_multiply_fusion.4
  2.5 0.1 mul.399
  2.8 0.7 add_select_fusion
  3.5 0.1 mul.435
  4.7 0.8 copy.78
  5.5 0.7 fusion.48
  6.3 0.1 reshape.1305
  6.4 1.1 %fusion.81 = (f32[256,1,128]{2,0,1:T(8,128)S(1)}, f32[256,1,128]{2,0,1:T(8,128)S(1)}, f32[256,1,128]{2,0,1:T(8,128)S(1)}) fusion(f32[256,3,128]{2,0,1:T(8,128)} %param.10), kind=kLoop, calls=%fused_computation.189 | loop fusion | bytes 786432 | tf_op jit(solution)/shard_map/slice | solution.py:58
  7.5 0.1 copy.95
  7.6 0.1 copy.96
  7.7 0.1 copy.97
  7.8 0.5 fusion.5
  8.3 0.2 copy.82
  8.5 0.2 reshape.1299
  8.7 0.6 concatenate.50.side_ref
  9.5 2.2 %convolution_bitcast_fusion.1.xa_ref = f32[3,1024,128]{2,1,0:T(8,128)} fusion(s32[1024]{0:T(1024)S(1)} %bitcast.271, f32[1,256,128]{1,2,0:T(8,128)S(1)} %get-tuple-element.11, f32[1,256,128]{1,2,0:T(8,128)S(1)} %get-tuple-element.13, f32[1,256,128]{1,2,0:T(8,128)S(1)} %get-tuple-element.15), kind=kOutput, calls=%fused_computation.4 | convolution fusion | flops 1208418304 | bytes 1970176 | tf_op jit(solution)/shard_map/sb,cbk->csk/dot_general | solution.py:283
  11.7 3.2 %shard_map.114 = f32[4224,128]{1,0:T(8,128)} custom-call(f32[3,1024,128]{2,1,0:T(8,128)} %convolution_bitcast_fusion.1.xa_ref, s32[1024,128]{1,0:T(8,128)} %bitcast.262, f32[128,128]{1,0:T(8,128)} %concatenate.50.side_ref), custom_call_target="tpu_custom_call" | custom-call | tf_op jit(solution)/shard_map/pallas_call | solution.py:188
  14.9 11.5 %all-to-all-start = ((f32[128,1,4224]{2,1,0:T(1,128)}), f32[128,1,4224]{2,1,0:T(1,128)S(1)}, u32[]{:S(2)}, u32[]{:S(2)}) async-start(f32[128,1,4224]{2,1,0:T(1,128)} %bitcast.260), calls=%async_computation | async-start | bytes 4325376 | tf_op jit(solution)/shard_map/all_to_all | solution.py:333
  26.4 0.6 fusion.84
  27.0 0.6 pad.31.clone
  27.6 0.6 pad.32.clone
  28.3 0.7 gather_fusion.1
  29.1 0.7 gather_fusion
  29.9 1.7 %fusion.80 = (f32[256,1,128]{2,0,1:T(8,128)S(1)}, f32[256,1,128]{2,0,1:T(8,128)S(1)}, f32[256,1,128]{2,0,1:T(8,128)}) fusion(f32[256,3,128]{2,0,1:T(8,128)} %param.11), kind=kLoop, calls=%fused_computation.188 | loop fusion | bytes 786432 | tf_op jit(solution)/shard_map/slice | solution.py:64
  31.7 0.1 copy.98
  31.8 0.1 copy.99
  31.9 1.0 %copy.100 = f32[256,1,128]{0,2,1:T(8,128)S(1)} copy(f32[256,1,128]{2,0,1:T(8,128)} %get-tuple-element.20) | data formatting | bytes 262144
  32.9 0.7 fusion.19
  33.7 2.2 %convolution_bitcast_fusion.3.xa_ref = f32[3,256,128]{2,1,0:T(8,128)} fusion(f32[1,256,128]{1,2,0:T(8,128)} %copy-done.2, f32[1,256,128]{1,2,0:T(8,128)} %copy-done.1, f32[1,256,128]{1,2,0:T(8,128)S(1)} %get-tuple-element.15, s32[256]{0:T(256)} %bitcast.273), kind=kOutput, calls=%fused_computation.6 | convolution fusion | flops 302252032 | bytes 787456 | tf_op jit(solution)/shard_map/sb,cbk->csk/dot_general | solution.py:283
  35.8 2.1 %convolution_bitcast_fusion.2.tb_ref = f32[6,256,128]{2,1,0:T(8,128)} fusion(f32[6,256,128]{1,2,0:T(8,128)S(1)} %fusion.21, s32[256]{0:T(256)} %bitcast.275), kind=kOutput, calls=%fused_computation.5 | convolution fusion | flops 604045312 | bytes 1573888 | tf_op jit(solution)/shard_map/sb,cbk->csk/dot_general | solution.py:283
  37.9 1.3 %maximum_maximum_fusion.1.aux_ref = f32[32,256]{1,0:T(8,128)} fusion(f32[12,256]{1,0:T(8,128)S(1)} %bitcast.265, f32[12,256]{1,0:T(8,128)S(1)} %bitcast.266, f32[32]{0:T(128)} %pad.32.clone, f32[32]{0:T(128)} %pad.31.clone), kind=kLoop, calls=%fused_computation.89 | loop fusion | flops 24576 | bytes 57600 | tf_op jit(solution)/shard_map/concatenate | solution.py:295
  39.3 3.4 %shard_map.113 = f32[32,256]{1,0:T(8,128)} custom-call(f32[3,256,128]{2,1,0:T(8,128)} %convolution_bitcast_fusion.3.xa_ref, f32[6,256,128]{2,1,0:T(8,128)} %convolution_bitcast_fusion.2.tb_ref, s32[256,128]{1,0:T(8,128)} %map_ref.1, f32[32,256]{1,0:T(8,128)} %maximum_maximum_fusion.1.aux_ref), custom_call_target="tpu_custom_call" | custom-call | tf_op jit(solution)/shard_map/pallas_call | solution.py:148
  42.6 0.8 slice_bitcast_fusion.1
  43.4 0.6 fusion.83
  44.0 0.6 fusion.60
  44.6 2.8 %gather_fusion.2 = f32[1024,12]{1,0:T(8,128)S(1)} fusion(f32[8,12]{1,0:T(8,128)S(1)} %bitcast.258, s32[1024]{0:T(1024)S(1)} %broadcast_clamp_fusion), kind=kCustom, calls=%fused_computation.2 | custom fusion | bytes 102400 | tf_op jit(solution)/shard_map/gather | solution.py:352
  47.4 0.2 copy.86
  47.6 0.7 fusion.62
  48.3 0.7 fusion.61
  49.0 0.7 and_select_fusion.4
  49.7 0.6 and_select_fusion.3
  50.3 0.7 slice_multiply_fusion.3
  51.0 0.7 slice_multiply_fusion.2
  51.7 0.3 fusion.44
  52.0 1.0 %convolution_add_fusion.1 = f32[8,18]{1,0:T(8,128)S(1)} fusion(f32[8,18]{1,0:T(8,128)S(1)} %fusion.44, s32[256]{0:T(256)S(1)} %and_select_fusion.3, f32[256,6]{0,1:T(8,128)S(1)} %fusion.62, f32[256,6]{0,1:T(8,128)S(1)} %fusion.61, f32[256,6]{0,1:T(8,128)} %fusion.60), kind=kOutput, calls=%fused_computation.8 | convolution fusion | flops 455824 | bytes 20608 | tf_op jit(solution)/shard_map/dot_general | solution.py:290
  53.0 3.2 %convolution_bitcast_fusion.tb_ref = f32[6,1024,128]{2,1,0:T(8,128)} fusion(f32[6,256,128]{1,2,0:T(8,128)S(1)} %fusion.21, s32[1024]{0:T(1024)S(1)} %bitcast.268), kind=kOutput, calls=%fused_computation.3 | convolution fusion | flops 2416181248 | bytes 3936256 | tf_op jit(solution)/shard_map/sb,cbk->csk/dot_general | solution.py:283
  56.2 1.4 %all-to-all-done = f32[128,1,4224]{2,1,0:T(1,128)S(1)} async-done(((f32[128,1,4224]{2,1,0:T(1,128)}), f32[128,1,4224]{2,1,0:T(1,128)S(1)}, u32[]{:S(2)}, u32[]{:S(2)}) %all-to-all-start) | async-done | bytes 2162720 | tf_op jit(solution)/shard_map/all_to_all | solution.py:333
  57.6 0.2 slice_reduce_fusion.1
  57.8 0.2 reshape_squeeze.3
  58.0 0.4 slice_reduce_fusion
  58.4 0.2 copy.101
  58.5 0.7 maximum_maximum_fusion.map_ref.aux_ref
  59.3 9.2 %shard_map.115 = f32[32,1024]{1,0:T(8,128)} custom-call(f32[4224,128]{1,0:T(8,128)} %bitcast.259, f32[6,1024,128]{2,1,0:T(8,128)} %convolution_bitcast_fusion.tb_ref, f32[32,1024]{1,0:T(8,128)} %maximum_maximum_fusion.map_ref.aux_ref, f32[32,1024]{1,0:T(8,128)} %maximum_maximum_fusion.map_ref.aux_ref), custom_call_target="tpu_custom_call" | custom-call | tf_op jit(solution)/shard_map/pallas_call | solution.py:148
  68.5 0.9 slice_bitcast_fusion
  69.5 0.2 copy.87
  69.7 1.1 %reshape.1334.x_ref = f32[128,1,144]{2,1,0:T(1,128)} reshape(f32[1024,18]{1,0:T(8,128)S(1)} %copy.87) | data formatting | bytes 147456 | tf_op jit(solution)/shard_map/reshape | solution.py:355
  70.8 16.6 %shard_map.116 = f32[128,1,144]{2,1,0:T(1,128)} custom-call(f32[128,1,144]{2,1,0:T(1,128)} %reshape.1334.x_ref), custom_call_target="tpu_custom_call" | custom-call | tf_op jit(solution)/shard_map/pallas_call | solution.py:265
  87.4 1.2 %reduce.2 = f32[128,144]{1,0:T(8,128)S(1)} reduce(f32[128,1,144]{2,1,0:T(1,128)} %shard_map.116, f32[]{:T(128)} %constant.99), dimensions={1}, to_apply=%pallas_call.15.reduce_sub_computation | reduce | bytes 147460 | tf_op jit(solution)/shard_map/pallas_call | solution.py:265
  88.7 0.2 reshape.1303
  88.9 0.6 convolution_add_fusion
  89.5 0.7 convolution_add_fusion.2
  90.3 0.7 copy.89
  91.1 0.7 copy.90
  (67 shorter events, 2.5 us)
Async XLA Ops:
  4.4 5.0 %copy-start.6 = (f32[256]{0:T(256)}, f32[256]{0:T(256)S(1)}, u32[]{:S(2)}) copy-start(f32[256]{0:T(256)S(1)} %mul.416) | copy-start | bytes 3076
  7.4 2.0 %copy-start.5 = (s32[1,1024]{1,0:T(1,128)S(1)}, s32[1,1024]{1,0:T(1,128)}, u32[]{:S(2)}) copy-start(s32[1,1024]{1,0:T(1,128)} %param.16) | copy-start | bytes 12292
  9.4 5.5 %copy-start.1 = (f32[1,256,128]{1,2,0:T(8,128)}, f32[1,256,128]{1,2,0:T(8,128)S(1)}, u32[]{:S(2)}) copy-start(f32[1,256,128]{1,2,0:T(8,128)S(1)} %get-tuple-element.13) | copy-start | bytes 393220
  9.5 5.4 %copy-start.2 = (f32[1,256,128]{1,2,0:T(8,128)}, f32[1,256,128]{1,2,0:T(8,128)S(1)}, u32[]{:S(2)}) copy-start(f32[1,256,128]{1,2,0:T(8,128)S(1)} %get-tuple-element.11) | copy-start | bytes 393220
  14.9 11.5 %copy-start.7 = (s32[2,256]{1,0:T(2,128)S(1)}, s32[2,256]{1,0:T(2,128)}, u32[]{:S(2)}) copy-start(s32[2,256]{1,0:T(2,128)} %param.14) | copy-start | bytes 6148
  14.9 13.4 %copy-start.4 = (s32[1,1024]{1,0:T(1,128)S(1)}, s32[1,1024]{1,0:T(1,128)}, u32[]{:S(2)}) copy-start(s32[1,1024]{1,0:T(1,128)} %param.18) | copy-start | bytes 12292
  14.9 42.7 %all-to-all-start = ((f32[128,1,4224]{2,1,0:T(1,128)}), f32[128,1,4224]{2,1,0:T(1,128)S(1)}, u32[]{:S(2)}, u32[]{:S(2)}) async-start(f32[128,1,4224]{2,1,0:T(1,128)} %bitcast.260), calls=%async_computation | async-start | bytes 4325376 | tf_op jit(solution)/shard_map/all_to_all | solution.py:333
  43.4 0.6 copy-start.3
  53.0 5.6 %copy-start.8 = (f32[32]{0:T(128)S(1)}, f32[32]{0:T(128)}, u32[]{:S(2)}) copy-start(f32[32]{0:T(128)} %pad.32.clone) | copy-start | bytes 388
  57.6 1.7 %copy-start = (f32[128,1,4224]{2,1,0:T(1,128)}, f32[128,1,4224]{2,1,0:T(1,128)S(1)}, u32[]{:S(2)}) copy-start(f32[128,1,4224]{2,1,0:T(1,128)S(1)} %all-to-all-done) | copy-start | bytes 6488068

commit v14 on v13

--- a/solution.py
+++ b/solution.py
@@ -66,7 +66,11 @@
     return jnp.stack(world_rows + normal_rows, axis=0)
 
 
-def _terms_kernel(from_cargo, xa_ref, tb_ref, map_ref, aux_ref, out_ref, xt_ref, gt_ref, cs_ref):
+def _terms_kernel(from_cargo, n_band, xa_ref, tb_ref, map_ref, aux_ref, out_ref, *rest):
+    if from_cargo:
+        recv_ref, xt_ref, gt_ref, cs_ref, ret_ref, send_sems, recv_sems, own_sem = rest
+    else:
+        xt_ref, gt_ref, cs_ref = rest
     chunk = out_ref.shape[1]
     if from_cargo:
         peers = chunk // CAP
@@ -132,22 +136,119 @@
     for q in range(N_QTY):
         out_ref[q : q + 1, :] = jnp.sum(accs[q], axis=0, keepdims=True) * valid
     out_ref[N_QTY:, :] = jnp.zeros((32 - N_QTY, chunk), jnp.float32)
-
-
-def pair_sums(xa, tb, maps, aux, chunk=128):
+    if from_cargo:
+        _send_back(n_band, out_ref, recv_ref, ret_ref, send_sems, recv_sems, own_sem)
+
+
+def _send_back(n_band, out_ref, recv_ref, ret_ref, send_sems, recv_sems, own_sem):
+    chunk = out_ref.shape[1]
+    peers = chunk // CAP
+    total = recv_ref.shape[0]
+    step = pl.program_id(0)
+    last = pl.num_programs(0) - 1
+    me = lax.axis_index("tile") * n_band + lax.axis_index("band")
+    barrier = pltpu.get_barrier_semaphore()
+
+    def device(p):
+        return (p // n_band, p % n_band)
+
+    def copy_to(p):
+        return pltpu.make_async_remote_copy(
+            src_ref=ret_ref.at[p],
+            dst_ref=recv_ref.at[me],
+            send_sem=send_sems.at[p],
+            recv_sem=recv_sems.at[me],
+            device_id=device(p),
+            device_id_type=MESH,
+        )
+
+    def copy_from(p):
+        return pltpu.make_async_remote_copy(
+            src_ref=ret_ref.at[p],
+            dst_ref=recv_ref.at[p],
+            send_sem=send_sems.at[p],
+            recv_sem=recv_sems.at[p],
+            device_id=device(p),
+            device_id_type=MESH,
+        )
+
+    own = pltpu.make_async_copy(ret_ref.at[me], recv_ref.at[me], own_sem)
+
+    @pl.when(step == 0)
+    def _():
+        def greet(k, carry):
+            p = lax.rem(me + k, total)
+            pl.semaphore_signal(barrier, inc=1, device_id=device(p), device_id_type=MESH)
+            return carry
+
+        lax.fori_loop(1, total, greet, 0)
+
+    padded = jnp.concatenate([out_ref[...], jnp.zeros((128 - 32, chunk), jnp.float32)], axis=0)
+    ret_ref[pl.ds(pl.multiple_of(step * peers, peers), peers)] = padded.T.reshape(peers, CAP, 128)
+
+    @pl.when(step == 0)
+    def _():
+        pl.semaphore_wait(barrier, total - 1)
+
+    def start(q, carry):
+        p = step * peers + q
+
+        @pl.when(p != me)
+        def _():
+            copy_to(p).start()
+
+        @pl.when(p == me)
+        def _():
+            own.start()
+
+        return carry
+
+    lax.fori_loop(0, peers, start, 0)
+
+    @pl.when(step == last)
+    def _():
+        def finish(k, carry):
+            p = lax.rem(me + k, total)
+            copy_to(p).wait_send()
+            copy_from(p).wait_recv()
+            return carry
+
+        lax.fori_loop(1, total, finish, 0)
+        own.wait()
+
+
+def pair_sums(xa, tb, maps, aux, n_band=1, chunk=128):
     pairs = tb.shape[1]
     from_cargo = maps is None
+    scratch = [
+        pltpu.VMEM((3, 128, chunk), jnp.float32),
+        pltpu.VMEM((6, 128, chunk), jnp.float32),
+        pltpu.VMEM((4, chunk, 128), jnp.float32),
+    ]
+    out_shape = jax.ShapeDtypeStruct((32, pairs), jnp.float32)
+    out_specs = pl.BlockSpec((32, chunk), lambda i: (0, i))
+    params = None
     if from_cargo:
         xa = xa.reshape(-1, 128)
         xa_spec = pl.BlockSpec((chunk // CAP * (4 * CAP + 1), 128), lambda i: (i, 0))
         maps = aux
         map_spec = pl.BlockSpec((8, 128), lambda i: (0, 0))
+        peers = pairs // CAP
+        out_shape = (out_shape, jax.ShapeDtypeStruct((peers, CAP, 128), jnp.float32))
+        out_specs = (out_specs, pl.BlockSpec(memory_space=pl.ANY))
+        scratch += [
+            pltpu.VMEM((peers, CAP, 128), jnp.float32),
+            pltpu.SemaphoreType.DMA((peers,)),
+            pltpu.SemaphoreType.DMA((peers,)),
+            pltpu.SemaphoreType.DMA(()),
+        ]
+        params = pltpu.CompilerParams(collective_id=0, has_side_effects=True)
     else:
         xa_spec = pl.BlockSpec((3, chunk, 128), lambda i: (0, i, 0))
         map_spec = pl.BlockSpec((chunk, 128), lambda i: (i, 0))
     return pl.pallas_call(
-        functools.partial(_terms_kernel, from_cargo),
-        out_shape=jax.ShapeDtypeStruct((32, pairs), jnp.float32),
+        functools.partial(_terms_kernel, from_cargo, n_band),
+        out_shape=out_shape,
         grid=(pairs // chunk,),
         in_specs=[
             xa_spec,
@@ -155,12 +256,9 @@
             map_spec,
             pl.BlockSpec((32, chunk), lambda i: (0, i)),
         ],
-        out_specs=pl.BlockSpec((32, chunk), lambda i: (0, i)),
-        scratch_shapes=[
-            pltpu.VMEM((3, 128, chunk), jnp.float32),
-            pltpu.VMEM((6, 128, chunk), jnp.float32),
-            pltpu.VMEM((4, chunk, 128), jnp.float32),
-        ],
+        out_specs=out_specs,
+        scratch_shapes=scratch,
+        compiler_params=params,
     )(xa, tb, maps, aux)
 
 
@@ -345,14 +443,15 @@
 
     target_blocks = remote_dst[0]
     side_in = arrived[:, 0, CAP * 4 * 128 : CAP * 4 * 128 + CAP * 13].reshape(peers * CAP, 13)
-    out_r = pair_sums(
+    out_r, back = pair_sums(
         arrived,
         pick_rows(target_blocks, rows6),
         None,
         make_aux(side_in[:, 0:12], frag_dirs[target_blocks // BF], side_in[:, 12]),
-    )
-    remote_a, remote_b = split_terms(out_r)
-    returned = exchange(remote_a.reshape(peers, 1, CAP * 18), n_band, 0).reshape(peers * CAP, 18)
+        n_band,
+    )
+    unused, remote_b = split_terms(out_r)
+    returned, unused = split_terms(back.reshape(peers * CAP, 128)[:, 0:32].T)
 
     totals = frag_sums(src_l, local_a, frag_count) + frag_sums(tgt_l, local_b, frag_count)
     totals = (

time: 92.8 us -> 89.9 us (0.969)
  the two profiles are of different devices: /device:TPU:1 before, /device:TPU:97 now
where the time goes in v14:
time: 89.9 us; the launch traced here: 89 us
  Pallas kernels  35.3 us (39%)
  local copies, waits for them, and re-layouts  21.2 us (24%)
  matrix products  12.6 us (14%)
  starting transfers between devices  10.2 us (11%)
  other arithmetic  8.71 us (10%)
  between operations  0.98 us (1%)
    pallas_call x2, Pallas kernels, pair_sums(): pl.pallas_call(functools.partial(_terms_kernel, from_cargo, n_band), out_...  32.2 us
    all_to_all x1, starting transfers between devices, local(): lax.all_to_all(cargo, axes, split_axis=0, concat_axis=0, tiled=True)  10.2 us
    dot_general x4, matrix products, pick_rows(): jnp.einsum('sb,cbk->csk', onehot, rows, precision=lax.Precision.HIGHEST)  9.72 us
    unnamed x31, local copies, waits for them, and re-layouts  5.07 us
    pallas_call x1, Pallas kernels, build_cargo(): pl.pallas_call(_cargo_kernel, out_shape=jax.ShapeDtypeStruct((slots // CA...  3.2 us
    gather x2, local copies, waits for them, and re-layouts, local(): frag_dirs[target_blocks // BF]  2.99 us
    dot_general x4, matrix products, frag_sums(): return jnp.dot(onehot.T, terms, precision=lax.Precision.HIGHEST)  2.38 us
    concatenate x2, other arithmetic, make_aux(): jnp.concatenate([dirs_a.T, dirs_b.T, valid[None, :], jnp.zeros((32 - 25,...  2.08 us
  transfers between devices with their start and end apart: 1, of which 0 were waited for; matrix products, arithmetic and copies ran while one was open for 28% of the time, Pallas kernels for 4%

profile of v14, /device:TPU:97, one launch (start us, length us, event | category | flops | bytes accessed | tf_op | source)
XLA Modules:
  0.0 89.0 jit_solution(17368091766068569885)
XLA Ops:
  0.6 0.8 slice_bitcast_fusion.5
  1.4 0.7 slice_multiply_fusion.4
  2.2 0.1 mul.431
  2.4 0.1 mul.439
  2.5 0.1 mul.399
  2.7 0.1 add.308
  2.8 0.7 add_select_fusion
  3.5 0.1 mul.435
  3.7 0.1 mul.427
  3.8 0.1 mul.412
  4.0 0.1 mul.406
  4.3 0.1 mul.416
  4.7 0.8 copy.76
  5.5 0.7 fusion.53
  6.3 0.1 reshape.1301
  6.4 1.1 %fusion.87 = (f32[256,1,128]{2,0,1:T(8,128)S(1)}, f32[256,1,128]{2,0,1:T(8,128)S(1)}, f32[256,1,128]{2,0,1:T(8,128)S(1)}) fusion(f32[256,3,128]{2,0,1:T(8,128)} %param.10), kind=kLoop, calls=%fused_computation.194 | loop fusion | bytes 786432 | tf_op jit(solution)/shard_map/slice | solution.py:58
  7.5 0.1 copy.92
  7.6 0.1 copy.93
  7.7 0.1 copy.94
  7.8 0.5 fusion.6
  8.3 0.2 copy.80
  8.5 0.2 reshape.1296
  8.7 0.6 concatenate.50.side_ref
  9.5 2.2 %convolution_bitcast_fusion.1.xa_ref = f32[3,1024,128]{2,1,0:T(8,128)} fusion(s32[1024]{0:T(1024)S(1)} %bitcast.277, f32[1,256,128]{1,2,0:T(8,128)S(1)} %get-tuple-element.15, f32[1,256,128]{1,2,0:T(8,128)S(1)} %get-tuple-element.17, f32[1,256,128]{1,2,0:T(8,128)S(1)} %get-tuple-element.19), kind=kOutput, calls=%fused_computation.4 | convolution fusion | flops 1208418304 | bytes 1970176 | tf_op jit(solution)/shard_map/sb,cbk->csk/dot_general | solution.py:381
  11.7 3.2 %shard_map.114 = f32[4224,128]{1,0:T(8,128)} custom-call(f32[3,1024,128]{2,1,0:T(8,128)} %convolution_bitcast_fusion.1.xa_ref, s32[1024,128]{1,0:T(8,128)} %bitcast.266, f32[128,128]{1,0:T(8,128)} %concatenate.50.side_ref), custom_call_target="tpu_custom_call" | custom-call | tf_op jit(solution)/shard_map/pallas_call | solution.py:286
  14.9 10.2 %all-to-all-start = ((f32[128,1,4224]{2,1,0:T(1,128)}), f32[128,1,4224]{2,1,0:T(1,128)S(1)}, u32[]{:S(2)}, u32[]{:S(2)}) async-start(f32[128,1,4224]{2,1,0:T(1,128)} %bitcast.264), calls=%async_computation | async-start | bytes 4325376 | tf_op jit(solution)/shard_map/all_to_all | solution.py:431
  25.1 0.6 fusion.90
  25.7 0.6 pad.31.clone
  26.3 0.6 pad.32.clone
  26.9 0.7 gather_fusion.1
  27.8 0.7 gather_fusion
  28.6 1.7 %fusion.86 = (f32[256,1,128]{2,0,1:T(8,128)S(1)}, f32[256,1,128]{2,0,1:T(8,128)S(1)}, f32[256,1,128]{2,0,1:T(8,128)}) fusion(f32[256,3,128]{2,0,1:T(8,128)} %param.11), kind=kLoop, calls=%fused_computation.193 | loop fusion | bytes 786432 | tf_op jit(solution)/shard_map/slice | solution.py:64
  30.3 0.1 copy.95
  30.4 0.1 copy.96
  30.5 1.0 %copy.97 = f32[256,1,128]{0,2,1:T(8,128)S(1)} copy(f32[256,1,128]{2,0,1:T(8,128)} %get-tuple-element.24) | data formatting | bytes 262144
  31.6 2.2 %convolution_bitcast_fusion.3.xa_ref = f32[3,256,128]{2,1,0:T(8,128)} fusion(f32[1,256,128]{1,2,0:T(8,128)} %copy-done.2, f32[1,256,128]{1,2,0:T(8,128)} %copy-done.1, f32[1,256,128]{1,2,0:T(8,128)S(1)} %get-tuple-element.19, s32[256]{0:T(256)} %bitcast.279), kind=kOutput, calls=%fused_computation.6 | convolution fusion | flops 302252032 | bytes 787456 | tf_op jit(solution)/shard_map/sb,cbk->csk/dot_general | solution.py:381
  33.8 2.1 %convolution_bitcast_fusion.2.tb_ref = f32[6,256,128]{2,1,0:T(8,128)} fusion(f32[6,256,128]{1,2,0:T(8,128)S(1)} %fusion.23, s32[256]{0:T(256)} %bitcast.281), kind=kOutput, calls=%fused_computation.5 | convolution fusion | flops 604045312 | bytes 1573888 | tf_op jit(solution)/shard_map/sb,cbk->csk/dot_general | solution.py:381
  35.9 1.3 %maximum_maximum_fusion.1.aux_ref = f32[32,256]{1,0:T(8,128)} fusion(f32[12,256]{1,0:T(8,128)S(1)} %bitcast.271, f32[12,256]{1,0:T(8,128)S(1)} %bitcast.272, f32[32]{0:T(128)} %pad.32.clone, f32[32]{0:T(128)} %pad.31.clone), kind=kLoop, calls=%fused_computation.93 | loop fusion | flops 24576 | bytes 57600 | tf_op jit(solution)/shard_map/concatenate | solution.py:393
  37.3 3.4 %shard_map.113 = f32[32,256]{1,0:T(8,128)} custom-call(f32[3,256,128]{2,1,0:T(8,128)} %convolution_bitcast_fusion.3.xa_ref, f32[6,256,128]{2,1,0:T(8,128)} %convolution_bitcast_fusion.2.tb_ref, s32[256,128]{1,0:T(8,128)} %map_ref.1, f32[32,256]{1,0:T(8,128)} %maximum_maximum_fusion.1.aux_ref), custom_call_target="tpu_custom_call" | custom-call | tf_op jit(solution)/shard_map/pallas_call | solution.py:249
  40.6 0.8 slice_bitcast_fusion.2
  41.4 0.6 fusion.89
  42.0 0.6 fusion.65
  42.6 2.8 %gather_fusion.2 = f32[1024,12]{1,0:T(8,128)S(1)} fusion(f32[8,12]{1,0:T(8,128)S(1)} %bitcast.262, s32[1024]{0:T(1024)S(1)} %broadcast_clamp_fusion), kind=kCustom, calls=%fused_computation.2 | custom fusion | bytes 102400 | tf_op jit(solution)/shard_map/gather | solution.py:450
  45.4 0.2 copy.84
  45.6 0.7 fusion.67
  46.3 0.7 and_select_fusion.4
  47.0 0.7 and_select_fusion.3
  47.7 0.7 slice_multiply_fusion.3
  48.4 0.7 slice_multiply_fusion.2
  49.1 0.3 fusion.49
  49.4 1.0 %convolution_add_fusion.2 = f32[8,18]{1,0:T(8,128)S(1)} fusion(f32[8,18]{1,0:T(8,128)S(1)} %fusion.49, s32[256]{0:T(256)S(1)} %and_select_fusion.3, f32[256,6]{0,1:T(8,128)S(1)} %fusion.67, f32[256,6]{0,1:T(8,128)S(1)} %fusion.66, f32[256,6]{0,1:T(8,128)} %fusion.65), kind=kOutput, calls=%fused_computation.9 | convolution fusion | flops 455824 | bytes 20608 | tf_op jit(solution)/shard_map/dot_general | solution.py:388
  50.4 3.2 %convolution_bitcast_fusion.tb_ref = f32[6,1024,128]{2,1,0:T(8,128)} fusion(f32[6,256,128]{1,2,0:T(8,128)S(1)} %fusion.23, s32[1024]{0:T(1024)S(1)} %bitcast.274), kind=kOutput, calls=%fused_computation.3 | convolution fusion | flops 2416181248 | bytes 3936256 | tf_op jit(solution)/shard_map/sb,cbk->csk/dot_general | solution.py:381
  53.6 0.2 slice_reduce_fusion.1
  53.8 0.2 reshape_squeeze.3
  54.0 0.4 slice_reduce_fusion
  54.3 0.2 copy.98
  54.5 0.7 maximum_maximum_fusion.map_ref.aux_ref
  55.3 28.8 %shard_map.115 = (f32[32,1024]{1,0:T(8,128)}, f32[128,8,128]{2,1,0:T(8,128)}) custom-call(f32[4224,128]{1,0:T(8,128)} %bitcast.263, f32[6,1024,128]{2,1,0:T(8,128)} %convolution_bitcast_fusion.tb_ref, f32[32,1024]{1,0:T(8,128)} %maximum_maximum_fusion.map_ref.aux_ref, f32[32,1024]{1,0:T(8,128)} %maximum_maximum_fusion.map_ref.aux_ref), custom_call_target="tpu_custom_call" | custom-call | tf_op jit(solution)/shard_map/pallas_call | solution.py:249
  84.1 1.2 %copy.99 = f32[1024,32]{0,1:T(8,128)S(1)} copy(f32[1024,32]{1,0:T(8,128)} %bitcast.267) | data formatting | bytes 262144
  85.3 0.9 %slice_bitcast_fusion.1 = f32[1024,27]{0,1:T(8,128)S(1)} fusion(f32[32,1024]{1,0:T(8,128)} %get-tuple-element.4), kind=kLoop, calls=%fused_computation.68 | loop fusion | bytes 221184 | tf_op jit(solution)/shard_map/transpose | solution.py:294
  86.3 0.6 convolution_add_fusion.1
  86.9 0.6 convolution_add_fusion
  87.6 0.7 copy.86
  88.3 0.7 copy.87
  (65 shorter events, 1.9 us)
Async XLA Ops:
  3.5 5.9 %copy-start.7 = (s32[1024]{0:T(1024)}, s32[1024]{0:T(1024)S(1)}, u32[]{:S(2)}) copy-start(s32[1024]{0:T(1024)S(1)} %add_select_fusion) | copy-start | bytes 12292
  7.4 2.0 %copy-start.5 = (s32[1,1024]{1,0:T(1,128)S(1)}, s32[1,1024]{1,0:T(1,128)}, u32[]{:S(2)}) copy-start(s32[1,1024]{1,0:T(1,128)} %param.16) | copy-start | bytes 12292
  9.4 5.5 %copy-start.1 = (f32[1,256,128]{1,2,0:T(8,128)}, f32[1,256,128]{1,2,0:T(8,128)S(1)}, u32[]{:S(2)}) copy-start(f32[1,256,128]{1,2,0:T(8,128)S(1)} %get-tuple-element.17) | copy-start | bytes 393220
  9.5 5.4 %copy-start.2 = (f32[1,256,128]{1,2,0:T(8,128)}, f32[1,256,128]{1,2,0:T(8,128)S(1)}, u32[]{:S(2)}) copy-start(f32[1,256,128]{1,2,0:T(8,128)S(1)} %get-tuple-element.15) | copy-start | bytes 393220
  14.9 10.2 %copy-start.6 = (s32[2,256]{1,0:T(2,128)S(1)}, s32[2,256]{1,0:T(2,128)}, u32[]{:S(2)}) copy-start(s32[2,256]{1,0:T(2,128)} %param.14) | copy-start | bytes 6148
  14.9 12.0 %copy-start.4 = (s32[1,1024]{1,0:T(1,128)S(1)}, s32[1,1024]{1,0:T(1,128)}, u32[]{:S(2)}) copy-start(s32[1,1024]{1,0:T(1,128)} %param.18) | copy-start | bytes 12292
  14.9 38.7 %all-to-all-start = ((f32[128,1,4224]{2,1,0:T(1,128)}), f32[128,1,4224]{2,1,0:T(1,128)S(1)}, u32[]{:S(2)}, u32[]{:S(2)}) async-start(f32[128,1,4224]{2,1,0:T(1,128)} %bitcast.264), calls=%async_computation | async-start | bytes 4325376 | tf_op jit(solution)/shard_map/all_to_all | solution.py:431
  41.4 0.6 copy-start.3
  50.4 4.1 %copy-start.9 = (f32[32]{0:T(128)S(1)}, f32[32]{0:T(128)}, u32[]{:S(2)}) copy-start(f32[32]{0:T(128)} %pad.32.clone) | copy-start | bytes 388
  53.6 1.7 %copy-start = (f32[128,1,4224]{2,1,0:T(1,128)}, f32[128,1,4224]{2,1,0:T(1,128)S(1)}, u32[]{:S(2)}) copy-start(f32[128,1,4224]{2,1,0:T(1,128)S(1)} %all-to-all-done) | copy-start | bytes 6488068
  55.3 31.6 %copy-start.8 = (s32[1024]{0:T(1024)S(1)}, s32[1024]{0:T(1024)}, u32[]{:S(2)}) copy-start(s32[1024]{0:T(1024)} %copy-done.7) | copy-start | bytes 12292

commit v15 on v14

--- a/solution.py
+++ b/solution.py
@@ -140,6 +140,11 @@
         _send_back(n_band, out_ref, recv_ref, ret_ref, send_sems, recv_sems, own_sem)
 
 
+def _first_chunk(n_band, chunks):
+    me = lax.axis_index("tile") * n_band + lax.axis_index("band")
+    return lax.rem(me, chunks)
+
+
 def _send_back(n_band, out_ref, recv_ref, ret_ref, send_sems, recv_sems, own_sem):
     chunk = out_ref.shape[1]
     peers = chunk // CAP
@@ -184,14 +189,16 @@
         lax.fori_loop(1, total, greet, 0)
 
     padded = jnp.concatenate([out_ref[...], jnp.zeros((128 - 32, chunk), jnp.float32)], axis=0)
-    ret_ref[pl.ds(pl.multiple_of(step * peers, peers), peers)] = padded.T.reshape(peers, CAP, 128)
+    first = _first_chunk(n_band, pl.num_programs(0))
+    part = lax.rem(step + first, pl.num_programs(0))
+    ret_ref[pl.ds(pl.multiple_of(part * peers, peers), peers)] = padded.T.reshape(peers, CAP, 128)
 
     @pl.when(step == 0)
     def _():
         pl.semaphore_wait(barrier, total - 1)
 
     def start(q, carry):
-        p = step * peers + q
+        p = part * peers + q
 
         @pl.when(p != me)
         def _():
@@ -226,11 +233,18 @@
         pltpu.VMEM((4, chunk, 128), jnp.float32),
     ]
     out_shape = jax.ShapeDtypeStruct((32, pairs), jnp.float32)
-    out_specs = pl.BlockSpec((32, chunk), lambda i: (0, i))
+    out_specs = pl.BlockSpec((32, chunk), lambda i: (0, blk(i)))
     params = None
+    chunks = pairs // chunk
+
+    def blk(i):
+        if from_cargo:
+            return lax.rem(i + _first_chunk(n_band, chunks), chunks)
+        return i
+
     if from_cargo:
         xa = xa.reshape(-1, 128)
-        xa_spec = pl.BlockSpec((chunk // CAP * (4 * CAP + 1), 128), lambda i: (i, 0))
+        xa_spec = pl.BlockSpec((chunk // CAP * (4 * CAP + 1), 128), lambda i: (blk(i), 0))
         maps = aux
         map_spec = pl.BlockSpec((8, 128), lambda i: (0, 0))
         peers = pairs // CAP
@@ -252,9 +266,9 @@
         grid=(pairs // chunk,),
         in_specs=[
             xa_spec,
-            pl.BlockSpec((6, chunk, 128), lambda i: (0, i, 0)),
+            pl.BlockSpec((6, chunk, 128), lambda i: (0, blk(i), 0)),
             map_spec,
-            pl.BlockSpec((32, chunk), lambda i: (0, i)),
+            pl.BlockSpec((32, chunk), lambda i: (0, blk(i))),
         ],
         out_specs=out_specs,
         scratch_shapes=scratch,

time: 89.9 us -> 90.7 us (level)
  the two profiles are of different devices: /device:TPU:97 before, /device:TPU:1 now
where the time goes in v15:
time: 90.7 us; the launch traced here: 89.9 us
  Pallas kernels  32.2 us (36%)
  local copies, waits for them, and re-layouts  21.2 us (23%)
  matrix products  12.6 us (14%)
  starting transfers between devices  11.5 us (13%)
  other arithmetic  8.71 us (10%)
  waiting for transfers between devices  2.71 us (3%)
  between operations  0.98 us (1%)
    pallas_call x2, Pallas kernels, pair_sums(): pl.pallas_call(functools.partial(_terms_kernel, from_cargo, n_band), out_...  29 us
    all_to_all x1, starting transfers between devices, local(): lax.all_to_all(cargo, axes, split_axis=0, concat_axis=0, tiled=True)  11.5 us
    dot_general x4, matrix products, pick_rows(): jnp.einsum('sb,cbk->csk', onehot, rows, precision=lax.Precision.HIGHEST)  9.72 us
    unnamed x31, local copies, waits for them, and re-layouts  5.07 us
    pallas_call x1, Pallas kernels, build_cargo(): pl.pallas_call(_cargo_kernel, out_shape=jax.ShapeDtypeStruct((slots // CA...  3.2 us
    gather x2, local copies, waits for them, and re-layouts, local(): frag_dirs[target_blocks // BF]  2.99 us
    all_to_all x1, waiting for transfers between devices, local(): lax.all_to_all(cargo, axes, split_axis=0, concat_axis=0, tiled=True)  2.71 us
    dot_general x4, matrix products, frag_sums(): return jnp.dot(onehot.T, terms, precision=lax.Precision.HIGHEST)  2.38 us
  transfers between devices with their start and end apart: 1, of which 1 were waited for; matrix products, arithmetic and copies ran while one was open for 28% of the time, Pallas kernels for 4%

profile of v15, /device:TPU:1, one launch (start us, length us, event | category | flops | bytes accessed | tf_op | source)
XLA Modules:
  0.0 89.9 jit_solution(13417485572528917112)
XLA Ops:
  0.6 0.8 slice_bitcast_fusion.5
  1.4 0.7 slice_multiply_fusion.4
  2.2 0.1 mul.431
  2.4 0.1 mul.439
  2.5 0.1 mul.399
  2.7 0.1 add.308
  2.8 0.7 add_select_fusion
  3.5 0.1 mul.435
  3.8 0.1 mul.412
  4.3 0.1 mul.416
  4.7 0.8 copy.76
  5.5 0.1 reshape.1295
  5.5 0.7 fusion.53
  6.3 0.1 reshape.1301
  6.4 1.1 %fusion.87 = (f32[256,1,128]{2,0,1:T(8,128)S(1)}, f32[256,1,128]{2,0,1:T(8,128)S(1)}, f32[256,1,128]{2,0,1:T(8,128)S(1)}) fusion(f32[256,3,128]{2,0,1:T(8,128)} %param.10), kind=kLoop, calls=%fused_computation.194 | loop fusion | bytes 786432 | tf_op jit(solution)/shard_map/slice | solution.py:58
  7.5 0.1 copy.92
  7.6 0.1 copy.93
  7.7 0.1 copy.94
  7.8 0.5 fusion.6
  8.3 0.2 copy.80
  8.5 0.2 reshape.1296
  8.7 0.6 concatenate.50.side_ref
  9.5 2.2 %convolution_bitcast_fusion.1.xa_ref = f32[3,1024,128]{2,1,0:T(8,128)} fusion(s32[1024]{0:T(1024)S(1)} %bitcast.277, f32[1,256,128]{1,2,0:T(8,128)S(1)} %get-tuple-element.15, f32[1,256,128]{1,2,0:T(8,128)S(1)} %get-tuple-element.17, f32[1,256,128]{1,2,0:T(8,128)S(1)} %get-tuple-element.19), kind=kOutput, calls=%fused_computation.4 | convolution fusion | flops 1208418304 | bytes 1970176 | tf_op jit(solution)/shard_map/sb,cbk->csk/dot_general | solution.py:395
  11.7 3.2 %shard_map.114 = f32[4224,128]{1,0:T(8,128)} custom-call(f32[3,1024,128]{2,1,0:T(8,128)} %convolution_bitcast_fusion.1.xa_ref, s32[1024,128]{1,0:T(8,128)} %bitcast.266, f32[128,128]{1,0:T(8,128)} %concatenate.50.side_ref), custom_call_target="tpu_custom_call" | custom-call | tf_op jit(solution)/shard_map/pallas_call | solution.py:300
  14.9 11.5 %all-to-all-start = ((f32[128,1,4224]{2,1,0:T(1,128)}), f32[128,1,4224]{2,1,0:T(1,128)S(1)}, u32[]{:S(2)}, u32[]{:S(2)}) async-start(f32[128,1,4224]{2,1,0:T(1,128)} %bitcast.264), calls=%async_computation | async-start | bytes 4325376 | tf_op jit(solution)/shard_map/all_to_all | solution.py:445
  26.4 0.6 fusion.90
  27.0 0.6 pad.31.clone
  27.6 0.6 pad.32.clone
  28.3 0.7 gather_fusion.1
  29.1 0.7 gather_fusion
  29.9 1.7 %fusion.86 = (f32[256,1,128]{2,0,1:T(8,128)S(1)}, f32[256,1,128]{2,0,1:T(8,128)S(1)}, f32[256,1,128]{2,0,1:T(8,128)}) fusion(f32[256,3,128]{2,0,1:T(8,128)} %param.11), kind=kLoop, calls=%fused_computation.193 | loop fusion | bytes 786432 | tf_op jit(solution)/shard_map/slice | solution.py:64
  31.6 0.1 copy.95
  31.7 0.1 copy.96
  31.8 1.0 %copy.97 = f32[256,1,128]{0,2,1:T(8,128)S(1)} copy(f32[256,1,128]{2,0,1:T(8,128)} %get-tuple-element.24) | data formatting | bytes 262144
  32.9 2.2 %convolution_bitcast_fusion.3.xa_ref = f32[3,256,128]{2,1,0:T(8,128)} fusion(f32[1,256,128]{1,2,0:T(8,128)} %copy-done.2, f32[1,256,128]{1,2,0:T(8,128)} %copy-done.1, f32[1,256,128]{1,2,0:T(8,128)S(1)} %get-tuple-element.19, s32[256]{0:T(256)} %bitcast.279), kind=kOutput, calls=%fused_computation.6 | convolution fusion | flops 302252032 | bytes 787456 | tf_op jit(solution)/shard_map/sb,cbk->csk/dot_general | solution.py:395
  35.1 2.1 %convolution_bitcast_fusion.2.tb_ref = f32[6,256,128]{2,1,0:T(8,128)} fusion(f32[6,256,128]{1,2,0:T(8,128)S(1)} %fusion.23, s32[256]{0:T(256)} %bitcast.281), kind=kOutput, calls=%fused_computation.5 | convolution fusion | flops 604045312 | bytes 1573888 | tf_op jit(solution)/shard_map/sb,cbk->csk/dot_general | solution.py:395
  37.2 1.3 %maximum_maximum_fusion.1.aux_ref = f32[32,256]{1,0:T(8,128)} fusion(f32[12,256]{1,0:T(8,128)S(1)} %bitcast.271, f32[12,256]{1,0:T(8,128)S(1)} %bitcast.272, f32[32]{0:T(128)} %pad.32.clone, f32[32]{0:T(128)} %pad.31.clone), kind=kLoop, calls=%fused_computation.93 | loop fusion | flops 24576 | bytes 57600 | tf_op jit(solution)/shard_map/concatenate | solution.py:407
  38.6 3.4 %shard_map.113 = f32[32,256]{1,0:T(8,128)} custom-call(f32[3,256,128]{2,1,0:T(8,128)} %convolution_bitcast_fusion.3.xa_ref, f32[6,256,128]{2,1,0:T(8,128)} %convolution_bitcast_fusion.2.tb_ref, s32[256,128]{1,0:T(8,128)} %map_ref.1, f32[32,256]{1,0:T(8,128)} %maximum_maximum_fusion.1.aux_ref), custom_call_target="tpu_custom_call" | custom-call | tf_op jit(solution)/shard_map/pallas_call | solution.py:263
  41.9 0.8 slice_bitcast_fusion.2
  42.7 0.6 fusion.89
  43.3 0.6 fusion.65
  43.9 2.8 %gather_fusion.2 = f32[1024,12]{1,0:T(8,128)S(1)} fusion(f32[8,12]{1,0:T(8,128)S(1)} %bitcast.262, s32[1024]{0:T(1024)S(1)} %broadcast_clamp_fusion), kind=kCustom, calls=%fused_computation.2 | custom fusion | bytes 102400 | tf_op jit(solution)/shard_map/gather | solution.py:464
  46.7 0.2 copy.84
  46.9 0.7 fusion.67
  47.6 0.7 and_select_fusion.4
  48.3 0.7 and_select_fusion.3
  49.0 0.7 slice_multiply_fusion.3
  49.7 0.7 slice_multiply_fusion.2
  50.4 0.3 fusion.49
  50.7 1.0 %convolution_add_fusion.2 = f32[8,18]{1,0:T(8,128)S(1)} fusion(f32[8,18]{1,0:T(8,128)S(1)} %fusion.49, s32[256]{0:T(256)S(1)} %and_select_fusion.3, f32[256,6]{0,1:T(8,128)S(1)} %fusion.67, f32[256,6]{0,1:T(8,128)S(1)} %fusion.66, f32[256,6]{0,1:T(8,128)} %fusion.65), kind=kOutput, calls=%fused_computation.9 | convolution fusion | flops 455824 | bytes 20608 | tf_op jit(solution)/shard_map/dot_general | solution.py:402
  51.7 3.2 %convolution_bitcast_fusion.tb_ref = f32[6,1024,128]{2,1,0:T(8,128)} fusion(f32[6,256,128]{1,2,0:T(8,128)S(1)} %fusion.23, s32[1024]{0:T(1024)S(1)} %bitcast.274), kind=kOutput, calls=%fused_computation.3 | convolution fusion | flops 2416181248 | bytes 3936256 | tf_op jit(solution)/shard_map/sb,cbk->csk/dot_general | solution.py:395
  54.9 2.7 %all-to-all-done = f32[128,1,4224]{2,1,0:T(1,128)S(1)} async-done(((f32[128,1,4224]{2,1,0:T(1,128)}), f32[128,1,4224]{2,1,0:T(1,128)S(1)}, u32[]{:S(2)}, u32[]{:S(2)}) %all-to-all-start) | async-done | bytes 2162720 | tf_op jit(solution)/shard_map/all_to_all | solution.py:445
  57.6 0.2 slice_reduce_fusion.1
  57.8 0.2 reshape_squeeze.3
  58.0 0.4 slice_reduce_fusion
  58.4 0.2 copy.98
  58.5 0.7 maximum_maximum_fusion.map_ref.aux_ref
  59.3 25.6 %shard_map.115 = (f32[32,1024]{1,0:T(8,128)}, f32[128,8,128]{2,1,0:T(8,128)}) custom-call(f32[4224,128]{1,0:T(8,128)} %bitcast.263, f32[6,1024,128]{2,1,0:T(8,128)} %convolution_bitcast_fusion.tb_ref, f32[32,1024]{1,0:T(8,128)} %maximum_maximum_fusion.map_ref.aux_ref, f32[32,1024]{1,0:T(8,128)} %maximum_maximum_fusion.map_ref.aux_ref), custom_call_target="tpu_custom_call" | custom-call | tf_op jit(solution)/shard_map/pallas_call | solution.py:263
  84.9 1.2 %copy.99 = f32[1024,32]{0,1:T(8,128)S(1)} copy(f32[1024,32]{1,0:T(8,128)} %bitcast.267) | data formatting | bytes 262144
  86.2 0.9 %slice_bitcast_fusion.1 = f32[1024,27]{0,1:T(8,128)S(1)} fusion(f32[32,1024]{1,0:T(8,128)} %get-tuple-element.4), kind=kLoop, calls=%fused_computation.68 | loop fusion | bytes 221184 | tf_op jit(solution)/shard_map/transpose | solution.py:308
  87.2 0.6 convolution_add_fusion.1
  87.7 0.6 convolution_add_fusion
  88.4 0.7 copy.86
  89.2 0.7 copy.87
  (65 shorter events, 2.0 us)
Async XLA Ops:
  3.5 5.9 %copy-start.7 = (s32[1024]{0:T(1024)}, s32[1024]{0:T(1024)S(1)}, u32[]{:S(2)}) copy-start(s32[1024]{0:T(1024)S(1)} %add_select_fusion) | copy-start | bytes 12292
  7.4 2.0 %copy-start.5 = (s32[1,1024]{1,0:T(1,128)S(1)}, s32[1,1024]{1,0:T(1,128)}, u32[]{:S(2)}) copy-start(s32[1,1024]{1,0:T(1,128)} %param.16) | copy-start | bytes 12292
  9.4 5.5 %copy-start.1 = (f32[1,256,128]{1,2,0:T(8,128)}, f32[1,256,128]{1,2,0:T(8,128)S(1)}, u32[]{:S(2)}) copy-start(f32[1,256,128]{1,2,0:T(8,128)S(1)} %get-tuple-element.17) | copy-start | bytes 393220
  9.5 5.4 %copy-start.2 = (f32[1,256,128]{1,2,0:T(8,128)}, f32[1,256,128]{1,2,0:T(8,128)S(1)}, u32[]{:S(2)}) copy-start(f32[1,256,128]{1,2,0:T(8,128)S(1)} %get-tuple-element.15) | copy-start | bytes 393220
  14.9 11.5 %copy-start.6 = (s32[2,256]{1,0:T(2,128)S(1)}, s32[2,256]{1,0:T(2,128)}, u32[]{:S(2)}) copy-start(s32[2,256]{1,0:T(2,128)} %param.14) | copy-start | bytes 6148
  14.9 13.3 %copy-start.4 = (s32[1,1024]{1,0:T(1,128)S(1)}, s32[1,1024]{1,0:T(1,128)}, u32[]{:S(2)}) copy-start(s32[1,1024]{1,0:T(1,128)} %param.18) | copy-start | bytes 12292
  14.9 42.7 %all-to-all-start = ((f32[128,1,4224]{2,1,0:T(1,128)}), f32[128,1,4224]{2,1,0:T(1,128)S(1)}, u32[]{:S(2)}, u32[]{:S(2)}) async-start(f32[128,1,4224]{2,1,0:T(1,128)} %bitcast.264), calls=%async_computation | async-start | bytes 4325376 | tf_op jit(solution)/shard_map/all_to_all | solution.py:445
  42.7 0.6 copy-start.3
  51.7 6.8 %copy-start.9 = (f32[32]{0:T(128)S(1)}, f32[32]{0:T(128)}, u32[]{:S(2)}) copy-start(f32[32]{0:T(128)} %pad.32.clone) | copy-start | bytes 388
  57.6 1.7 %copy-start = (f32[128,1,4224]{2,1,0:T(1,128)}, f32[128,1,4224]{2,1,0:T(1,128)S(1)}, u32[]{:S(2)}) copy-start(f32[128,1,4224]{2,1,0:T(1,128)S(1)} %all-to-all-done) | copy-start | bytes 6488068
  59.3 28.4 %copy-start.8 = (s32[1024]{0:T(1024)S(1)}, s32[1024]{0:T(1024)}, u32[]{:S(2)}) copy-start(s32[1024]{0:T(1024)} %copy-done.7) | copy-start | bytes 12292

commit v16 on v14

--- a/solution.py
+++ b/solution.py
@@ -186,12 +186,14 @@
     padded = jnp.concatenate([out_ref[...], jnp.zeros((128 - 32, chunk), jnp.float32)], axis=0)
     ret_ref[pl.ds(pl.multiple_of(step * peers, peers), peers)] = padded.T.reshape(peers, CAP, 128)
 
-    @pl.when(step == 0)
+    hold = jnp.minimum(2, last)
+
+    @pl.when(step == hold)
     def _():
         pl.semaphore_wait(barrier, total - 1)
 
     def start(q, carry):
-        p = step * peers + q
+        p = q
 
         @pl.when(p != me)
         def _():
@@ -203,7 +205,13 @@
 
         return carry
 
-    lax.fori_loop(0, peers, start, 0)
+    @pl.when(step == hold)
+    def _():
+        lax.fori_loop(0, (hold + 1) * peers, start, 0)
+
+    @pl.when(step > hold)
+    def _():
+        lax.fori_loop(step * peers, (step + 1) * peers, start, 0)
 
     @pl.when(step == last)
     def _():

time: 89.9 us -> 87.9 us (0.978)
  Pallas kernels: 35.3 us -> 33.4 us
    pallas_call x2, Pallas kernels: 32.2 us -> 30.2 us  [pair_sums(): pl.pallas_call(functools.partial(_terms_kernel, from_cargo, n_band), out_...]
  transfers between devices with their start and end apart: 1 -> 1, of which waited for: 0 -> 0; matrix products, arithmetic and copies ran while one was open for 28% -> 29% of each run, Pallas kernels for 4% -> 4%
where the time goes in v16:
time: 87.9 us; the launch traced here: 87 us
  Pallas kernels  33.4 us (38%)
  local copies, waits for them, and re-layouts  21.2 us (24%)
  matrix products  12.6 us (14%)
  starting transfers between devices  10.2 us (12%)
  other arithmetic  8.71 us (10%)
  between operations  0.98 us (1%)
    pallas_call x2, Pallas kernels, pair_sums(): pl.pallas_call(functools.partial(_terms_kernel, from_cargo, n_band), out_...  30.2 us
    all_to_all x1, starting transfers between devices, local(): lax.all_to_all(cargo, axes, split_axis=0, concat_axis=0, tiled=True)  10.2 us
    dot_general x4, matrix products, pick_rows(): jnp.einsum('sb,cbk->csk', onehot, rows, precision=lax.Precision.HIGHEST)  9.72 us
    unnamed x31, local copies, waits for them, and re-layouts  5.07 us
    pallas_call x1, Pallas kernels, build_cargo(): pl.pallas_call(_cargo_kernel, out_shape=jax.ShapeDtypeStruct((slots // CA...  3.2 us
    gather x2, local copies, waits for them, and re-layouts, local(): frag_dirs[target_blocks // BF]  2.99 us
    dot_general x4, matrix products, frag_sums(): return jnp.dot(onehot.T, terms, precision=lax.Precision.HIGHEST)  2.38 us
    concatenate x2, other arithmetic, make_aux(): jnp.concatenate([dirs_a.T, dirs_b.T, valid[None, :], jnp.zeros((32 - 25,...  2.08 us
  transfers between devices with their start and end apart: 1, of which 0 were waited for; matrix products, arithmetic and copies ran while one was open for 29% of the time, Pallas kernels for 4%

profile of v16, /device:TPU:97, one launch (start us, length us, event | category | flops | bytes accessed | tf_op | source)
XLA Modules:
  0.0 87.0 jit_solution(107843134876899534)
XLA Ops:
  0.6 0.8 slice_bitcast_fusion.5
  1.4 0.7 slice_multiply_fusion.4
  2.2 0.1 mul.431
  2.4 0.1 mul.439
  2.5 0.1 mul.399
  2.7 0.1 add.308
  2.8 0.7 add_select_fusion
  3.5 0.1 mul.435
  3.7 0.1 mul.427
  3.8 0.1 mul.412
  4.0 0.1 mul.406
  4.3 0.1 mul.416
  4.7 0.8 copy.76
  5.5 0.7 fusion.53
  6.3 0.1 reshape.1301
  6.4 1.1 %fusion.87 = (f32[256,1,128]{2,0,1:T(8,128)S(1)}, f32[256,1,128]{2,0,1:T(8,128)S(1)}, f32[256,1,128]{2,0,1:T(8,128)S(1)}) fusion(f32[256,3,128]{2,0,1:T(8,128)} %param.10), kind=kLoop, calls=%fused_computation.194 | loop fusion | bytes 786432 | tf_op jit(solution)/shard_map/slice | solution.py:58
  7.5 0.1 copy.92
  7.6 0.1 copy.93
  7.7 0.1 copy.94
  7.8 0.5 fusion.6
  8.3 0.2 copy.80
  8.5 0.2 reshape.1296
  8.7 0.6 concatenate.50.side_ref
  9.5 2.2 %convolution_bitcast_fusion.1.xa_ref = f32[3,1024,128]{2,1,0:T(8,128)} fusion(s32[1024]{0:T(1024)S(1)} %bitcast.277, f32[1,256,128]{1,2,0:T(8,128)S(1)} %get-tuple-element.15, f32[1,256,128]{1,2,0:T(8,128)S(1)} %get-tuple-element.17, f32[1,256,128]{1,2,0:T(8,128)S(1)} %get-tuple-element.19), kind=kOutput, calls=%fused_computation.4 | convolution fusion | flops 1208418304 | bytes 1970176 | tf_op jit(solution)/shard_map/sb,cbk->csk/dot_general | solution.py:389
  11.7 3.2 %shard_map.114 = f32[4224,128]{1,0:T(8,128)} custom-call(f32[3,1024,128]{2,1,0:T(8,128)} %convolution_bitcast_fusion.1.xa_ref, s32[1024,128]{1,0:T(8,128)} %bitcast.266, f32[128,128]{1,0:T(8,128)} %concatenate.50.side_ref), custom_call_target="tpu_custom_call" | custom-call | tf_op jit(solution)/shard_map/pallas_call | solution.py:294
  14.9 10.2 %all-to-all-start = ((f32[128,1,4224]{2,1,0:T(1,128)}), f32[128,1,4224]{2,1,0:T(1,128)S(1)}, u32[]{:S(2)}, u32[]{:S(2)}) async-start(f32[128,1,4224]{2,1,0:T(1,128)} %bitcast.264), calls=%async_computation | async-start | bytes 4325376 | tf_op jit(solution)/shard_map/all_to_all | solution.py:439
  25.1 0.6 fusion.90
  25.7 0.6 pad.31.clone
  26.3 0.6 pad.32.clone
  26.9 0.7 gather_fusion.1
  27.8 0.7 gather_fusion
  28.6 1.7 %fusion.86 = (f32[256,1,128]{2,0,1:T(8,128)S(1)}, f32[256,1,128]{2,0,1:T(8,128)S(1)}, f32[256,1,128]{2,0,1:T(8,128)}) fusion(f32[256,3,128]{2,0,1:T(8,128)} %param.11), kind=kLoop, calls=%fused_computation.193 | loop fusion | bytes 786432 | tf_op jit(solution)/shard_map/slice | solution.py:64
  30.3 0.1 copy.95
  30.4 0.1 copy.96
  30.5 1.0 %copy.97 = f32[256,1,128]{0,2,1:T(8,128)S(1)} copy(f32[256,1,128]{2,0,1:T(8,128)} %get-tuple-element.24) | data formatting | bytes 262144
  31.6 2.2 %convolution_bitcast_fusion.3.xa_ref = f32[3,256,128]{2,1,0:T(8,128)} fusion(f32[1,256,128]{1,2,0:T(8,128)} %copy-done.2, f32[1,256,128]{1,2,0:T(8,128)} %copy-done.1, f32[1,256,128]{1,2,0:T(8,128)S(1)} %get-tuple-element.19, s32[256]{0:T(256)} %bitcast.279), kind=kOutput, calls=%fused_computation.6 | convolution fusion | flops 302252032 | bytes 787456 | tf_op jit(solution)/shard_map/sb,cbk->csk/dot_general | solution.py:389
  33.8 2.1 %convolution_bitcast_fusion.2.tb_ref = f32[6,256,128]{2,1,0:T(8,128)} fusion(f32[6,256,128]{1,2,0:T(8,128)S(1)} %fusion.23, s32[256]{0:T(256)} %bitcast.281), kind=kOutput, calls=%fused_computation.5 | convolution fusion | flops 604045312 | bytes 1573888 | tf_op jit(solution)/shard_map/sb,cbk->csk/dot_general | solution.py:389
  35.9 1.3 %maximum_maximum_fusion.1.aux_ref = f32[32,256]{1,0:T(8,128)} fusion(f32[12,256]{1,0:T(8,128)S(1)} %bitcast.271, f32[12,256]{1,0:T(8,128)S(1)} %bitcast.272, f32[32]{0:T(128)} %pad.32.clone, f32[32]{0:T(128)} %pad.31.clone), kind=kLoop, calls=%fused_computation.93 | loop fusion | flops 24576 | bytes 57600 | tf_op jit(solution)/shard_map/concatenate | solution.py:401
  37.3 3.4 %shard_map.113 = f32[32,256]{1,0:T(8,128)} custom-call(f32[3,256,128]{2,1,0:T(8,128)} %convolution_bitcast_fusion.3.xa_ref, f32[6,256,128]{2,1,0:T(8,128)} %convolution_bitcast_fusion.2.tb_ref, s32[256,128]{1,0:T(8,128)} %map_ref.1, f32[32,256]{1,0:T(8,128)} %maximum_maximum_fusion.1.aux_ref), custom_call_target="tpu_custom_call" | custom-call | tf_op jit(solution)/shard_map/pallas_call | solution.py:257
  40.6 0.8 slice_bitcast_fusion.2
  41.4 0.6 fusion.89
  42.0 0.6 fusion.65
  42.6 2.8 %gather_fusion.2 = f32[1024,12]{1,0:T(8,128)S(1)} fusion(f32[8,12]{1,0:T(8,128)S(1)} %bitcast.262, s32[1024]{0:T(1024)S(1)} %broadcast_clamp_fusion), kind=kCustom, calls=%fused_computation.2 | custom fusion | bytes 102400 | tf_op jit(solution)/shard_map/gather | solution.py:458
  45.4 0.2 copy.84
  45.6 0.7 fusion.67
  46.3 0.7 and_select_fusion.4
  47.0 0.7 and_select_fusion.3
  47.7 0.7 slice_multiply_fusion.3
  48.4 0.7 slice_multiply_fusion.2
  49.1 0.3 fusion.49
  49.4 1.0 %convolution_add_fusion.2 = f32[8,18]{1,0:T(8,128)S(1)} fusion(f32[8,18]{1,0:T(8,128)S(1)} %fusion.49, s32[256]{0:T(256)S(1)} %and_select_fusion.3, f32[256,6]{0,1:T(8,128)S(1)} %fusion.67, f32[256,6]{0,1:T(8,128)S(1)} %fusion.66, f32[256,6]{0,1:T(8,128)} %fusion.65), kind=kOutput, calls=%fused_computation.9 | convolution fusion | flops 455824 | bytes 20608 | tf_op jit(solution)/shard_map/dot_general | solution.py:396
  50.4 3.2 %convolution_bitcast_fusion.tb_ref = f32[6,1024,128]{2,1,0:T(8,128)} fusion(f32[6,256,128]{1,2,0:T(8,128)S(1)} %fusion.23, s32[1024]{0:T(1024)S(1)} %bitcast.274), kind=kOutput, calls=%fused_computation.3 | convolution fusion | flops 2416181248 | bytes 3936256 | tf_op jit(solution)/shard_map/sb,cbk->csk/dot_general | solution.py:389
  53.6 0.2 slice_reduce_fusion.1
  53.8 0.2 reshape_squeeze.3
  54.0 0.4 slice_reduce_fusion
  54.3 0.2 copy.98
  54.5 0.7 maximum_maximum_fusion.map_ref.aux_ref
  55.3 26.8 %shard_map.115 = (f32[32,1024]{1,0:T(8,128)}, f32[128,8,128]{2,1,0:T(8,128)}) custom-call(f32[4224,128]{1,0:T(8,128)} %bitcast.263, f32[6,1024,128]{2,1,0:T(8,128)} %convolution_bitcast_fusion.tb_ref, f32[32,1024]{1,0:T(8,128)} %maximum_maximum_fusion.map_ref.aux_ref, f32[32,1024]{1,0:T(8,128)} %maximum_maximum_fusion.map_ref.aux_ref), custom_call_target="tpu_custom_call" | custom-call | tf_op jit(solution)/shard_map/pallas_call | solution.py:257
  82.1 1.2 %copy.99 = f32[1024,32]{0,1:T(8,128)S(1)} copy(f32[1024,32]{1,0:T(8,128)} %bitcast.267) | data formatting | bytes 262144
  83.4 0.9 %slice_bitcast_fusion.1 = f32[1024,27]{0,1:T(8,128)S(1)} fusion(f32[32,1024]{1,0:T(8,128)} %get-tuple-element.4), kind=kLoop, calls=%fused_computation.68 | loop fusion | bytes 221184 | tf_op jit(solution)/shard_map/transpose | solution.py:302
  84.4 0.6 convolution_add_fusion.1
  84.9 0.6 convolution_add_fusion
  85.6 0.7 copy.86
  86.4 0.7 copy.87
  (65 shorter events, 1.9 us)
Async XLA Ops:
  3.5 5.9 %copy-start.7 = (s32[1024]{0:T(1024)}, s32[1024]{0:T(1024)S(1)}, u32[]{:S(2)}) copy-start(s32[1024]{0:T(1024)S(1)} %add_select_fusion) | copy-start | bytes 12292
  7.4 2.0 %copy-start.5 = (s32[1,1024]{1,0:T(1,128)S(1)}, s32[1,1024]{1,0:T(1,128)}, u32[]{:S(2)}) copy-start(s32[1,1024]{1,0:T(1,128)} %param.16) | copy-start | bytes 12292
  9.4 5.5 %copy-start.1 = (f32[1,256,128]{1,2,0:T(8,128)}, f32[1,256,128]{1,2,0:T(8,128)S(1)}, u32[]{:S(2)}) copy-start(f32[1,256,128]{1,2,0:T(8,128)S(1)} %get-tuple-element.17) | copy-start | bytes 393220
  9.5 5.4 %copy-start.2 = (f32[1,256,128]{1,2,0:T(8,128)}, f32[1,256,128]{1,2,0:T(8,128)S(1)}, u32[]{:S(2)}) copy-start(f32[1,256,128]{1,2,0:T(8,128)S(1)} %get-tuple-element.15) | copy-start | bytes 393220
  14.9 10.2 %copy-start.6 = (s32[2,256]{1,0:T(2,128)S(1)}, s32[2,256]{1,0:T(2,128)}, u32[]{:S(2)}) copy-start(s32[2,256]{1,0:T(2,128)} %param.14) | copy-start | bytes 6148
  14.9 12.0 %copy-start.4 = (s32[1,1024]{1,0:T(1,128)S(1)}, s32[1,1024]{1,0:T(1,128)}, u32[]{:S(2)}) copy-start(s32[1,1024]{1,0:T(1,128)} %param.18) | copy-start | bytes 12292
  14.9 38.7 %all-to-all-start = ((f32[128,1,4224]{2,1,0:T(1,128)}), f32[128,1,4224]{2,1,0:T(1,128)S(1)}, u32[]{:S(2)}, u32[]{:S(2)}) async-start(f32[128,1,4224]{2,1,0:T(1,128)} %bitcast.264), calls=%async_computation | async-start | bytes 4325376 | tf_op jit(solution)/shard_map/all_to_all | solution.py:439
  41.4 0.6 copy-start.3
  50.4 4.1 %copy-start.9 = (f32[32]{0:T(128)S(1)}, f32[32]{0:T(128)}, u32[]{:S(2)}) copy-start(f32[32]{0:T(128)} %pad.32.clone) | copy-start | bytes 388
  53.6 1.7 %copy-start = (f32[128,1,4224]{2,1,0:T(1,128)}, f32[128,1,4224]{2,1,0:T(1,128)S(1)}, u32[]{:S(2)}) copy-start(f32[128,1,4224]{2,1,0:T(1,128)S(1)} %all-to-all-done) | copy-start | bytes 6488068
  55.3 29.6 %copy-start.8 = (s32[1024]{0:T(1024)S(1)}, s32[1024]{0:T(1024)}, u32[]{:S(2)}) copy-start(s32[1024]{0:T(1024)} %copy-done.7) | copy-start | bytes 12292

commit v17 on v16

--- a/solution.py
+++ b/solution.py
@@ -186,7 +186,7 @@
     padded = jnp.concatenate([out_ref[...], jnp.zeros((128 - 32, chunk), jnp.float32)], axis=0)
     ret_ref[pl.ds(pl.multiple_of(step * peers, peers), peers)] = padded.T.reshape(peers, CAP, 128)
 
-    hold = jnp.minimum(2, last)
+    hold = jnp.minimum(4, last)
 
     @pl.when(step == hold)
     def _():

time: 87.9 us -> 86.4 us (0.983)
  Pallas kernels: 33.4 us -> 31.7 us
    pallas_call x2, Pallas kernels: 30.2 us -> 28.5 us  [pair_sums(): pl.pallas_call(functools.partial(_terms_kernel, from_cargo, n_band), out_...]
where the time goes in v17:
time: 86.4 us; the launch traced here: 85.4 us
  Pallas kernels  31.7 us (37%)
  local copies, waits for them, and re-layouts  21.2 us (25%)
  matrix products  12.6 us (15%)
  starting transfers between devices  10.2 us (12%)
  other arithmetic  8.71 us (10%)
  between operations  0.98 us (1%)
    pallas_call x2, Pallas kernels, pair_sums(): pl.pallas_call(functools.partial(_terms_kernel, from_cargo, n_band), out_...  28.5 us
    all_to_all x1, starting transfers between devices, local(): lax.all_to_all(cargo, axes, split_axis=0, concat_axis=0, tiled=True)  10.2 us
    dot_general x4, matrix products, pick_rows(): jnp.einsum('sb,cbk->csk', onehot, rows, precision=lax.Precision.HIGHEST)  9.72 us
    unnamed x31, local copies, waits for them, and re-layouts  5.07 us
    pallas_call x1, Pallas kernels, build_cargo(): pl.pallas_call(_cargo_kernel, out_shape=jax.ShapeDtypeStruct((slots // CA...  3.2 us
    gather x2, local copies, waits for them, and re-layouts, local(): frag_dirs[target_blocks // BF]  2.99 us
    dot_general x4, matrix products, frag_sums(): return jnp.dot(onehot.T, terms, precision=lax.Precision.HIGHEST)  2.38 us
    concatenate x2, other arithmetic, make_aux(): jnp.concatenate([dirs_a.T, dirs_b.T, valid[None, :], jnp.zeros((32 - 25,...  2.08 us
  transfers between devices with their start and end apart: 1, of which 0 were waited for; matrix products, arithmetic and copies ran while one was open for 29% of the time, Pallas kernels for 4%

profile of v17, /device:TPU:97, one launch (start us, length us, event | category | flops | bytes accessed | tf_op | source)
XLA Modules:
  0.0 85.4 jit_solution(9406614962958259541)
XLA Ops:
  0.6 0.8 slice_bitcast_fusion.5
  1.4 0.7 slice_multiply_fusion.4
  2.2 0.1 mul.431
  2.4 0.1 mul.439
  2.5 0.1 mul.399
  2.7 0.1 add.308
  2.8 0.7 add_select_fusion
  3.5 0.1 mul.435
  3.7 0.1 mul.427
  3.8 0.1 mul.412
  4.0 0.1 mul.406
  4.3 0.1 mul.416
  4.7 0.8 copy.76
  5.5 0.7 fusion.53
  6.3 0.1 reshape.1301
  6.4 1.1 %fusion.87 = (f32[256,1,128]{2,0,1:T(8,128)S(1)}, f32[256,1,128]{2,0,1:T(8,128)S(1)}, f32[256,1,128]{2,0,1:T(8,128)S(1)}) fusion(f32[256,3,128]{2,0,1:T(8,128)} %param.10), kind=kLoop, calls=%fused_computation.194 | loop fusion | bytes 786432 | tf_op jit(solution)/shard_map/slice | solution.py:58
  7.5 0.1 copy.92
  7.6 0.1 copy.93
  7.7 0.1 copy.94
  7.8 0.5 fusion.6
  8.3 0.2 copy.80
  8.5 0.2 reshape.1296
  8.7 0.6 concatenate.50.side_ref
  9.5 2.2 %convolution_bitcast_fusion.1.xa_ref = f32[3,1024,128]{2,1,0:T(8,128)} fusion(s32[1024]{0:T(1024)S(1)} %bitcast.277, f32[1,256,128]{1,2,0:T(8,128)S(1)} %get-tuple-element.15, f32[1,256,128]{1,2,0:T(8,128)S(1)} %get-tuple-element.17, f32[1,256,128]{1,2,0:T(8,128)S(1)} %get-tuple-element.19), kind=kOutput, calls=%fused_computation.4 | convolution fusion | flops 1208418304 | bytes 1970176 | tf_op jit(solution)/shard_map/sb,cbk->csk/dot_general | solution.py:389
  11.7 3.2 %shard_map.114 = f32[4224,128]{1,0:T(8,128)} custom-call(f32[3,1024,128]{2,1,0:T(8,128)} %convolution_bitcast_fusion.1.xa_ref, s32[1024,128]{1,0:T(8,128)} %bitcast.266, f32[128,128]{1,0:T(8,128)} %concatenate.50.side_ref), custom_call_target="tpu_custom_call" | custom-call | tf_op jit(solution)/shard_map/pallas_call | solution.py:294
  14.9 10.2 %all-to-all-start = ((f32[128,1,4224]{2,1,0:T(1,128)}), f32[128,1,4224]{2,1,0:T(1,128)S(1)}, u32[]{:S(2)}, u32[]{:S(2)}) async-start(f32[128,1,4224]{2,1,0:T(1,128)} %bitcast.264), calls=%async_computation | async-start | bytes 4325376 | tf_op jit(solution)/shard_map/all_to_all | solution.py:439
  25.1 0.6 fusion.90
  25.7 0.6 pad.31.clone
  26.3 0.6 pad.32.clone
  26.9 0.7 gather_fusion.1
  27.8 0.7 gather_fusion
  28.6 1.7 %fusion.86 = (f32[256,1,128]{2,0,1:T(8,128)S(1)}, f32[256,1,128]{2,0,1:T(8,128)S(1)}, f32[256,1,128]{2,0,1:T(8,128)}) fusion(f32[256,3,128]{2,0,1:T(8,128)} %param.11), kind=kLoop, calls=%fused_computation.193 | loop fusion | bytes 786432 | tf_op jit(solution)/shard_map/slice | solution.py:64
  30.3 0.1 copy.95
  30.4 0.1 copy.96
  30.5 1.0 %copy.97 = f32[256,1,128]{0,2,1:T(8,128)S(1)} copy(f32[256,1,128]{2,0,1:T(8,128)} %get-tuple-element.24) | data formatting | bytes 262144
  31.6 2.2 %convolution_bitcast_fusion.3.xa_ref = f32[3,256,128]{2,1,0:T(8,128)} fusion(f32[1,256,128]{1,2,0:T(8,128)} %copy-done.2, f32[1,256,128]{1,2,0:T(8,128)} %copy-done.1, f32[1,256,128]{1,2,0:T(8,128)S(1)} %get-tuple-element.19, s32[256]{0:T(256)} %bitcast.279), kind=kOutput, calls=%fused_computation.6 | convolution fusion | flops 302252032 | bytes 787456 | tf_op jit(solution)/shard_map/sb,cbk->csk/dot_general | solution.py:389
  33.8 2.1 %convolution_bitcast_fusion.2.tb_ref = f32[6,256,128]{2,1,0:T(8,128)} fusion(f32[6,256,128]{1,2,0:T(8,128)S(1)} %fusion.23, s32[256]{0:T(256)} %bitcast.281), kind=kOutput, calls=%fused_computation.5 | convolution fusion | flops 604045312 | bytes 1573888 | tf_op jit(solution)/shard_map/sb,cbk->csk/dot_general | solution.py:389
  35.9 1.3 %maximum_maximum_fusion.1.aux_ref = f32[32,256]{1,0:T(8,128)} fusion(f32[12,256]{1,0:T(8,128)S(1)} %bitcast.271, f32[12,256]{1,0:T(8,128)S(1)} %bitcast.272, f32[32]{0:T(128)} %pad.32.clone, f32[32]{0:T(128)} %pad.31.clone), kind=kLoop, calls=%fused_computation.93 | loop fusion | flops 24576 | bytes 57600 | tf_op jit(solution)/shard_map/concatenate | solution.py:401
  37.3 3.4 %shard_map.113 = f32[32,256]{1,0:T(8,128)} custom-call(f32[3,256,128]{2,1,0:T(8,128)} %convolution_bitcast_fusion.3.xa_ref, f32[6,256,128]{2,1,0:T(8,128)} %convolution_bitcast_fusion.2.tb_ref, s32[256,128]{1,0:T(8,128)} %map_ref.1, f32[32,256]{1,0:T(8,128)} %maximum_maximum_fusion.1.aux_ref), custom_call_target="tpu_custom_call" | custom-call | tf_op jit(solution)/shard_map/pallas_call | solution.py:257
  40.6 0.8 slice_bitcast_fusion.2
  41.4 0.6 fusion.89
  42.0 0.6 fusion.65
  42.6 2.8 %gather_fusion.2 = f32[1024,12]{1,0:T(8,128)S(1)} fusion(f32[8,12]{1,0:T(8,128)S(1)} %bitcast.262, s32[1024]{0:T(1024)S(1)} %broadcast_clamp_fusion), kind=kCustom, calls=%fused_computation.2 | custom fusion | bytes 102400 | tf_op jit(solution)/shard_map/gather | solution.py:458
  45.4 0.2 copy.84
  45.6 0.7 fusion.67
  46.3 0.7 and_select_fusion.4
  47.0 0.7 and_select_fusion.3
  47.7 0.7 slice_multiply_fusion.3
  48.4 0.7 slice_multiply_fusion.2
  49.1 0.3 fusion.49
  49.4 1.0 %convolution_add_fusion.2 = f32[8,18]{1,0:T(8,128)S(1)} fusion(f32[8,18]{1,0:T(8,128)S(1)} %fusion.49, s32[256]{0:T(256)S(1)} %and_select_fusion.3, f32[256,6]{0,1:T(8,128)S(1)} %fusion.67, f32[256,6]{0,1:T(8,128)S(1)} %fusion.66, f32[256,6]{0,1:T(8,128)} %fusion.65), kind=kOutput, calls=%fused_computation.9 | convolution fusion | flops 455824 | bytes 20608 | tf_op jit(solution)/shard_map/dot_general | solution.py:396
  50.4 3.2 %convolution_bitcast_fusion.tb_ref = f32[6,1024,128]{2,1,0:T(8,128)} fusion(f32[6,256,128]{1,2,0:T(8,128)S(1)} %fusion.23, s32[1024]{0:T(1024)S(1)} %bitcast.274), kind=kOutput, calls=%fused_computation.3 | convolution fusion | flops 2416181248 | bytes 3936256 | tf_op jit(solution)/shard_map/sb,cbk->csk/dot_general | solution.py:389
  53.6 0.2 slice_reduce_fusion.1
  53.8 0.2 reshape_squeeze.3
  54.0 0.4 slice_reduce_fusion
  54.3 0.2 copy.98
  54.5 0.7 maximum_maximum_fusion.map_ref.aux_ref
  55.3 25.2 %shard_map.115 = (f32[32,1024]{1,0:T(8,128)}, f32[128,8,128]{2,1,0:T(8,128)}) custom-call(f32[4224,128]{1,0:T(8,128)} %bitcast.263, f32[6,1024,128]{2,1,0:T(8,128)} %convolution_bitcast_fusion.tb_ref, f32[32,1024]{1,0:T(8,128)} %maximum_maximum_fusion.map_ref.aux_ref, f32[32,1024]{1,0:T(8,128)} %maximum_maximum_fusion.map_ref.aux_ref), custom_call_target="tpu_custom_call" | custom-call | tf_op jit(solution)/shard_map/pallas_call | solution.py:257
  80.5 1.2 %copy.99 = f32[1024,32]{0,1:T(8,128)S(1)} copy(f32[1024,32]{1,0:T(8,128)} %bitcast.267) | data formatting | bytes 262144
  81.7 0.9 %slice_bitcast_fusion.1 = f32[1024,27]{0,1:T(8,128)S(1)} fusion(f32[32,1024]{1,0:T(8,128)} %get-tuple-element.4), kind=kLoop, calls=%fused_computation.68 | loop fusion | bytes 221184 | tf_op jit(solution)/shard_map/transpose | solution.py:302
  82.7 0.6 convolution_add_fusion.1
  83.3 0.6 convolution_add_fusion
  84.0 0.7 copy.86
  84.7 0.7 copy.87
  (65 shorter events, 1.9 us)
Async XLA Ops:
  3.5 5.9 %copy-start.7 = (s32[1024]{0:T(1024)}, s32[1024]{0:T(1024)S(1)}, u32[]{:S(2)}) copy-start(s32[1024]{0:T(1024)S(1)} %add_select_fusion) | copy-start | bytes 12292
  7.4 2.0 %copy-start.5 = (s32[1,1024]{1,0:T(1,128)S(1)}, s32[1,1024]{1,0:T(1,128)}, u32[]{:S(2)}) copy-start(s32[1,1024]{1,0:T(1,128)} %param.16) | copy-start | bytes 12292
  9.4 5.5 %copy-start.1 = (f32[1,256,128]{1,2,0:T(8,128)}, f32[1,256,128]{1,2,0:T(8,128)S(1)}, u32[]{:S(2)}) copy-start(f32[1,256,128]{1,2,0:T(8,128)S(1)} %get-tuple-element.17) | copy-start | bytes 393220
  9.5 5.4 %copy-start.2 = (f32[1,256,128]{1,2,0:T(8,128)}, f32[1,256,128]{1,2,0:T(8,128)S(1)}, u32[]{:S(2)}) copy-start(f32[1,256,128]{1,2,0:T(8,128)S(1)} %get-tuple-element.15) | copy-start | bytes 393220
  14.9 10.2 %copy-start.6 = (s32[2,256]{1,0:T(2,128)S(1)}, s32[2,256]{1,0:T(2,128)}, u32[]{:S(2)}) copy-start(s32[2,256]{1,0:T(2,128)} %param.14) | copy-start | bytes 6148
  14.9 12.0 %copy-start.4 = (s32[1,1024]{1,0:T(1,128)S(1)}, s32[1,1024]{1,0:T(1,128)}, u32[]{:S(2)}) copy-start(s32[1,1024]{1,0:T(1,128)} %param.18) | copy-start | bytes 12292
  14.9 38.7 %all-to-all-start = ((f32[128,1,4224]{2,1,0:T(1,128)}), f32[128,1,4224]{2,1,0:T(1,128)S(1)}, u32[]{:S(2)}, u32[]{:S(2)}) async-start(f32[128,1,4224]{2,1,0:T(1,128)} %bitcast.264), calls=%async_computation | async-start | bytes 4325376 | tf_op jit(solution)/shard_map/all_to_all | solution.py:439
  41.4 0.6 copy-start.3
  50.4 4.1 %copy-start.9 = (f32[32]{0:T(128)S(1)}, f32[32]{0:T(128)}, u32[]{:S(2)}) copy-start(f32[32]{0:T(128)} %pad.32.clone) | copy-start | bytes 388
  53.6 1.7 %copy-start = (f32[128,1,4224]{2,1,0:T(1,128)}, f32[128,1,4224]{2,1,0:T(1,128)S(1)}, u32[]{:S(2)}) copy-start(f32[128,1,4224]{2,1,0:T(1,128)S(1)} %all-to-all-done) | copy-start | bytes 6488068
  55.3 28.0 %copy-start.8 = (s32[1024]{0:T(1024)S(1)}, s32[1024]{0:T(1024)}, u32[]{:S(2)}) copy-start(s32[1024]{0:T(1024)} %copy-done.7) | copy-start | bytes 12292

commit v18 on v17

--- a/solution.py
+++ b/solution.py
@@ -186,7 +186,7 @@
     padded = jnp.concatenate([out_ref[...], jnp.zeros((128 - 32, chunk), jnp.float32)], axis=0)
     ret_ref[pl.ds(pl.multiple_of(step * peers, peers), peers)] = padded.T.reshape(peers, CAP, 128)
 
-    hold = jnp.minimum(4, last)
+    hold = jnp.minimum(6, last)
 
     @pl.when(step == hold)
     def _():

time: 86.4 us -> 87.9 us (1.017)
  the two profiles are of different devices: /device:TPU:97 before, /device:TPU:1 now
where the time goes in v18:
time: 87.9 us; the launch traced here: 86.2 us
  Pallas kernels  28.5 us (32%)
  local copies, waits for them, and re-layouts  21.2 us (24%)
  matrix products  12.6 us (14%)
  starting transfers between devices  11.5 us (13%)
  other arithmetic  8.71 us (10%)
  waiting for transfers between devices  2.71 us (3%)
  between operations  0.98 us (1%)
    pallas_call x2, Pallas kernels, pair_sums(): pl.pallas_call(functools.partial(_terms_kernel, from_cargo, n_band), out_...  25.3 us
    all_to_all x1, starting transfers between devices, local(): lax.all_to_all(cargo, axes, split_axis=0, concat_axis=0, tiled=True)  11.5 us
    dot_general x4, matrix products, pick_rows(): jnp.einsum('sb,cbk->csk', onehot, rows, precision=lax.Precision.HIGHEST)  9.71 us
    unnamed x31, local copies, waits for them, and re-layouts  5.07 us
    pallas_call x1, Pallas kernels, build_cargo(): pl.pallas_call(_cargo_kernel, out_shape=jax.ShapeDtypeStruct((slots // CA...  3.2 us
    gather x2, local copies, waits for them, and re-layouts, local(): frag_dirs[target_blocks // BF]  2.99 us
    all_to_all x1, waiting for transfers between devices, local(): lax.all_to_all(cargo, axes, split_axis=0, concat_axis=0, tiled=True)  2.71 us
    dot_general x4, matrix products, frag_sums(): return jnp.dot(onehot.T, terms, precision=lax.Precision.HIGHEST)  2.38 us
  transfers between devices with their start and end apart: 1, of which 1 were waited for; matrix products, arithmetic and copies ran while one was open for 29% of the time, Pallas kernels for 4%

profile of v18, /device:TPU:1, one launch (start us, length us, event | category | flops | bytes accessed | tf_op | source)
XLA Modules:
  0.0 86.2 jit_solution(3683725206942932576)
XLA Ops:
  0.6 0.8 slice_bitcast_fusion.5
  1.4 0.7 slice_multiply_fusion.4
  2.2 0.1 mul.431
  2.4 0.1 mul.439
  2.5 0.1 mul.399
  2.7 0.1 add.308
  2.8 0.7 add_select_fusion
  3.5 0.1 mul.435
  3.8 0.1 mul.412
  4.3 0.1 mul.416
  4.7 0.8 copy.76
  5.5 0.1 reshape.1295
  5.5 0.7 fusion.53
  6.3 0.1 reshape.1301
  6.4 1.1 %fusion.87 = (f32[256,1,128]{2,0,1:T(8,128)S(1)}, f32[256,1,128]{2,0,1:T(8,128)S(1)}, f32[256,1,128]{2,0,1:T(8,128)S(1)}) fusion(f32[256,3,128]{2,0,1:T(8,128)} %param.10), kind=kLoop, calls=%fused_computation.194 | loop fusion | bytes 786432 | tf_op jit(solution)/shard_map/slice | solution.py:58
  7.5 0.1 copy.92
  7.6 0.1 copy.93
  7.7 0.1 copy.94
  7.8 0.5 fusion.6
  8.3 0.2 copy.80
  8.5 0.2 reshape.1296
  8.7 0.6 concatenate.50.side_ref
  9.5 2.2 %convolution_bitcast_fusion.1.xa_ref = f32[3,1024,128]{2,1,0:T(8,128)} fusion(s32[1024]{0:T(1024)S(1)} %bitcast.277, f32[1,256,128]{1,2,0:T(8,128)S(1)} %get-tuple-element.15, f32[1,256,128]{1,2,0:T(8,128)S(1)} %get-tuple-element.17, f32[1,256,128]{1,2,0:T(8,128)S(1)} %get-tuple-element.19), kind=kOutput, calls=%fused_computation.4 | convolution fusion | flops 1208418304 | bytes 1970176 | tf_op jit(solution)/shard_map/sb,cbk->csk/dot_general | solution.py:389
  11.7 3.2 %shard_map.114 = f32[4224,128]{1,0:T(8,128)} custom-call(f32[3,1024,128]{2,1,0:T(8,128)} %convolution_bitcast_fusion.1.xa_ref, s32[1024,128]{1,0:T(8,128)} %bitcast.266, f32[128,128]{1,0:T(8,128)} %concatenate.50.side_ref), custom_call_target="tpu_custom_call" | custom-call | tf_op jit(solution)/shard_map/pallas_call | solution.py:294
  14.9 11.5 %all-to-all-start = ((f32[128,1,4224]{2,1,0:T(1,128)}), f32[128,1,4224]{2,1,0:T(1,128)S(1)}, u32[]{:S(2)}, u32[]{:S(2)}) async-start(f32[128,1,4224]{2,1,0:T(1,128)} %bitcast.264), calls=%async_computation | async-start | bytes 4325376 | tf_op jit(solution)/shard_map/all_to_all | solution.py:439
  26.4 0.6 fusion.90
  27.0 0.6 pad.31.clone
  27.6 0.6 pad.32.clone
  28.3 0.7 gather_fusion.1
  29.1 0.7 gather_fusion
  29.9 1.7 %fusion.86 = (f32[256,1,128]{2,0,1:T(8,128)S(1)}, f32[256,1,128]{2,0,1:T(8,128)S(1)}, f32[256,1,128]{2,0,1:T(8,128)}) fusion(f32[256,3,128]{2,0,1:T(8,128)} %param.11), kind=kLoop, calls=%fused_computation.193 | loop fusion | bytes 786432 | tf_op jit(solution)/shard_map/slice | solution.py:64
  31.6 0.1 copy.95
  31.7 0.1 copy.96
  31.8 1.0 %copy.97 = f32[256,1,128]{0,2,1:T(8,128)S(1)} copy(f32[256,1,128]{2,0,1:T(8,128)} %get-tuple-element.24) | data formatting | bytes 262144
  32.9 2.2 %convolution_bitcast_fusion.3.xa_ref = f32[3,256,128]{2,1,0:T(8,128)} fusion(f32[1,256,128]{1,2,0:T(8,128)} %copy-done.2, f32[1,256,128]{1,2,0:T(8,128)} %copy-done.1, f32[1,256,128]{1,2,0:T(8,128)S(1)} %get-tuple-element.19, s32[256]{0:T(256)} %bitcast.279), kind=kOutput, calls=%fused_computation.6 | convolution fusion | flops 302252032 | bytes 787456 | tf_op jit(solution)/shard_map/sb,cbk->csk/dot_general | solution.py:389
  35.1 2.1 %convolution_bitcast_fusion.2.tb_ref = f32[6,256,128]{2,1,0:T(8,128)} fusion(f32[6,256,128]{1,2,0:T(8,128)S(1)} %fusion.23, s32[256]{0:T(256)} %bitcast.281), kind=kOutput, calls=%fused_computation.5 | convolution fusion | flops 604045312 | bytes 1573888 | tf_op jit(solution)/shard_map/sb,cbk->csk/dot_general | solution.py:389
  37.2 1.3 %maximum_maximum_fusion.1.aux_ref = f32[32,256]{1,0:T(8,128)} fusion(f32[12,256]{1,0:T(8,128)S(1)} %bitcast.271, f32[12,256]{1,0:T(8,128)S(1)} %bitcast.272, f32[32]{0:T(128)} %pad.32.clone, f32[32]{0:T(128)} %pad.31.clone), kind=kLoop, calls=%fused_computation.93 | loop fusion | flops 24576 | bytes 57600 | tf_op jit(solution)/shard_map/concatenate | solution.py:401
  38.6 3.4 %shard_map.113 = f32[32,256]{1,0:T(8,128)} custom-call(f32[3,256,128]{2,1,0:T(8,128)} %convolution_bitcast_fusion.3.xa_ref, f32[6,256,128]{2,1,0:T(8,128)} %convolution_bitcast_fusion.2.tb_ref, s32[256,128]{1,0:T(8,128)} %map_ref.1, f32[32,256]{1,0:T(8,128)} %maximum_maximum_fusion.1.aux_ref), custom_call_target="tpu_custom_call" | custom-call | tf_op jit(solution)/shard_map/pallas_call | solution.py:257
  41.9 0.8 slice_bitcast_fusion.2
  42.7 0.6 fusion.89
  43.3 0.6 fusion.65
  43.9 2.8 %gather_fusion.2 = f32[1024,12]{1,0:T(8,128)S(1)} fusion(f32[8,12]{1,0:T(8,128)S(1)} %bitcast.262, s32[1024]{0:T(1024)S(1)} %broadcast_clamp_fusion), kind=kCustom, calls=%fused_computation.2 | custom fusion | bytes 102400 | tf_op jit(solution)/shard_map/gather | solution.py:458
  46.7 0.2 copy.84
  46.9 0.7 fusion.67
  47.6 0.7 and_select_fusion.4
  48.3 0.7 and_select_fusion.3
  49.0 0.7 slice_multiply_fusion.3
  49.7 0.7 slice_multiply_fusion.2
  50.4 0.3 fusion.49
  50.7 1.0 %convolution_add_fusion.2 = f32[8,18]{1,0:T(8,128)S(1)} fusion(f32[8,18]{1,0:T(8,128)S(1)} %fusion.49, s32[256]{0:T(256)S(1)} %and_select_fusion.3, f32[256,6]{0,1:T(8,128)S(1)} %fusion.67, f32[256,6]{0,1:T(8,128)S(1)} %fusion.66, f32[256,6]{0,1:T(8,128)} %fusion.65), kind=kOutput, calls=%fused_computation.9 | convolution fusion | flops 455824 | bytes 20608 | tf_op jit(solution)/shard_map/dot_general | solution.py:396
  51.7 3.2 %convolution_bitcast_fusion.tb_ref = f32[6,1024,128]{2,1,0:T(8,128)} fusion(f32[6,256,128]{1,2,0:T(8,128)S(1)} %fusion.23, s32[1024]{0:T(1024)S(1)} %bitcast.274), kind=kOutput, calls=%fused_computation.3 | convolution fusion | flops 2416181248 | bytes 3936256 | tf_op jit(solution)/shard_map/sb,cbk->csk/dot_general | solution.py:389
  54.9 2.7 %all-to-all-done = f32[128,1,4224]{2,1,0:T(1,128)S(1)} async-done(((f32[128,1,4224]{2,1,0:T(1,128)}), f32[128,1,4224]{2,1,0:T(1,128)S(1)}, u32[]{:S(2)}, u32[]{:S(2)}) %all-to-all-start) | async-done | bytes 2162720 | tf_op jit(solution)/shard_map/all_to_all | solution.py:439
  57.6 0.2 slice_reduce_fusion.1
  57.8 0.2 reshape_squeeze.3
  58.0 0.4 slice_reduce_fusion
  58.4 0.2 copy.98
  58.5 0.7 maximum_maximum_fusion.map_ref.aux_ref
  59.3 22.0 %shard_map.115 = (f32[32,1024]{1,0:T(8,128)}, f32[128,8,128]{2,1,0:T(8,128)}) custom-call(f32[4224,128]{1,0:T(8,128)} %bitcast.263, f32[6,1024,128]{2,1,0:T(8,128)} %convolution_bitcast_fusion.tb_ref, f32[32,1024]{1,0:T(8,128)} %maximum_maximum_fusion.map_ref.aux_ref, f32[32,1024]{1,0:T(8,128)} %maximum_maximum_fusion.map_ref.aux_ref), custom_call_target="tpu_custom_call" | custom-call | tf_op jit(solution)/shard_map/pallas_call | solution.py:257
  81.3 1.2 %copy.99 = f32[1024,32]{0,1:T(8,128)S(1)} copy(f32[1024,32]{1,0:T(8,128)} %bitcast.267) | data formatting | bytes 262144
  82.5 0.9 %slice_bitcast_fusion.1 = f32[1024,27]{0,1:T(8,128)S(1)} fusion(f32[32,1024]{1,0:T(8,128)} %get-tuple-element.4), kind=kLoop, calls=%fused_computation.68 | loop fusion | bytes 221184 | tf_op jit(solution)/shard_map/transpose | solution.py:302
  83.5 0.6 convolution_add_fusion.1
  84.1 0.6 convolution_add_fusion
  84.8 0.7 copy.86
  85.5 0.7 copy.87
  (65 shorter events, 2.0 us)
Async XLA Ops:
  3.5 5.9 %copy-start.7 = (s32[1024]{0:T(1024)}, s32[1024]{0:T(1024)S(1)}, u32[]{:S(2)}) copy-start(s32[1024]{0:T(1024)S(1)} %add_select_fusion) | copy-start | bytes 12292
  7.4 2.0 %copy-start.5 = (s32[1,1024]{1,0:T(1,128)S(1)}, s32[1,1024]{1,0:T(1,128)}, u32[]{:S(2)}) copy-start(s32[1,1024]{1,0:T(1,128)} %param.16) | copy-start | bytes 12292
  9.4 5.5 %copy-start.1 = (f32[1,256,128]{1,2,0:T(8,128)}, f32[1,256,128]{1,2,0:T(8,128)S(1)}, u32[]{:S(2)}) copy-start(f32[1,256,128]{1,2,0:T(8,128)S(1)} %get-tuple-element.17) | copy-start | bytes 393220
  9.5 5.4 %copy-start.2 = (f32[1,256,128]{1,2,0:T(8,128)}, f32[1,256,128]{1,2,0:T(8,128)S(1)}, u32[]{:S(2)}) copy-start(f32[1,256,128]{1,2,0:T(8,128)S(1)} %get-tuple-element.15) | copy-start | bytes 393220
  14.9 11.5 %copy-start.6 = (s32[2,256]{1,0:T(2,128)S(1)}, s32[2,256]{1,0:T(2,128)}, u32[]{:S(2)}) copy-start(s32[2,256]{1,0:T(2,128)} %param.14) | copy-start | bytes 6148
  14.9 13.3 %copy-start.4 = (s32[1,1024]{1,0:T(1,128)S(1)}, s32[1,1024]{1,0:T(1,128)}, u32[]{:S(2)}) copy-start(s32[1,1024]{1,0:T(1,128)} %param.18) | copy-start | bytes 12292
  14.9 42.7 %all-to-all-start = ((f32[128,1,4224]{2,1,0:T(1,128)}), f32[128,1,4224]{2,1,0:T(1,128)S(1)}, u32[]{:S(2)}, u32[]{:S(2)}) async-start(f32[128,1,4224]{2,1,0:T(1,128)} %bitcast.264), calls=%async_computation | async-start | bytes 4325376 | tf_op jit(solution)/shard_map/all_to_all | solution.py:439
  42.7 0.6 copy-start.3
  51.7 6.8 %copy-start.9 = (f32[32]{0:T(128)S(1)}, f32[32]{0:T(128)}, u32[]{:S(2)}) copy-start(f32[32]{0:T(128)} %pad.32.clone) | copy-start | bytes 388
  57.6 1.7 %copy-start = (f32[128,1,4224]{2,1,0:T(1,128)}, f32[128,1,4224]{2,1,0:T(1,128)S(1)}, u32[]{:S(2)}) copy-start(f32[128,1,4224]{2,1,0:T(1,128)S(1)} %all-to-all-done) | copy-start | bytes 6488068
  59.3 24.8 %copy-start.8 = (s32[1024]{0:T(1024)S(1)}, s32[1024]{0:T(1024)}, u32[]{:S(2)}) copy-start(s32[1024]{0:T(1024)} %copy-done.7) | copy-start | bytes 12292

commit v19 on v17

--- a/solution.py
+++ b/solution.py
@@ -459,13 +459,14 @@
         n_band,
     )
     unused, remote_b = split_terms(out_r)
-    returned, unused = split_terms(back.reshape(peers * CAP, 128)[:, 0:32].T)
+    back_sums = frag_sums(source_blocks, back.reshape(peers * CAP, 128), frag_count)
+    returned = jnp.concatenate([back_sums[:, 0:6] * (1.0 / 128), back_sums[:, 6:18] * (1.0 / 4096)], axis=1)
 
     totals = frag_sums(src_l, local_a, frag_count) + frag_sums(tgt_l, local_b, frag_count)
     totals = (
         totals
         + frag_sums(target_blocks, remote_b, frag_count)
-        + frag_sums(source_blocks, returned, frag_count)
+        + returned
     )
     gradient = totals[:, 0:6].T
     hess_products = totals[:, 6:18].T.reshape(2, 6, frag_count)

time: 86.4 us -> 87.4 us (1.012)
  the two profiles are of different devices: /device:TPU:97 before, /device:TPU:1 now
where the time goes in v19:
time: 87.4 us; the launch traced here: 85.7 us
  Pallas kernels  28 us (32%)
  local copies, waits for them, and re-layouts  20.1 us (23%)
  matrix products  13.7 us (16%)
  starting transfers between devices  11.5 us (13%)
  other arithmetic  10.1 us (12%)
  waiting for transfers between devices  1.31 us (1%)
  between operations  0.96 us (1%)
    pallas_call x2, Pallas kernels, pair_sums(): pl.pallas_call(functools.partial(_terms_kernel, from_cargo, n_band), out_...  24.8 us
    all_to_all x1, starting transfers between devices, local(): lax.all_to_all(cargo, axes, split_axis=0, concat_axis=0, tiled=True)  11.5 us
    dot_general x4, matrix products, pick_rows(): jnp.einsum('sb,cbk->csk', onehot, rows, precision=lax.Precision.HIGHEST)  9.71 us
    unnamed x28, local copies, waits for them, and re-layouts  3.86 us
    dot_general x4, matrix products, frag_sums(): return jnp.dot(onehot.T, terms, precision=lax.Precision.HIGHEST)  3.54 us
    pallas_call x1, Pallas kernels, build_cargo(): pl.pallas_call(_cargo_kernel, out_shape=jax.ShapeDtypeStruct((slots // CA...  3.2 us
    gather x2, local copies, waits for them, and re-layouts, local(): frag_dirs[target_blocks // BF]  2.99 us
    concatenate x2, other arithmetic, make_aux(): jnp.concatenate([dirs_a.T, dirs_b.T, valid[None, :], jnp.zeros((32 - 25,...  2.08 us
  transfers between devices with their start and end apart: 1, of which 1 were waited for; matrix products, arithmetic and copies ran while one was open for 31% of the time, Pallas kernels for 4%

profile of v19, /device:TPU:1, one launch (start us, length us, event | category | flops | bytes accessed | tf_op | source)
XLA Modules:
  0.0 85.7 jit_solution(15128914891255130821)
XLA Ops:
  0.6 0.8 slice_bitcast_fusion.4
  1.4 0.7 slice_multiply_fusion.4
  2.2 0.1 mul.437
  2.4 0.1 mul.445
  2.5 0.1 mul.405
  2.7 0.1 add.308
  2.8 0.7 add_select_fusion
  3.5 0.1 mul.441
  4.0 0.1 mul.412
  4.7 0.8 copy.73
  5.5 0.1 reshape.1295
  5.5 0.7 fusion.51
  6.3 0.1 reshape.1301
  6.4 1.1 %fusion.84 = (f32[256,1,128]{2,0,1:T(8,128)S(1)}, f32[256,1,128]{2,0,1:T(8,128)S(1)}, f32[256,1,128]{2,0,1:T(8,128)S(1)}) fusion(f32[256,3,128]{2,0,1:T(8,128)} %param.10), kind=kLoop, calls=%fused_computation.190 | loop fusion | bytes 786432 | tf_op jit(solution)/shard_map/slice | solution.py:58
  7.5 0.1 copy.88
  7.6 0.1 copy.89
  7.7 0.1 copy.90
  7.8 0.5 fusion.8
  8.3 0.2 copy.77
  8.5 0.2 reshape.1296
  8.7 0.6 concatenate.50.side_ref
  9.5 2.2 %convolution_bitcast_fusion.1.xa_ref = f32[3,1024,128]{2,1,0:T(8,128)} fusion(s32[1024]{0:T(1024)S(1)} %bitcast.273, f32[1,256,128]{1,2,0:T(8,128)S(1)} %get-tuple-element.15, f32[1,256,128]{1,2,0:T(8,128)S(1)} %get-tuple-element.17, f32[1,256,128]{1,2,0:T(8,128)S(1)} %get-tuple-element.19), kind=kOutput, calls=%fused_computation.4 | convolution fusion | flops 1208418304 | bytes 1970176 | tf_op jit(solution)/shard_map/sb,cbk->csk/dot_general | solution.py:389
  11.7 3.2 %shard_map.114 = f32[4224,128]{1,0:T(8,128)} custom-call(f32[3,1024,128]{2,1,0:T(8,128)} %convolution_bitcast_fusion.1.xa_ref, s32[1024,128]{1,0:T(8,128)} %bitcast.264, f32[128,128]{1,0:T(8,128)} %concatenate.50.side_ref), custom_call_target="tpu_custom_call" | custom-call | tf_op jit(solution)/shard_map/pallas_call | solution.py:294
  14.9 11.5 %all-to-all-start = ((f32[128,1,4224]{2,1,0:T(1,128)}), f32[128,1,4224]{2,1,0:T(1,128)S(1)}, u32[]{:S(2)}, u32[]{:S(2)}) async-start(f32[128,1,4224]{2,1,0:T(1,128)} %bitcast.262), calls=%async_computation | async-start | bytes 4325376 | tf_op jit(solution)/shard_map/all_to_all | solution.py:439
  26.4 0.6 fusion.87
  27.0 0.6 pad.31.clone
  27.6 0.7 pad.32.clone
  28.3 0.7 gather_fusion.1
  29.1 0.7 gather_fusion
  30.0 1.7 %fusion.83 = (f32[256,1,128]{2,0,1:T(8,128)S(1)}, f32[256,1,128]{2,0,1:T(8,128)S(1)}, f32[256,1,128]{2,0,1:T(8,128)}) fusion(f32[256,3,128]{2,0,1:T(8,128)} %param.11), kind=kLoop, calls=%fused_computation.189 | loop fusion | bytes 786432 | tf_op jit(solution)/shard_map/slice | solution.py:64
  31.7 0.1 copy.91
  31.8 0.1 copy.92
  31.9 1.0 %copy.93 = f32[256,1,128]{0,2,1:T(8,128)S(1)} copy(f32[256,1,128]{2,0,1:T(8,128)} %get-tuple-element.24) | data formatting | bytes 262144
  32.9 0.7 fusion.22
  33.7 2.2 %convolution_bitcast_fusion.3.xa_ref = f32[3,256,128]{2,1,0:T(8,128)} fusion(f32[1,256,128]{1,2,0:T(8,128)} %copy-done.2, f32[1,256,128]{1,2,0:T(8,128)} %copy-done.1, f32[1,256,128]{1,2,0:T(8,128)S(1)} %get-tuple-element.19, s32[256]{0:T(256)} %bitcast.275), kind=kOutput, calls=%fused_computation.6 | convolution fusion | flops 302252032 | bytes 787456 | tf_op jit(solution)/shard_map/sb,cbk->csk/dot_general | solution.py:389
  35.9 2.1 %convolution_bitcast_fusion.2.tb_ref = f32[6,256,128]{2,1,0:T(8,128)} fusion(f32[6,256,128]{1,2,0:T(8,128)S(1)} %fusion.24, s32[256]{0:T(256)} %bitcast.277), kind=kOutput, calls=%fused_computation.5 | convolution fusion | flops 604045312 | bytes 1573888 | tf_op jit(solution)/shard_map/sb,cbk->csk/dot_general | solution.py:389
  38.0 1.4 %maximum_maximum_fusion.1.aux_ref = f32[32,256]{1,0:T(8,128)} fusion(f32[12,256]{1,0:T(8,128)S(1)} %bitcast.267, f32[12,256]{1,0:T(8,128)S(1)} %bitcast.268, f32[32]{0:T(128)} %pad.32.clone, f32[32]{0:T(128)} %pad.31.clone), kind=kLoop, calls=%fused_computation.88 | loop fusion | flops 24576 | bytes 57600 | tf_op jit(solution)/shard_map/concatenate | solution.py:401
  39.3 3.4 %shard_map.113 = f32[32,256]{1,0:T(8,128)} custom-call(f32[3,256,128]{2,1,0:T(8,128)} %convolution_bitcast_fusion.3.xa_ref, f32[6,256,128]{2,1,0:T(8,128)} %convolution_bitcast_fusion.2.tb_ref, s32[256,128]{1,0:T(8,128)} %map_ref.1, f32[32,256]{1,0:T(8,128)} %maximum_maximum_fusion.1.aux_ref), custom_call_target="tpu_custom_call" | custom-call | tf_op jit(solution)/shard_map/pallas_call | solution.py:257
  42.7 0.8 slice_bitcast_fusion.1
  43.4 0.6 fusion.86
  44.1 0.6 fusion.63
  44.7 2.8 %gather_fusion.2 = f32[1024,12]{1,0:T(8,128)S(1)} fusion(f32[8,12]{1,0:T(8,128)S(1)} %bitcast.260, s32[1024]{0:T(1024)S(1)} %broadcast_clamp_fusion), kind=kCustom, calls=%fused_computation.2 | custom fusion | bytes 102400 | tf_op jit(solution)/shard_map/gather | solution.py:458
  47.5 0.2 copy.81
  47.7 0.7 fusion.65
  48.4 0.7 fusion.64
  49.1 0.7 and_select_fusion.4
  49.7 0.7 and_select_fusion.3
  50.4 0.7 slice_multiply_fusion.1
  51.1 0.7 slice_multiply_fusion
  51.8 0.3 fusion.47
  52.1 1.0 %convolution_add_fusion.1 = f32[8,18]{1,0:T(8,128)S(1)} fusion(f32[8,18]{1,0:T(8,128)S(1)} %fusion.47, s32[256]{0:T(256)S(1)} %and_select_fusion.3, f32[256,6]{0,1:T(8,128)S(1)} %fusion.65, f32[256,6]{0,1:T(8,128)S(1)} %fusion.64, f32[256,6]{0,1:T(8,128)} %fusion.63), kind=kOutput, calls=%fused_computation.8 | convolution fusion | flops 455824 | bytes 20608 | tf_op jit(solution)/shard_map/dot_general | solution.py:396
  53.1 3.2 %convolution_bitcast_fusion.tb_ref = f32[6,1024,128]{2,1,0:T(8,128)} fusion(f32[6,256,128]{1,2,0:T(8,128)S(1)} %fusion.24, s32[1024]{0:T(1024)S(1)} %bitcast.270), kind=kOutput, calls=%fused_computation.3 | convolution fusion | flops 2416181248 | bytes 3936256 | tf_op jit(solution)/shard_map/sb,cbk->csk/dot_general | solution.py:389
  56.3 1.3 %all-to-all-done = f32[128,1,4224]{2,1,0:T(1,128)S(1)} async-done(((f32[128,1,4224]{2,1,0:T(1,128)}), f32[128,1,4224]{2,1,0:T(1,128)S(1)}, u32[]{:S(2)}, u32[]{:S(2)}) %all-to-all-start) | async-done | bytes 2162720 | tf_op jit(solution)/shard_map/all_to_all | solution.py:439
  57.6 0.2 slice_reduce_fusion.1
  57.8 0.2 reshape_squeeze.3
  58.0 0.4 slice_reduce_fusion
  58.4 0.2 copy.94
  58.5 0.7 maximum_maximum_fusion.map_ref.aux_ref
  59.3 21.5 %shard_map.115 = (f32[32,1024]{1,0:T(8,128)}, f32[128,8,128]{2,1,0:T(8,128)}) custom-call(f32[4224,128]{1,0:T(8,128)} %bitcast.261, f32[6,1024,128]{2,1,0:T(8,128)} %convolution_bitcast_fusion.tb_ref, f32[32,1024]{1,0:T(8,128)} %maximum_maximum_fusion.map_ref.aux_ref, f32[32,1024]{1,0:T(8,128)} %maximum_maximum_fusion.map_ref.aux_ref), custom_call_target="tpu_custom_call" | custom-call | tf_op jit(solution)/shard_map/pallas_call | solution.py:257
  80.7 1.7 %fusion.5 = f32[8,128]{1,0:T(8,128)S(1)} fusion(f32[128,8,128]{2,1,0:T(8,128)} %get-tuple-element.5, s32[1024]{0:T(1024)S(1)} %add_select_fusion), kind=kOutput, calls=%fused_computation.15 | convolution fusion | flops 12591104 | bytes 532480 | tf_op jit(solution)/shard_map/dot_general | solution.py:396
  82.6 0.9 %slice_bitcast_fusion = f32[1024,27]{0,1:T(8,128)S(1)} fusion(f32[32,1024]{1,0:T(8,128)} %get-tuple-element.4), kind=kLoop, calls=%fused_computation.68 | loop fusion | bytes 221184 | tf_op jit(solution)/shard_map/transpose | solution.py:302
  83.6 0.6 fusion
  84.2 0.7 copy.82
  85.0 0.7 copy.83
  (61 shorter events, 2.1 us)
Async XLA Ops:
  4.4 5.0 %copy-start.6 = (f32[256]{0:T(256)}, f32[256]{0:T(256)S(1)}, u32[]{:S(2)}) copy-start(f32[256]{0:T(256)S(1)} %mul.422) | copy-start | bytes 3076
  7.4 2.0 %copy-start.5 = (s32[1,1024]{1,0:T(1,128)S(1)}, s32[1,1024]{1,0:T(1,128)}, u32[]{:S(2)}) copy-start(s32[1,1024]{1,0:T(1,128)} %param.16) | copy-start | bytes 12292
  9.4 5.5 %copy-start.1 = (f32[1,256,128]{1,2,0:T(8,128)}, f32[1,256,128]{1,2,0:T(8,128)S(1)}, u32[]{:S(2)}) copy-start(f32[1,256,128]{1,2,0:T(8,128)S(1)} %get-tuple-element.17) | copy-start | bytes 393220
  9.4 5.4 %copy-start.2 = (f32[1,256,128]{1,2,0:T(8,128)}, f32[1,256,128]{1,2,0:T(8,128)S(1)}, u32[]{:S(2)}) copy-start(f32[1,256,128]{1,2,0:T(8,128)S(1)} %get-tuple-element.15) | copy-start | bytes 393220
  14.9 11.5 %copy-start.7 = (s32[2,256]{1,0:T(2,128)S(1)}, s32[2,256]{1,0:T(2,128)}, u32[]{:S(2)}) copy-start(s32[2,256]{1,0:T(2,128)} %param.14) | copy-start | bytes 6148
  14.9 13.4 %copy-start.4 = (s32[1,1024]{1,0:T(1,128)S(1)}, s32[1,1024]{1,0:T(1,128)}, u32[]{:S(2)}) copy-start(s32[1,1024]{1,0:T(1,128)} %param.18) | copy-start | bytes 12292
  14.9 42.7 %all-to-all-start = ((f32[128,1,4224]{2,1,0:T(1,128)}), f32[128,1,4224]{2,1,0:T(1,128)S(1)}, u32[]{:S(2)}, u32[]{:S(2)}) async-start(f32[128,1,4224]{2,1,0:T(1,128)} %bitcast.262), calls=%async_computation | async-start | bytes 4325376 | tf_op jit(solution)/shard_map/all_to_all | solution.py:439
  43.4 0.6 copy-start.3
  53.1 5.5 %copy-start.8 = (f32[32]{0:T(128)S(1)}, f32[32]{0:T(128)}, u32[]{:S(2)}) copy-start(f32[32]{0:T(128)} %pad.32.clone) | copy-start | bytes 388
  57.6 1.7 %copy-start = (f32[128,1,4224]{2,1,0:T(1,128)}, f32[128,1,4224]{2,1,0:T(1,128)S(1)}, u32[]{:S(2)}) copy-start(f32[128,1,4224]{2,1,0:T(1,128)S(1)} %all-to-all-done) | copy-start | bytes 6488068

commit v20 on v17

--- a/solution.py
+++ b/solution.py
@@ -147,7 +147,6 @@
     step = pl.program_id(0)
     last = pl.num_programs(0) - 1
     me = lax.axis_index("tile") * n_band + lax.axis_index("band")
-    barrier = pltpu.get_barrier_semaphore()
 
     def device(p):
         return (p // n_band, p % n_band)
@@ -174,23 +173,10 @@
 
     own = pltpu.make_async_copy(ret_ref.at[me], recv_ref.at[me], own_sem)
 
-    @pl.when(step == 0)
-    def _():
-        def greet(k, carry):
-            p = lax.rem(me + k, total)
-            pl.semaphore_signal(barrier, inc=1, device_id=device(p), device_id_type=MESH)
-            return carry
-
-        lax.fori_loop(1, total, greet, 0)
-
     padded = jnp.concatenate([out_ref[...], jnp.zeros((128 - 32, chunk), jnp.float32)], axis=0)
     ret_ref[pl.ds(pl.multiple_of(step * peers, peers), peers)] = padded.T.reshape(peers, CAP, 128)
 
     hold = jnp.minimum(4, last)
-
-    @pl.when(step == hold)
-    def _():
-        pl.semaphore_wait(barrier, total - 1)
 
     def start(q, carry):
         p = q
@@ -250,7 +236,7 @@
             pltpu.SemaphoreType.DMA((peers,)),
             pltpu.SemaphoreType.DMA(()),
         ]
-        params = pltpu.CompilerParams(collective_id=0, has_side_effects=True)
+        params = pltpu.CompilerParams(has_side_effects=True)
     else:
         xa_spec = pl.BlockSpec((3, chunk, 128), lambda i: (0, i, 0))
         map_spec = pl.BlockSpec((chunk, 128), lambda i: (i, 0))
@@ -316,7 +302,6 @@
         p = lax.rem(me + k, peers)
         return p, (p // n_band, p % n_band)
 
-    barrier = pltpu.get_barrier_semaphore()
 
     def greet(k, carry):
         _, dev = peer_of(k)

time: 86.4 us -> 92.5 us (1.071)
  the two profiles are of different devices: /device:TPU:97 before, /device:TPU:31 now
where the time goes in v20:
time: 92.5 us; the launch traced here: 91.6 us
  Pallas kernels  37.5 us (41%)
  local copies, waits for them, and re-layouts  21.2 us (23%)
  matrix products  12.6 us (14%)
  starting transfers between devices  10.6 us (11%)
  other arithmetic  8.71 us (9%)
  between operations  0.98 us (1%)
    pallas_call x2, Pallas kernels, pair_sums(): pl.pallas_call(functools.partial(_terms_kernel, from_cargo, n_band), out_...  34.3 us
    all_to_all x1, starting transfers between devices, local(): lax.all_to_all(cargo, axes, split_axis=0, concat_axis=0, tiled=True)  10.6 us
    dot_general x4, matrix products, pick_rows(): jnp.einsum('sb,cbk->csk', onehot, rows, precision=lax.Precision.HIGHEST)  9.72 us
    unnamed x31, local copies, waits for them, and re-layouts  5.07 us
    pallas_call x1, Pallas kernels, build_cargo(): pl.pallas_call(_cargo_kernel, out_shape=jax.ShapeDtypeStruct((slots // CA...  3.2 us
    gather x2, local copies, waits for them, and re-layouts, local(): frag_dirs[target_blocks // BF]  2.99 us
    dot_general x4, matrix products, frag_sums(): return jnp.dot(onehot.T, terms, precision=lax.Precision.HIGHEST)  2.38 us
    concatenate x2, other arithmetic, make_aux(): jnp.concatenate([dirs_a.T, dirs_b.T, valid[None, :], jnp.zeros((32 - 25,...  2.08 us
  transfers between devices with their start and end apart: 1, of which 0 were waited for; matrix products, arithmetic and copies ran while one was open for 27% of the time, Pallas kernels for 4%

profile of v20, /device:TPU:31, one launch (start us, length us, event | category | flops | bytes accessed | tf_op | source)
XLA Modules:
  0.0 91.6 jit_solution(90559237032984908)
XLA Ops:
  0.6 0.8 slice_bitcast_fusion.5
  1.4 0.7 slice_multiply_fusion.4
  2.2 0.1 mul.431
  2.4 0.1 mul.439
  2.5 0.1 mul.399
  2.7 0.1 add.308
  2.8 0.7 add_select_fusion
  3.5 0.1 mul.435
  3.7 0.1 mul.427
  3.8 0.1 mul.412
  4.0 0.1 mul.406
  4.3 0.1 mul.416
  4.7 0.8 copy.76
  5.5 0.7 fusion.53
  6.3 0.1 reshape.1301
  6.4 1.1 %fusion.87 = (f32[256,1,128]{2,0,1:T(8,128)S(1)}, f32[256,1,128]{2,0,1:T(8,128)S(1)}, f32[256,1,128]{2,0,1:T(8,128)S(1)}) fusion(f32[256,3,128]{2,0,1:T(8,128)} %param.10), kind=kLoop, calls=%fused_computation.194 | loop fusion | bytes 786432 | tf_op jit(solution)/shard_map/slice | solution.py:58
  7.5 0.1 copy.92
  7.6 0.1 copy.93
  7.7 0.1 copy.94
  7.8 0.5 fusion.6
  8.3 0.2 copy.80
  8.5 0.2 reshape.1296
  8.7 0.6 concatenate.50.side_ref
  9.5 2.2 %convolution_bitcast_fusion.1.xa_ref = f32[3,1024,128]{2,1,0:T(8,128)} fusion(s32[1024]{0:T(1024)S(1)} %bitcast.277, f32[1,256,128]{1,2,0:T(8,128)S(1)} %get-tuple-element.15, f32[1,256,128]{1,2,0:T(8,128)S(1)} %get-tuple-element.17, f32[1,256,128]{1,2,0:T(8,128)S(1)} %get-tuple-element.19), kind=kOutput, calls=%fused_computation.4 | convolution fusion | flops 1208418304 | bytes 1970176 | tf_op jit(solution)/shard_map/sb,cbk->csk/dot_general | solution.py:374
  11.7 3.2 %shard_map.114 = f32[4224,128]{1,0:T(8,128)} custom-call(f32[3,1024,128]{2,1,0:T(8,128)} %convolution_bitcast_fusion.1.xa_ref, s32[1024,128]{1,0:T(8,128)} %bitcast.266, f32[128,128]{1,0:T(8,128)} %concatenate.50.side_ref), custom_call_target="tpu_custom_call" | custom-call | tf_op jit(solution)/shard_map/pallas_call | solution.py:280
  14.9 10.6 %all-to-all-start = ((f32[128,1,4224]{2,1,0:T(1,128)}), f32[128,1,4224]{2,1,0:T(1,128)S(1)}, u32[]{:S(2)}, u32[]{:S(2)}) async-start(f32[128,1,4224]{2,1,0:T(1,128)} %bitcast.264), calls=%async_computation | async-start | bytes 4325376 | tf_op jit(solution)/shard_map/all_to_all | solution.py:424
  25.5 0.6 fusion.90
  26.1 0.6 pad.31.clone
  26.7 0.6 pad.32.clone
  27.3 0.7 gather_fusion.1
  28.1 0.7 gather_fusion
  29.0 1.7 %fusion.86 = (f32[256,1,128]{2,0,1:T(8,128)S(1)}, f32[256,1,128]{2,0,1:T(8,128)S(1)}, f32[256,1,128]{2,0,1:T(8,128)}) fusion(f32[256,3,128]{2,0,1:T(8,128)} %param.11), kind=kLoop, calls=%fused_computation.193 | loop fusion | bytes 786432 | tf_op jit(solution)/shard_map/slice | solution.py:64
  30.7 0.1 copy.95
  30.8 0.1 copy.96
  30.9 1.0 %copy.97 = f32[256,1,128]{0,2,1:T(8,128)S(1)} copy(f32[256,1,128]{2,0,1:T(8,128)} %get-tuple-element.24) | data formatting | bytes 262144
  32.0 2.2 %convolution_bitcast_fusion.3.xa_ref = f32[3,256,128]{2,1,0:T(8,128)} fusion(f32[1,256,128]{1,2,0:T(8,128)} %copy-done.2, f32[1,256,128]{1,2,0:T(8,128)} %copy-done.1, f32[1,256,128]{1,2,0:T(8,128)S(1)} %get-tuple-element.19, s32[256]{0:T(256)} %bitcast.279), kind=kOutput, calls=%fused_computation.6 | convolution fusion | flops 302252032 | bytes 787456 | tf_op jit(solution)/shard_map/sb,cbk->csk/dot_general | solution.py:374
  34.2 2.1 %convolution_bitcast_fusion.2.tb_ref = f32[6,256,128]{2,1,0:T(8,128)} fusion(f32[6,256,128]{1,2,0:T(8,128)S(1)} %fusion.23, s32[256]{0:T(256)} %bitcast.281), kind=kOutput, calls=%fused_computation.5 | convolution fusion | flops 604045312 | bytes 1573888 | tf_op jit(solution)/shard_map/sb,cbk->csk/dot_general | solution.py:374
  36.3 1.3 %maximum_maximum_fusion.1.aux_ref = f32[32,256]{1,0:T(8,128)} fusion(f32[12,256]{1,0:T(8,128)S(1)} %bitcast.271, f32[12,256]{1,0:T(8,128)S(1)} %bitcast.272, f32[32]{0:T(128)} %pad.32.clone, f32[32]{0:T(128)} %pad.31.clone), kind=kLoop, calls=%fused_computation.93 | loop fusion | flops 24576 | bytes 57600 | tf_op jit(solution)/shard_map/concatenate | solution.py:386
  37.6 3.4 %shard_map.113 = f32[32,256]{1,0:T(8,128)} custom-call(f32[3,256,128]{2,1,0:T(8,128)} %convolution_bitcast_fusion.3.xa_ref, f32[6,256,128]{2,1,0:T(8,128)} %convolution_bitcast_fusion.2.tb_ref, s32[256,128]{1,0:T(8,128)} %map_ref.1, f32[32,256]{1,0:T(8,128)} %maximum_maximum_fusion.1.aux_ref), custom_call_target="tpu_custom_call" | custom-call | tf_op jit(solution)/shard_map/pallas_call | solution.py:243
  41.0 0.8 slice_bitcast_fusion.2
  41.8 0.6 fusion.89
  42.4 0.6 fusion.65
  43.0 2.8 %gather_fusion.2 = f32[1024,12]{1,0:T(8,128)S(1)} fusion(f32[8,12]{1,0:T(8,128)S(1)} %bitcast.262, s32[1024]{0:T(1024)S(1)} %broadcast_clamp_fusion), kind=kCustom, calls=%fused_computation.2 | custom fusion | bytes 102400 | tf_op jit(solution)/shard_map/gather | solution.py:443
  45.8 0.2 copy.84
  46.0 0.7 fusion.67
  46.7 0.7 and_select_fusion.4
  47.4 0.7 and_select_fusion.3
  48.1 0.7 slice_multiply_fusion.3
  48.8 0.7 slice_multiply_fusion.2
  49.5 0.3 fusion.49
  49.8 1.0 %convolution_add_fusion.2 = f32[8,18]{1,0:T(8,128)S(1)} fusion(f32[8,18]{1,0:T(8,128)S(1)} %fusion.49, s32[256]{0:T(256)S(1)} %and_select_fusion.3, f32[256,6]{0,1:T(8,128)S(1)} %fusion.67, f32[256,6]{0,1:T(8,128)S(1)} %fusion.66, f32[256,6]{0,1:T(8,128)} %fusion.65), kind=kOutput, calls=%fused_computation.9 | convolution fusion | flops 455824 | bytes 20608 | tf_op jit(solution)/shard_map/dot_general | solution.py:381
  50.8 3.2 %convolution_bitcast_fusion.tb_ref = f32[6,1024,128]{2,1,0:T(8,128)} fusion(f32[6,256,128]{1,2,0:T(8,128)S(1)} %fusion.23, s32[1024]{0:T(1024)S(1)} %bitcast.274), kind=kOutput, calls=%fused_computation.3 | convolution fusion | flops 2416181248 | bytes 3936256 | tf_op jit(solution)/shard_map/sb,cbk->csk/dot_general | solution.py:374
  54.0 0.2 slice_reduce_fusion.1
  54.2 0.2 reshape_squeeze.3
  54.3 0.4 slice_reduce_fusion
  54.7 0.2 copy.98
  54.9 0.7 maximum_maximum_fusion.map_ref.aux_ref
  55.7 31.0 %shard_map.115 = (f32[32,1024]{1,0:T(8,128)}, f32[128,8,128]{2,1,0:T(8,128)}) custom-call(f32[4224,128]{1,0:T(8,128)} %bitcast.263, f32[6,1024,128]{2,1,0:T(8,128)} %convolution_bitcast_fusion.tb_ref, f32[32,1024]{1,0:T(8,128)} %maximum_maximum_fusion.map_ref.aux_ref, f32[32,1024]{1,0:T(8,128)} %maximum_maximum_fusion.map_ref.aux_ref), custom_call_target="tpu_custom_call" | custom-call | tf_op jit(solution)/shard_map/pallas_call | solution.py:243
  86.6 1.2 %copy.99 = f32[1024,32]{0,1:T(8,128)S(1)} copy(f32[1024,32]{1,0:T(8,128)} %bitcast.267) | data formatting | bytes 262144
  87.9 0.9 slice_bitcast_fusion.1
  88.9 0.6 convolution_add_fusion.1
  89.5 0.6 convolution_add_fusion
  90.1 0.7 copy.86
  90.9 0.7 copy.87
  (65 shorter events, 1.9 us)
Async XLA Ops:
  3.5 5.9 %copy-start.7 = (s32[1024]{0:T(1024)}, s32[1024]{0:T(1024)S(1)}, u32[]{:S(2)}) copy-start(s32[1024]{0:T(1024)S(1)} %add_select_fusion) | copy-start | bytes 12292
  7.4 2.0 %copy-start.5 = (s32[1,1024]{1,0:T(1,128)S(1)}, s32[1,1024]{1,0:T(1,128)}, u32[]{:S(2)}) copy-start(s32[1,1024]{1,0:T(1,128)} %param.16) | copy-start | bytes 12292
  9.4 5.5 %copy-start.1 = (f32[1,256,128]{1,2,0:T(8,128)}, f32[1,256,128]{1,2,0:T(8,128)S(1)}, u32[]{:S(2)}) copy-start(f32[1,256,128]{1,2,0:T(8,128)S(1)} %get-tuple-element.17) | copy-start | bytes 393220
  9.5 5.4 %copy-start.2 = (f32[1,256,128]{1,2,0:T(8,128)}, f32[1,256,128]{1,2,0:T(8,128)S(1)}, u32[]{:S(2)}) copy-start(f32[1,256,128]{1,2,0:T(8,128)S(1)} %get-tuple-element.15) | copy-start | bytes 393220
  14.9 10.6 %copy-start.6 = (s32[2,256]{1,0:T(2,128)S(1)}, s32[2,256]{1,0:T(2,128)}, u32[]{:S(2)}) copy-start(s32[2,256]{1,0:T(2,128)} %param.14) | copy-start | bytes 6148
  14.9 12.4 %copy-start.4 = (s32[1,1024]{1,0:T(1,128)S(1)}, s32[1,1024]{1,0:T(1,128)}, u32[]{:S(2)}) copy-start(s32[1,1024]{1,0:T(1,128)} %param.18) | copy-start | bytes 12292
  14.9 39.1 %all-to-all-start = ((f32[128,1,4224]{2,1,0:T(1,128)}), f32[128,1,4224]{2,1,0:T(1,128)S(1)}, u32[]{:S(2)}, u32[]{:S(2)}) async-start(f32[128,1,4224]{2,1,0:T(1,128)} %bitcast.264), calls=%async_computation | async-start | bytes 4325376 | tf_op jit(solution)/shard_map/all_to_all | solution.py:424
  41.8 0.6 copy-start.3
  50.8 4.1 %copy-start.9 = (f32[32]{0:T(128)S(1)}, f32[32]{0:T(128)}, u32[]{:S(2)}) copy-start(f32[32]{0:T(128)} %pad.32.clone) | copy-start | bytes 388
  54.0 1.7 %copy-start = (f32[128,1,4224]{2,1,0:T(1,128)}, f32[128,1,4224]{2,1,0:T(1,128)S(1)}, u32[]{:S(2)}) copy-start(f32[128,1,4224]{2,1,0:T(1,128)S(1)} %all-to-all-done) | copy-start | bytes 6488068
  55.7 33.8 %copy-start.8 = (s32[1024]{0:T(1024)S(1)}, s32[1024]{0:T(1024)}, u32[]{:S(2)}) copy-start(s32[1024]{0:T(1024)} %copy-done.7) | copy-start | bytes 12292

commit v21 on v17

--- a/solution.py
+++ b/solution.py
@@ -291,9 +291,18 @@
 def build_cargo(xa3, maps, side):
     slots = maps.shape[0]
     height = 4 * CAP + 1
+    chunk = slots // 4
+    peers = chunk // CAP
     cargo = pl.pallas_call(
         _cargo_kernel,
         out_shape=jax.ShapeDtypeStruct((slots // CAP * height, 128), jnp.float32),
+        grid=(slots // chunk,),
+        in_specs=[
+            pl.BlockSpec((3, chunk, 128), lambda i: (0, i, 0)),
+            pl.BlockSpec((chunk, 128), lambda i: (i, 0)),
+            pl.BlockSpec((peers, 128), lambda i: (i, 0)),
+        ],
+        out_specs=pl.BlockSpec((peers * height, 128), lambda i: (i, 0)),
     )(xa3, maps, side)
     return cargo.reshape(slots // CAP, 1, height * 128)
 

time: 86.4 us -> 87 us (level)
  no operation moved by 1% of the time
where the time goes in v21:
time: 87 us; the launch traced here: 86 us
  Pallas kernels  32.3 us (37%)
  local copies, waits for them, and re-layouts  21.2 us (24%)
  matrix products  12.6 us (14%)
  starting transfers between devices  10.2 us (12%)
  other arithmetic  8.71 us (10%)
  between operations  0.99 us (1%)
    pallas_call x2, Pallas kernels, pair_sums(): pl.pallas_call(functools.partial(_terms_kernel, from_cargo, n_band), out_...  28.6 us
    all_to_all x1, starting transfers between devices, local(): lax.all_to_all(cargo, axes, split_axis=0, concat_axis=0, tiled=True)  10.2 us
    dot_general x4, matrix products, pick_rows(): jnp.einsum('sb,cbk->csk', onehot, rows, precision=lax.Precision.HIGHEST)  9.71 us
    unnamed x31, local copies, waits for them, and re-layouts  5.07 us
    pallas_call x1, Pallas kernels, build_cargo(): pl.pallas_call(_cargo_kernel, out_shape=jax.ShapeDtypeStruct((slots // CA...  3.79 us
    gather x2, local copies, waits for them, and re-layouts, local(): frag_dirs[target_blocks // BF]  2.99 us
    dot_general x4, matrix products, frag_sums(): return jnp.dot(onehot.T, terms, precision=lax.Precision.HIGHEST)  2.38 us
    concatenate x2, other arithmetic, make_aux(): jnp.concatenate([dirs_a.T, dirs_b.T, valid[None, :], jnp.zeros((32 - 25,...  2.08 us
  transfers between devices with their start and end apart: 1, of which 0 were waited for; matrix products, arithmetic and copies ran while one was open for 29% of the time, Pallas kernels for 4%

profile of v21, /device:TPU:97, one launch (start us, length us, event | category | flops | bytes accessed | tf_op | source)
XLA Modules:
  0.0 86.0 jit_solution(11398688981235182558)
XLA Ops:
  0.6 0.8 slice_bitcast_fusion.5
  1.4 0.7 slice_multiply_fusion.4
  2.2 0.1 mul.431
  2.4 0.1 mul.439
  2.5 0.1 mul.399
  2.7 0.1 add.308
  2.8 0.7 add_select_fusion
  3.5 0.1 mul.435
  3.7 0.1 mul.427
  3.8 0.1 mul.412
  4.0 0.1 mul.406
  4.3 0.1 mul.416
  4.7 0.8 copy.76
  5.5 0.7 fusion.53
  6.3 0.1 reshape.1301
  6.4 1.1 %fusion.87 = (f32[256,1,128]{2,0,1:T(8,128)S(1)}, f32[256,1,128]{2,0,1:T(8,128)S(1)}, f32[256,1,128]{2,0,1:T(8,128)S(1)}) fusion(f32[256,3,128]{2,0,1:T(8,128)} %param.10), kind=kLoop, calls=%fused_computation.194 | loop fusion | bytes 786432 | tf_op jit(solution)/shard_map/slice | solution.py:58
  7.5 0.1 copy.92
  7.6 0.1 copy.93
  7.7 0.1 copy.94
  7.8 0.5 fusion.6
  8.3 0.2 copy.80
  8.5 0.2 reshape.1296
  8.7 0.6 concatenate.50.side_ref
  9.5 2.2 %convolution_bitcast_fusion.1.xa_ref = f32[3,1024,128]{2,1,0:T(8,128)} fusion(s32[1024]{0:T(1024)S(1)} %bitcast.277, f32[1,256,128]{1,2,0:T(8,128)S(1)} %get-tuple-element.15, f32[1,256,128]{1,2,0:T(8,128)S(1)} %get-tuple-element.17, f32[1,256,128]{1,2,0:T(8,128)S(1)} %get-tuple-element.19), kind=kOutput, calls=%fused_computation.4 | convolution fusion | flops 1208418304 | bytes 1970176 | tf_op jit(solution)/shard_map/sb,cbk->csk/dot_general | solution.py:398
  11.7 3.8 %shard_map.114 = f32[4224,128]{1,0:T(8,128)} custom-call(f32[3,1024,128]{2,1,0:T(8,128)} %convolution_bitcast_fusion.1.xa_ref, s32[1024,128]{1,0:T(8,128)} %bitcast.266, f32[128,128]{1,0:T(8,128)} %concatenate.50.side_ref), custom_call_target="tpu_custom_call" | custom-call | tf_op jit(solution)/shard_map/pallas_call | solution.py:296
  15.5 10.2 %all-to-all-start = ((f32[128,1,4224]{2,1,0:T(1,128)}), f32[128,1,4224]{2,1,0:T(1,128)S(1)}, u32[]{:S(2)}, u32[]{:S(2)}) async-start(f32[128,1,4224]{2,1,0:T(1,128)} %bitcast.264), calls=%async_computation | async-start | bytes 4325376 | tf_op jit(solution)/shard_map/all_to_all | solution.py:448
  25.7 0.6 fusion.90
  26.3 0.6 pad.31.clone
  26.9 0.6 pad.32.clone
  27.5 0.7 gather_fusion.1
  28.3 0.7 gather_fusion
  29.2 1.7 %fusion.86 = (f32[256,1,128]{2,0,1:T(8,128)S(1)}, f32[256,1,128]{2,0,1:T(8,128)S(1)}, f32[256,1,128]{2,0,1:T(8,128)}) fusion(f32[256,3,128]{2,0,1:T(8,128)} %param.11), kind=kLoop, calls=%fused_computation.193 | loop fusion | bytes 786432 | tf_op jit(solution)/shard_map/slice | solution.py:64
  30.9 0.1 copy.95
  31.0 0.1 copy.96
  31.1 1.0 %copy.97 = f32[256,1,128]{0,2,1:T(8,128)S(1)} copy(f32[256,1,128]{2,0,1:T(8,128)} %get-tuple-element.24) | data formatting | bytes 262144
  32.2 2.2 %convolution_bitcast_fusion.3.xa_ref = f32[3,256,128]{2,1,0:T(8,128)} fusion(f32[1,256,128]{1,2,0:T(8,128)} %copy-done.2, f32[1,256,128]{1,2,0:T(8,128)} %copy-done.1, f32[1,256,128]{1,2,0:T(8,128)S(1)} %get-tuple-element.19, s32[256]{0:T(256)} %bitcast.279), kind=kOutput, calls=%fused_computation.6 | convolution fusion | flops 302252032 | bytes 787456 | tf_op jit(solution)/shard_map/sb,cbk->csk/dot_general | solution.py:398
  34.4 2.1 %convolution_bitcast_fusion.2.tb_ref = f32[6,256,128]{2,1,0:T(8,128)} fusion(f32[6,256,128]{1,2,0:T(8,128)S(1)} %fusion.23, s32[256]{0:T(256)} %bitcast.281), kind=kOutput, calls=%fused_computation.5 | convolution fusion | flops 604045312 | bytes 1573888 | tf_op jit(solution)/shard_map/sb,cbk->csk/dot_general | solution.py:398
  36.5 1.3 %maximum_maximum_fusion.1.aux_ref = f32[32,256]{1,0:T(8,128)} fusion(f32[12,256]{1,0:T(8,128)S(1)} %bitcast.271, f32[12,256]{1,0:T(8,128)S(1)} %bitcast.272, f32[32]{0:T(128)} %pad.32.clone, f32[32]{0:T(128)} %pad.31.clone), kind=kLoop, calls=%fused_computation.93 | loop fusion | flops 24576 | bytes 57600 | tf_op jit(solution)/shard_map/concatenate | solution.py:410
  37.8 3.4 %shard_map.113 = f32[32,256]{1,0:T(8,128)} custom-call(f32[3,256,128]{2,1,0:T(8,128)} %convolution_bitcast_fusion.3.xa_ref, f32[6,256,128]{2,1,0:T(8,128)} %convolution_bitcast_fusion.2.tb_ref, s32[256,128]{1,0:T(8,128)} %map_ref.1, f32[32,256]{1,0:T(8,128)} %maximum_maximum_fusion.1.aux_ref), custom_call_target="tpu_custom_call" | custom-call | tf_op jit(solution)/shard_map/pallas_call | solution.py:257
  41.2 0.8 slice_bitcast_fusion.2
  42.0 0.6 fusion.89
  42.6 0.6 fusion.65
  43.2 2.8 %gather_fusion.2 = f32[1024,12]{1,0:T(8,128)S(1)} fusion(f32[8,12]{1,0:T(8,128)S(1)} %bitcast.262, s32[1024]{0:T(1024)S(1)} %broadcast_clamp_fusion), kind=kCustom, calls=%fused_computation.2 | custom fusion | bytes 102400 | tf_op jit(solution)/shard_map/gather | solution.py:467
  46.0 0.2 copy.84
  46.2 0.7 fusion.67
  46.9 0.7 and_select_fusion.4
  47.6 0.7 and_select_fusion.3
  48.3 0.7 slice_multiply_fusion.3
  49.0 0.7 slice_multiply_fusion.2
  49.7 0.3 fusion.49
  50.0 1.0 %convolution_add_fusion.2 = f32[8,18]{1,0:T(8,128)S(1)} fusion(f32[8,18]{1,0:T(8,128)S(1)} %fusion.49, s32[256]{0:T(256)S(1)} %and_select_fusion.3, f32[256,6]{0,1:T(8,128)S(1)} %fusion.67, f32[256,6]{0,1:T(8,128)S(1)} %fusion.66, f32[256,6]{0,1:T(8,128)} %fusion.65), kind=kOutput, calls=%fused_computation.9 | convolution fusion | flops 455824 | bytes 20608 | tf_op jit(solution)/shard_map/dot_general | solution.py:405
  51.0 3.2 %convolution_bitcast_fusion.tb_ref = f32[6,1024,128]{2,1,0:T(8,128)} fusion(f32[6,256,128]{1,2,0:T(8,128)S(1)} %fusion.23, s32[1024]{0:T(1024)S(1)} %bitcast.274), kind=kOutput, calls=%fused_computation.3 | convolution fusion | flops 2416181248 | bytes 3936256 | tf_op jit(solution)/shard_map/sb,cbk->csk/dot_general | solution.py:398
  54.2 0.2 slice_reduce_fusion.1
  54.4 0.2 reshape_squeeze.3
  54.5 0.4 slice_reduce_fusion
  54.9 0.2 copy.98
  55.1 0.7 maximum_maximum_fusion.map_ref.aux_ref
  55.9 25.2 %shard_map.115 = (f32[32,1024]{1,0:T(8,128)}, f32[128,8,128]{2,1,0:T(8,128)}) custom-call(f32[4224,128]{1,0:T(8,128)} %bitcast.263, f32[6,1024,128]{2,1,0:T(8,128)} %convolution_bitcast_fusion.tb_ref, f32[32,1024]{1,0:T(8,128)} %maximum_maximum_fusion.map_ref.aux_ref, f32[32,1024]{1,0:T(8,128)} %maximum_maximum_fusion.map_ref.aux_ref), custom_call_target="tpu_custom_call" | custom-call | tf_op jit(solution)/shard_map/pallas_call | solution.py:257
  81.1 1.2 %copy.99 = f32[1024,32]{0,1:T(8,128)S(1)} copy(f32[1024,32]{1,0:T(8,128)} %bitcast.267) | data formatting | bytes 262144
  82.3 0.9 %slice_bitcast_fusion.1 = f32[1024,27]{0,1:T(8,128)S(1)} fusion(f32[32,1024]{1,0:T(8,128)} %get-tuple-element.4), kind=kLoop, calls=%fused_computation.68 | loop fusion | bytes 221184 | tf_op jit(solution)/shard_map/transpose | solution.py:311
  83.3 0.6 convolution_add_fusion.1
  83.9 0.6 convolution_add_fusion
  84.6 0.7 copy.86
  85.3 0.7 copy.87
  (65 shorter events, 1.9 us)
Async XLA Ops:
  3.5 5.9 %copy-start.7 = (s32[1024]{0:T(1024)}, s32[1024]{0:T(1024)S(1)}, u32[]{:S(2)}) copy-start(s32[1024]{0:T(1024)S(1)} %add_select_fusion) | copy-start | bytes 12292
  7.4 2.0 %copy-start.5 = (s32[1,1024]{1,0:T(1,128)S(1)}, s32[1,1024]{1,0:T(1,128)}, u32[]{:S(2)}) copy-start(s32[1,1024]{1,0:T(1,128)} %param.16) | copy-start | bytes 12292
  9.4 6.1 %copy-start.1 = (f32[1,256,128]{1,2,0:T(8,128)}, f32[1,256,128]{1,2,0:T(8,128)S(1)}, u32[]{:S(2)}) copy-start(f32[1,256,128]{1,2,0:T(8,128)S(1)} %get-tuple-element.17) | copy-start | bytes 393220
  9.5 6.0 %copy-start.2 = (f32[1,256,128]{1,2,0:T(8,128)}, f32[1,256,128]{1,2,0:T(8,128)S(1)}, u32[]{:S(2)}) copy-start(f32[1,256,128]{1,2,0:T(8,128)S(1)} %get-tuple-element.15) | copy-start | bytes 393220
  15.5 10.2 %copy-start.6 = (s32[2,256]{1,0:T(2,128)S(1)}, s32[2,256]{1,0:T(2,128)}, u32[]{:S(2)}) copy-start(s32[2,256]{1,0:T(2,128)} %param.14) | copy-start | bytes 6148
  15.5 12.0 %copy-start.4 = (s32[1,1024]{1,0:T(1,128)S(1)}, s32[1,1024]{1,0:T(1,128)}, u32[]{:S(2)}) copy-start(s32[1,1024]{1,0:T(1,128)} %param.18) | copy-start | bytes 12292
  15.5 38.7 %all-to-all-start = ((f32[128,1,4224]{2,1,0:T(1,128)}), f32[128,1,4224]{2,1,0:T(1,128)S(1)}, u32[]{:S(2)}, u32[]{:S(2)}) async-start(f32[128,1,4224]{2,1,0:T(1,128)} %bitcast.264), calls=%async_computation | async-start | bytes 4325376 | tf_op jit(solution)/shard_map/all_to_all | solution.py:448
  42.0 0.6 copy-start.3
  51.0 4.1 %copy-start.9 = (f32[32]{0:T(128)S(1)}, f32[32]{0:T(128)}, u32[]{:S(2)}) copy-start(f32[32]{0:T(128)} %pad.32.clone) | copy-start | bytes 388
  54.2 1.7 %copy-start = (f32[128,1,4224]{2,1,0:T(1,128)}, f32[128,1,4224]{2,1,0:T(1,128)S(1)}, u32[]{:S(2)}) copy-start(f32[128,1,4224]{2,1,0:T(1,128)S(1)} %all-to-all-done) | copy-start | bytes 6488068
  55.9 28.0 %copy-start.8 = (s32[1024]{0:T(1024)S(1)}, s32[1024]{0:T(1024)}, u32[]{:S(2)}) copy-start(s32[1024]{0:T(1024)} %copy-done.7) | copy-start | bytes 12292

commit v22 on v20

--- a/solution.py
+++ b/solution.py
@@ -69,6 +69,7 @@
 def _terms_kernel(from_cargo, n_band, xa_ref, tb_ref, map_ref, aux_ref, out_ref, *rest):
     if from_cargo:
         recv_ref, xt_ref, gt_ref, cs_ref, ret_ref, send_sems, recv_sems, own_sem = rest
+        _greet(n_band, recv_ref.shape[0])
     else:
         xt_ref, gt_ref, cs_ref = rest
     chunk = out_ref.shape[1]
@@ -140,6 +141,22 @@
         _send_back(n_band, out_ref, recv_ref, ret_ref, send_sems, recv_sems, own_sem)
 
 
+def _greet(n_band, total):
+    me = lax.axis_index("tile") * n_band + lax.axis_index("band")
+    barrier = pltpu.get_barrier_semaphore()
+
+    @pl.when(pl.program_id(0) == 0)
+    def _():
+        def greet(k, carry):
+            p = lax.rem(me + k, total)
+            pl.semaphore_signal(
+                barrier, inc=1, device_id=(p // n_band, p % n_band), device_id_type=MESH
+            )
+            return carry
+
+        lax.fori_loop(1, total, greet, 0)
+
+
 def _send_back(n_band, out_ref, recv_ref, ret_ref, send_sems, recv_sems, own_sem):
     chunk = out_ref.shape[1]
     peers = chunk // CAP
@@ -147,6 +164,7 @@
     step = pl.program_id(0)
     last = pl.num_programs(0) - 1
     me = lax.axis_index("tile") * n_band + lax.axis_index("band")
+    barrier = pltpu.get_barrier_semaphore()
 
     def device(p):
         return (p // n_band, p % n_band)
@@ -177,6 +195,10 @@
     ret_ref[pl.ds(pl.multiple_of(step * peers, peers), peers)] = padded.T.reshape(peers, CAP, 128)
 
     hold = jnp.minimum(4, last)
+
+    @pl.when(step == hold)
+    def _():
+        pl.semaphore_wait(barrier, total - 1)
 
     def start(q, carry):
         p = q
@@ -236,7 +258,7 @@
             pltpu.SemaphoreType.DMA((peers,)),
             pltpu.SemaphoreType.DMA(()),
         ]
-        params = pltpu.CompilerParams(has_side_effects=True)
+        params = pltpu.CompilerParams(collective_id=0, has_side_effects=True)
     else:
         xa_spec = pl.BlockSpec((3, chunk, 128), lambda i: (0, i, 0))
         map_spec = pl.BlockSpec((chunk, 128), lambda i: (i, 0))
@@ -302,6 +324,7 @@
         p = lax.rem(me + k, peers)
         return p, (p // n_band, p % n_band)
 
+    barrier = pltpu.get_barrier_semaphore()
 
     def greet(k, carry):
         _, dev = peer_of(k)

time: 92.5 us -> 85.8 us (0.928)
  the two profiles are of different devices: /device:TPU:31 before, /device:TPU:23 now
where the time goes in v22:
time: 85.8 us; the launch traced here: 84.8 us
  Pallas kernels  30.7 us (36%)
  local copies, waits for them, and re-layouts  21.2 us (25%)
  matrix products  12.6 us (15%)
  starting transfers between devices  10.6 us (12%)
  other arithmetic  8.71 us (10%)
  between operations  0.98 us (1%)
    pallas_call x2, Pallas kernels, pair_sums(): pl.pallas_call(functools.partial(_terms_kernel, from_cargo, n_band), out_...  27.5 us
    all_to_all x1, starting transfers between devices, local(): lax.all_to_all(cargo, axes, split_axis=0, concat_axis=0, tiled=True)  10.6 us
    dot_general x4, matrix products, pick_rows(): jnp.einsum('sb,cbk->csk', onehot, rows, precision=lax.Precision.HIGHEST)  9.71 us
    unnamed x31, local copies, waits for them, and re-layouts  5.07 us
    pallas_call x1, Pallas kernels, build_cargo(): pl.pallas_call(_cargo_kernel, out_shape=jax.ShapeDtypeStruct((slots // CA...  3.2 us
    gather x2, local copies, waits for them, and re-layouts, local(): frag_dirs[target_blocks // BF]  2.99 us
    dot_general x4, matrix products, frag_sums(): return jnp.dot(onehot.T, terms, precision=lax.Precision.HIGHEST)  2.38 us
    concatenate x2, other arithmetic, make_aux(): jnp.concatenate([dirs_a.T, dirs_b.T, valid[None, :], jnp.zeros((32 - 25,...  2.08 us
  transfers between devices with their start and end apart: 1, of which 0 were waited for; matrix products, arithmetic and copies ran while one was open for 29% of the time, Pallas kernels for 4%

profile of v22, /device:TPU:23, one launch (start us, length us, event | category | flops | bytes accessed | tf_op | source)
XLA Modules:
  0.0 84.8 jit_solution(17410502761904649643)
XLA Ops:
  0.6 0.8 slice_bitcast_fusion.5
  1.4 0.7 slice_multiply_fusion.4
  2.2 0.1 mul.431
  2.4 0.1 mul.439
  2.5 0.1 mul.399
  2.7 0.1 add.308
  2.8 0.7 add_select_fusion
  3.5 0.1 mul.435
  3.7 0.1 mul.427
  3.8 0.1 mul.412
  4.1 0.1 mul.421
  4.6 0.1 add.301
  4.7 0.8 copy.76
  5.5 0.7 fusion.53
  6.3 0.1 reshape.1301
  6.4 1.1 %fusion.87 = (f32[256,1,128]{2,0,1:T(8,128)S(1)}, f32[256,1,128]{2,0,1:T(8,128)S(1)}, f32[256,1,128]{2,0,1:T(8,128)S(1)}) fusion(f32[256,3,128]{2,0,1:T(8,128)} %param.10), kind=kLoop, calls=%fused_computation.194 | loop fusion | bytes 786432 | tf_op jit(solution)/shard_map/slice | solution.py:58
  7.5 0.1 copy.92
  7.6 0.1 copy.93
  7.7 0.1 copy.94
  7.8 0.5 fusion.6
  8.3 0.2 copy.80
  8.5 0.2 reshape.1296
  8.7 0.6 concatenate.50.side_ref
  9.5 2.2 %convolution_bitcast_fusion.1.xa_ref = f32[3,1024,128]{2,1,0:T(8,128)} fusion(s32[1024]{0:T(1024)S(1)} %bitcast.277, f32[1,256,128]{1,2,0:T(8,128)S(1)} %get-tuple-element.15, f32[1,256,128]{1,2,0:T(8,128)S(1)} %get-tuple-element.17, f32[1,256,128]{1,2,0:T(8,128)S(1)} %get-tuple-element.19), kind=kOutput, calls=%fused_computation.4 | convolution fusion | flops 1208418304 | bytes 1970176 | tf_op jit(solution)/shard_map/sb,cbk->csk/dot_general | solution.py:397
  11.7 3.2 %shard_map.114 = f32[4224,128]{1,0:T(8,128)} custom-call(f32[3,1024,128]{2,1,0:T(8,128)} %convolution_bitcast_fusion.1.xa_ref, s32[1024,128]{1,0:T(8,128)} %bitcast.266, f32[128,128]{1,0:T(8,128)} %concatenate.50.side_ref), custom_call_target="tpu_custom_call" | custom-call | tf_op jit(solution)/shard_map/pallas_call | solution.py:302
  14.9 10.6 %all-to-all-start = ((f32[128,1,4224]{2,1,0:T(1,128)}), f32[128,1,4224]{2,1,0:T(1,128)S(1)}, u32[]{:S(2)}, u32[]{:S(2)}) async-start(f32[128,1,4224]{2,1,0:T(1,128)} %bitcast.264), calls=%async_computation | async-start | bytes 4325376 | tf_op jit(solution)/shard_map/all_to_all | solution.py:447
  25.5 0.6 fusion.90
  26.1 0.6 pad.31.clone
  26.7 0.6 pad.32.clone
  27.4 0.7 gather_fusion.1
  28.2 0.7 gather_fusion
  29.0 1.7 %fusion.86 = (f32[256,1,128]{2,0,1:T(8,128)S(1)}, f32[256,1,128]{2,0,1:T(8,128)S(1)}, f32[256,1,128]{2,0,1:T(8,128)}) fusion(f32[256,3,128]{2,0,1:T(8,128)} %param.11), kind=kLoop, calls=%fused_computation.193 | loop fusion | bytes 786432 | tf_op jit(solution)/shard_map/slice | solution.py:64
  30.7 0.1 copy.95
  30.8 0.1 copy.96
  30.9 1.0 %copy.97 = f32[256,1,128]{0,2,1:T(8,128)S(1)} copy(f32[256,1,128]{2,0,1:T(8,128)} %get-tuple-element.24) | data formatting | bytes 262144
  32.0 2.2 %convolution_bitcast_fusion.3.xa_ref = f32[3,256,128]{2,1,0:T(8,128)} fusion(f32[1,256,128]{1,2,0:T(8,128)} %copy-done.2, f32[1,256,128]{1,2,0:T(8,128)} %copy-done.1, f32[1,256,128]{1,2,0:T(8,128)S(1)} %get-tuple-element.19, s32[256]{0:T(256)} %bitcast.279), kind=kOutput, calls=%fused_computation.6 | convolution fusion | flops 302252032 | bytes 787456 | tf_op jit(solution)/shard_map/sb,cbk->csk/dot_general | solution.py:397
  34.2 2.1 %convolution_bitcast_fusion.2.tb_ref = f32[6,256,128]{2,1,0:T(8,128)} fusion(f32[6,256,128]{1,2,0:T(8,128)S(1)} %fusion.23, s32[256]{0:T(256)} %bitcast.281), kind=kOutput, calls=%fused_computation.5 | convolution fusion | flops 604045312 | bytes 1573888 | tf_op jit(solution)/shard_map/sb,cbk->csk/dot_general | solution.py:397
  36.3 1.3 %maximum_maximum_fusion.1.aux_ref = f32[32,256]{1,0:T(8,128)} fusion(f32[12,256]{1,0:T(8,128)S(1)} %bitcast.271, f32[12,256]{1,0:T(8,128)S(1)} %bitcast.272, f32[32]{0:T(128)} %pad.32.clone, f32[32]{0:T(128)} %pad.31.clone), kind=kLoop, calls=%fused_computation.93 | loop fusion | flops 24576 | bytes 57600 | tf_op jit(solution)/shard_map/concatenate | solution.py:409
  37.7 3.4 %shard_map.113 = f32[32,256]{1,0:T(8,128)} custom-call(f32[3,256,128]{2,1,0:T(8,128)} %convolution_bitcast_fusion.3.xa_ref, f32[6,256,128]{2,1,0:T(8,128)} %convolution_bitcast_fusion.2.tb_ref, s32[256,128]{1,0:T(8,128)} %map_ref.1, f32[32,256]{1,0:T(8,128)} %maximum_maximum_fusion.1.aux_ref), custom_call_target="tpu_custom_call" | custom-call | tf_op jit(solution)/shard_map/pallas_call | solution.py:265
  41.0 0.8 slice_bitcast_fusion.2
  41.8 0.6 fusion.89
  42.4 0.6 fusion.65
  43.0 2.8 %gather_fusion.2 = f32[1024,12]{1,0:T(8,128)S(1)} fusion(f32[8,12]{1,0:T(8,128)S(1)} %bitcast.262, s32[1024]{0:T(1024)S(1)} %broadcast_clamp_fusion), kind=kCustom, calls=%fused_computation.2 | custom fusion | bytes 102400 | tf_op jit(solution)/shard_map/gather | solution.py:466
  45.8 0.2 copy.84
  46.0 0.7 fusion.67
  46.7 0.7 and_select_fusion.4
  47.4 0.7 and_select_fusion.3
  48.1 0.7 slice_multiply_fusion.3
  48.8 0.7 slice_multiply_fusion.2
  49.5 0.3 fusion.49
  49.8 1.0 %convolution_add_fusion.2 = f32[8,18]{1,0:T(8,128)S(1)} fusion(f32[8,18]{1,0:T(8,128)S(1)} %fusion.49, s32[256]{0:T(256)S(1)} %and_select_fusion.3, f32[256,6]{0,1:T(8,128)S(1)} %fusion.67, f32[256,6]{0,1:T(8,128)S(1)} %fusion.66, f32[256,6]{0,1:T(8,128)} %fusion.65), kind=kOutput, calls=%fused_computation.9 | convolution fusion | flops 455824 | bytes 20608 | tf_op jit(solution)/shard_map/dot_general | solution.py:404
  50.8 3.2 %convolution_bitcast_fusion.tb_ref = f32[6,1024,128]{2,1,0:T(8,128)} fusion(f32[6,256,128]{1,2,0:T(8,128)S(1)} %fusion.23, s32[1024]{0:T(1024)S(1)} %bitcast.274), kind=kOutput, calls=%fused_computation.3 | convolution fusion | flops 2416181248 | bytes 3936256 | tf_op jit(solution)/shard_map/sb,cbk->csk/dot_general | solution.py:397
  54.0 0.2 slice_reduce_fusion.1
  54.2 0.2 reshape_squeeze.3
  54.4 0.4 slice_reduce_fusion
  54.8 0.2 copy.98
  54.9 0.7 maximum_maximum_fusion.map_ref.aux_ref
  55.7 24.2 %shard_map.115 = (f32[32,1024]{1,0:T(8,128)}, f32[128,8,128]{2,1,0:T(8,128)}) custom-call(f32[4224,128]{1,0:T(8,128)} %bitcast.263, f32[6,1024,128]{2,1,0:T(8,128)} %convolution_bitcast_fusion.tb_ref, f32[32,1024]{1,0:T(8,128)} %maximum_maximum_fusion.map_ref.aux_ref, f32[32,1024]{1,0:T(8,128)} %maximum_maximum_fusion.map_ref.aux_ref), custom_call_target="tpu_custom_call" | custom-call | tf_op jit(solution)/shard_map/pallas_call | solution.py:265
  79.9 1.2 %copy.99 = f32[1024,32]{0,1:T(8,128)S(1)} copy(f32[1024,32]{1,0:T(8,128)} %bitcast.267) | data formatting | bytes 262144
  81.1 0.9 %slice_bitcast_fusion.1 = f32[1024,27]{0,1:T(8,128)S(1)} fusion(f32[32,1024]{1,0:T(8,128)} %get-tuple-element.4), kind=kLoop, calls=%fused_computation.68 | loop fusion | bytes 221184 | tf_op jit(solution)/shard_map/transpose | solution.py:310
  82.1 0.6 convolution_add_fusion.1
  82.7 0.6 convolution_add_fusion
  83.3 0.7 copy.86
  84.1 0.7 copy.87
  (65 shorter events, 1.9 us)
Async XLA Ops:
  3.5 5.9 %copy-start.7 = (s32[1024]{0:T(1024)}, s32[1024]{0:T(1024)S(1)}, u32[]{:S(2)}) copy-start(s32[1024]{0:T(1024)S(1)} %add_select_fusion) | copy-start | bytes 12292
  7.4 2.0 %copy-start.5 = (s32[1,1024]{1,0:T(1,128)S(1)}, s32[1,1024]{1,0:T(1,128)}, u32[]{:S(2)}) copy-start(s32[1,1024]{1,0:T(1,128)} %param.16) | copy-start | bytes 12292
  9.4 5.5 %copy-start.1 = (f32[1,256,128]{1,2,0:T(8,128)}, f32[1,256,128]{1,2,0:T(8,128)S(1)}, u32[]{:S(2)}) copy-start(f32[1,256,128]{1,2,0:T(8,128)S(1)} %get-tuple-element.17) | copy-start | bytes 393220
  9.5 5.4 %copy-start.2 = (f32[1,256,128]{1,2,0:T(8,128)}, f32[1,256,128]{1,2,0:T(8,128)S(1)}, u32[]{:S(2)}) copy-start(f32[1,256,128]{1,2,0:T(8,128)S(1)} %get-tuple-element.15) | copy-start | bytes 393220
  14.9 10.6 %copy-start.6 = (s32[2,256]{1,0:T(2,128)S(1)}, s32[2,256]{1,0:T(2,128)}, u32[]{:S(2)}) copy-start(s32[2,256]{1,0:T(2,128)} %param.14) | copy-start | bytes 6148
  14.9 12.4 %copy-start.4 = (s32[1,1024]{1,0:T(1,128)S(1)}, s32[1,1024]{1,0:T(1,128)}, u32[]{:S(2)}) copy-start(s32[1,1024]{1,0:T(1,128)} %param.18) | copy-start | bytes 12292
  14.9 39.1 %all-to-all-start = ((f32[128,1,4224]{2,1,0:T(1,128)}), f32[128,1,4224]{2,1,0:T(1,128)S(1)}, u32[]{:S(2)}, u32[]{:S(2)}) async-start(f32[128,1,4224]{2,1,0:T(1,128)} %bitcast.264), calls=%async_computation | async-start | bytes 4325376 | tf_op jit(solution)/shard_map/all_to_all | solution.py:447
  41.8 0.6 copy-start.3
  50.8 4.1 %copy-start.9 = (f32[32]{0:T(128)S(1)}, f32[32]{0:T(128)}, u32[]{:S(2)}) copy-start(f32[32]{0:T(128)} %pad.32.clone) | copy-start | bytes 388
  54.0 1.7 %copy-start = (f32[128,1,4224]{2,1,0:T(1,128)}, f32[128,1,4224]{2,1,0:T(1,128)S(1)}, u32[]{:S(2)}) copy-start(f32[128,1,4224]{2,1,0:T(1,128)S(1)} %all-to-all-done) | copy-start | bytes 6488068
  55.7 27.0 %copy-start.8 = (s32[1024]{0:T(1024)S(1)}, s32[1024]{0:T(1024)}, u32[]{:S(2)}) copy-start(s32[1024]{0:T(1024)} %copy-done.7) | copy-start | bytes 12292

commit v23 on v22

--- a/solution.py
+++ b/solution.py
@@ -194,7 +194,7 @@
     padded = jnp.concatenate([out_ref[...], jnp.zeros((128 - 32, chunk), jnp.float32)], axis=0)
     ret_ref[pl.ds(pl.multiple_of(step * peers, peers), peers)] = padded.T.reshape(peers, CAP, 128)
 
-    hold = jnp.minimum(4, last)
+    hold = jnp.minimum(3, last)
 
     @pl.when(step == hold)
     def _():

time: 85.8 us -> 86 us (level)
  the two profiles are of different devices: /device:TPU:23 before, /device:TPU:97 now
where the time goes in v23:
time: 86 us; the launch traced here: 85.1 us
  Pallas kernels  31.4 us (37%)
  local copies, waits for them, and re-layouts  21.2 us (25%)
  matrix products  12.6 us (15%)
  starting transfers between devices  10.2 us (12%)
  other arithmetic  8.71 us (10%)
  between operations  0.98 us (1%)
    pallas_call x2, Pallas kernels, pair_sums(): pl.pallas_call(functools.partial(_terms_kernel, from_cargo, n_band), out_...  28.2 us
    all_to_all x1, starting transfers between devices, local(): lax.all_to_all(cargo, axes, split_axis=0, concat_axis=0, tiled=True)  10.2 us
    dot_general x4, matrix products, pick_rows(): jnp.einsum('sb,cbk->csk', onehot, rows, precision=lax.Precision.HIGHEST)  9.72 us
    unnamed x31, local copies, waits for them, and re-layouts  5.07 us
    pallas_call x1, Pallas kernels, build_cargo(): pl.pallas_call(_cargo_kernel, out_shape=jax.ShapeDtypeStruct((slots // CA...  3.2 us
    gather x2, local copies, waits for them, and re-layouts, local(): frag_dirs[target_blocks // BF]  2.99 us
    dot_general x4, matrix products, frag_sums(): return jnp.dot(onehot.T, terms, precision=lax.Precision.HIGHEST)  2.38 us
    concatenate x2, other arithmetic, make_aux(): jnp.concatenate([dirs_a.T, dirs_b.T, valid[None, :], jnp.zeros((32 - 25,...  2.08 us
  transfers between devices with their start and end apart: 1, of which 0 were waited for; matrix products, arithmetic and copies ran while one was open for 29% of the time, Pallas kernels for 4%

profile of v23, /device:TPU:97, one launch (start us, length us, event | category | flops | bytes accessed | tf_op | source)
XLA Modules:
  0.0 85.1 jit_solution(1963155504284283906)
XLA Ops:
  0.6 0.8 slice_bitcast_fusion.5
  1.4 0.7 slice_multiply_fusion.4
  2.2 0.1 mul.431
  2.4 0.1 mul.439
  2.5 0.1 mul.399
  2.7 0.1 add.308
  2.8 0.7 add_select_fusion
  3.5 0.1 mul.435
  3.7 0.1 mul.427
  3.8 0.1 mul.412
  4.0 0.1 mul.406
  4.3 0.1 mul.416
  4.7 0.8 copy.76
  5.5 0.7 fusion.53
  6.3 0.1 reshape.1301
  6.4 1.1 %fusion.87 = (f32[256,1,128]{2,0,1:T(8,128)S(1)}, f32[256,1,128]{2,0,1:T(8,128)S(1)}, f32[256,1,128]{2,0,1:T(8,128)S(1)}) fusion(f32[256,3,128]{2,0,1:T(8,128)} %param.10), kind=kLoop, calls=%fused_computation.194 | loop fusion | bytes 786432 | tf_op jit(solution)/shard_map/slice | solution.py:58
  7.5 0.1 copy.92
  7.6 0.1 copy.93
  7.7 0.1 copy.94
  7.8 0.5 fusion.6
  8.3 0.2 copy.80
  8.5 0.2 reshape.1296
  8.7 0.6 concatenate.50.side_ref
  9.5 2.2 %convolution_bitcast_fusion.1.xa_ref = f32[3,1024,128]{2,1,0:T(8,128)} fusion(s32[1024]{0:T(1024)S(1)} %bitcast.277, f32[1,256,128]{1,2,0:T(8,128)S(1)} %get-tuple-element.15, f32[1,256,128]{1,2,0:T(8,128)S(1)} %get-tuple-element.17, f32[1,256,128]{1,2,0:T(8,128)S(1)} %get-tuple-element.19), kind=kOutput, calls=%fused_computation.4 | convolution fusion | flops 1208418304 | bytes 1970176 | tf_op jit(solution)/shard_map/sb,cbk->csk/dot_general | solution.py:397
  11.7 3.2 %shard_map.114 = f32[4224,128]{1,0:T(8,128)} custom-call(f32[3,1024,128]{2,1,0:T(8,128)} %convolution_bitcast_fusion.1.xa_ref, s32[1024,128]{1,0:T(8,128)} %bitcast.266, f32[128,128]{1,0:T(8,128)} %concatenate.50.side_ref), custom_call_target="tpu_custom_call" | custom-call | tf_op jit(solution)/shard_map/pallas_call | solution.py:302
  14.9 10.2 %all-to-all-start = ((f32[128,1,4224]{2,1,0:T(1,128)}), f32[128,1,4224]{2,1,0:T(1,128)S(1)}, u32[]{:S(2)}, u32[]{:S(2)}) async-start(f32[128,1,4224]{2,1,0:T(1,128)} %bitcast.264), calls=%async_computation | async-start | bytes 4325376 | tf_op jit(solution)/shard_map/all_to_all | solution.py:447
  25.1 0.6 fusion.90
  25.7 0.6 pad.31.clone
  26.3 0.6 pad.32.clone
  26.9 0.7 gather_fusion.1
  27.8 0.7 gather_fusion
  28.6 1.7 %fusion.86 = (f32[256,1,128]{2,0,1:T(8,128)S(1)}, f32[256,1,128]{2,0,1:T(8,128)S(1)}, f32[256,1,128]{2,0,1:T(8,128)}) fusion(f32[256,3,128]{2,0,1:T(8,128)} %param.11), kind=kLoop, calls=%fused_computation.193 | loop fusion | bytes 786432 | tf_op jit(solution)/shard_map/slice | solution.py:64
  30.3 0.1 copy.95
  30.4 0.1 copy.96
  30.5 1.0 %copy.97 = f32[256,1,128]{0,2,1:T(8,128)S(1)} copy(f32[256,1,128]{2,0,1:T(8,128)} %get-tuple-element.24) | data formatting | bytes 262144
  31.6 2.2 %convolution_bitcast_fusion.3.xa_ref = f32[3,256,128]{2,1,0:T(8,128)} fusion(f32[1,256,128]{1,2,0:T(8,128)} %copy-done.2, f32[1,256,128]{1,2,0:T(8,128)} %copy-done.1, f32[1,256,128]{1,2,0:T(8,128)S(1)} %get-tuple-element.19, s32[256]{0:T(256)} %bitcast.279), kind=kOutput, calls=%fused_computation.6 | convolution fusion | flops 302252032 | bytes 787456 | tf_op jit(solution)/shard_map/sb,cbk->csk/dot_general | solution.py:397
  33.8 2.1 %convolution_bitcast_fusion.2.tb_ref = f32[6,256,128]{2,1,0:T(8,128)} fusion(f32[6,256,128]{1,2,0:T(8,128)S(1)} %fusion.23, s32[256]{0:T(256)} %bitcast.281), kind=kOutput, calls=%fused_computation.5 | convolution fusion | flops 604045312 | bytes 1573888 | tf_op jit(solution)/shard_map/sb,cbk->csk/dot_general | solution.py:397
  35.9 1.3 %maximum_maximum_fusion.1.aux_ref = f32[32,256]{1,0:T(8,128)} fusion(f32[12,256]{1,0:T(8,128)S(1)} %bitcast.271, f32[12,256]{1,0:T(8,128)S(1)} %bitcast.272, f32[32]{0:T(128)} %pad.32.clone, f32[32]{0:T(128)} %pad.31.clone), kind=kLoop, calls=%fused_computation.93 | loop fusion | flops 24576 | bytes 57600 | tf_op jit(solution)/shard_map/concatenate | solution.py:409
  37.3 3.4 %shard_map.113 = f32[32,256]{1,0:T(8,128)} custom-call(f32[3,256,128]{2,1,0:T(8,128)} %convolution_bitcast_fusion.3.xa_ref, f32[6,256,128]{2,1,0:T(8,128)} %convolution_bitcast_fusion.2.tb_ref, s32[256,128]{1,0:T(8,128)} %map_ref.1, f32[32,256]{1,0:T(8,128)} %maximum_maximum_fusion.1.aux_ref), custom_call_target="tpu_custom_call" | custom-call | tf_op jit(solution)/shard_map/pallas_call | solution.py:265
  40.6 0.8 slice_bitcast_fusion.2
  41.4 0.6 fusion.89
  42.0 0.6 fusion.65
  42.6 2.8 %gather_fusion.2 = f32[1024,12]{1,0:T(8,128)S(1)} fusion(f32[8,12]{1,0:T(8,128)S(1)} %bitcast.262, s32[1024]{0:T(1024)S(1)} %broadcast_clamp_fusion), kind=kCustom, calls=%fused_computation.2 | custom fusion | bytes 102400 | tf_op jit(solution)/shard_map/gather | solution.py:466
  45.4 0.2 copy.84
  45.6 0.7 fusion.67
  46.3 0.7 and_select_fusion.4
  47.0 0.7 and_select_fusion.3
  47.7 0.7 slice_multiply_fusion.3
  48.4 0.7 slice_multiply_fusion.2
  49.1 0.3 fusion.49
  49.4 1.0 %convolution_add_fusion.2 = f32[8,18]{1,0:T(8,128)S(1)} fusion(f32[8,18]{1,0:T(8,128)S(1)} %fusion.49, s32[256]{0:T(256)S(1)} %and_select_fusion.3, f32[256,6]{0,1:T(8,128)S(1)} %fusion.67, f32[256,6]{0,1:T(8,128)S(1)} %fusion.66, f32[256,6]{0,1:T(8,128)} %fusion.65), kind=kOutput, calls=%fused_computation.9 | convolution fusion | flops 455824 | bytes 20608 | tf_op jit(solution)/shard_map/dot_general | solution.py:404
  50.4 3.2 %convolution_bitcast_fusion.tb_ref = f32[6,1024,128]{2,1,0:T(8,128)} fusion(f32[6,256,128]{1,2,0:T(8,128)S(1)} %fusion.23, s32[1024]{0:T(1024)S(1)} %bitcast.274), kind=kOutput, calls=%fused_computation.3 | convolution fusion | flops 2416181248 | bytes 3936256 | tf_op jit(solution)/shard_map/sb,cbk->csk/dot_general | solution.py:397
  53.6 0.2 slice_reduce_fusion.1
  53.8 0.2 reshape_squeeze.3
  54.0 0.4 slice_reduce_fusion
  54.3 0.2 copy.98
  54.5 0.7 maximum_maximum_fusion.map_ref.aux_ref
  55.3 24.8 %shard_map.115 = (f32[32,1024]{1,0:T(8,128)}, f32[128,8,128]{2,1,0:T(8,128)}) custom-call(f32[4224,128]{1,0:T(8,128)} %bitcast.263, f32[6,1024,128]{2,1,0:T(8,128)} %convolution_bitcast_fusion.tb_ref, f32[32,1024]{1,0:T(8,128)} %maximum_maximum_fusion.map_ref.aux_ref, f32[32,1024]{1,0:T(8,128)} %maximum_maximum_fusion.map_ref.aux_ref), custom_call_target="tpu_custom_call" | custom-call | tf_op jit(solution)/shard_map/pallas_call | solution.py:265
  80.1 1.2 %copy.99 = f32[1024,32]{0,1:T(8,128)S(1)} copy(f32[1024,32]{1,0:T(8,128)} %bitcast.267) | data formatting | bytes 262144
  81.4 0.9 %slice_bitcast_fusion.1 = f32[1024,27]{0,1:T(8,128)S(1)} fusion(f32[32,1024]{1,0:T(8,128)} %get-tuple-element.4), kind=kLoop, calls=%fused_computation.68 | loop fusion | bytes 221184 | tf_op jit(solution)/shard_map/transpose | solution.py:310
  82.4 0.6 convolution_add_fusion.1
  82.9 0.6 convolution_add_fusion
  83.6 0.7 copy.86
  84.4 0.7 copy.87
  (65 shorter events, 1.9 us)
Async XLA Ops:
  3.5 5.9 %copy-start.7 = (s32[1024]{0:T(1024)}, s32[1024]{0:T(1024)S(1)}, u32[]{:S(2)}) copy-start(s32[1024]{0:T(1024)S(1)} %add_select_fusion) | copy-start | bytes 12292
  7.4 2.0 %copy-start.5 = (s32[1,1024]{1,0:T(1,128)S(1)}, s32[1,1024]{1,0:T(1,128)}, u32[]{:S(2)}) copy-start(s32[1,1024]{1,0:T(1,128)} %param.16) | copy-start | bytes 12292
  9.4 5.5 %copy-start.1 = (f32[1,256,128]{1,2,0:T(8,128)}, f32[1,256,128]{1,2,0:T(8,128)S(1)}, u32[]{:S(2)}) copy-start(f32[1,256,128]{1,2,0:T(8,128)S(1)} %get-tuple-element.17) | copy-start | bytes 393220
  9.5 5.4 %copy-start.2 = (f32[1,256,128]{1,2,0:T(8,128)}, f32[1,256,128]{1,2,0:T(8,128)S(1)}, u32[]{:S(2)}) copy-start(f32[1,256,128]{1,2,0:T(8,128)S(1)} %get-tuple-element.15) | copy-start | bytes 393220
  14.9 10.2 %copy-start.6 = (s32[2,256]{1,0:T(2,128)S(1)}, s32[2,256]{1,0:T(2,128)}, u32[]{:S(2)}) copy-start(s32[2,256]{1,0:T(2,128)} %param.14) | copy-start | bytes 6148
  14.9 12.0 %copy-start.4 = (s32[1,1024]{1,0:T(1,128)S(1)}, s32[1,1024]{1,0:T(1,128)}, u32[]{:S(2)}) copy-start(s32[1,1024]{1,0:T(1,128)} %param.18) | copy-start | bytes 12292
  14.9 38.7 %all-to-all-start = ((f32[128,1,4224]{2,1,0:T(1,128)}), f32[128,1,4224]{2,1,0:T(1,128)S(1)}, u32[]{:S(2)}, u32[]{:S(2)}) async-start(f32[128,1,4224]{2,1,0:T(1,128)} %bitcast.264), calls=%async_computation | async-start | bytes 4325376 | tf_op jit(solution)/shard_map/all_to_all | solution.py:447
  41.4 0.6 copy-start.3
  50.4 4.1 %copy-start.9 = (f32[32]{0:T(128)S(1)}, f32[32]{0:T(128)}, u32[]{:S(2)}) copy-start(f32[32]{0:T(128)} %pad.32.clone) | copy-start | bytes 388
  53.6 1.7 %copy-start = (f32[128,1,4224]{2,1,0:T(1,128)}, f32[128,1,4224]{2,1,0:T(1,128)S(1)}, u32[]{:S(2)}) copy-start(f32[128,1,4224]{2,1,0:T(1,128)S(1)} %all-to-all-done) | copy-start | bytes 6488068
  55.3 27.7 %copy-start.8 = (s32[1024]{0:T(1024)S(1)}, s32[1024]{0:T(1024)}, u32[]{:S(2)}) copy-start(s32[1024]{0:T(1024)} %copy-done.7) | copy-start | bytes 12292

commit v24 on v23

--- a/solution.py
+++ b/solution.py
@@ -194,7 +194,7 @@
     padded = jnp.concatenate([out_ref[...], jnp.zeros((128 - 32, chunk), jnp.float32)], axis=0)
     ret_ref[pl.ds(pl.multiple_of(step * peers, peers), peers)] = padded.T.reshape(peers, CAP, 128)
 
-    hold = jnp.minimum(3, last)
+    hold = jnp.minimum(2, last)
 
     @pl.when(step == hold)
     def _():

time: 86 us -> 86.9 us (1.010)
  Pallas kernels: 31.4 us -> 32.3 us
    pallas_call x2, Pallas kernels: 28.2 us -> 29.2 us  [pair_sums(): pl.pallas_call(functools.partial(_terms_kernel, from_cargo, n_band), out_...]
where the time goes in v24:
time: 86.9 us; the launch traced here: 86 us
  Pallas kernels  32.3 us (37%)
  local copies, waits for them, and re-layouts  21.2 us (24%)
  matrix products  12.6 us (14%)
  starting transfers between devices  10.2 us (12%)
  other arithmetic  8.71 us (10%)
  between operations  0.98 us (1%)
    pallas_call x2, Pallas kernels, pair_sums(): pl.pallas_call(functools.partial(_terms_kernel, from_cargo, n_band), out_...  29.2 us
    all_to_all x1, starting transfers between devices, local(): lax.all_to_all(cargo, axes, split_axis=0, concat_axis=0, tiled=True)  10.2 us
    dot_general x4, matrix products, pick_rows(): jnp.einsum('sb,cbk->csk', onehot, rows, precision=lax.Precision.HIGHEST)  9.72 us
    unnamed x31, local copies, waits for them, and re-layouts  5.07 us
    pallas_call x1, Pallas kernels, build_cargo(): pl.pallas_call(_cargo_kernel, out_shape=jax.ShapeDtypeStruct((slots // CA...  3.2 us
    gather x2, local copies, waits for them, and re-layouts, local(): frag_dirs[target_blocks // BF]  2.99 us
    dot_general x4, matrix products, frag_sums(): return jnp.dot(onehot.T, terms, precision=lax.Precision.HIGHEST)  2.38 us
    concatenate x2, other arithmetic, make_aux(): jnp.concatenate([dirs_a.T, dirs_b.T, valid[None, :], jnp.zeros((32 - 25,...  2.08 us
  transfers between devices with their start and end apart: 1, of which 0 were waited for; matrix products, arithmetic and copies ran while one was open for 29% of the time, Pallas kernels for 4%

profile of v24, /device:TPU:97, one launch (start us, length us, event | category | flops | bytes accessed | tf_op | source)
XLA Modules:
  0.0 86.0 jit_solution(7719320931647717262)
XLA Ops:
  0.6 0.8 slice_bitcast_fusion.5
  1.4 0.7 slice_multiply_fusion.4
  2.2 0.1 mul.431
  2.4 0.1 mul.439
  2.5 0.1 mul.399
  2.7 0.1 add.308
  2.8 0.7 add_select_fusion
  3.5 0.1 mul.435
  3.7 0.1 mul.427
  3.8 0.1 mul.412
  4.0 0.1 mul.406
  4.3 0.1 mul.416
  4.7 0.8 copy.76
  5.5 0.7 fusion.53
  6.3 0.1 reshape.1301
  6.4 1.1 %fusion.87 = (f32[256,1,128]{2,0,1:T(8,128)S(1)}, f32[256,1,128]{2,0,1:T(8,128)S(1)}, f32[256,1,128]{2,0,1:T(8,128)S(1)}) fusion(f32[256,3,128]{2,0,1:T(8,128)} %param.10), kind=kLoop, calls=%fused_computation.194 | loop fusion | bytes 786432 | tf_op jit(solution)/shard_map/slice | solution.py:58
  7.5 0.1 copy.92
  7.6 0.1 copy.93
  7.7 0.1 copy.94
  7.8 0.5 fusion.6
  8.3 0.2 copy.80
  8.5 0.2 reshape.1296
  8.7 0.6 concatenate.50.side_ref
  9.5 2.2 %convolution_bitcast_fusion.1.xa_ref = f32[3,1024,128]{2,1,0:T(8,128)} fusion(s32[1024]{0:T(1024)S(1)} %bitcast.277, f32[1,256,128]{1,2,0:T(8,128)S(1)} %get-tuple-element.15, f32[1,256,128]{1,2,0:T(8,128)S(1)} %get-tuple-element.17, f32[1,256,128]{1,2,0:T(8,128)S(1)} %get-tuple-element.19), kind=kOutput, calls=%fused_computation.4 | convolution fusion | flops 1208418304 | bytes 1970176 | tf_op jit(solution)/shard_map/sb,cbk->csk/dot_general | solution.py:397
  11.7 3.2 %shard_map.114 = f32[4224,128]{1,0:T(8,128)} custom-call(f32[3,1024,128]{2,1,0:T(8,128)} %convolution_bitcast_fusion.1.xa_ref, s32[1024,128]{1,0:T(8,128)} %bitcast.266, f32[128,128]{1,0:T(8,128)} %concatenate.50.side_ref), custom_call_target="tpu_custom_call" | custom-call | tf_op jit(solution)/shard_map/pallas_call | solution.py:302
  14.9 10.2 %all-to-all-start = ((f32[128,1,4224]{2,1,0:T(1,128)}), f32[128,1,4224]{2,1,0:T(1,128)S(1)}, u32[]{:S(2)}, u32[]{:S(2)}) async-start(f32[128,1,4224]{2,1,0:T(1,128)} %bitcast.264), calls=%async_computation | async-start | bytes 4325376 | tf_op jit(solution)/shard_map/all_to_all | solution.py:447
  25.1 0.6 fusion.90
  25.7 0.6 pad.31.clone
  26.3 0.6 pad.32.clone
  26.9 0.7 gather_fusion.1
  27.8 0.7 gather_fusion
  28.6 1.7 %fusion.86 = (f32[256,1,128]{2,0,1:T(8,128)S(1)}, f32[256,1,128]{2,0,1:T(8,128)S(1)}, f32[256,1,128]{2,0,1:T(8,128)}) fusion(f32[256,3,128]{2,0,1:T(8,128)} %param.11), kind=kLoop, calls=%fused_computation.193 | loop fusion | bytes 786432 | tf_op jit(solution)/shard_map/slice | solution.py:64
  30.3 0.1 copy.95
  30.4 0.1 copy.96
  30.5 1.0 %copy.97 = f32[256,1,128]{0,2,1:T(8,128)S(1)} copy(f32[256,1,128]{2,0,1:T(8,128)} %get-tuple-element.24) | data formatting | bytes 262144
  31.6 2.2 %convolution_bitcast_fusion.3.xa_ref = f32[3,256,128]{2,1,0:T(8,128)} fusion(f32[1,256,128]{1,2,0:T(8,128)} %copy-done.2, f32[1,256,128]{1,2,0:T(8,128)} %copy-done.1, f32[1,256,128]{1,2,0:T(8,128)S(1)} %get-tuple-element.19, s32[256]{0:T(256)} %bitcast.279), kind=kOutput, calls=%fused_computation.6 | convolution fusion | flops 302252032 | bytes 787456 | tf_op jit(solution)/shard_map/sb,cbk->csk/dot_general | solution.py:397
  33.8 2.1 %convolution_bitcast_fusion.2.tb_ref = f32[6,256,128]{2,1,0:T(8,128)} fusion(f32[6,256,128]{1,2,0:T(8,128)S(1)} %fusion.23, s32[256]{0:T(256)} %bitcast.281), kind=kOutput, calls=%fused_computation.5 | convolution fusion | flops 604045312 | bytes 1573888 | tf_op jit(solution)/shard_map/sb,cbk->csk/dot_general | solution.py:397
  35.9 1.3 %maximum_maximum_fusion.1.aux_ref = f32[32,256]{1,0:T(8,128)} fusion(f32[12,256]{1,0:T(8,128)S(1)} %bitcast.271, f32[12,256]{1,0:T(8,128)S(1)} %bitcast.272, f32[32]{0:T(128)} %pad.32.clone, f32[32]{0:T(128)} %pad.31.clone), kind=kLoop, calls=%fused_computation.93 | loop fusion | flops 24576 | bytes 57600 | tf_op jit(solution)/shard_map/concatenate | solution.py:409
  37.3 3.4 %shard_map.113 = f32[32,256]{1,0:T(8,128)} custom-call(f32[3,256,128]{2,1,0:T(8,128)} %convolution_bitcast_fusion.3.xa_ref, f32[6,256,128]{2,1,0:T(8,128)} %convolution_bitcast_fusion.2.tb_ref, s32[256,128]{1,0:T(8,128)} %map_ref.1, f32[32,256]{1,0:T(8,128)} %maximum_maximum_fusion.1.aux_ref), custom_call_target="tpu_custom_call" | custom-call | tf_op jit(solution)/shard_map/pallas_call | solution.py:265
  40.6 0.8 slice_bitcast_fusion.2
  41.4 0.6 fusion.89
  42.0 0.6 fusion.65
  42.6 2.8 %gather_fusion.2 = f32[1024,12]{1,0:T(8,128)S(1)} fusion(f32[8,12]{1,0:T(8,128)S(1)} %bitcast.262, s32[1024]{0:T(1024)S(1)} %broadcast_clamp_fusion), kind=kCustom, calls=%fused_computation.2 | custom fusion | bytes 102400 | tf_op jit(solution)/shard_map/gather | solution.py:466
  45.4 0.2 copy.84
  45.6 0.7 fusion.67
  46.3 0.7 and_select_fusion.4
  47.0 0.7 and_select_fusion.3
  47.7 0.7 slice_multiply_fusion.3
  48.4 0.7 slice_multiply_fusion.2
  49.1 0.3 fusion.49
  49.4 1.0 %convolution_add_fusion.2 = f32[8,18]{1,0:T(8,128)S(1)} fusion(f32[8,18]{1,0:T(8,128)S(1)} %fusion.49, s32[256]{0:T(256)S(1)} %and_select_fusion.3, f32[256,6]{0,1:T(8,128)S(1)} %fusion.67, f32[256,6]{0,1:T(8,128)S(1)} %fusion.66, f32[256,6]{0,1:T(8,128)} %fusion.65), kind=kOutput, calls=%fused_computation.9 | convolution fusion | flops 455824 | bytes 20608 | tf_op jit(solution)/shard_map/dot_general | solution.py:404
  50.4 3.2 %convolution_bitcast_fusion.tb_ref = f32[6,1024,128]{2,1,0:T(8,128)} fusion(f32[6,256,128]{1,2,0:T(8,128)S(1)} %fusion.23, s32[1024]{0:T(1024)S(1)} %bitcast.274), kind=kOutput, calls=%fused_computation.3 | convolution fusion | flops 2416181248 | bytes 3936256 | tf_op jit(solution)/shard_map/sb,cbk->csk/dot_general | solution.py:397
  53.6 0.2 slice_reduce_fusion.1
  53.8 0.2 reshape_squeeze.3
  54.0 0.4 slice_reduce_fusion
  54.3 0.2 copy.98
  54.5 0.7 maximum_maximum_fusion.map_ref.aux_ref
  55.3 25.8 %shard_map.115 = (f32[32,1024]{1,0:T(8,128)}, f32[128,8,128]{2,1,0:T(8,128)}) custom-call(f32[4224,128]{1,0:T(8,128)} %bitcast.263, f32[6,1024,128]{2,1,0:T(8,128)} %convolution_bitcast_fusion.tb_ref, f32[32,1024]{1,0:T(8,128)} %maximum_maximum_fusion.map_ref.aux_ref, f32[32,1024]{1,0:T(8,128)} %maximum_maximum_fusion.map_ref.aux_ref), custom_call_target="tpu_custom_call" | custom-call | tf_op jit(solution)/shard_map/pallas_call | solution.py:265
  81.1 1.2 %copy.99 = f32[1024,32]{0,1:T(8,128)S(1)} copy(f32[1024,32]{1,0:T(8,128)} %bitcast.267) | data formatting | bytes 262144
  82.3 0.9 %slice_bitcast_fusion.1 = f32[1024,27]{0,1:T(8,128)S(1)} fusion(f32[32,1024]{1,0:T(8,128)} %get-tuple-element.4), kind=kLoop, calls=%fused_computation.68 | loop fusion | bytes 221184 | tf_op jit(solution)/shard_map/transpose | solution.py:310
  83.3 0.6 convolution_add_fusion.1
  83.9 0.6 convolution_add_fusion
  84.6 0.7 copy.86
  85.3 0.7 copy.87
  (65 shorter events, 1.9 us)
Async XLA Ops:
  3.5 5.9 %copy-start.7 = (s32[1024]{0:T(1024)}, s32[1024]{0:T(1024)S(1)}, u32[]{:S(2)}) copy-start(s32[1024]{0:T(1024)S(1)} %add_select_fusion) | copy-start | bytes 12292
  7.4 2.0 %copy-start.5 = (s32[1,1024]{1,0:T(1,128)S(1)}, s32[1,1024]{1,0:T(1,128)}, u32[]{:S(2)}) copy-start(s32[1,1024]{1,0:T(1,128)} %param.16) | copy-start | bytes 12292
  9.4 5.5 %copy-start.1 = (f32[1,256,128]{1,2,0:T(8,128)}, f32[1,256,128]{1,2,0:T(8,128)S(1)}, u32[]{:S(2)}) copy-start(f32[1,256,128]{1,2,0:T(8,128)S(1)} %get-tuple-element.17) | copy-start | bytes 393220
  9.5 5.4 %copy-start.2 = (f32[1,256,128]{1,2,0:T(8,128)}, f32[1,256,128]{1,2,0:T(8,128)S(1)}, u32[]{:S(2)}) copy-start(f32[1,256,128]{1,2,0:T(8,128)S(1)} %get-tuple-element.15) | copy-start | bytes 393220
  14.9 10.2 %copy-start.6 = (s32[2,256]{1,0:T(2,128)S(1)}, s32[2,256]{1,0:T(2,128)}, u32[]{:S(2)}) copy-start(s32[2,256]{1,0:T(2,128)} %param.14) | copy-start | bytes 6148
  14.9 12.0 %copy-start.4 = (s32[1,1024]{1,0:T(1,128)S(1)}, s32[1,1024]{1,0:T(1,128)}, u32[]{:S(2)}) copy-start(s32[1,1024]{1,0:T(1,128)} %param.18) | copy-start | bytes 12292
  14.9 38.7 %all-to-all-start = ((f32[128,1,4224]{2,1,0:T(1,128)}), f32[128,1,4224]{2,1,0:T(1,128)S(1)}, u32[]{:S(2)}, u32[]{:S(2)}) async-start(f32[128,1,4224]{2,1,0:T(1,128)} %bitcast.264), calls=%async_computation | async-start | bytes 4325376 | tf_op jit(solution)/shard_map/all_to_all | solution.py:447
  41.4 0.6 copy-start.3
  50.4 4.1 %copy-start.9 = (f32[32]{0:T(128)S(1)}, f32[32]{0:T(128)}, u32[]{:S(2)}) copy-start(f32[32]{0:T(128)} %pad.32.clone) | copy-start | bytes 388
  53.6 1.7 %copy-start = (f32[128,1,4224]{2,1,0:T(1,128)}, f32[128,1,4224]{2,1,0:T(1,128)S(1)}, u32[]{:S(2)}) copy-start(f32[128,1,4224]{2,1,0:T(1,128)S(1)} %all-to-all-done) | copy-start | bytes 6488068
  55.3 28.6 %copy-start.8 = (s32[1024]{0:T(1024)S(1)}, s32[1024]{0:T(1024)}, u32[]{:S(2)}) copy-start(s32[1024]{0:T(1024)} %copy-done.7) | copy-start | bytes 12292

commit v25 on v23

--- a/solution.py
+++ b/solution.py
@@ -132,7 +132,7 @@
         return tuple(a + v for a, v in zip(accs, vals))
 
     zero = jnp.zeros((8, chunk), jnp.float32)
-    accs = lax.fori_loop(0, 128 // 8, body, (zero,) * N_QTY, unroll=8)
+    accs = lax.fori_loop(0, 128 // 8, body, (zero,) * N_QTY, unroll=True)
     valid = aux_ref[24:25, :]
     for q in range(N_QTY):
         out_ref[q : q + 1, :] = jnp.sum(accs[q], axis=0, keepdims=True) * valid

time: 86 us -> 85 us (0.988)
  the two profiles are of different devices: /device:TPU:97 before, /device:TPU:121 now
where the time goes in v25:
time: 85 us; the launch traced here: 84 us
  Pallas kernels  30.5 us (36%)
  local copies, waits for them, and re-layouts  21.2 us (25%)
  matrix products  12.6 us (15%)
  starting transfers between devices  10 us (12%)
  other arithmetic  8.71 us (10%)
  between operations  0.98 us (1%)
    pallas_call x2, Pallas kernels, pair_sums(): pl.pallas_call(functools.partial(_terms_kernel, from_cargo, n_band), out_...  27.3 us
    all_to_all x1, starting transfers between devices, local(): lax.all_to_all(cargo, axes, split_axis=0, concat_axis=0, tiled=True)  10 us
    dot_general x4, matrix products, pick_rows(): jnp.einsum('sb,cbk->csk', onehot, rows, precision=lax.Precision.HIGHEST)  9.72 us
    unnamed x31, local copies, waits for them, and re-layouts  5.07 us
    pallas_call x1, Pallas kernels, build_cargo(): pl.pallas_call(_cargo_kernel, out_shape=jax.ShapeDtypeStruct((slots // CA...  3.2 us
    gather x2, local copies, waits for them, and re-layouts, local(): frag_dirs[target_blocks // BF]  2.99 us
    dot_general x4, matrix products, frag_sums(): return jnp.dot(onehot.T, terms, precision=lax.Precision.HIGHEST)  2.38 us
    concatenate x2, other arithmetic, make_aux(): jnp.concatenate([dirs_a.T, dirs_b.T, valid[None, :], jnp.zeros((32 - 25,...  2.08 us
  transfers between devices with their start and end apart: 1, of which 0 were waited for; matrix products, arithmetic and copies ran while one was open for 30% of the time, Pallas kernels for 4%

profile of v25, /device:TPU:121, one launch (start us, length us, event | category | flops | bytes accessed | tf_op | source)
XLA Modules:
  0.0 84.0 jit_solution(3156018720483739344)
XLA Ops:
  0.6 0.8 slice_bitcast_fusion.5
  1.4 0.7 slice_multiply_fusion.4
  2.2 0.1 mul.431
  2.4 0.1 mul.439
  2.5 0.1 mul.399
  2.7 0.1 add.308
  2.8 0.7 add_select_fusion
  3.5 0.1 mul.435
  3.7 0.1 mul.427
  3.8 0.1 mul.412
  4.0 0.1 mul.406
  4.4 0.1 add.294
  4.7 0.8 copy.76
  5.5 0.7 fusion.53
  6.3 0.1 reshape.1301
  6.4 1.1 %fusion.87 = (f32[256,1,128]{2,0,1:T(8,128)S(1)}, f32[256,1,128]{2,0,1:T(8,128)S(1)}, f32[256,1,128]{2,0,1:T(8,128)S(1)}) fusion(f32[256,3,128]{2,0,1:T(8,128)} %param.10), kind=kLoop, calls=%fused_computation.194 | loop fusion | bytes 786432 | tf_op jit(solution)/shard_map/slice | solution.py:58
  7.5 0.1 copy.92
  7.6 0.1 copy.93
  7.7 0.1 copy.94
  7.8 0.5 fusion.6
  8.3 0.2 copy.80
  8.5 0.2 reshape.1296
  8.7 0.6 concatenate.50.side_ref
  9.5 2.2 %convolution_bitcast_fusion.1.xa_ref = f32[3,1024,128]{2,1,0:T(8,128)} fusion(s32[1024]{0:T(1024)S(1)} %bitcast.277, f32[1,256,128]{1,2,0:T(8,128)S(1)} %get-tuple-element.15, f32[1,256,128]{1,2,0:T(8,128)S(1)} %get-tuple-element.17, f32[1,256,128]{1,2,0:T(8,128)S(1)} %get-tuple-element.19), kind=kOutput, calls=%fused_computation.4 | convolution fusion | flops 1208418304 | bytes 1970176 | tf_op jit(solution)/shard_map/sb,cbk->csk/dot_general | solution.py:397
  11.7 3.2 %shard_map.114 = f32[4224,128]{1,0:T(8,128)} custom-call(f32[3,1024,128]{2,1,0:T(8,128)} %convolution_bitcast_fusion.1.xa_ref, s32[1024,128]{1,0:T(8,128)} %bitcast.266, f32[128,128]{1,0:T(8,128)} %concatenate.50.side_ref), custom_call_target="tpu_custom_call" | custom-call | tf_op jit(solution)/shard_map/pallas_call | solution.py:302
  14.9 10.0 %all-to-all-start = ((f32[128,1,4224]{2,1,0:T(1,128)}), f32[128,1,4224]{2,1,0:T(1,128)S(1)}, u32[]{:S(2)}, u32[]{:S(2)}) async-start(f32[128,1,4224]{2,1,0:T(1,128)} %bitcast.264), calls=%async_computation | async-start | bytes 4325376 | tf_op jit(solution)/shard_map/all_to_all | solution.py:447
  25.0 0.6 fusion.90
  25.6 0.6 pad.31.clone
  26.2 0.6 pad.32.clone
  26.8 0.7 gather_fusion.1
  27.6 0.7 gather_fusion
  28.4 1.7 %fusion.86 = (f32[256,1,128]{2,0,1:T(8,128)S(1)}, f32[256,1,128]{2,0,1:T(8,128)S(1)}, f32[256,1,128]{2,0,1:T(8,128)}) fusion(f32[256,3,128]{2,0,1:T(8,128)} %param.11), kind=kLoop, calls=%fused_computation.193 | loop fusion | bytes 786432 | tf_op jit(solution)/shard_map/slice | solution.py:64
  30.2 0.1 copy.95
  30.3 0.1 copy.96
  30.4 1.0 %copy.97 = f32[256,1,128]{0,2,1:T(8,128)S(1)} copy(f32[256,1,128]{2,0,1:T(8,128)} %get-tuple-element.24) | data formatting | bytes 262144
  31.5 2.2 %convolution_bitcast_fusion.3.xa_ref = f32[3,256,128]{2,1,0:T(8,128)} fusion(f32[1,256,128]{1,2,0:T(8,128)} %copy-done.2, f32[1,256,128]{1,2,0:T(8,128)} %copy-done.1, f32[1,256,128]{1,2,0:T(8,128)S(1)} %get-tuple-element.19, s32[256]{0:T(256)} %bitcast.279), kind=kOutput, calls=%fused_computation.6 | convolution fusion | flops 302252032 | bytes 787456 | tf_op jit(solution)/shard_map/sb,cbk->csk/dot_general | solution.py:397
  33.6 2.1 %convolution_bitcast_fusion.2.tb_ref = f32[6,256,128]{2,1,0:T(8,128)} fusion(f32[6,256,128]{1,2,0:T(8,128)S(1)} %fusion.23, s32[256]{0:T(256)} %bitcast.281), kind=kOutput, calls=%fused_computation.5 | convolution fusion | flops 604045312 | bytes 1573888 | tf_op jit(solution)/shard_map/sb,cbk->csk/dot_general | solution.py:397
  35.8 1.3 %maximum_maximum_fusion.1.aux_ref = f32[32,256]{1,0:T(8,128)} fusion(f32[12,256]{1,0:T(8,128)S(1)} %bitcast.271, f32[12,256]{1,0:T(8,128)S(1)} %bitcast.272, f32[32]{0:T(128)} %pad.32.clone, f32[32]{0:T(128)} %pad.31.clone), kind=kLoop, calls=%fused_computation.93 | loop fusion | flops 24576 | bytes 57600 | tf_op jit(solution)/shard_map/concatenate | solution.py:409
  37.1 3.1 %shard_map.113 = f32[32,256]{1,0:T(8,128)} custom-call(f32[3,256,128]{2,1,0:T(8,128)} %convolution_bitcast_fusion.3.xa_ref, f32[6,256,128]{2,1,0:T(8,128)} %convolution_bitcast_fusion.2.tb_ref, s32[256,128]{1,0:T(8,128)} %map_ref.1, f32[32,256]{1,0:T(8,128)} %maximum_maximum_fusion.1.aux_ref), custom_call_target="tpu_custom_call" | custom-call | tf_op jit(solution)/shard_map/pallas_call | solution.py:265
  40.3 0.8 slice_bitcast_fusion.2
  41.0 0.6 fusion.89
  41.6 0.6 fusion.65
  42.2 2.8 %gather_fusion.2 = f32[1024,12]{1,0:T(8,128)S(1)} fusion(f32[8,12]{1,0:T(8,128)S(1)} %bitcast.262, s32[1024]{0:T(1024)S(1)} %broadcast_clamp_fusion), kind=kCustom, calls=%fused_computation.2 | custom fusion | bytes 102400 | tf_op jit(solution)/shard_map/gather | solution.py:466
  45.0 0.2 copy.84
  45.2 0.7 fusion.67
  46.0 0.7 and_select_fusion.4
  46.7 0.7 and_select_fusion.3
  47.3 0.7 slice_multiply_fusion.3
  48.0 0.7 slice_multiply_fusion.2
  48.8 0.3 fusion.49
  49.1 1.0 %convolution_add_fusion.2 = f32[8,18]{1,0:T(8,128)S(1)} fusion(f32[8,18]{1,0:T(8,128)S(1)} %fusion.49, s32[256]{0:T(256)S(1)} %and_select_fusion.3, f32[256,6]{0,1:T(8,128)S(1)} %fusion.67, f32[256,6]{0,1:T(8,128)S(1)} %fusion.66, f32[256,6]{0,1:T(8,128)} %fusion.65), kind=kOutput, calls=%fused_computation.9 | convolution fusion | flops 455824 | bytes 20608 | tf_op jit(solution)/shard_map/dot_general | solution.py:404
  50.0 3.2 %convolution_bitcast_fusion.tb_ref = f32[6,1024,128]{2,1,0:T(8,128)} fusion(f32[6,256,128]{1,2,0:T(8,128)S(1)} %fusion.23, s32[1024]{0:T(1024)S(1)} %bitcast.274), kind=kOutput, calls=%fused_computation.3 | convolution fusion | flops 2416181248 | bytes 3936256 | tf_op jit(solution)/shard_map/sb,cbk->csk/dot_general | solution.py:397
  53.2 0.2 slice_reduce_fusion.1
  53.4 0.2 reshape_squeeze.3
  53.6 0.4 slice_reduce_fusion
  54.0 0.2 copy.98
  54.2 0.7 maximum_maximum_fusion.map_ref.aux_ref
  54.9 24.2 %shard_map.115 = (f32[32,1024]{1,0:T(8,128)}, f32[128,8,128]{2,1,0:T(8,128)}) custom-call(f32[4224,128]{1,0:T(8,128)} %bitcast.263, f32[6,1024,128]{2,1,0:T(8,128)} %convolution_bitcast_fusion.tb_ref, f32[32,1024]{1,0:T(8,128)} %maximum_maximum_fusion.map_ref.aux_ref, f32[32,1024]{1,0:T(8,128)} %maximum_maximum_fusion.map_ref.aux_ref), custom_call_target="tpu_custom_call" | custom-call | tf_op jit(solution)/shard_map/pallas_call | solution.py:265
  79.1 1.2 %copy.99 = f32[1024,32]{0,1:T(8,128)S(1)} copy(f32[1024,32]{1,0:T(8,128)} %bitcast.267) | data formatting | bytes 262144
  80.3 0.9 %slice_bitcast_fusion.1 = f32[1024,27]{0,1:T(8,128)S(1)} fusion(f32[32,1024]{1,0:T(8,128)} %get-tuple-element.4), kind=kLoop, calls=%fused_computation.68 | loop fusion | bytes 221184 | tf_op jit(solution)/shard_map/transpose | solution.py:310
  81.3 0.6 convolution_add_fusion.1
  81.9 0.6 convolution_add_fusion
  82.6 0.7 copy.86
  83.3 0.7 copy.87
  (65 shorter events, 1.9 us)
Async XLA Ops:
  3.5 5.9 %copy-start.7 = (s32[1024]{0:T(1024)}, s32[1024]{0:T(1024)S(1)}, u32[]{:S(2)}) copy-start(s32[1024]{0:T(1024)S(1)} %add_select_fusion) | copy-start | bytes 12292
  7.4 2.0 %copy-start.5 = (s32[1,1024]{1,0:T(1,128)S(1)}, s32[1,1024]{1,0:T(1,128)}, u32[]{:S(2)}) copy-start(s32[1,1024]{1,0:T(1,128)} %param.16) | copy-start | bytes 12292
  9.4 5.5 %copy-start.1 = (f32[1,256,128]{1,2,0:T(8,128)}, f32[1,256,128]{1,2,0:T(8,128)S(1)}, u32[]{:S(2)}) copy-start(f32[1,256,128]{1,2,0:T(8,128)S(1)} %get-tuple-element.17) | copy-start | bytes 393220
  9.5 5.4 %copy-start.2 = (f32[1,256,128]{1,2,0:T(8,128)}, f32[1,256,128]{1,2,0:T(8,128)S(1)}, u32[]{:S(2)}) copy-start(f32[1,256,128]{1,2,0:T(8,128)S(1)} %get-tuple-element.15) | copy-start | bytes 393220
  14.9 10.1 %copy-start.6 = (s32[2,256]{1,0:T(2,128)S(1)}, s32[2,256]{1,0:T(2,128)}, u32[]{:S(2)}) copy-start(s32[2,256]{1,0:T(2,128)} %param.14) | copy-start | bytes 6148
  14.9 11.9 %copy-start.4 = (s32[1,1024]{1,0:T(1,128)S(1)}, s32[1,1024]{1,0:T(1,128)}, u32[]{:S(2)}) copy-start(s32[1,1024]{1,0:T(1,128)} %param.18) | copy-start | bytes 12292
  14.9 38.3 %all-to-all-start = ((f32[128,1,4224]{2,1,0:T(1,128)}), f32[128,1,4224]{2,1,0:T(1,128)S(1)}, u32[]{:S(2)}, u32[]{:S(2)}) async-start(f32[128,1,4224]{2,1,0:T(1,128)} %bitcast.264), calls=%async_computation | async-start | bytes 4325376 | tf_op jit(solution)/shard_map/all_to_all | solution.py:447
  41.0 0.6 copy-start.3
  50.0 4.1 %copy-start.9 = (f32[32]{0:T(128)S(1)}, f32[32]{0:T(128)}, u32[]{:S(2)}) copy-start(f32[32]{0:T(128)} %pad.32.clone) | copy-start | bytes 388
  53.2 1.7 %copy-start = (f32[128,1,4224]{2,1,0:T(1,128)}, f32[128,1,4224]{2,1,0:T(1,128)S(1)}, u32[]{:S(2)}) copy-start(f32[128,1,4224]{2,1,0:T(1,128)S(1)} %all-to-all-done) | copy-start | bytes 6488068
  54.9 27.0 %copy-start.8 = (s32[1024]{0:T(1024)S(1)}, s32[1024]{0:T(1024)}, u32[]{:S(2)}) copy-start(s32[1024]{0:T(1024)} %copy-done.7) | copy-start | bytes 12292

commit v26 on v25

--- a/solution.py
+++ b/solution.py
@@ -194,7 +194,7 @@
     padded = jnp.concatenate([out_ref[...], jnp.zeros((128 - 32, chunk), jnp.float32)], axis=0)
     ret_ref[pl.ds(pl.multiple_of(step * peers, peers), peers)] = padded.T.reshape(peers, CAP, 128)
 
-    hold = jnp.minimum(3, last)
+    hold = jnp.minimum(4, last)
 
     @pl.when(step == hold)
     def _():

time: 85 us -> 85.2 us (level)
  the two profiles are of different devices: /device:TPU:121 before, /device:TPU:31 now
where the time goes in v26:
time: 85.2 us; the launch traced here: 84.2 us
  Pallas kernels  30.2 us (35%)
  local copies, waits for them, and re-layouts  21.2 us (25%)
  matrix products  12.6 us (15%)
  starting transfers between devices  10.6 us (12%)
  other arithmetic  8.71 us (10%)
  between operations  0.98 us (1%)
    pallas_call x2, Pallas kernels, pair_sums(): pl.pallas_call(functools.partial(_terms_kernel, from_cargo, n_band), out_...  27 us
    all_to_all x1, starting transfers between devices, local(): lax.all_to_all(cargo, axes, split_axis=0, concat_axis=0, tiled=True)  10.6 us
    dot_general x4, matrix products, pick_rows(): jnp.einsum('sb,cbk->csk', onehot, rows, precision=lax.Precision.HIGHEST)  9.72 us
    unnamed x31, local copies, waits for them, and re-layouts  5.07 us
    pallas_call x1, Pallas kernels, build_cargo(): pl.pallas_call(_cargo_kernel, out_shape=jax.ShapeDtypeStruct((slots // CA...  3.2 us
    gather x2, local copies, waits for them, and re-layouts, local(): frag_dirs[target_blocks // BF]  2.99 us
    dot_general x4, matrix products, frag_sums(): return jnp.dot(onehot.T, terms, precision=lax.Precision.HIGHEST)  2.38 us
    concatenate x2, other arithmetic, make_aux(): jnp.concatenate([dirs_a.T, dirs_b.T, valid[None, :], jnp.zeros((32 - 25,...  2.08 us
  transfers between devices with their start and end apart: 1, of which 0 were waited for; matrix products, arithmetic and copies ran while one was open for 30% of the time, Pallas kernels for 4%

profile of v26, /device:TPU:31, one launch (start us, length us, event | category | flops | bytes accessed | tf_op | source)
XLA Modules:
  0.0 84.2 jit_solution(14644588747698157379)
XLA Ops:
  0.6 0.8 slice_bitcast_fusion.5
  1.4 0.7 slice_multiply_fusion.4
  2.2 0.1 mul.431
  2.4 0.1 mul.439
  2.5 0.1 mul.399
  2.7 0.1 add.308
  2.8 0.7 add_select_fusion
  3.5 0.1 mul.435
  3.7 0.1 mul.427
  3.8 0.1 mul.412
  4.0 0.1 mul.406
  4.3 0.1 mul.416
  4.7 0.8 copy.76
  5.5 0.7 fusion.53
  6.3 0.1 reshape.1301
  6.4 1.1 %fusion.87 = (f32[256,1,128]{2,0,1:T(8,128)S(1)}, f32[256,1,128]{2,0,1:T(8,128)S(1)}, f32[256,1,128]{2,0,1:T(8,128)S(1)}) fusion(f32[256,3,128]{2,0,1:T(8,128)} %param.10), kind=kLoop, calls=%fused_computation.194 | loop fusion | bytes 786432 | tf_op jit(solution)/shard_map/slice | solution.py:58
  7.5 0.1 copy.92
  7.6 0.1 copy.93
  7.7 0.1 copy.94
  7.8 0.5 fusion.6
  8.3 0.2 copy.80
  8.5 0.2 reshape.1296
  8.7 0.6 concatenate.50.side_ref
  9.5 2.2 %convolution_bitcast_fusion.1.xa_ref = f32[3,1024,128]{2,1,0:T(8,128)} fusion(s32[1024]{0:T(1024)S(1)} %bitcast.277, f32[1,256,128]{1,2,0:T(8,128)S(1)} %get-tuple-element.15, f32[1,256,128]{1,2,0:T(8,128)S(1)} %get-tuple-element.17, f32[1,256,128]{1,2,0:T(8,128)S(1)} %get-tuple-element.19), kind=kOutput, calls=%fused_computation.4 | convolution fusion | flops 1208418304 | bytes 1970176 | tf_op jit(solution)/shard_map/sb,cbk->csk/dot_general | solution.py:397
  11.7 3.2 %shard_map.114 = f32[4224,128]{1,0:T(8,128)} custom-call(f32[3,1024,128]{2,1,0:T(8,128)} %convolution_bitcast_fusion.1.xa_ref, s32[1024,128]{1,0:T(8,128)} %bitcast.266, f32[128,128]{1,0:T(8,128)} %concatenate.50.side_ref), custom_call_target="tpu_custom_call" | custom-call | tf_op jit(solution)/shard_map/pallas_call | solution.py:302
  14.9 10.6 %all-to-all-start = ((f32[128,1,4224]{2,1,0:T(1,128)}), f32[128,1,4224]{2,1,0:T(1,128)S(1)}, u32[]{:S(2)}, u32[]{:S(2)}) async-start(f32[128,1,4224]{2,1,0:T(1,128)} %bitcast.264), calls=%async_computation | async-start | bytes 4325376 | tf_op jit(solution)/shard_map/all_to_all | solution.py:447
  25.5 0.6 fusion.90
  26.1 0.6 pad.31.clone
  26.7 0.6 pad.32.clone
  27.3 0.7 gather_fusion.1
  28.1 0.7 gather_fusion
  29.0 1.7 %fusion.86 = (f32[256,1,128]{2,0,1:T(8,128)S(1)}, f32[256,1,128]{2,0,1:T(8,128)S(1)}, f32[256,1,128]{2,0,1:T(8,128)}) fusion(f32[256,3,128]{2,0,1:T(8,128)} %param.11), kind=kLoop, calls=%fused_computation.193 | loop fusion | bytes 786432 | tf_op jit(solution)/shard_map/slice | solution.py:64
  30.7 0.1 copy.95
  30.8 0.1 copy.96
  30.9 1.0 %copy.97 = f32[256,1,128]{0,2,1:T(8,128)S(1)} copy(f32[256,1,128]{2,0,1:T(8,128)} %get-tuple-element.24) | data formatting | bytes 262144
  32.0 2.2 %convolution_bitcast_fusion.3.xa_ref = f32[3,256,128]{2,1,0:T(8,128)} fusion(f32[1,256,128]{1,2,0:T(8,128)} %copy-done.2, f32[1,256,128]{1,2,0:T(8,128)} %copy-done.1, f32[1,256,128]{1,2,0:T(8,128)S(1)} %get-tuple-element.19, s32[256]{0:T(256)} %bitcast.279), kind=kOutput, calls=%fused_computation.6 | convolution fusion | flops 302252032 | bytes 787456 | tf_op jit(solution)/shard_map/sb,cbk->csk/dot_general | solution.py:397
  34.2 2.1 %convolution_bitcast_fusion.2.tb_ref = f32[6,256,128]{2,1,0:T(8,128)} fusion(f32[6,256,128]{1,2,0:T(8,128)S(1)} %fusion.23, s32[256]{0:T(256)} %bitcast.281), kind=kOutput, calls=%fused_computation.5 | convolution fusion | flops 604045312 | bytes 1573888 | tf_op jit(solution)/shard_map/sb,cbk->csk/dot_general | solution.py:397
  36.3 1.3 %maximum_maximum_fusion.1.aux_ref = f32[32,256]{1,0:T(8,128)} fusion(f32[12,256]{1,0:T(8,128)S(1)} %bitcast.271, f32[12,256]{1,0:T(8,128)S(1)} %bitcast.272, f32[32]{0:T(128)} %pad.32.clone, f32[32]{0:T(128)} %pad.31.clone), kind=kLoop, calls=%fused_computation.93 | loop fusion | flops 24576 | bytes 57600 | tf_op jit(solution)/shard_map/concatenate | solution.py:409
  37.6 3.1 %shard_map.113 = f32[32,256]{1,0:T(8,128)} custom-call(f32[3,256,128]{2,1,0:T(8,128)} %convolution_bitcast_fusion.3.xa_ref, f32[6,256,128]{2,1,0:T(8,128)} %convolution_bitcast_fusion.2.tb_ref, s32[256,128]{1,0:T(8,128)} %map_ref.1, f32[32,256]{1,0:T(8,128)} %maximum_maximum_fusion.1.aux_ref), custom_call_target="tpu_custom_call" | custom-call | tf_op jit(solution)/shard_map/pallas_call | solution.py:265
  40.8 0.8 slice_bitcast_fusion.2
  41.6 0.6 fusion.89
  42.2 0.6 fusion.65
  42.8 2.8 %gather_fusion.2 = f32[1024,12]{1,0:T(8,128)S(1)} fusion(f32[8,12]{1,0:T(8,128)S(1)} %bitcast.262, s32[1024]{0:T(1024)S(1)} %broadcast_clamp_fusion), kind=kCustom, calls=%fused_computation.2 | custom fusion | bytes 102400 | tf_op jit(solution)/shard_map/gather | solution.py:466
  45.6 0.2 copy.84
  45.8 0.7 fusion.67
  46.5 0.7 and_select_fusion.4
  47.2 0.7 and_select_fusion.3
  47.9 0.7 slice_multiply_fusion.3
  48.6 0.7 slice_multiply_fusion.2
  49.3 0.3 fusion.49
  49.6 1.0 %convolution_add_fusion.2 = f32[8,18]{1,0:T(8,128)S(1)} fusion(f32[8,18]{1,0:T(8,128)S(1)} %fusion.49, s32[256]{0:T(256)S(1)} %and_select_fusion.3, f32[256,6]{0,1:T(8,128)S(1)} %fusion.67, f32[256,6]{0,1:T(8,128)S(1)} %fusion.66, f32[256,6]{0,1:T(8,128)} %fusion.65), kind=kOutput, calls=%fused_computation.9 | convolution fusion | flops 455824 | bytes 20608 | tf_op jit(solution)/shard_map/dot_general | solution.py:404
  50.6 3.2 %convolution_bitcast_fusion.tb_ref = f32[6,1024,128]{2,1,0:T(8,128)} fusion(f32[6,256,128]{1,2,0:T(8,128)S(1)} %fusion.23, s32[1024]{0:T(1024)S(1)} %bitcast.274), kind=kOutput, calls=%fused_computation.3 | convolution fusion | flops 2416181248 | bytes 3936256 | tf_op jit(solution)/shard_map/sb,cbk->csk/dot_general | solution.py:397
  53.8 0.2 slice_reduce_fusion.1
  53.9 0.2 reshape_squeeze.3
  54.1 0.4 slice_reduce_fusion
  54.5 0.2 copy.98
  54.7 0.7 maximum_maximum_fusion.map_ref.aux_ref
  55.4 23.8 %shard_map.115 = (f32[32,1024]{1,0:T(8,128)}, f32[128,8,128]{2,1,0:T(8,128)}) custom-call(f32[4224,128]{1,0:T(8,128)} %bitcast.263, f32[6,1024,128]{2,1,0:T(8,128)} %convolution_bitcast_fusion.tb_ref, f32[32,1024]{1,0:T(8,128)} %maximum_maximum_fusion.map_ref.aux_ref, f32[32,1024]{1,0:T(8,128)} %maximum_maximum_fusion.map_ref.aux_ref), custom_call_target="tpu_custom_call" | custom-call | tf_op jit(solution)/shard_map/pallas_call | solution.py:265
  79.3 1.2 %copy.99 = f32[1024,32]{0,1:T(8,128)S(1)} copy(f32[1024,32]{1,0:T(8,128)} %bitcast.267) | data formatting | bytes 262144
  80.6 0.9 %slice_bitcast_fusion.1 = f32[1024,27]{0,1:T(8,128)S(1)} fusion(f32[32,1024]{1,0:T(8,128)} %get-tuple-element.4), kind=kLoop, calls=%fused_computation.68 | loop fusion | bytes 221184 | tf_op jit(solution)/shard_map/transpose | solution.py:310
  81.6 0.6 convolution_add_fusion.1
  82.1 0.6 convolution_add_fusion
  82.8 0.7 copy.86
  83.6 0.7 copy.87
  (65 shorter events, 1.9 us)
Async XLA Ops:
  3.5 5.9 %copy-start.7 = (s32[1024]{0:T(1024)}, s32[1024]{0:T(1024)S(1)}, u32[]{:S(2)}) copy-start(s32[1024]{0:T(1024)S(1)} %add_select_fusion) | copy-start | bytes 12292
  7.4 2.0 %copy-start.5 = (s32[1,1024]{1,0:T(1,128)S(1)}, s32[1,1024]{1,0:T(1,128)}, u32[]{:S(2)}) copy-start(s32[1,1024]{1,0:T(1,128)} %param.16) | copy-start | bytes 12292
  9.4 5.5 %copy-start.1 = (f32[1,256,128]{1,2,0:T(8,128)}, f32[1,256,128]{1,2,0:T(8,128)S(1)}, u32[]{:S(2)}) copy-start(f32[1,256,128]{1,2,0:T(8,128)S(1)} %get-tuple-element.17) | copy-start | bytes 393220
  9.5 5.4 %copy-start.2 = (f32[1,256,128]{1,2,0:T(8,128)}, f32[1,256,128]{1,2,0:T(8,128)S(1)}, u32[]{:S(2)}) copy-start(f32[1,256,128]{1,2,0:T(8,128)S(1)} %get-tuple-element.15) | copy-start | bytes 393220
  14.9 10.6 %copy-start.6 = (s32[2,256]{1,0:T(2,128)S(1)}, s32[2,256]{1,0:T(2,128)}, u32[]{:S(2)}) copy-start(s32[2,256]{1,0:T(2,128)} %param.14) | copy-start | bytes 6148
  14.9 12.4 %copy-start.4 = (s32[1,1024]{1,0:T(1,128)S(1)}, s32[1,1024]{1,0:T(1,128)}, u32[]{:S(2)}) copy-start(s32[1,1024]{1,0:T(1,128)} %param.18) | copy-start | bytes 12292
  14.9 38.9 %all-to-all-start = ((f32[128,1,4224]{2,1,0:T(1,128)}), f32[128,1,4224]{2,1,0:T(1,128)S(1)}, u32[]{:S(2)}, u32[]{:S(2)}) async-start(f32[128,1,4224]{2,1,0:T(1,128)} %bitcast.264), calls=%async_computation | async-start | bytes 4325376 | tf_op jit(solution)/shard_map/all_to_all | solution.py:447
  41.6 0.6 copy-start.3
  50.6 4.1 %copy-start.9 = (f32[32]{0:T(128)S(1)}, f32[32]{0:T(128)}, u32[]{:S(2)}) copy-start(f32[32]{0:T(128)} %pad.32.clone) | copy-start | bytes 388
  53.8 1.7 %copy-start = (f32[128,1,4224]{2,1,0:T(1,128)}, f32[128,1,4224]{2,1,0:T(1,128)S(1)}, u32[]{:S(2)}) copy-start(f32[128,1,4224]{2,1,0:T(1,128)S(1)} %all-to-all-done) | copy-start | bytes 6488068
  55.4 26.7 %copy-start.8 = (s32[1024]{0:T(1024)S(1)}, s32[1024]{0:T(1024)}, u32[]{:S(2)}) copy-start(s32[1024]{0:T(1024)} %copy-done.7) | copy-start | bytes 12292
